TPU v7x, 32 devices: a whole 2x2x4 slice. The times are simulated.
32 devices in a mesh: fsdp: 32 (over z, y, x, core).
Axes of the slice: x: 2, y: 2, z: 4, core: 2. Of those that a mesh axis runs over, the one named last changes fastest.
Arguments:
- tokens: bfloat16 [64, 128, 2048], P(None, 'fsdp'), may hold values from -6 to 6
- lengths: int32 [64], replicated, may hold values from 1 to 128, 6144 in all
- dealing: int32 [64], replicated, may hold values from 0 to 63, each once
- w_query: bfloat16 [2048, 2048], P('fsdp'), may hold values from -0.125 to 0.125
- w_key: bfloat16 [2048, 2048], P('fsdp'), may hold values from -0.125 to 0.125
- w_value: bfloat16 [2048, 2048], P('fsdp'), may hold values from -0.125 to 0.125
- w_output: bfloat16 [2048, 2048], P('fsdp'), may hold values from -0.125 to 0.125
- query_gain: bfloat16 [2048], P('fsdp'), may hold values from 1 to 2.5
- key_gain: bfloat16 [2048], P('fsdp'), may hold values from 1 to 2.5
- attn_gain: bfloat16 [2048], P('fsdp'), may hold values from 0.099609375 to 1.8984375
- w_gate: bfloat16 [2048, 8192], P(None, 'fsdp'), may hold values from -0.125 to 0.125
- w_up: bfloat16 [2048, 8192], P(None, 'fsdp'), may hold values from -0.125 to 0.125
- w_down: bfloat16 [8192, 2048], P('fsdp'), may hold values from -0.0625 to 0.0625
- mlp_gain: bfloat16 [2048], P('fsdp'), may hold values from 0.099609375 to 1.8984375
- cotangent: bfloat16 [64, 128, 2048], P('fsdp'), may hold values from -6 to 6
Outputs:
- block_out: bfloat16 [64, 128, 2048], P('fsdp')
- input_grad: bfloat16 [64, 128, 2048], P(None, 'fsdp')
- w_query_grad: float32 [2048, 2048], P('fsdp')
- w_key_grad: float32 [2048, 2048], P('fsdp')
- w_value_grad: float32 [2048, 2048], P('fsdp')
- w_output_grad: float32 [2048, 2048], P('fsdp')
- query_gain_grad: float32 [2048], P('fsdp')
- key_gain_grad: float32 [2048], P('fsdp')
- attn_gain_grad: float32 [2048], P('fsdp')
- w_gate_grad: float32 [2048, 8192], P(None, 'fsdp')
- w_up_grad: float32 [2048, 8192], P(None, 'fsdp')
- w_down_grad: float32 [8192, 2048], P('fsdp')
- mlp_gain_grad: float32 [2048], P('fsdp')
Inputs may be any that keep to these rules, and one draw needn't show every extreme that they name: `lengths`: the longest sequence has exactly 128 used slots. `dealing`: each sequence number appears once.
All inputs are finite; a program needn't handle non-finite values.
Results may differ from a plain program's by a relative error of at most 0.017.
Values may be sent and summed in bfloat16 or wider, within the bound.
No kernel may reach another device: no remote copies, remote signals or barrier semaphores. Data moves between devices by JAX's collectives and lax.ppermute only.
A program may use at most 512 MiB of HBM per device.

v0:
```python
import math

import jax
import jax.numpy as jnp
from jax import lax
from jax.sharding import PartitionSpec as P

HEADS = 16


norm_eps = 1e-06
rope_base = 500000.0


def rotary_tables(length, head_dim):
    half_dim = head_dim // 2
    exponents = jnp.arange(half_dim, dtype=jnp.float32) * (2.0 / head_dim)
    frequency = jnp.power(jnp.float32(rope_base), -exponents)
    angles = jnp.arange(length, dtype=jnp.float32)[:, None] * frequency[None, :]
    return (jnp.cos(angles), jnp.sin(angles))


def rotate(values, cosines, sines):
    half_dim = values.shape[-1] // 2
    first_half = values[..., :half_dim]
    second_half = values[..., half_dim:]
    cos_rows = cosines[:, None, :]
    sin_rows = sines[:, None, :]
    return jnp.concatenate(
        [
            first_half * cos_rows - second_half * sin_rows,
            second_half * cos_rows + first_half * sin_rows,
        ],
        axis=-1,
    )


def norm_forward(values, gain_vec):
    inverse = lax.rsqrt(jnp.mean(values * values, axis=-1, keepdims=True) + norm_eps)
    return (values * inverse * gain_vec, inverse)


def norm_backward(values, inverse, gain_vec, grad_out):
    normed = values * inverse
    gain_grad = jnp.sum(normed * grad_out, axis=0)
    scaled = grad_out * gain_vec
    return (
        inverse * (scaled - normed * jnp.mean(scaled * normed, axis=-1, keepdims=True)),
        gain_grad,
    )


def per_device(
    tokens,
    lengths,
    dealing,
    w_query,
    w_key,
    w_value,
    w_output,
    query_gain,
    key_gain,
    attn_gain,
    w_gate,
    w_up,
    w_down,
    mlp_gain,
    cotangent,
):
    rank = lax.axis_index("fsdp")
    micro_count = cotangent.shape[0]
    seq_len = cotangent.shape[1]
    model_width = cotangent.shape[2]
    row_count = micro_count * seq_len
    head_dim = model_width // HEADS
    cosines, sines = rotary_tables(seq_len, head_dim)
    positions = jnp.arange(seq_len, dtype=jnp.int32)
    causal = (positions[None, :] <= positions[:, None])[None, None]
    qk_scale = 1.0 / math.sqrt(head_dim)
    outgoing = jnp.take(tokens, dealing, axis=0)
    arrived = lax.all_to_all(outgoing, "fsdp", split_axis=0, concat_axis=1, tiled=True)
    x_low = arrived.reshape(row_count, model_width)
    own_seqs = lax.dynamic_slice_in_dim(dealing, rank * micro_count, micro_count)
    own_lengths = jnp.take(lengths, own_seqs)
    valid_mask = (
        (positions[None, :] < own_lengths[:, None]).astype(jnp.float32).reshape(row_count, 1)
    )
    attn_set = (
        lax.all_gather(w_query, "fsdp", axis=0, tiled=True),
        lax.all_gather(w_key, "fsdp", axis=0, tiled=True),
        lax.all_gather(w_value, "fsdp", axis=0, tiled=True),
        lax.all_gather(w_output, "fsdp", axis=0, tiled=True),
        lax.all_gather(query_gain, "fsdp", axis=0, tiled=True),
        lax.all_gather(key_gain, "fsdp", axis=0, tiled=True),
        lax.all_gather(attn_gain, "fsdp", axis=0, tiled=True),
    )
    full_query, full_key, full_value, full_output, gain_query, gain_key, gain_attn = attn_set
    query_raw = jnp.dot(x_low, full_query, preferred_element_type=jnp.float32)
    key_raw = jnp.dot(x_low, full_key, preferred_element_type=jnp.float32)
    value_raw = jnp.dot(x_low, full_value, preferred_element_type=jnp.float32)
    query_norm, query_inv = norm_forward(query_raw, gain_query.astype(jnp.float32))
    key_norm, key_inv = norm_forward(key_raw, gain_key.astype(jnp.float32))
    head_shape = (micro_count, seq_len, HEADS, head_dim)
    query_low = rotate(query_norm.reshape(head_shape), cosines, sines).astype(jnp.bfloat16)
    key_low = rotate(key_norm.reshape(head_shape), cosines, sines).astype(jnp.bfloat16)
    value_low = value_raw.astype(jnp.bfloat16).reshape(head_shape)
    scores = (
        jnp.einsum("gthe,guhe->ghtu", query_low, key_low, preferred_element_type=jnp.float32)
        * qk_scale
    )
    scores = jnp.where(causal, scores, -1e30)
    row_peak = jnp.max(scores, axis=-1, keepdims=True)
    exp_scores = jnp.exp(scores - row_peak)
    row_total = jnp.sum(exp_scores, axis=-1, keepdims=True)
    log_total = row_peak + jnp.log(row_total)
    soft_low = (exp_scores / row_total).astype(jnp.bfloat16)
    attended = jnp.einsum(
        "ghtu,guhe->gthe", soft_low, value_low, preferred_element_type=jnp.float32
    ).reshape(row_count, model_width)
    attended_low = attended.astype(jnp.bfloat16)
    out_raw = jnp.dot(attended_low, full_output, preferred_element_type=jnp.float32)
    out_norm, out_inv = norm_forward(out_raw, gain_attn.astype(jnp.float32))
    hidden = x_low.astype(jnp.float32) + out_norm
    hidden_low = hidden.astype(jnp.bfloat16)
    mlp_set = (
        lax.all_gather(w_gate, "fsdp", axis=1, tiled=True),
        lax.all_gather(w_up, "fsdp", axis=1, tiled=True),
        lax.all_gather(w_down, "fsdp", axis=0, tiled=True),
        lax.all_gather(mlp_gain, "fsdp", axis=0, tiled=True),
    )
    full_gate, full_up, full_down, gain_mlp = mlp_set
    gate_proj = jnp.dot(hidden_low, full_gate, preferred_element_type=jnp.float32)
    up_proj = jnp.dot(hidden_low, full_up, preferred_element_type=jnp.float32)
    act_value = jax.nn.silu(gate_proj)
    act_low = (act_value * up_proj).astype(jnp.bfloat16)
    down_proj = jnp.dot(act_low, full_down, preferred_element_type=jnp.float32)
    down_norm, down_inv = norm_forward(down_proj, gain_mlp.astype(jnp.float32))
    block_out = (
        (valid_mask * (hidden + down_norm))
        .astype(jnp.bfloat16)
        .reshape(micro_count, seq_len, model_width)
    )
    grad_out = valid_mask * cotangent.reshape(row_count, model_width).astype(jnp.float32)
    back_gate, back_up, back_down, back_gain_mlp = mlp_set
    grad_down, grad_gain_mlp = norm_backward(
        down_proj, down_inv, back_gain_mlp.astype(jnp.float32), grad_out
    )
    grad_down_low = grad_down.astype(jnp.bfloat16)
    grad_act = jnp.einsum("td,fd->tf", grad_down_low, back_down, preferred_element_type=jnp.float32)
    sigma_gate = jax.nn.sigmoid(gate_proj)
    grad_gate = grad_act * up_proj * sigma_gate * (1.0 + gate_proj * (1.0 - sigma_gate))
    grad_up = grad_act * act_value
    grad_gate_low = grad_gate.astype(jnp.bfloat16)
    grad_up_low = grad_up.astype(jnp.bfloat16)
    grad_hidden = grad_out + jnp.einsum(
        "tf,df->td", grad_gate_low, back_gate, preferred_element_type=jnp.float32
    )
    grad_hidden = grad_hidden + jnp.einsum(
        "tf,df->td", grad_up_low, back_up, preferred_element_type=jnp.float32
    )
    down_term = jnp.einsum("tf,td->fd", act_low, grad_down_low, preferred_element_type=jnp.float32)
    down_part = lax.psum_scatter(down_term, "fsdp", scatter_dimension=0, tiled=True)
    gate_term = jnp.einsum(
        "td,tf->df", hidden_low, grad_gate_low, preferred_element_type=jnp.float32
    )
    gate_part = lax.psum_scatter(gate_term, "fsdp", scatter_dimension=1, tiled=True)
    up_term = jnp.einsum("td,tf->df", hidden_low, grad_up_low, preferred_element_type=jnp.float32)
    up_part = lax.psum_scatter(up_term, "fsdp", scatter_dimension=1, tiled=True)
    back_query, back_key, back_value, back_output, back_gain_q, back_gain_k, back_gain_a = attn_set
    grad_out_raw, grad_gain_attn = norm_backward(
        out_raw, out_inv, back_gain_a.astype(jnp.float32), grad_hidden
    )
    grad_out_low = grad_out_raw.astype(jnp.bfloat16)
    grad_attended = jnp.einsum(
        "te,de->td", grad_out_low, back_output, preferred_element_type=jnp.float32
    )
    grad_att_low = grad_attended.astype(jnp.bfloat16).reshape(head_shape)
    scores_again = (
        jnp.einsum("gthe,guhe->ghtu", query_low, key_low, preferred_element_type=jnp.float32)
        * qk_scale
    )
    scores_again = jnp.where(causal, scores_again, -1e30)
    soft_again = jnp.exp(scores_again - log_total)
    grad_soft = jnp.einsum(
        "gthe,guhe->ghtu", grad_att_low, value_low, preferred_element_type=jnp.float32
    )
    row_delta = jnp.sum(soft_again * grad_soft, axis=-1, keepdims=True)
    grad_scores = (soft_again * (grad_soft - row_delta)).astype(jnp.bfloat16)
    grad_q_rot = (
        jnp.einsum("ghtu,guhe->gthe", grad_scores, key_low, preferred_element_type=jnp.float32)
        * qk_scale
    )
    grad_k_rot = (
        jnp.einsum("ghtu,gthe->guhe", grad_scores, query_low, preferred_element_type=jnp.float32)
        * qk_scale
    )
    grad_value_low = (
        jnp.einsum("ghtu,gthe->guhe", soft_low, grad_att_low, preferred_element_type=jnp.float32)
        .reshape(row_count, model_width)
        .astype(jnp.bfloat16)
    )
    grad_q_norm = rotate(grad_q_rot, cosines, -sines).reshape(row_count, model_width)
    grad_k_norm = rotate(grad_k_rot, cosines, -sines).reshape(row_count, model_width)
    grad_query, grad_gain_q = norm_backward(
        query_raw, query_inv, back_gain_q.astype(jnp.float32), grad_q_norm
    )
    grad_key, grad_gain_k = norm_backward(
        key_raw, key_inv, back_gain_k.astype(jnp.float32), grad_k_norm
    )
    grad_query_low = grad_query.astype(jnp.bfloat16)
    grad_key_low = grad_key.astype(jnp.bfloat16)
    grad_input = grad_hidden + jnp.einsum(
        "te,de->td", grad_query_low, back_query, preferred_element_type=jnp.float32
    )
    grad_input = grad_input + jnp.einsum(
        "te,de->td", grad_key_low, back_key, preferred_element_type=jnp.float32
    )
    grad_input = grad_input + jnp.einsum(
        "te,de->td", grad_value_low, back_value, preferred_element_type=jnp.float32
    )
    qkv_term = jnp.einsum(
        "td,te->de",
        x_low,
        jnp.concatenate([grad_query_low, grad_key_low, grad_value_low], axis=1),
        preferred_element_type=jnp.float32,
    )
    output_term = jnp.einsum(
        "td,te->de", attended_low, grad_out_low, preferred_element_type=jnp.float32
    )
    gain_terms = jnp.stack([grad_gain_q, grad_gain_k, grad_gain_attn, grad_gain_mlp])
    qkv_part, output_part, gain_part = (
        lax.psum_scatter(qkv_term, "fsdp", scatter_dimension=0, tiled=True),
        lax.psum_scatter(output_term, "fsdp", scatter_dimension=0, tiled=True),
        lax.psum_scatter(gain_terms, "fsdp", scatter_dimension=1, tiled=True),
    )
    returned = lax.all_to_all(
        grad_input.astype(jnp.bfloat16).reshape(micro_count, seq_len, model_width),
        "fsdp",
        split_axis=1,
        concat_axis=0,
        tiled=True,
    )
    input_grad = jnp.zeros_like(tokens).at[dealing].set(returned)
    return (
        block_out,
        input_grad,
        qkv_part[:, :model_width],
        qkv_part[:, model_width : 2 * model_width],
        qkv_part[:, 2 * model_width :],
        output_part,
        gain_part[0],
        gain_part[1],
        gain_part[2],
        gate_part,
        up_part,
        down_part,
        gain_part[3],
    )


def solution(mesh):
    placed = (
        P(None, "fsdp", None),
        P(),
        P(),
        P("fsdp", None),
        P("fsdp", None),
        P("fsdp", None),
        P("fsdp", None),
        P("fsdp"),
        P("fsdp"),
        P("fsdp"),
        P(None, "fsdp"),
        P(None, "fsdp"),
        P("fsdp", None),
        P("fsdp"),
        P("fsdp", None, None),
    )
    return jax.shard_map(
        per_device,
        mesh=mesh,
        in_specs=placed,
        out_specs=(
            P("fsdp", None, None),
            P(None, "fsdp", None),
            P("fsdp", None),
            P("fsdp", None),
            P("fsdp", None),
            P("fsdp", None),
            P("fsdp"),
            P("fsdp"),
            P("fsdp"),
            P(None, "fsdp"),
            P(None, "fsdp"),
            P("fsdp", None),
            P("fsdp"),
        ),
        check_vma=False,
    )
```

profile of v0, /device:TPU:0, one launch (start us, length us, event | category | flops | bytes accessed | tf_op | source)
XLA Modules:
  0.0 3931.7 jit_solution(14557478950918816996)
XLA Ops:
  12.5 1.4 gather_fusion.1
  14.0 1.5 broadcast_select_fusion
  15.6 7.3 all-to-all-start
  24.0 57.3 %all-reduce.4 = (bf16[2048]{0:T(1024)(128)(2,1)S(1)}, bf16[2048]{0:T(1024)(128)(2,1)S(1)}, bf16[2048]{0:T(1024)(128)(2,1)S(1)}, bf16[2048]{0:T(1024)(128)(2,1)S(1)}) all-reduce(bf16[2048]{0:T(1024)(128)(2,1)S(1)} %dynamic-update-slice.1, bf16[2048]{0:T(1024)(128)(2,1)S(1)} %dynamic-update-slice, ...), channel_id=1, replica_groups=mesh['fsdp'=32] {'fsdp'}, use_global_device_ids=true, to_apply=%add.1 | all-reduce | flops 8192 | bytes 32768
  84.2 17.5 all-gather.8.cloned.1.call-done
  101.6 5.7 fusion.21
  107.4 1.2 copy.112
  108.6 72.0 %all-gather.10.cloned.1.call-done = bf16[2048,2048]{1,0:T(8,128)(2,1)} async-done(((bf16[64,2048]{1,0:T(8,128)(2,1)}), bf16[2048,2048]{1,0:T(8,128)(2,1)}) %all-gather.10.cloned.1.call-update) | async-done | bytes 8388624 | tf_op jit(solution)/shard_map/all_gather | solution.py:89
  180.6 5.8 multiply_reduce_fusion.8
  188.1 71.4 %all-gather.12.cloned.1.call-done = bf16[2048,2048]{1,0:T(8,128)(2,1)} async-done(((bf16[64,2048]{1,0:T(8,128)(2,1)}), bf16[2048,2048]{1,0:T(8,128)(2,1)}) %all-gather.12.cloned.1.call-update) | async-done | bytes 8388624 | tf_op jit(solution)/shard_map/all_gather | solution.py:90
  259.5 5.8 multiply_reduce_fusion.7
  267.1 1.4 fusion.41
  268.5 2.7 subtract_convert_fusion.1
  271.3 1.7 fusion.45
  274.5 1.7 fusion.19
  276.2 2.6 copy.78
  278.9 59.5 %all-gather.14.cloned.1.call-done = bf16[2048,2048]{1,0:T(8,128)(2,1)} async-done(((bf16[64,2048]{1,0:T(8,128)(2,1)}), bf16[2048,2048]{1,0:T(8,128)(2,1)}) %all-gather.14.cloned.1.call-update) | async-done | bytes 8388624 | tf_op jit(solution)/shard_map/all_gather | solution.py:92
  338.3 6.1 multiply_reduce_fusion.6
  344.5 1.3 copy-done.7
  345.8 1.4 fusion.23
  347.2 185.3 %all-gather.16.cloned.1.call-done = bf16[2048,8192]{1,0:T(8,128)(2,1)} async-done(((bf16[2048,256]{1,0:T(8,128)(2,1)}), bf16[2048,8192]{1,0:T(8,128)(2,1)}) %all-gather.16.cloned.1.call-update) | async-done | bytes 33554448 | tf_op jit(solution)/shard_map/all_gather | solution.py:126
  532.5 18.0 fusion.46
  550.5 176.2 %all-gather.18.cloned.1.call-done = bf16[2048,8192]{1,0:T(8,128)(2,1)} async-done(((bf16[2048,256]{1,0:T(8,128)(2,1)}), bf16[2048,8192]{1,0:T(8,128)(2,1)}) %all-gather.18.cloned.1.call-update) | async-done | bytes 33554448 | tf_op jit(solution)/shard_map/all_gather | solution.py:127
  726.7 24.5 multiply_convert_fusion.2
  751.3 171.6 %all-gather.20.cloned.1.call-done = bf16[8192,2048]{1,0:T(8,128)(2,1)} async-done(((bf16[256,2048]{1,0:T(8,128)(2,1)}), bf16[8192,2048]{1,0:T(8,128)(2,1)}) %all-gather.20.cloned.1.call-update) | async-done | bytes 33554448 | tf_op jit(solution)/shard_map/all_gather | solution.py:128
  922.9 16.4 multiply_reduce_fusion.5
  940.9 2.2 fusion.16
  943.1 22.0 multiply_convert_fusion
  965.1 17.4 convolution_add_fusion.1
  982.5 18.7 multiply_reduce_fusion
  1001.1 2.7 multiply_convert_fusion.6
  1003.8 6.1 fusion.22
  1009.9 1.2 copy.116
  1011.2 2.8 copy.89
  1014.0 2.2 multiply_reduce_fusion.3
  1020.5 1.8 fusion.20
  1022.4 1.6 multiply_subtract_fusion
  1024.6 1.2 copy.84
  1028.8 1.2 copy.88
  1031.4 2.3 multiply_convert_fusion.3
  1033.7 1.9 copy.91
  1035.6 1.3 copy.153
  1037.0 1.4 copy.102
  1038.4 21.0 fusion.1
  1059.5 1.2 copy-done.18
  1061.0 8.1 fusion.24
  1070.4 25.4 fusion.47
  1095.8 25.4 fusion.48
  1121.3 1.2 copy-done.20
  1122.4 25.6 fusion.49
  1148.1 6.5 convolution_add_fusion.4
  1154.6 6.0 convolution_add_fusion.3
  1160.6 2.4 fusion.7
  1163.0 2.0 copy.92
  1165.1 2.9 all-to-all-start.1
  1168.0 3.5 reduce-scatter.19.cloned.1.call-done
  1174.8 19.4 all-to-all-done.1
  1195.3 2.5 scatter_fusion
  1197.8 408.7 %reduce-scatter.9.cloned.1.call-done = f32[64,6144]{1,0:T(8,128)} async-done(((f32[2048,6144]{1,0:T(8,128)}), f32[64,6144]{1,0:T(8,128)}) %reduce-scatter.9.cloned.1.call-update) | async-done | bytes 1572880 | tf_op jit(solution)/shard_map/reduce_scatter | solution.py:232
  1606.5 2.5 fusion.43
  1609.1 182.0 %reduce-scatter.11.cloned.1.call-done = f32[64,2048]{1,0:T(8,128)} async-done(((f32[2048,2048]{1,0:T(8,128)}), f32[64,2048]{1,0:T(8,128)}) %reduce-scatter.11.cloned.1.call-update) | async-done | bytes 524304 | tf_op jit(solution)/shard_map/reduce_scatter | solution.py:233
  1791.1 707.4 %reduce-scatter.13.cloned.1.call-done = f32[2048,256]{1,0:T(8,128)} async-done(((f32[2048,8192]{1,0:T(8,128)}), f32[2048,256]{1,0:T(8,128)}) %reduce-scatter.13.cloned.1.call-update) | async-done | bytes 2097168 | tf_op jit(solution)/shard_map/reduce_scatter | solution.py:166
  2498.5 713.1 %reduce-scatter.15.cloned.1.call-done = f32[2048,256]{1,0:T(8,128)} async-done(((f32[2048,8192]{1,0:T(8,128)}), f32[2048,256]{1,0:T(8,128)}) %reduce-scatter.15.cloned.1.call-update) | async-done | bytes 2097168 | tf_op jit(solution)/shard_map/reduce_scatter | solution.py:168
  3211.7 713.4 %reduce-scatter.17.cloned.1.call-done = f32[256,2048]{1,0:T(8,128)} async-done(((f32[8192,2048]{1,0:T(8,128)}), f32[256,2048]{1,0:T(8,128)}) %reduce-scatter.17.cloned.1.call-update) | async-done | bytes 2097168 | tf_op jit(solution)/shard_map/reduce_scatter | solution.py:162
  (181 shorter events, 31.0 us)
Async XLA Ops:
  7.2 5.3 copy-start
  7.2 4.7 copy-start.43
  7.2 94.4 %all-gather.8.cloned.1.call-start = ((), (), s32[]{:S(2)}) async-start(), calls=%async_computation.8 | async-start | bytes 8650752 | tf_op jit(solution)/shard_map/all_gather | solution.py:91
  7.9 172.6 %all-gather.10.cloned.1.call-start = ((), (), s32[]{:S(2)}) async-start(), calls=%async_computation.9 | async-start | bytes 8650752 | tf_op jit(solution)/shard_map/all_gather | solution.py:89
  8.7 250.8 %all-gather.12.cloned.1.call-start = ((), (), s32[]{:S(2)}) async-start(), calls=%async_computation.10 | async-start | bytes 8650752 | tf_op jit(solution)/shard_map/all_gather | solution.py:90
  9.4 328.9 %all-gather.14.cloned.1.call-start = ((), (), s32[]{:S(2)}) async-start(), calls=%async_computation.11 | async-start | bytes 8650752 | tf_op jit(solution)/shard_map/all_gather | solution.py:92
  10.0 522.5 %all-gather.16.cloned.1.call-start = ((), (), s32[]{:S(2)}) async-start(), calls=%async_computation.12 | async-start | bytes 34603008 | tf_op jit(solution)/shard_map/all_gather | solution.py:126
  10.6 716.1 %all-gather.18.cloned.1.call-start = ((), (), s32[]{:S(2)}) async-start(), calls=%async_computation.13 | async-start | bytes 34603008 | tf_op jit(solution)/shard_map/all_gather | solution.py:127
  11.2 911.7 %all-gather.20.cloned.1.call-start = ((), (), s32[]{:S(2)}) async-start(), calls=%async_computation.14 | async-start | bytes 34603008 | tf_op jit(solution)/shard_map/all_gather | solution.py:128
  14.0 9.0 copy-start.44
  14.0 9.2 copy-start.45
  14.0 9.5 copy-start.46
  14.0 9.7 copy-start.47
  14.0 67.4 %copy-start.2 = (s32[64]{0:T(128)S(1)}, s32[64]{0:T(128)}, u32[]{:S(2)}) copy-start(s32[64]{0:T(128)} %param.16) | copy-start | bytes 772
  15.6 67.6 %all-to-all-start = ((bf16[64,4,2048]{2,1,0:T(4,128)(2,1)}), bf16[64,4,2048]{2,1,0:T(4,128)(2,1)S(1)}, u32[]{:S(2)}, u32[]{:S(2)}) async-start(bf16[64,4,2048]{2,1,0:T(4,128)(2,1)} %broadcast_select_fusion), calls=%async_computation | async-start | bytes 2097152 | tf_op jit(solution)/shard_map/all_to_all | solution.py:81
  22.9 1148.6 %reduce-scatter.19.cloned.1.call-start = ((), (), s32[]{:S(2)}) async-start(), calls=%async_computation.20 | async-start | bytes 1081344
  81.3 105.1 %copy-start.35 = (f32[2048]{0:T(1024)}, f32[2048]{0:T(1024)S(1)}, u32[]{:S(2)}) copy-start(f32[2048]{0:T(1024)S(1)} %convert_element_type.101) | copy-start | bytes 24580
  81.3 184.1 %copy-start.33 = (f32[2048]{0:T(1024)}, f32[2048]{0:T(1024)S(1)}, u32[]{:S(2)}) copy-start(f32[2048]{0:T(1024)S(1)} %convert_element_type.102) | copy-start | bytes 24580
  83.1 185.3 %copy-start.30 = (f32[128,64]{1,0:T(8,128)}, f32[128,64]{1,0:T(8,128)S(1)}, u32[]{:S(2)}) copy-start(f32[128,64]{1,0:T(8,128)S(1)} %get-tuple-element.54) | copy-start | bytes 98308
  186.4 1.3 copy-start.5
  186.4 1.3 copy-start.39
  265.3 1.4 copy-start.3
  265.3 1.4 copy-start.37
  271.2 1.7 copy-start.10
  271.2 1.7 copy-start.12
  271.3 1.7 copy-start.14
  271.3 2.0 copy-start.16
  273.3 1.2 copy-start.26
  344.5 1.3 copy-start.7
  922.9 16.4 copy-start.28
  939.3 1.6 copy-start.8
  943.1 22.0 copy-start.19
  1003.8 6.1 copy-start.21
  1016.2 1.2 copy-start.15
  1016.2 1.5 copy-start.17
  1017.7 1.2 copy-start.11
  1017.7 1.5 copy-start.13
  1019.3 1.2 copy-start.27
  1020.5 1.8 copy-start.31
  1020.5 1.8 copy-start.32
  1024.6 1.6 copy-start.6
  1024.6 1.6 copy-start.36
  1024.6 1.6 copy-start.40
  1028.8 1.6 copy-start.4
  1028.8 1.6 copy-start.34
  1028.8 1.6 copy-start.38
  1035.6 2.7 copy-start.23
  1038.4 568.2 %reduce-scatter.9.cloned.1.call-start = ((), (), s32[]{:S(2)}) async-start(), calls=%async_computation.15 | async-start | bytes 51904512 | tf_op jit(solution)/shard_map/reduce_scatter | solution.py:232
  1059.4 1.2 copy-start.18
  1059.4 1.5 copy-start.22
  1059.5 731.6 %reduce-scatter.11.cloned.1.call-start = ((), (), s32[]{:S(2)}) async-start(), calls=%async_computation.16 | async-start | bytes 17301504 | tf_op jit(solution)/shard_map/reduce_scatter | solution.py:233
  1069.1 1.2 copy-start.9
  1069.2 1429.4 %reduce-scatter.13.cloned.1.call-start = ((), (), s32[]{:S(2)}) async-start(), calls=%async_computation.17 | async-start | bytes 69206016 | tf_op jit(solution)/shard_map/reduce_scatter | solution.py:166
  1095.8 2115.9 %reduce-scatter.15.cloned.1.call-start = ((), (), s32[]{:S(2)}) async-start(), calls=%async_computation.18 | async-start | bytes 69206016 | tf_op jit(solution)/shard_map/reduce_scatter | solution.py:168
  1121.2 1.2 copy-start.20
  1121.2 2803.8 %reduce-scatter.17.cloned.1.call-start = ((), (), s32[]{:S(2)}) async-start(), calls=%async_computation.19 | async-start | bytes 69206016 | tf_op jit(solution)/shard_map/reduce_scatter | solution.py:162
  1148.0 6.5 copy-start.29
  1148.1 12.5 slice-start
  1154.6 6.0 copy-start.24
  1154.6 6.0 slice-start.1
  1165.1 29.2 all-to-all-start.1
  1168.0 27.3 copy-start.42
  1195.3 2729.7 %copy-start.1 = (bf16[64,4,2048]{2,1,0:T(4,128)(2,1)S(1)}, bf16[64,4,2048]{2,1,0:T(4,128)(2,1)}, u32[]{:S(2)}) copy-start(bf16[64,4,2048]{2,1,0:T(4,128)(2,1)} %param.15) | copy-start | bytes 3145732
  1197.8 2727.2 %copy-start.25 = (bf16[64,4,2048]{2,1,0:T(4,128)(2,1)}, bf16[64,4,2048]{2,1,0:T(4,128)(2,1)S(1)}, u32[]{:S(2)}) copy-start(bf16[64,4,2048]{2,1,0:T(4,128)(2,1)S(1)} %scatter_fusion) | copy-start | bytes 3145732
  (1 other events, 0.6 us)
Sparse Core Ops, SparseCore 0:
  10.9 90.6 all-gather.7
  104.5 76.0 all-gather.9
  183.4 76.0 all-gather.11
  262.2 76.0 all-gather.13
  339.7 192.7 all-gather.15
  533.9 192.8 all-gather.17
  729.6 193.2 all-gather.19
  1038.5 132.9 reduce-scatter.18
  1179.0 427.4 reduce-scatter.8
  1609.4 181.7 reduce-scatter.10
  1794.2 704.3 reduce-scatter.12
  2501.4 710.1 reduce-scatter.14
  3214.7 710.2 reduce-scatter.16
where the time goes:
time: 3940 us; the launch traced here: 3930 us
  waiting for transfers between devices  3510 us (89%)
  matrix products  276 us (7%)
  blocking collectives  57.3 us (1%)
  local copies, waits for them, and re-layouts  44.9 us (1%)
    reduce_scatter x1, waiting for transfers between devices, per_device(): lax.psum_scatter(down_term, 'fsdp', scatter_dimension=0, tiled=True)  713 us
    reduce_scatter x1, waiting for transfers between devices, per_device(): up_part = lax.psum_scatter(up_term, 'fsdp', scatter_dimension=1, tiled=True)  713 us
    reduce_scatter x1, waiting for transfers between devices, per_device(): lax.psum_scatter(gate_term, 'fsdp', scatter_dimension=1, tiled=True)  707 us
    reduce_scatter x1, waiting for transfers between devices, per_device(): lax.psum_scatter(qkv_term, 'fsdp', scatter_dimension=0, tiled=True)  409 us
    all_gather x1, waiting for transfers between devices, per_device(): lax.all_gather(w_gate, 'fsdp', axis=1, tiled=True)  185 us
    reduce_scatter x1, waiting for transfers between devices, per_device(): lax.psum_scatter(output_term, 'fsdp', scatter_dimension=0, tiled=True)  182 us
    all_gather x1, waiting for transfers between devices, per_device(): lax.all_gather(w_up, 'fsdp', axis=1, tiled=True)  176 us
    all_gather x1, waiting for transfers between devices, per_device(): lax.all_gather(w_down, 'fsdp', axis=0, tiled=True)  172 us
  transfers between devices with their start and end apart: 15, of which 14 were waited for; matrix products, arithmetic and copies ran while one was open for 6% of the time, Pallas kernels for 0%

commit v1 on v0

v1 whole, which is shorter than its diff:
```python
import math

import jax
import jax.numpy as jnp
from jax import lax
from jax.sharding import Mesh
from jax.sharding import PartitionSpec as P

HEADS = 16
PLANE = 8
BF = jnp.bfloat16
F32 = jnp.float32

norm_eps = 1e-06
rope_base = 500000.0

ALL = ("a", "y", "x", "c")
GROUP = ("y", "x", "c")
SWAP = [(0, 1), (1, 0)]


def swap(value, axis):
    return lax.ppermute(value, axis, SWAP)


def rotary_tables(length, head_dim):
    half_dim = head_dim // 2
    exponents = jnp.arange(half_dim, dtype=F32) * (2.0 / head_dim)
    frequency = jnp.power(F32(rope_base), -exponents)
    angles = jnp.arange(length, dtype=F32)[:, None] * frequency[None, :]
    return (jnp.cos(angles), jnp.sin(angles))


def rotate(values, cosines, sines):
    half_dim = values.shape[-1] // 2
    first_half = values[..., :half_dim]
    second_half = values[..., half_dim:]
    cos_rows = cosines[:, None, :]
    sin_rows = sines[:, None, :]
    return jnp.concatenate(
        [
            first_half * cos_rows - second_half * sin_rows,
            second_half * cos_rows + first_half * sin_rows,
        ],
        axis=-1,
    )


def group_gather(block):
    half = block.shape[0] // 2
    low, high = block[:half], block[half:]
    low_x = swap(low, "x")
    high_y = swap(high, "y")
    low_y, low_xy = swap(low, "y"), swap(low_x, "y")
    high_x, high_xy = swap(high, "x"), swap(high_y, "x")
    pieces = [
        (low, high),
        (low_x, high_x),
        (low_y, high_y),
        (low_xy, high_xy),
    ]
    out = []
    for first, second in pieces:
        out += [first, second, swap(first, "c"), swap(second, "c")]
    return jnp.concatenate(out, axis=0)


def group_scatter(partial):
    rows = partial.shape[0] // PLANE
    half = rows // 2
    low, high = [], []
    for place in range(4):
        base = partial[2 * place * rows : (2 * place + 1) * rows]
        away = swap(partial[(2 * place + 1) * rows : (2 * place + 2) * rows], "c")
        both = base.astype(F32) + away.astype(F32)
        low.append(both[:half])
        high.append(both[half:])
    low0 = low[0] + swap(low[2].astype(BF), "y").astype(F32)
    low1 = low[1] + swap(low[3].astype(BF), "y").astype(F32)
    low_sum = low0 + swap(low1.astype(BF), "x").astype(F32)
    high0 = high[0] + swap(high[1].astype(BF), "x").astype(F32)
    high1 = high[2] + swap(high[3].astype(BF), "x").astype(F32)
    high_sum = high0 + swap(high1.astype(BF), "y").astype(F32)
    return jnp.concatenate([low_sum, high_sum], axis=0)


def group_total(value):
    kinds, wide = value.shape
    split = value.reshape(kinds, 2, 2, 2, wide // PLANE)
    for axis, dim in (("c", 3), ("x", 2), ("y", 1)):
        split = split + jnp.flip(swap(split, axis), dim)
    return split.reshape(kinds, wide)


def per_device(
    tokens,
    lengths,
    dealing,
    w_query,
    w_key,
    w_value,
    w_output,
    query_gain,
    key_gain,
    attn_gain,
    w_gate,
    w_up,
    w_down,
    mlp_gain,
    cotangent,
):
    groups = lax.axis_size("a")
    total = groups * PLANE
    rank = lax.axis_index(ALL)
    place = lax.axis_index(GROUP)
    micro_count, seq_len, width = cotangent.shape
    rows = micro_count * seq_len
    wide = rows * PLANE
    shard = width // total
    head_dim = width // HEADS
    own_heads = HEADS // PLANE
    own_width = own_heads * head_dim
    spread = head_dim // shard
    head_axes = GROUP[3 - (spread.bit_length() - 1) :]
    fan = PLANE // spread
    lead, lane = place // spread, place % spread

    cosines, sines = rotary_tables(seq_len, head_dim)
    positions = jnp.arange(seq_len, dtype=jnp.int32)
    causal = (positions[None, :] <= positions[:, None])[None, None]
    qk_scale = 1.0 / math.sqrt(head_dim)

    def heads_out(weight):
        split = weight.reshape(shard, spread, own_heads, fan, head_dim)
        return split.transpose(3, 1, 0, 2, 4).reshape(PLANE, shard, own_width)

    outgoing = jnp.take(tokens, dealing, axis=0)
    arrived = lax.all_to_all(outgoing, ALL, split_axis=0, concat_axis=1, tiled=True)
    x_low = arrived.reshape(rows, width)

    qkv_out = jnp.concatenate([heads_out(w_query), heads_out(w_key), heads_out(w_value)], axis=2)
    qkv_in = lax.all_to_all(qkv_out, GROUP, split_axis=0, concat_axis=0, tiled=True)
    w_qkv = lax.all_gather(qkv_in, "a", axis=0, tiled=True).reshape(width, 3 * own_width)

    gains = jnp.stack([query_gain, key_gain, attn_gain, mlp_gain])
    gains = lax.all_to_all(
        jnp.broadcast_to(gains[None], (total, 4, shard)), ALL, split_axis=0, concat_axis=0, tiled=True
    )
    gains = gains.transpose(1, 0, 2).reshape(4, width).astype(F32)
    by_head = gains[:2].reshape(2, spread, own_heads, fan, head_dim)
    by_head = lax.dynamic_index_in_dim(by_head, lane, 1, keepdims=False)
    by_head = lax.dynamic_index_in_dim(by_head, lead, 2, keepdims=False)
    gain_query, gain_key = by_head[0].reshape(own_width), by_head[1].reshape(own_width)
    gain_attn, gain_mlp = gains[2], gains[3]

    out_all = lax.all_gather(w_output, "a", axis=0, tiled=False)
    w_out = lax.all_to_all(out_all, head_axes, split_axis=0, concat_axis=1, tiled=True)
    w_out = w_out.reshape(own_width, width)

    gate = lax.all_gather(w_gate.T, "a", axis=0, tiled=True)
    up = lax.all_gather(w_up.T, "a", axis=0, tiled=True)
    down = lax.all_gather(w_down, "a", axis=0, tiled=True)

    own_seqs = lax.dynamic_slice_in_dim(dealing, rank * micro_count, micro_count)
    own_lengths = jnp.take(lengths, own_seqs)
    valid_mask = (positions[None, :] < own_lengths[:, None]).astype(F32).reshape(rows, 1)

    x_wide = group_gather(x_low)
    qkv_raw = jnp.dot(x_wide, w_qkv, preferred_element_type=F32)
    query_raw = qkv_raw[:, :own_width]
    key_raw = qkv_raw[:, own_width : 2 * own_width]
    value_low = qkv_raw[:, 2 * own_width :].astype(BF)
    squares = group_total(
        jnp.stack([jnp.sum(query_raw * query_raw, axis=1), jnp.sum(key_raw * key_raw, axis=1)])
    )
    inverses = lax.rsqrt(squares * (1.0 / width) + norm_eps)
    query_inv, key_inv = inverses[0][:, None], inverses[1][:, None]
    head_shape = (wide // seq_len, seq_len, own_heads, head_dim)
    query_low = rotate((query_raw * query_inv * gain_query).reshape(head_shape), cosines, sines).astype(BF)
    key_low = rotate((key_raw * key_inv * gain_key).reshape(head_shape), cosines, sines).astype(BF)
    value_low = value_low.reshape(head_shape)
    scores = jnp.einsum("gthe,guhe->ghtu", query_low, key_low, preferred_element_type=F32) * qk_scale
    scores = jnp.where(causal, scores, -1e30)
    row_peak = jnp.max(scores, axis=-1, keepdims=True)
    exp_scores = jnp.exp(scores - row_peak)
    row_total = jnp.sum(exp_scores, axis=-1, keepdims=True)
    soft = exp_scores / row_total
    soft_low = soft.astype(BF)
    attended_low = (
        jnp.einsum("ghtu,guhe->gthe", soft_low, value_low, preferred_element_type=F32)
        .reshape(wide, own_width)
        .astype(BF)
    )
    out_raw = group_scatter(jnp.dot(attended_low, w_out, preferred_element_type=F32).astype(BF))
    out_inv = lax.rsqrt(jnp.mean(out_raw * out_raw, axis=-1, keepdims=True) + norm_eps)
    out_normed = out_raw * out_inv
    hidden = x_low.astype(F32) + out_normed * gain_attn

    hidden_wide = group_gather(hidden.astype(BF))
    contract_last = (((1,), (1,)), ((), ()))
    contract_rows = (((0,), (0,)), ((), ()))
    gate_proj = lax.dot_general(hidden_wide, gate, contract_last, preferred_element_type=F32)
    up_proj = lax.dot_general(hidden_wide, up, contract_last, preferred_element_type=F32)
    sigma_gate = jax.nn.sigmoid(gate_proj)
    act_value = gate_proj * sigma_gate
    act_low = (act_value * up_proj).astype(BF)
    down_raw = group_scatter(jnp.dot(act_low, down, preferred_element_type=F32).astype(BF))
    down_inv = lax.rsqrt(jnp.mean(down_raw * down_raw, axis=-1, keepdims=True) + norm_eps)
    down_normed = down_raw * down_inv
    block_out = (
        (valid_mask * (hidden + down_normed * gain_mlp)).astype(BF).reshape(micro_count, seq_len, width)
    )

    grad_out = valid_mask * cotangent.reshape(rows, width).astype(F32)
    grad_gain_mlp = jnp.sum(down_normed * grad_out, axis=0)
    scaled = grad_out * gain_mlp
    grad_down = down_inv * (scaled - down_normed * jnp.mean(scaled * down_normed, axis=-1, keepdims=True))
    grad_down_wide = group_gather(grad_down.astype(BF))

    grad_act = lax.dot_general(grad_down_wide, down, contract_last, preferred_element_type=F32)
    grad_gate_low = (grad_act * up_proj * sigma_gate * (1.0 + gate_proj * (1.0 - sigma_gate))).astype(BF)
    grad_up_low = (grad_act * act_value).astype(BF)
    grad_hidden = jnp.dot(grad_gate_low, gate, preferred_element_type=F32) + jnp.dot(
        grad_up_low, up, preferred_element_type=F32
    )
    grad_hidden = grad_out + group_scatter(grad_hidden.astype(BF))

    def owners(term):
        return lax.psum_scatter(term.astype(BF), "a", scatter_dimension=0, tiled=True).astype(F32)

    down_part = owners(
        lax.dot_general(act_low, grad_down_wide, contract_rows, preferred_element_type=F32)
    )
    gate_part = owners(
        lax.dot_general(grad_gate_low, hidden_wide, contract_rows, preferred_element_type=F32)
    ).T
    up_part = owners(
        lax.dot_general(grad_up_low, hidden_wide, contract_rows, preferred_element_type=F32)
    ).T

    grad_gain_attn = jnp.sum(out_normed * grad_hidden, axis=0)
    scaled = grad_hidden * gain_attn
    grad_out_raw = out_inv * (scaled - out_normed * jnp.mean(scaled * out_normed, axis=-1, keepdims=True))
    grad_out_wide = group_gather(grad_out_raw.astype(BF))

    output_term = lax.dot_general(attended_low, grad_out_wide, contract_rows, preferred_element_type=F32)
    output_term = lax.all_to_all(
        output_term.astype(BF).reshape(own_heads, head_dim, width),
        head_axes,
        split_axis=1,
        concat_axis=0,
        tiled=True,
    )
    output_part = owners(output_term.reshape(groups * shard, width))

    grad_att_low = (
        lax.dot_general(grad_out_wide, w_out, contract_last, preferred_element_type=F32)
        .astype(BF)
        .reshape(head_shape)
    )
    grad_soft = jnp.einsum("gthe,guhe->ghtu", grad_att_low, value_low, preferred_element_type=F32)
    row_delta = jnp.sum(soft * grad_soft, axis=-1, keepdims=True)
    grad_scores = (soft * (grad_soft - row_delta)).astype(BF)
    grad_q_rot = (
        jnp.einsum("ghtu,guhe->gthe", grad_scores, key_low, preferred_element_type=F32) * qk_scale
    )
    grad_k_rot = (
        jnp.einsum("ghtu,gthe->guhe", grad_scores, query_low, preferred_element_type=F32) * qk_scale
    )
    grad_value_low = (
        jnp.einsum("ghtu,gthe->guhe", soft_low, grad_att_low, preferred_element_type=F32)
        .reshape(wide, own_width)
        .astype(BF)
    )
    grad_q_norm = rotate(grad_q_rot, cosines, -sines).reshape(wide, own_width)
    grad_k_norm = rotate(grad_k_rot, cosines, -sines).reshape(wide, own_width)
    query_normed, key_normed = query_raw * query_inv, key_raw * key_inv
    grad_gain_q = jnp.sum(query_normed * grad_q_norm, axis=0)
    grad_gain_k = jnp.sum(key_normed * grad_k_norm, axis=0)
    scaled_q, scaled_k = grad_q_norm * gain_query, grad_k_norm * gain_key
    means = group_total(
        jnp.stack([jnp.sum(scaled_q * query_normed, axis=1), jnp.sum(scaled_k * key_normed, axis=1)])
    ) * (1.0 / width)
    grad_query = query_inv * (scaled_q - query_normed * means[0][:, None])
    grad_key = key_inv * (scaled_k - key_normed * means[1][:, None])
    grad_qkv = jnp.concatenate([grad_query.astype(BF), grad_key.astype(BF), grad_value_low], axis=1)

    grad_input = lax.dot_general(grad_qkv, w_qkv, contract_last, preferred_element_type=F32)
    grad_input = grad_hidden + group_scatter(grad_input.astype(BF))
    returned = lax.all_to_all(
        grad_input.astype(BF).reshape(micro_count, seq_len, width),
        ALL,
        split_axis=1,
        concat_axis=0,
        tiled=True,
    )
    input_grad = jnp.zeros_like(tokens).at[dealing].set(returned)

    qkv_term = lax.dot_general(x_wide, grad_qkv, contract_rows, preferred_element_type=F32)
    qkv_rows = lax.psum_scatter(qkv_term.astype(BF), "a", scatter_dimension=0, tiled=True)
    qkv_back = lax.all_to_all(
        qkv_rows.reshape(PLANE, shard, 3 * own_width), GROUP, split_axis=0, concat_axis=0, tiled=True
    )

    def heads_in(columns):
        split = columns.reshape(fan, spread, shard, own_heads, head_dim)
        return split.transpose(2, 1, 3, 0, 4).reshape(shard, width).astype(F32)

    query_part = heads_in(qkv_back[:, :, :own_width])
    key_part = heads_in(qkv_back[:, :, own_width : 2 * own_width])
    value_part = heads_in(qkv_back[:, :, 2 * own_width :])

    placed = jnp.zeros((2, spread, own_heads, fan, head_dim), F32)
    own = jnp.stack([grad_gain_q, grad_gain_k]).reshape(2, 1, own_heads, 1, head_dim)
    placed = lax.dynamic_update_slice(placed, own, (0, lane, 0, lead, 0)).reshape(2, width)
    gain_terms = jnp.concatenate([placed, jnp.stack([grad_gain_attn, grad_gain_mlp])])
    gain_terms = gain_terms.reshape(4, total, shard).transpose(1, 0, 2)
    gain_part = jnp.sum(
        lax.all_to_all(gain_terms, ALL, split_axis=0, concat_axis=0, tiled=True), axis=0
    )
    return (
        block_out,
        input_grad,
        query_part,
        key_part,
        value_part,
        output_part,
        gain_part[0],
        gain_part[1],
        gain_part[2],
        gate_part,
        up_part,
        down_part,
        gain_part[3],
    )


def solution(mesh):
    count = mesh.devices.size
    inner = Mesh(mesh.devices.reshape(count // PLANE, 2, 2, 2), ALL)
    first, second = P(ALL, None), P(None, ALL)
    vector = P(ALL)
    placed = (
        P(None, ALL, None),
        P(),
        P(),
        first,
        first,
        first,
        first,
        vector,
        vector,
        vector,
        second,
        second,
        first,
        vector,
        P(ALL, None, None),
    )
    return jax.shard_map(
        per_device,
        mesh=inner,
        in_specs=placed,
        out_specs=(
            P(ALL, None, None),
            P(None, ALL, None),
            first,
            first,
            first,
            first,
            vector,
            vector,
            vector,
            second,
            second,
            first,
            vector,
        ),
        check_vma=False,
    )
```

time: 3940 us -> 1080 us (0.27)
  waiting for transfers between devices: 3510 us -> 528 us
  local copies, waits for them, and re-layouts: 44.9 us -> 135 us
  matrix products: 276 us -> 191 us
  starting transfers between devices: 10.7 us -> 81.4 us
  other arithmetic: 22.1 us -> 89.6 us
    reduce_scatter x5, waiting for transfers between devices: 2720 us -> 148 us  [the longest x4 148 us: owners(): lax.psum_scatter(term.astype(BF), 'a', scatter_dimension=0, tiled=True)]
    all_gather x7 -> x5, waiting for transfers between devices: 754 us -> 22 us  [the longest x1 21.9 us: per_device(): down = lax.all_gather(w_down, 'a', axis=0, tiled=True)]
    ppermute x0 -> x102, waiting for transfers between devices: none -> 252 us  [swap(): return lax.ppermute(value, axis, SWAP)]
    dot_general x20 -> x15, matrix products: 269 us -> 178 us  [the longest x1 22.6 us: per_device(): lax.dot_general(grad_down_wide, down, contract_last, preferred_element_ty...]
    all_to_all x2 -> x5, waiting for transfers between devices: 19.4 us -> 105 us  [the longest x1 51.1 us: per_device(): lax.all_to_all(outgoing, ALL, split_axis=0, concat_axis=1, tiled=True)]
    ppermute x0 -> x102, starting transfers between devices: none -> 63.1 us  [swap(): return lax.ppermute(value, axis, SWAP)]
    unnamed x1 -> x0, blocking collectives: 57.3 us -> none
    unnamed x118 -> x221, local copies, waits for them, and re-layouts: 21.5 us -> 73 us
  transfers between devices with their start and end apart: 15 -> 117, of which waited for: 14 -> 58; matrix products, arithmetic and copies ran while one was open for 6% -> 25% of each run, Pallas kernels for 0% -> 0%
where the time goes in v1:
time: 1080 us; the launch traced here: 1070 us
  waiting for transfers between devices  528 us (49%)
  matrix products  191 us (18%)
  local copies, waits for them, and re-layouts  135 us (12%)
  other arithmetic  89.6 us (8%)
  starting transfers between devices  81.4 us (8%)
  blocking collectives  27.9 us (3%)
  between operations  16.5 us (2%)
    ppermute x102, waiting for transfers between devices, swap(): return lax.ppermute(value, axis, SWAP)  252 us
    reduce_scatter x4, waiting for transfers between devices, owners(): lax.psum_scatter(term.astype(BF), 'a', scatter_dimension=0, tiled=True)  148 us
    unnamed x221, local copies, waits for them, and re-layouts  73 us
    ppermute x102, starting transfers between devices, swap(): return lax.ppermute(value, axis, SWAP)  63.1 us
    all_to_all x1, waiting for transfers between devices, per_device(): lax.all_to_all(outgoing, ALL, split_axis=0, concat_axis=1, tiled=True)  51.1 us
    all_to_all x1, waiting for transfers between devices, per_device(): lax.all_to_all(grad_input.astype(BF).reshape(micro_count, seq_len, width)...  50.9 us
    dot_general x1, matrix products, per_device(): lax.dot_general(grad_down_wide, down, contract_last, preferred_element_ty...  22.6 us
    all_gather x1, waiting for transfers between devices, per_device(): down = lax.all_gather(w_down, 'a', axis=0, tiled=True)  21.9 us
  transfers between devices with their start and end apart: 117, of which 58 were waited for; matrix products, arithmetic and copies ran while one was open for 25% of the time, Pallas kernels for 0%

profile of v1, /device:TPU:0, one launch (start us, length us, event | category | flops | bytes accessed | tf_op | source)
XLA Modules:
  0.0 1069.8 jit_solution(2776979869479821740)
XLA Ops:
  11.0 17.6 %all_to_all.83 = bf16[8,64,768]{2,1,0:T(8,128)(2,1)} all-to-all(bf16[8,64,768]{2,1,0:T(8,128)(2,1)S(1)} %pad_maximum_fusion.11), channel_id=1, replica_groups=mesh['a'=4,'y'=2,'x'=2,'c'=2] {'y','x','c'}, dimensions={0} | all-to-all | bytes 1572864 | tf_op jit(solution)/shard_map/all_to_all | solution.py:142
  32.3 4.0 all-to-all-start
  39.4 51.1 %all-to-all-done = bf16[64,4,2048]{2,1,0:T(4,128)(2,1)S(1)} async-done(((bf16[64,4,2048]{2,1,0:T(4,128)(2,1)}), bf16[64,4,2048]{2,1,0:T(4,128)(2,1)S(1)}, u32[]{:S(2)}, u32[]{:S(2)}) %all-to-all-start) | async-done | bytes 1048608 | tf_op jit(solution)/shard_map/all_to_all | solution.py:138
  90.6 3.5 all-to-all-start.2
  106.9 5.0 collective-permute-done.2
  115.5 6.9 collective-permute-done.3
  125.1 4.9 collective-permute-done.7
  135.1 5.3 collective-permute-done.10
  140.4 4.7 collective-permute-done.11
  151.1 10.6 fusion.68
  168.0 5.7 all_to_all.84
  179.8 3.9 multiply_bitcast_fusion.3
  198.7 6.3 subtract_convert_fusion.1
  205.0 5.2 fusion.67
  228.5 7.4 convert_add_fusion.9
  241.8 9.0 collective-permute-done.22
  255.6 6.4 collective-permute-done.19
  263.1 10.2 collective-permute-done.23
  285.9 10.1 collective-permute-done.29
  297.9 9.0 collective-permute-done.30
  313.9 6.3 collective-permute-done.37
  320.2 4.9 collective-permute-done.38
  331.0 14.6 %fusion.69 = f32[2048,1024]{1,0:T(8,128)} fusion(bf16[2048,2048]{1,0:T(8,128)(2,1)} %constant_dynamic-update-slice_fusion.18, bf16[1024,2048]{0,1:T(8,128)(2,1)} %all-gather.9.cloned.1.call-done), kind=kOutput, calls=%fused_computation.289 | convolution fusion | flops 8589934592 | bytes 20971520 | tf_op jit(solution)/shard_map/dot_general | solution.py:202
  345.6 16.9 %multiply_convert_fusion.2 = (bf16[2048,1024]{1,0:T(8,128)(2,1)}, f32[2048,1024]{1,0:T(8,128)}) fusion(f32[2048,1024]{1,0:T(8,128)} %fusion.69, bf16[2048,2048]{1,0:T(8,128)(2,1)} %constant_dynamic-update-slice_fusion.18, bf16[1024,2048]{0,1:T(8,128)(2,1)} %all-gather.11.cloned.1.call-done), kind=kOutput, calls=%fused_computation.7 | convolution fusion | flops 8602517504 | bytes 33554432 | tf_op jit(solution)/shard_map/dot_general | solution.py:203
  362.5 21.9 %all-gather.13.cloned.1.call-done = bf16[1024,2048]{1,0:T(8,128)(2,1)} async-done(((bf16[256,2048]{1,0:T(8,128)(2,1)}), bf16[1024,2048]{1,0:T(8,128)(2,1)}) %all-gather.13.cloned.1.call-update) | async-done | bytes 4194320 | tf_op jit(solution)/shard_map/all_gather | solution.py:162
  384.5 12.1 %convolution_convert_fusion.1 = bf16[2048,2048]{1,0:T(8,128)(2,1)S(1)} fusion(bf16[2048,1024]{1,0:T(8,128)(2,1)} %get-tuple-element.242, bf16[1024,2048]{1,0:T(8,128)(2,1)} %all-gather.13.cloned.1.call-done), kind=kOutput, calls=%fused_computation.11 | convolution fusion | flops 8594128896 | bytes 16777216 | tf_op jit(solution)/shard_map/dot_general | solution.py:207
  404.1 3.9 convert_add_fusion.6
  417.6 6.6 collective-permute-done.46
  431.0 4.4 collective-permute-done.43
  437.0 10.1 collective-permute-done.47
  457.3 10.5 collective-permute-done.53
  468.5 10.2 collective-permute-done.54
  483.3 8.4 collective-permute-done.61
  491.7 4.1 collective-permute-done.62
  501.1 22.6 %multiply_convert_fusion = (bf16[2048,1024]{1,0:T(8,128)(2,1)}, bf16[2048,1024]{1,0:T(8,128)(2,1)}) fusion(f32[2048,1024]{1,0:T(8,128)} %fusion.69, f32[2048,1024]{1,0:T(8,128)} %get-tuple-element.243, bf16[2048,2048]{1,0:T(8,128)(2,1)} %copy-done.49, bf16[1024,2048]{1,0:T(8,128)(2,1)} %all-gather.13.cloned.1.call-done), kind=kOutput, calls=%fused_computation.5 | convolution fusion | flops 8617197568 | bytes 37748736 | tf_op jit(solution)/shard_map/dot_general | solution.py:220
  523.7 14.0 %fusion.70 = f32[2048,2048]{1,0:T(8,128)} fusion(bf16[2048,1024]{1,0:T(8,128)(2,1)} %get-tuple-element.134, bf16[1024,2048]{0,1:T(8,128)(2,1)S(1)} %copy-done.71), kind=kOutput, calls=%fused_computation.290 | convolution fusion | flops 8589934592 | bytes 25165824 | tf_op jit(solution)/shard_map/dot_general | solution.py:223
  537.7 14.6 %add_convert_fusion = bf16[2048,2048]{1,0:T(8,128)(2,1)S(1)} fusion(f32[2048,2048]{1,0:T(8,128)} %fusion.70, bf16[2048,1024]{1,0:T(8,128)(2,1)} %get-tuple-element.133, bf16[1024,2048]{0,1:T(8,128)(2,1)} %all-gather.11.cloned.1.call-done), kind=kOutput, calls=%fused_computation.4 | convolution fusion | flops 8598323200 | bytes 33554432 | tf_op jit(solution)/shard_map/dot_general | solution.py:223
  569.1 9.0 collective-permute-done.70
  583.6 5.8 collective-permute-done.67
  590.0 10.1 collective-permute-done.71
  613.4 10.5 collective-permute-done.77
  625.5 9.2 collective-permute-done.78
  639.3 8.4 collective-permute-done.85
  647.7 4.1 collective-permute-done.86
  657.2 3.5 convolution_convert_fusion.8
  678.7 3.4 copy.326
  682.2 5.6 fusion.3
  690.8 5.8 convolution_convert_fusion.7
  702.0 4.6 all_to_all.85
  708.1 6.4 multiply_convert_fusion.4
  715.4 10.6 convolution_convert_fusion.6
  726.1 14.1 %convolution_convert_fusion.5 = bf16[1024,2048]{1,0:T(8,128)(2,1)} fusion(bf16[2048,1024]{1,0:T(8,128)(2,1)} %get-tuple-element.134, bf16[2048,2048]{1,0:T(8,128)(2,1)} %constant_dynamic-update-slice_fusion.18), kind=kOutput, calls=%fused_computation.15 | convolution fusion | flops 8592031744 | bytes 16777216 | tf_op jit(solution)/shard_map/dot_general | solution.py:235
  740.3 14.1 %convolution_convert_fusion.4 = bf16[1024,2048]{1,0:T(8,128)(2,1)} fusion(bf16[2048,1024]{1,0:T(8,128)(2,1)} %get-tuple-element.133, bf16[2048,2048]{1,0:T(8,128)(2,1)} %constant_dynamic-update-slice_fusion.18), kind=kOutput, calls=%fused_computation.14 | convolution fusion | flops 8592031744 | bytes 16777216 | tf_op jit(solution)/shard_map/dot_general | solution.py:238
  754.4 9.3 convolution_convert_fusion
  765.5 3.5 copy-done.19
  770.1 13.1 %convolution_convert_fusion.3 = bf16[1024,2048]{1,0:T(8,128)(2,1)} fusion(bf16[2048,1024]{1,0:T(8,128)(2,1)S(1)} %copy-done.72, bf16[2048,2048]{1,0:T(8,128)(2,1)} %copy-done.49), kind=kOutput, calls=%fused_computation.13 | convolution fusion | flops 8592031744 | bytes 16777216 | tf_op jit(solution)/shard_map/dot_general | solution.py:232
  783.2 6.7 convert_add_fusion
  795.8 9.0 collective-permute-done.97
  812.4 3.6 collective-permute-done.94
  816.8 10.5 collective-permute-done.98
  839.8 50.9 %all-to-all-done.4 = bf16[2,128,2048]{2,0,1:T(2,128)(2,1)S(1)} async-done(((bf16[2,128,2048]{2,0,1:T(2,128)(2,1)}), bf16[2,128,2048]{2,0,1:T(2,128)(2,1)S(1)}, u32[]{:S(2)}, u32[]{:S(2)}) %all-to-all-start.4) | async-done | bytes 1048608 | tf_op jit(solution)/shard_map/all_to_all | solution.py:290
  894.3 4.2 all-to-all-start.5
  901.8 72.2 %reduce-scatter.12.cloned.1.call-done = bf16[256,2048]{1,0:T(8,128)(2,1)} async-done(((bf16[1024,2048]{1,0:T(8,128)(2,1)}), bf16[256,2048]{1,0:T(8,128)(2,1)}) %reduce-scatter.12.cloned.1.call-update) | async-done | bytes 1048592 | tf_op jit(solution)/shard_map/reduce_scatter | solution.py:229
  977.3 76.3 %reduce-scatter.14.cloned.1.call-done = bf16[256,2048]{1,0:T(8,128)(2,1)} async-done(((bf16[1024,2048]{1,0:T(8,128)(2,1)}), bf16[256,2048]{1,0:T(8,128)(2,1)}) %reduce-scatter.14.cloned.1.call-update) | async-done | bytes 1048592 | tf_op jit(solution)/shard_map/reduce_scatter | solution.py:229
  (583 shorter events, 295.9 us)
Async XLA Ops:
  7.2 143.9 %all-gather.7.cloned.1.call-start = ((), (), s32[]{:S(2)}) async-start(), calls=%async_computation.13 | async-start | bytes 3932160 | tf_op jit(solution)/shard_map/all_gather | solution.py:143
  32.3 58.3 %all-to-all-start = ((bf16[64,4,2048]{2,1,0:T(4,128)(2,1)}), bf16[64,4,2048]{2,1,0:T(4,128)(2,1)S(1)}, u32[]{:S(2)}, u32[]{:S(2)}) async-start(bf16[64,4,2048]{2,1,0:T(4,128)(2,1)} %broadcast_select_fusion), calls=%async_computation | async-start | bytes 2097152 | tf_op jit(solution)/shard_map/all_to_all | solution.py:138
  36.2 131.8 %all-gather.15.cloned.1.call-start = ((), (), s32[]{:S(2)}) async-start(), calls=%async_computation.22 | async-start | bytes 1310720 | tf_op jit(solution)/shard_map/all_gather | solution.py:156
  37.0 294.1 %all-gather.9.cloned.1.call-start = ((), (), s32[]{:S(2)}) async-start(), calls=%async_computation.14 | async-start | bytes 5242880 | tf_op jit(solution)/shard_map/all_gather | solution.py:160
  94.1 251.5 %all-gather.11.cloned.1.call-start = ((), (), s32[]{:S(2)}) async-start(), calls=%async_computation.15 | async-start | bytes 5242880 | tf_op jit(solution)/shard_map/all_gather | solution.py:161
  97.0 14.9 %collective-permute-start.2 = (bf16[128,2048]{1,0:T(8,128)(2,1)S(1)}, bf16[128,2048]{1,0:T(8,128)(2,1)}, u32[]{:S(2)}, u32[]{:S(2)}) collective-permute-start(bf16[128,2048]{1,0:T(8,128)(2,1)S(1)} %slice.333), channel_id=1, source_target_pairs={{0,2},{2,0},{1,3},{3,1},{4,6},{6,4},{5,7},{7,5},{8,10},{10,8},{9,1... | collective-permute-start | bytes 1572872 | tf_op jit(solution)/shard_map/ppermute | solution.py:23
  102.6 19.8 %collective-permute-start.3 = (bf16[128,2048]{1,0:T(8,128)(2,1)S(1)}, bf16[128,2048]{1,0:T(8,128)(2,1)S(1)}, u32[]{:S(2)}, u32[]{:S(2)}) collective-permute-start(bf16[128,2048]{1,0:T(8,128)(2,1)S(1)} %slice.335), channel_id=1, source_target_pairs={{0,2},{2,0},{1,3},{3,1},{4,6},{6,4},{5,7},{7,5},{8,10},{10,8},{9,1... | collective-permute-start | bytes 1572872 | tf_op jit(solution)/shard_map/ppermute | solution.py:23
  104.0 26.8 %collective-permute-start.6 = (bf16[128,2048]{1,0:T(8,128)(2,1)S(1)}, bf16[128,2048]{1,0:T(8,128)(2,1)S(1)}, u32[]{:S(2)}, u32[]{:S(2)}) collective-permute-start(bf16[128,2048]{1,0:T(8,128)(2,1)S(1)} %slice.333), channel_id=1, source_target_pairs={{0,4},{4,0},{1,5},{5,1},{2,6},{6,2},{3,7},{7,3},{8,12},{12,8},{9,1... | collective-permute-start | bytes 1572872 | tf_op jit(solution)/shard_map/ppermute | solution.py:23
  105.6 24.4 %collective-permute-start.7 = (bf16[128,2048]{1,0:T(8,128)(2,1)S(1)}, bf16[128,2048]{1,0:T(8,128)(2,1)S(1)}, u32[]{:S(2)}, u32[]{:S(2)}) collective-permute-start(bf16[128,2048]{1,0:T(8,128)(2,1)S(1)} %slice.335), channel_id=1, source_target_pairs={{0,4},{4,0},{1,5},{5,1},{2,6},{6,2},{3,7},{7,3},{8,12},{12,8},{9,1... | collective-permute-start | bytes 1572872 | tf_op jit(solution)/shard_map/ppermute | solution.py:23
  111.9 20.5 %collective-permute-start.4 = (bf16[128,2048]{1,0:T(8,128)(2,1)}, bf16[128,2048]{1,0:T(8,128)(2,1)S(1)}, u32[]{:S(2)}, u32[]{:S(2)}) collective-permute-start(bf16[128,2048]{1,0:T(8,128)(2,1)} %collective-permute-done.2), channel_id=1, source_target_pairs={{0,1},{1,0},{2,3},{3,2},{4,5},{5,4},{6,7},{7,6},{8,9},{9,8},{10,11... | collective-permute-start | bytes 1572872 | tf_op jit(solution)/shard_map/ppermute | solution.py:23
  113.8 26.6 %collective-permute-start.10 = (bf16[128,2048]{1,0:T(8,128)(2,1)}, bf16[128,2048]{1,0:T(8,128)(2,1)S(1)}, u32[]{:S(2)}, u32[]{:S(2)}) collective-permute-start(bf16[128,2048]{1,0:T(8,128)(2,1)} %collective-permute-done.2), channel_id=1, source_target_pairs={{0,4},{4,0},{1,5},{5,1},{2,6},{6,2},{3,7},{7,3},{8,12},{12,8},{9,1... | collective-permute-start | bytes 1572872 | tf_op jit(solution)/shard_map/ppermute | solution.py:23
  130.0 16.9 %collective-permute-start.9 = (bf16[128,2048]{1,0:T(8,128)(2,1)S(1)}, bf16[128,2048]{1,0:T(8,128)(2,1)S(1)}, u32[]{:S(2)}, u32[]{:S(2)}) collective-permute-start(bf16[128,2048]{1,0:T(8,128)(2,1)S(1)} %collective-permute-done.7), channel_id=1, source_target_pairs={{0,1},{1,0},{2,3},{3,2},{4,5},{5,4},{6,7},{7,6},{8,9},{9,8},{10,11... | collective-permute-start | bytes 1572872 | tf_op jit(solution)/shard_map/ppermute | solution.py:23
  222.1 162.4 %all-gather.13.cloned.1.call-start = ((), (), s32[]{:S(2)}) async-start(), calls=%async_computation.16 | async-start | bytes 5242880 | tf_op jit(solution)/shard_map/all_gather | solution.py:162
  236.0 14.8 %collective-permute-start.22 = (bf16[128,2048]{1,0:T(8,128)(2,1)S(1)}, bf16[128,2048]{1,0:T(8,128)(2,1)S(1)}, u32[]{:S(2)}, u32[]{:S(2)}) collective-permute-start(bf16[128,2048]{1,0:T(8,128)(2,1)S(1)} %get-tuple-element.208), channel_id=1, source_target_pairs={{0,4},{4,0},{1,5},{5,1},{2,6},{6,2},{3,7},{7,3},{8,12},{12,8},{9,1... | collective-permute-start | bytes 1572872 | tf_op jit(solution)/shard_map/ppermute | solution.py:23
  237.1 14.9 %collective-permute-start.25 = (bf16[128,2048]{1,0:T(8,128)(2,1)S(1)}, bf16[128,2048]{1,0:T(8,128)(2,1)S(1)}, u32[]{:S(2)}, u32[]{:S(2)}) collective-permute-start(bf16[128,2048]{1,0:T(8,128)(2,1)S(1)} %get-tuple-element.209), channel_id=1, source_target_pairs={{0,2},{2,0},{1,3},{3,1},{4,6},{6,4},{5,7},{7,5},{8,10},{10,8},{9,1... | collective-permute-start | bytes 1572872 | tf_op jit(solution)/shard_map/ppermute | solution.py:23
  238.0 24.0 %collective-permute-start.19 = (bf16[128,2048]{1,0:T(8,128)(2,1)}, bf16[128,2048]{1,0:T(8,128)(2,1)S(1)}, u32[]{:S(2)}, u32[]{:S(2)}) collective-permute-start(bf16[128,2048]{1,0:T(8,128)(2,1)} %slice.649), channel_id=1, source_target_pairs={{0,4},{4,0},{1,5},{5,1},{2,6},{6,2},{3,7},{7,3},{8,12},{12,8},{9,1... | collective-permute-start | bytes 1572872 | tf_op jit(solution)/shard_map/ppermute | solution.py:23
  240.0 23.1 %collective-permute-start.24 = (bf16[128,2048]{1,0:T(8,128)(2,1)}, bf16[128,2048]{1,0:T(8,128)(2,1)S(1)}, u32[]{:S(2)}, u32[]{:S(2)}) collective-permute-start(bf16[128,2048]{1,0:T(8,128)(2,1)} %slice.648), channel_id=1, source_target_pairs={{0,2},{2,0},{1,3},{3,1},{4,6},{6,4},{5,7},{7,5},{8,10},{10,8},{9,1... | collective-permute-start | bytes 1572872 | tf_op jit(solution)/shard_map/ppermute | solution.py:23
  251.7 21.6 %collective-permute-start.23 = (bf16[128,2048]{1,0:T(8,128)(2,1)}, bf16[128,2048]{1,0:T(8,128)(2,1)}, u32[]{:S(2)}, u32[]{:S(2)}) collective-permute-start(bf16[128,2048]{1,0:T(8,128)(2,1)} %fusion.25), channel_id=1, source_target_pairs={{0,2},{2,0},{1,3},{3,1},{4,6},{6,4},{5,7},{7,5},{8,10},{10,8},{9,1... | collective-permute-start | bytes 1572872 | tf_op jit(solution)/shard_map/ppermute | solution.py:23
  252.9 20.5 %collective-permute-start.26 = (bf16[128,2048]{1,0:T(8,128)(2,1)}, bf16[128,2048]{1,0:T(8,128)(2,1)}, u32[]{:S(2)}, u32[]{:S(2)}) collective-permute-start(bf16[128,2048]{1,0:T(8,128)(2,1)} %fusion.23), channel_id=1, source_target_pairs={{0,4},{4,0},{1,5},{5,1},{2,6},{6,2},{3,7},{7,3},{8,12},{12,8},{9,1... | collective-permute-start | bytes 1572872 | tf_op jit(solution)/shard_map/ppermute | solution.py:23
  281.6 15.3 %collective-permute-start.28 = (bf16[128,2048]{1,0:T(8,128)(2,1)}, bf16[128,2048]{1,0:T(8,128)(2,1)S(1)}, u32[]{:S(2)}, u32[]{:S(2)}) collective-permute-start(bf16[128,2048]{1,0:T(8,128)(2,1)} %get-tuple-element.206), channel_id=1, source_target_pairs={{0,1},{1,0},{2,3},{3,2},{4,5},{5,4},{6,7},{7,6},{8,9},{9,8},{10,11... | collective-permute-start | bytes 1572872 | tf_op jit(solution)/shard_map/ppermute | solution.py:23
  281.9 25.1 %collective-permute-start.30 = (bf16[128,2048]{1,0:T(8,128)(2,1)}, bf16[128,2048]{1,0:T(8,128)(2,1)S(1)}, u32[]{:S(2)}, u32[]{:S(2)}) collective-permute-start(bf16[128,2048]{1,0:T(8,128)(2,1)} %get-tuple-element.206), channel_id=1, source_target_pairs={{0,2},{2,0},{1,3},{3,1},{4,6},{6,4},{5,7},{7,5},{8,10},{10,8},{9,1... | collective-permute-start | bytes 1572872 | tf_op jit(solution)/shard_map/ppermute | solution.py:23
  283.6 554.4 %reduce-scatter.8.cloned.1.call-start = ((), (), s32[]{:S(2)}) async-start(), calls=%async_computation.18 | async-start | bytes 1310720 | tf_op jit(solution)/shard_map/reduce_scatter | solution.py:229
  283.8 26.9 %collective-permute-start.33 = (bf16[128,2048]{1,0:T(8,128)(2,1)S(1)}, bf16[128,2048]{1,0:T(8,128)(2,1)S(1)}, u32[]{:S(2)}, u32[]{:S(2)}) collective-permute-start(bf16[128,2048]{1,0:T(8,128)(2,1)S(1)} %get-tuple-element.207), channel_id=1, source_target_pairs={{0,4},{4,0},{1,5},{5,1},{2,6},{6,2},{3,7},{7,3},{8,12},{12,8},{9,1... | collective-permute-start | bytes 1572872 | tf_op jit(solution)/shard_map/ppermute | solution.py:23
  284.8 25.1 %collective-permute-start.34 = (bf16[128,2048]{1,0:T(8,128)(2,1)}, bf16[128,2048]{1,0:T(8,128)(2,1)S(1)}, u32[]{:S(2)}, u32[]{:S(2)}) collective-permute-start(bf16[128,2048]{1,0:T(8,128)(2,1)} %get-tuple-element.206), channel_id=1, source_target_pairs={{0,4},{4,0},{1,5},{5,1},{2,6},{6,2},{3,7},{7,3},{8,12},{12,8},{9,1... | collective-permute-start | bytes 1572872 | tf_op jit(solution)/shard_map/ppermute | solution.py:23
  296.1 15.0 %collective-permute-start.31 = (bf16[128,2048]{1,0:T(8,128)(2,1)S(1)}, bf16[128,2048]{1,0:T(8,128)(2,1)S(1)}, u32[]{:S(2)}, u32[]{:S(2)}) collective-permute-start(bf16[128,2048]{1,0:T(8,128)(2,1)S(1)} %collective-permute-done.29), channel_id=1, source_target_pairs={{0,1},{1,0},{2,3},{3,2},{4,5},{5,4},{6,7},{7,6},{8,9},{9,8},{10,11... | collective-permute-start | bytes 1572872 | tf_op jit(solution)/shard_map/ppermute | solution.py:23
  296.9 23.3 %collective-permute-start.37 = (bf16[128,2048]{1,0:T(8,128)(2,1)S(1)}, bf16[128,2048]{1,0:T(8,128)(2,1)S(1)}, u32[]{:S(2)}, u32[]{:S(2)}) collective-permute-start(bf16[128,2048]{1,0:T(8,128)(2,1)S(1)} %collective-permute-done.29), channel_id=1, source_target_pairs={{0,4},{4,0},{1,5},{5,1},{2,6},{6,2},{3,7},{7,3},{8,12},{12,8},{9,1... | collective-permute-start | bytes 1572872 | tf_op jit(solution)/shard_map/ppermute | solution.py:23
  309.9 16.9 %collective-permute-start.36 = (bf16[128,2048]{1,0:T(8,128)(2,1)S(1)}, bf16[128,2048]{1,0:T(8,128)(2,1)S(1)}, u32[]{:S(2)}, u32[]{:S(2)}) collective-permute-start(bf16[128,2048]{1,0:T(8,128)(2,1)S(1)} %collective-permute-done.34), channel_id=1, source_target_pairs={{0,1},{1,0},{2,3},{3,2},{4,5},{5,4},{6,7},{7,6},{8,9},{9,8},{10,11... | collective-permute-start | bytes 1572872 | tf_op jit(solution)/shard_map/ppermute | solution.py:23
  311.1 14.9 %collective-permute-start.35 = (bf16[128,2048]{1,0:T(8,128)(2,1)S(1)}, bf16[128,2048]{1,0:T(8,128)(2,1)S(1)}, u32[]{:S(2)}, u32[]{:S(2)}) collective-permute-start(bf16[128,2048]{1,0:T(8,128)(2,1)S(1)} %collective-permute-done.33), channel_id=1, source_target_pairs={{0,1},{1,0},{2,3},{3,2},{4,5},{5,4},{6,7},{7,6},{8,9},{9,8},{10,11... | collective-permute-start | bytes 1572872 | tf_op jit(solution)/shard_map/ppermute | solution.py:23
  409.2 15.1 %collective-permute-start.46 = (bf16[128,2048]{1,0:T(8,128)(2,1)}, bf16[128,2048]{1,0:T(8,128)(2,1)}, u32[]{:S(2)}, u32[]{:S(2)}) collective-permute-start(bf16[128,2048]{1,0:T(8,128)(2,1)} %get-tuple-element.204), channel_id=1, source_target_pairs={{0,4},{4,0},{1,5},{5,1},{2,6},{6,2},{3,7},{7,3},{8,12},{12,8},{9,1... | collective-permute-start | bytes 1572872 | tf_op jit(solution)/shard_map/ppermute | solution.py:23
  410.7 17.0 %collective-permute-start.49 = (bf16[128,2048]{1,0:T(8,128)(2,1)}, bf16[128,2048]{1,0:T(8,128)(2,1)S(1)}, u32[]{:S(2)}, u32[]{:S(2)}) collective-permute-start(bf16[128,2048]{1,0:T(8,128)(2,1)} %get-tuple-element.205), channel_id=1, source_target_pairs={{0,2},{2,0},{1,3},{3,1},{4,6},{6,4},{5,7},{7,5},{8,10},{10,8},{9,1... | collective-permute-start | bytes 1572872 | tf_op jit(solution)/shard_map/ppermute | solution.py:23
  414.4 20.9 %collective-permute-start.43 = (bf16[128,2048]{1,0:T(8,128)(2,1)}, bf16[128,2048]{1,0:T(8,128)(2,1)S(1)}, u32[]{:S(2)}, u32[]{:S(2)}) collective-permute-start(bf16[128,2048]{1,0:T(8,128)(2,1)} %slice.647), channel_id=1, source_target_pairs={{0,4},{4,0},{1,5},{5,1},{2,6},{6,2},{3,7},{7,3},{8,12},{12,8},{9,1... | collective-permute-start | bytes 1572872 | tf_op jit(solution)/shard_map/ppermute | solution.py:23
  417.1 19.9 %collective-permute-start.48 = (bf16[128,2048]{1,0:T(8,128)(2,1)}, bf16[128,2048]{1,0:T(8,128)(2,1)}, u32[]{:S(2)}, u32[]{:S(2)}) collective-permute-start(bf16[128,2048]{1,0:T(8,128)(2,1)} %slice.646), channel_id=1, source_target_pairs={{0,2},{2,0},{1,3},{3,1},{4,6},{6,4},{5,7},{7,5},{8,10},{10,8},{9,1... | collective-permute-start | bytes 1572872 | tf_op jit(solution)/shard_map/ppermute | solution.py:23
  426.2 21.0 %collective-permute-start.47 = (bf16[128,2048]{1,0:T(8,128)(2,1)}, bf16[128,2048]{1,0:T(8,128)(2,1)}, u32[]{:S(2)}, u32[]{:S(2)}) collective-permute-start(bf16[128,2048]{1,0:T(8,128)(2,1)} %fusion.21), channel_id=1, source_target_pairs={{0,2},{2,0},{1,3},{3,1},{4,6},{6,4},{5,7},{7,5},{8,10},{10,8},{9,1... | collective-permute-start | bytes 1572872 | tf_op jit(solution)/shard_map/ppermute | solution.py:23
  428.6 18.5 %collective-permute-start.50 = (bf16[128,2048]{1,0:T(8,128)(2,1)}, bf16[128,2048]{1,0:T(8,128)(2,1)}, u32[]{:S(2)}, u32[]{:S(2)}) collective-permute-start(bf16[128,2048]{1,0:T(8,128)(2,1)} %fusion.19), channel_id=1, source_target_pairs={{0,4},{4,0},{1,5},{5,1},{2,6},{6,2},{3,7},{7,3},{8,12},{12,8},{9,1... | collective-permute-start | bytes 1572872 | tf_op jit(solution)/shard_map/ppermute | solution.py:23
  453.0 14.8 %collective-permute-start.53 = (bf16[128,2048]{1,0:T(8,128)(2,1)S(1)}, bf16[128,2048]{1,0:T(8,128)(2,1)S(1)}, u32[]{:S(2)}, u32[]{:S(2)}) collective-permute-start(bf16[128,2048]{1,0:T(8,128)(2,1)S(1)} %get-tuple-element.203), channel_id=1, source_target_pairs={{0,2},{2,0},{1,3},{3,1},{4,6},{6,4},{5,7},{7,5},{8,10},{10,8},{9,1... | collective-permute-start | bytes 1572872 | tf_op jit(solution)/shard_map/ppermute | solution.py:23
  454.7 23.9 %collective-permute-start.54 = (bf16[128,2048]{1,0:T(8,128)(2,1)S(1)}, bf16[128,2048]{1,0:T(8,128)(2,1)S(1)}, u32[]{:S(2)}, u32[]{:S(2)}) collective-permute-start(bf16[128,2048]{1,0:T(8,128)(2,1)S(1)} %get-tuple-element.202), channel_id=1, source_target_pairs={{0,2},{2,0},{1,3},{3,1},{4,6},{6,4},{5,7},{7,5},{8,10},{10,8},{9,1... | collective-permute-start | bytes 1572872 | tf_op jit(solution)/shard_map/ppermute | solution.py:23
  455.3 26.1 %collective-permute-start.57 = (bf16[128,2048]{1,0:T(8,128)(2,1)S(1)}, bf16[128,2048]{1,0:T(8,128)(2,1)S(1)}, u32[]{:S(2)}, u32[]{:S(2)}) collective-permute-start(bf16[128,2048]{1,0:T(8,128)(2,1)S(1)} %get-tuple-element.203), channel_id=1, source_target_pairs={{0,4},{4,0},{1,5},{5,1},{2,6},{6,2},{3,7},{7,3},{8,12},{12,8},{9,1... | collective-permute-start | bytes 1572872 | tf_op jit(solution)/shard_map/ppermute | solution.py:23
  455.8 25.5 %collective-permute-start.58 = (bf16[128,2048]{1,0:T(8,128)(2,1)S(1)}, bf16[128,2048]{1,0:T(8,128)(2,1)S(1)}, u32[]{:S(2)}, u32[]{:S(2)}) collective-permute-start(bf16[128,2048]{1,0:T(8,128)(2,1)S(1)} %get-tuple-element.202), channel_id=1, source_target_pairs={{0,4},{4,0},{1,5},{5,1},{2,6},{6,2},{3,7},{7,3},{8,12},{12,8},{9,1... | collective-permute-start | bytes 1572872 | tf_op jit(solution)/shard_map/ppermute | solution.py:23
  467.8 15.1 %collective-permute-start.55 = (bf16[128,2048]{1,0:T(8,128)(2,1)S(1)}, bf16[128,2048]{1,0:T(8,128)(2,1)S(1)}, u32[]{:S(2)}, u32[]{:S(2)}) collective-permute-start(bf16[128,2048]{1,0:T(8,128)(2,1)S(1)} %collective-permute-done.53), channel_id=1, source_target_pairs={{0,1},{1,0},{2,3},{3,2},{4,5},{5,4},{6,7},{7,6},{8,9},{9,8},{10,11... | collective-permute-start | bytes 1572872 | tf_op jit(solution)/shard_map/ppermute | solution.py:23
  467.9 23.8 %collective-permute-start.61 = (bf16[128,2048]{1,0:T(8,128)(2,1)S(1)}, bf16[128,2048]{1,0:T(8,128)(2,1)S(1)}, u32[]{:S(2)}, u32[]{:S(2)}) collective-permute-start(bf16[128,2048]{1,0:T(8,128)(2,1)S(1)} %collective-permute-done.53), channel_id=1, source_target_pairs={{0,4},{4,0},{1,5},{5,1},{2,6},{6,2},{3,7},{7,3},{8,12},{12,8},{9,1... | collective-permute-start | bytes 1572872 | tf_op jit(solution)/shard_map/ppermute | solution.py:23
  563.2 14.8 %collective-permute-start.70 = (bf16[128,2048]{1,0:T(8,128)(2,1)S(1)}, bf16[128,2048]{1,0:T(8,128)(2,1)S(1)}, u32[]{:S(2)}, u32[]{:S(2)}) collective-permute-start(bf16[128,2048]{1,0:T(8,128)(2,1)S(1)} %get-tuple-element.200), channel_id=1, source_target_pairs={{0,4},{4,0},{1,5},{5,1},{2,6},{6,2},{3,7},{7,3},{8,12},{12,8},{9,1... | collective-permute-start | bytes 1572872 | tf_op jit(solution)/shard_map/ppermute | solution.py:23
  563.8 16.6 %collective-permute-start.73 = (bf16[128,2048]{1,0:T(8,128)(2,1)S(1)}, bf16[128,2048]{1,0:T(8,128)(2,1)S(1)}, u32[]{:S(2)}, u32[]{:S(2)}) collective-permute-start(bf16[128,2048]{1,0:T(8,128)(2,1)S(1)} %get-tuple-element.201), channel_id=1, source_target_pairs={{0,2},{2,0},{1,3},{3,1},{4,6},{6,4},{5,7},{7,5},{8,10},{10,8},{9,1... | collective-permute-start | bytes 1572872 | tf_op jit(solution)/shard_map/ppermute | solution.py:23
  566.2 23.2 %collective-permute-start.67 = (bf16[128,2048]{1,0:T(8,128)(2,1)}, bf16[128,2048]{1,0:T(8,128)(2,1)}, u32[]{:S(2)}, u32[]{:S(2)}) collective-permute-start(bf16[128,2048]{1,0:T(8,128)(2,1)} %slice.645), channel_id=1, source_target_pairs={{0,4},{4,0},{1,5},{5,1},{2,6},{6,2},{3,7},{7,3},{8,12},{12,8},{9,1... | collective-permute-start | bytes 1572872 | tf_op jit(solution)/shard_map/ppermute | solution.py:23
  568.5 21.4 %collective-permute-start.72 = (bf16[128,2048]{1,0:T(8,128)(2,1)}, bf16[128,2048]{1,0:T(8,128)(2,1)}, u32[]{:S(2)}, u32[]{:S(2)}) collective-permute-start(bf16[128,2048]{1,0:T(8,128)(2,1)} %slice.644), channel_id=1, source_target_pairs={{0,2},{2,0},{1,3},{3,1},{4,6},{6,4},{5,7},{7,5},{8,10},{10,8},{9,1... | collective-permute-start | bytes 1572872 | tf_op jit(solution)/shard_map/ppermute | solution.py:23
  579.0 21.1 %collective-permute-start.71 = (bf16[128,2048]{1,0:T(8,128)(2,1)}, bf16[128,2048]{1,0:T(8,128)(2,1)}, u32[]{:S(2)}, u32[]{:S(2)}) collective-permute-start(bf16[128,2048]{1,0:T(8,128)(2,1)} %fusion.17), channel_id=1, source_target_pairs={{0,2},{2,0},{1,3},{3,1},{4,6},{6,4},{5,7},{7,5},{8,10},{10,8},{9,1... | collective-permute-start | bytes 1572872 | tf_op jit(solution)/shard_map/ppermute | solution.py:23
  581.4 18.7 %collective-permute-start.74 = (bf16[128,2048]{1,0:T(8,128)(2,1)}, bf16[128,2048]{1,0:T(8,128)(2,1)}, u32[]{:S(2)}, u32[]{:S(2)}) collective-permute-start(bf16[128,2048]{1,0:T(8,128)(2,1)} %fusion.15), channel_id=1, source_target_pairs={{0,4},{4,0},{1,5},{5,1},{2,6},{6,2},{3,7},{7,3},{8,12},{12,8},{9,1... | collective-permute-start | bytes 1572872 | tf_op jit(solution)/shard_map/ppermute | solution.py:23
  610.8 23.8 %collective-permute-start.78 = (bf16[128,2048]{1,0:T(8,128)(2,1)S(1)}, bf16[128,2048]{1,0:T(8,128)(2,1)S(1)}, u32[]{:S(2)}, u32[]{:S(2)}) collective-permute-start(bf16[128,2048]{1,0:T(8,128)(2,1)S(1)} %get-tuple-element.198), channel_id=1, source_target_pairs={{0,2},{2,0},{1,3},{3,1},{4,6},{6,4},{5,7},{7,5},{8,10},{10,8},{9,1... | collective-permute-start | bytes 1572872 | tf_op jit(solution)/shard_map/ppermute | solution.py:23
  611.3 26.1 %collective-permute-start.81 = (bf16[128,2048]{1,0:T(8,128)(2,1)S(1)}, bf16[128,2048]{1,0:T(8,128)(2,1)S(1)}, u32[]{:S(2)}, u32[]{:S(2)}) collective-permute-start(bf16[128,2048]{1,0:T(8,128)(2,1)S(1)} %get-tuple-element.199), channel_id=1, source_target_pairs={{0,4},{4,0},{1,5},{5,1},{2,6},{6,2},{3,7},{7,3},{8,12},{12,8},{9,1... | collective-permute-start | bytes 1572872 | tf_op jit(solution)/shard_map/ppermute | solution.py:23
  612.9 24.5 %collective-permute-start.82 = (bf16[128,2048]{1,0:T(8,128)(2,1)S(1)}, bf16[128,2048]{1,0:T(8,128)(2,1)S(1)}, u32[]{:S(2)}, u32[]{:S(2)}) collective-permute-start(bf16[128,2048]{1,0:T(8,128)(2,1)S(1)} %get-tuple-element.198), channel_id=1, source_target_pairs={{0,4},{4,0},{1,5},{5,1},{2,6},{6,2},{3,7},{7,3},{8,12},{12,8},{9,1... | collective-permute-start | bytes 1572872 | tf_op jit(solution)/shard_map/ppermute | solution.py:23
  623.9 15.1 %collective-permute-start.79 = (bf16[128,2048]{1,0:T(8,128)(2,1)S(1)}, bf16[128,2048]{1,0:T(8,128)(2,1)S(1)}, u32[]{:S(2)}, u32[]{:S(2)}) collective-permute-start(bf16[128,2048]{1,0:T(8,128)(2,1)S(1)} %collective-permute-done.77), channel_id=1, source_target_pairs={{0,1},{1,0},{2,3},{3,2},{4,5},{5,4},{6,7},{7,6},{8,9},{9,8},{10,11... | collective-permute-start | bytes 1572872 | tf_op jit(solution)/shard_map/ppermute | solution.py:23
  623.9 23.8 %collective-permute-start.85 = (bf16[128,2048]{1,0:T(8,128)(2,1)S(1)}, bf16[128,2048]{1,0:T(8,128)(2,1)S(1)}, u32[]{:S(2)}, u32[]{:S(2)}) collective-permute-start(bf16[128,2048]{1,0:T(8,128)(2,1)S(1)} %collective-permute-done.77), channel_id=1, source_target_pairs={{0,4},{4,0},{1,5},{5,1},{2,6},{6,2},{3,7},{7,3},{8,12},{12,8},{9,1... | collective-permute-start | bytes 1572872 | tf_op jit(solution)/shard_map/ppermute | solution.py:23
  707.9 186.3 %reduce-scatter.6.cloned.1.call-start = ((), (), s32[]{:S(2)}) async-start(), calls=%async_computation.17 | async-start | bytes 3932160 | tf_op jit(solution)/shard_map/reduce_scatter | solution.py:300
  726.0 172.5 %reduce-scatter.10.cloned.1.call-start = ((), (), s32[]{:S(2)}) async-start(), calls=%async_computation.19 | async-start | bytes 5242880 | tf_op jit(solution)/shard_map/reduce_scatter | solution.py:229
  740.2 233.8 %reduce-scatter.12.cloned.1.call-start = ((), (), s32[]{:S(2)}) async-start(), calls=%async_computation.20 | async-start | bytes 5242880 | tf_op jit(solution)/shard_map/reduce_scatter | solution.py:229
  754.3 299.2 %reduce-scatter.14.cloned.1.call-start = ((), (), s32[]{:S(2)}) async-start(), calls=%async_computation.21 | async-start | bytes 5242880 | tf_op jit(solution)/shard_map/reduce_scatter | solution.py:229
  790.0 14.8 %collective-permute-start.97 = (bf16[128,2048]{1,0:T(8,128)(2,1)S(1)}, bf16[128,2048]{1,0:T(8,128)(2,1)S(1)}, u32[]{:S(2)}, u32[]{:S(2)}) collective-permute-start(bf16[128,2048]{1,0:T(8,128)(2,1)S(1)} %get-tuple-element.196), channel_id=1, source_target_pairs={{0,4},{4,0},{1,5},{5,1},{2,6},{6,2},{3,7},{7,3},{8,12},{12,8},{9,1... | collective-permute-start | bytes 1572872 | tf_op jit(solution)/shard_map/ppermute | solution.py:23
  790.7 15.8 %collective-permute-start.100 = (bf16[128,2048]{1,0:T(8,128)(2,1)S(1)}, bf16[128,2048]{1,0:T(8,128)(2,1)S(1)}, u32[]{:S(2)}, u32[]{:S(2)}) collective-permute-start(bf16[128,2048]{1,0:T(8,128)(2,1)S(1)} %get-tuple-element.197), channel_id=1, source_target_pairs={{0,2},{2,0},{1,3},{3,1},{4,6},{6,4},{5,7},{7,5},{8,10},{10,8},{9,1... | collective-permute-start | bytes 1572872 | tf_op jit(solution)/shard_map/ppermute | solution.py:23
  792.5 23.6 %collective-permute-start.94 = (bf16[128,2048]{1,0:T(8,128)(2,1)}, bf16[128,2048]{1,0:T(8,128)(2,1)S(1)}, u32[]{:S(2)}, u32[]{:S(2)}) collective-permute-start(bf16[128,2048]{1,0:T(8,128)(2,1)} %slice.643), channel_id=1, source_target_pairs={{0,4},{4,0},{1,5},{5,1},{2,6},{6,2},{3,7},{7,3},{8,12},{12,8},{9,1... | collective-permute-start | bytes 1572872 | tf_op jit(solution)/shard_map/ppermute | solution.py:23
  794.5 22.2 %collective-permute-start.99 = (bf16[128,2048]{1,0:T(8,128)(2,1)}, bf16[128,2048]{1,0:T(8,128)(2,1)S(1)}, u32[]{:S(2)}, u32[]{:S(2)}) collective-permute-start(bf16[128,2048]{1,0:T(8,128)(2,1)} %slice.642), channel_id=1, source_target_pairs={{0,2},{2,0},{1,3},{3,1},{4,6},{6,4},{5,7},{7,5},{8,10},{10,8},{9,1... | collective-permute-start | bytes 1572872 | tf_op jit(solution)/shard_map/ppermute | solution.py:23
  805.7 21.6 %collective-permute-start.98 = (bf16[128,2048]{1,0:T(8,128)(2,1)}, bf16[128,2048]{1,0:T(8,128)(2,1)}, u32[]{:S(2)}, u32[]{:S(2)}) collective-permute-start(bf16[128,2048]{1,0:T(8,128)(2,1)} %fusion.13), channel_id=1, source_target_pairs={{0,2},{2,0},{1,3},{3,1},{4,6},{6,4},{5,7},{7,5},{8,10},{10,8},{9,1... | collective-permute-start | bytes 1572872 | tf_op jit(solution)/shard_map/ppermute | solution.py:23
  807.4 19.9 %collective-permute-start.101 = (bf16[128,2048]{1,0:T(8,128)(2,1)}, bf16[128,2048]{1,0:T(8,128)(2,1)}, u32[]{:S(2)}, u32[]{:S(2)}) collective-permute-start(bf16[128,2048]{1,0:T(8,128)(2,1)} %fusion.11), channel_id=1, source_target_pairs={{0,4},{4,0},{1,5},{5,1},{2,6},{6,2},{3,7},{7,3},{8,12},{12,8},{9,1... | collective-permute-start | bytes 1572872 | tf_op jit(solution)/shard_map/ppermute | solution.py:23
  809.2 24.2 %all-to-all-start.7 = ((f32[32,1,256]{2,1,0:T(1,128)}), f32[32,1,256]{2,1,0:T(1,128)S(1)}, u32[]{:S(2)}, u32[]{:S(2)}) async-start(f32[32,1,256]{2,1,0:T(1,128)} %reshape.498), calls=%async_computation.9 | async-start | bytes 65536 | tf_op jit(solution)/shard_map/all_to_all | solution.py:319
  833.4 57.2 %all-to-all-start.4 = ((bf16[2,128,2048]{2,0,1:T(2,128)(2,1)}), bf16[2,128,2048]{2,0,1:T(2,128)(2,1)S(1)}, u32[]{:S(2)}, u32[]{:S(2)}) async-start(bf16[2,128,2048]{2,0,1:T(2,128)(2,1)} %copy.330), calls=%async_computation.4 | async-start | bytes 2097152 | tf_op jit(solution)/shard_map/all_to_all | solution.py:290
  894.3 162.1 %all-to-all-start.5 = ((bf16[8,64,768]{2,1,0:T(8,128)(2,1)}), bf16[8,64,768]{2,1,0:T(8,128)(2,1)}, u32[]{:S(2)}, u32[]{:S(2)}) async-start(bf16[8,64,768]{2,1,0:T(8,128)(2,1)} %bitcast.233), calls=%async_computation.6 | async-start | bytes 1572864 | tf_op jit(solution)/shard_map/all_to_all | solution.py:301
  (126 other events, 1210.2 us)
Sparse Core Ops, SparseCore 0:
  28.8 84.9 all-gather.6
  115.3 26.8 all-gather.14
  143.8 80.0 all-gather.8
  225.3 78.7 all-gather.10
  305.5 78.9 all-gather.12
  708.1 23.9 reduce-scatter.7
  734.5 58.8 reduce-scatter.5
  795.8 93.7 reduce-scatter.9
  891.9 82.0 reduce-scatter.11
  976.2 77.2 reduce-scatter.13

commit v2 on v1

--- a/solution.py
+++ b/solution.py
@@ -44,6 +44,10 @@
         ],
         axis=-1,
     )
+
+
+def after(value, *earlier):
+    return lax.optimization_barrier((value,) + earlier)[0]
 
 
 def group_gather(block):
@@ -138,6 +142,7 @@
     arrived = lax.all_to_all(outgoing, ALL, split_axis=0, concat_axis=1, tiled=True)
     x_low = arrived.reshape(rows, width)
 
+    w_query, w_key, w_value, outgoing = lax.optimization_barrier((w_query, w_key, w_value, outgoing))
     qkv_out = jnp.concatenate([heads_out(w_query), heads_out(w_key), heads_out(w_value)], axis=2)
     qkv_in = lax.all_to_all(qkv_out, GROUP, split_axis=0, concat_axis=0, tiled=True)
     w_qkv = lax.all_gather(qkv_in, "a", axis=0, tiled=True).reshape(width, 3 * own_width)
@@ -157,9 +162,9 @@
     w_out = lax.all_to_all(out_all, head_axes, split_axis=0, concat_axis=1, tiled=True)
     w_out = w_out.reshape(own_width, width)
 
-    gate = lax.all_gather(w_gate.T, "a", axis=0, tiled=True)
-    up = lax.all_gather(w_up.T, "a", axis=0, tiled=True)
-    down = lax.all_gather(w_down, "a", axis=0, tiled=True)
+    gate = lax.all_gather(after(w_gate.T, qkv_in), "a", axis=0, tiled=True)
+    up = lax.all_gather(after(w_up.T, qkv_in), "a", axis=0, tiled=True)
+    down = lax.all_gather(after(w_down, qkv_in), "a", axis=0, tiled=True)
 
     own_seqs = lax.dynamic_slice_in_dim(dealing, rank * micro_count, micro_count)
     own_lengths = jnp.take(lengths, own_seqs)
@@ -217,6 +222,10 @@
     grad_down = down_inv * (scaled - down_normed * jnp.mean(scaled * down_normed, axis=-1, keepdims=True))
     grad_down_wide = group_gather(grad_down.astype(BF))
 
+    down_term = lax.dot_general(
+        act_low, grad_down_wide, contract_rows, preferred_element_type=F32
+    ).astype(BF)
+    grad_down_wide = after(grad_down_wide, down_term)
     grad_act = lax.dot_general(grad_down_wide, down, contract_last, preferred_element_type=F32)
     grad_gate_low = (grad_act * up_proj * sigma_gate * (1.0 + gate_proj * (1.0 - sigma_gate))).astype(BF)
     grad_up_low = (grad_act * act_value).astype(BF)
@@ -226,17 +235,18 @@
     grad_hidden = grad_out + group_scatter(grad_hidden.astype(BF))
 
     def owners(term):
-        return lax.psum_scatter(term.astype(BF), "a", scatter_dimension=0, tiled=True).astype(F32)
-
-    down_part = owners(
-        lax.dot_general(act_low, grad_down_wide, contract_rows, preferred_element_type=F32)
-    )
-    gate_part = owners(
-        lax.dot_general(grad_gate_low, hidden_wide, contract_rows, preferred_element_type=F32)
-    ).T
-    up_part = owners(
-        lax.dot_general(grad_up_low, hidden_wide, contract_rows, preferred_element_type=F32)
-    ).T
+        return lax.psum_scatter(term, "a", scatter_dimension=0, tiled=True)
+
+    gate_term = lax.dot_general(
+        grad_gate_low, hidden_wide, contract_rows, preferred_element_type=F32
+    ).astype(BF)
+    up_term = lax.dot_general(
+        grad_up_low, hidden_wide, contract_rows, preferred_element_type=F32
+    ).astype(BF)
+    down_part = owners(down_term)
+    gate_part = owners(after(gate_term, down_part))
+    up_part = owners(after(up_term, gate_part))
+    grad_hidden = after(grad_hidden, gate_term, up_term)
 
     grad_gain_attn = jnp.sum(out_normed * grad_hidden, axis=0)
     scaled = grad_hidden * gain_attn
@@ -251,7 +261,7 @@
         concat_axis=0,
         tiled=True,
     )
-    output_part = owners(output_term.reshape(groups * shard, width))
+    output_part = owners(after(output_term.reshape(groups * shard, width), up_part))
 
     grad_att_low = (
         lax.dot_general(grad_out_wide, w_out, contract_last, preferred_element_type=F32)
@@ -297,7 +307,7 @@
     input_grad = jnp.zeros_like(tokens).at[dealing].set(returned)
 
     qkv_term = lax.dot_general(x_wide, grad_qkv, contract_rows, preferred_element_type=F32)
-    qkv_rows = lax.psum_scatter(qkv_term.astype(BF), "a", scatter_dimension=0, tiled=True)
+    qkv_rows = owners(after(qkv_term.astype(BF), output_part))
     qkv_back = lax.all_to_all(
         qkv_rows.reshape(PLANE, shard, 3 * own_width), GROUP, split_axis=0, concat_axis=0, tiled=True
     )
@@ -324,13 +334,13 @@
         query_part,
         key_part,
         value_part,
-        output_part,
+        output_part.astype(F32),
         gain_part[0],
         gain_part[1],
         gain_part[2],
-        gate_part,
-        up_part,
-        down_part,
+        gate_part.astype(F32).T,
+        up_part.astype(F32).T,
+        down_part.astype(F32),
         gain_part[3],
     )
 

time: 1080 us -> 912 us (0.84)
  waiting for transfers between devices: 528 us -> 330 us
  starting transfers between devices: 81.4 us -> 99.5 us
  local copies, waits for them, and re-layouts: 135 us -> 151 us
    reduce_scatter x5, waiting for transfers between devices: 148 us -> 18.1 us  [owners(): return lax.psum_scatter(term, 'a', scatter_dimension=0, tiled=True)]
    ppermute x102, waiting for transfers between devices: 252 us -> 209 us  [swap(): return lax.ppermute(value, axis, SWAP)]
    all_to_all x1, waiting for transfers between devices: 50.9 us -> 29.8 us  [per_device(): lax.all_to_all(grad_input.astype(BF).reshape(micro_count, seq_len, width)...]
    all_gather x3, starting transfers between devices: 0.34 us -> 12.1 us  [the longest x1 11.8 us: per_device(): down = lax.all_gather(after(w_down, qkv_in), 'a', axis=0, tiled=True)]
    unnamed x221 -> x227, local copies, waits for them, and re-layouts: 73 us -> 83.1 us
  transfers between devices with their start and end apart: 117 -> 117, of which waited for: 58 -> 47; matrix products, arithmetic and copies ran while one was open for 25% -> 40% of each run, Pallas kernels for 0% -> 0%
where the time goes in v2:
time: 912 us; the launch traced here: 906 us
  waiting for transfers between devices  330 us (36%)
  matrix products  191 us (21%)
  local copies, waits for them, and re-layouts  151 us (17%)
  starting transfers between devices  99.5 us (11%)
  other arithmetic  90.6 us (10%)
  blocking collectives  27.9 us (3%)
  between operations  16.4 us (2%)
    ppermute x102, waiting for transfers between devices, swap(): return lax.ppermute(value, axis, SWAP)  209 us
    unnamed x227, local copies, waits for them, and re-layouts  83.1 us
    ppermute x102, starting transfers between devices, swap(): return lax.ppermute(value, axis, SWAP)  66.4 us
    all_to_all x1, waiting for transfers between devices, per_device(): lax.all_to_all(outgoing, ALL, split_axis=0, concat_axis=1, tiled=True)  47.8 us
    all_to_all x1, waiting for transfers between devices, per_device(): lax.all_to_all(grad_input.astype(BF).reshape(micro_count, seq_len, width)...  29.8 us
    add x4, other arithmetic, group_scatter(): both = base.astype(F32) + away.astype(F32)  23.2 us
    dot_general x1, matrix products, per_device(): lax.dot_general(grad_down_wide, down, contract_last, preferred_element_ty...  23.2 us
  transfers between devices with their start and end apart: 117, of which 47 were waited for; matrix products, arithmetic and copies ran while one was open for 40% of the time, Pallas kernels for 0%

profile of v2, /device:TPU:0, one launch (start us, length us, event | category | flops | bytes accessed | tf_op | source)
XLA Modules:
  0.0 905.9 jit_solution(17013066839786619586)
XLA Ops:
  13.5 17.6 %all_to_all.83 = bf16[8,64,768]{2,1,0:T(8,128)(2,1)} all-to-all(bf16[8,64,768]{2,1,0:T(8,128)(2,1)S(1)} %pad_maximum_fusion.9), channel_id=1, replica_groups=mesh['a'=4,'y'=2,'x'=2,'c'=2] {'y','x','c'}, dimensions={0} | all-to-all | bytes 1572864 | tf_op jit(solution)/shard_map/all_to_all | solution.py:147
  31.2 4.0 all-to-all-start
  37.6 47.8 %all-to-all-done = bf16[64,4,2048]{2,1,0:T(4,128)(2,1)S(1)} async-done(((bf16[64,4,2048]{2,1,0:T(4,128)(2,1)}), bf16[64,4,2048]{2,1,0:T(4,128)(2,1)S(1)}, u32[]{:S(2)}, u32[]{:S(2)}) %all-to-all-start) | async-done | bytes 1048608 | tf_op jit(solution)/shard_map/all_to_all | solution.py:142
  85.4 6.8 all-to-all-start.2
  105.2 4.3 collective-permute-done.2
  113.1 7.0 collective-permute-done.3
  122.8 5.5 collective-permute-done.7
  133.5 5.3 collective-permute-done.10
  138.8 4.7 collective-permute-done.11
  149.4 10.8 %fusion.68 = f32[2048,768]{0,1:T(8,128)S(1)} fusion(bf16[2048,2048]{1,0:T(8,128)(2,1)} %constant_dynamic-update-slice_fusion, bf16[2048,768]{1,0:T(8,128)(2,1)} %bitcast.254), kind=kOutput, calls=%fused_computation.287 | convolution fusion | flops 6442450944 | bytes 17825792 | tf_op jit(solution)/shard_map/dot_general | solution.py:174
  166.5 5.7 all_to_all.84
  178.1 3.9 multiply_bitcast_fusion.3
  191.8 3.2 copy.199
  197.0 6.3 subtract_convert_fusion.1
  203.3 5.2 fusion.67
  219.9 11.8 %all-gather.13.cloned.1.call-start = ((), (), s32[]{:S(2)}) async-start(), calls=%async_computation.16 | async-start | bytes 5242880 | tf_op jit(solution)/shard_map/all_gather | solution.py:167
  232.7 6.8 convert_add_fusion.9
  245.4 9.0 collective-permute-done.25
  259.8 6.6 collective-permute-done.19
  266.4 10.1 %collective-permute-done.26 = bf16[128,2048]{1,0:T(8,128)(2,1)} collective-permute-done((bf16[128,2048]{1,0:T(8,128)(2,1)}, bf16[128,2048]{1,0:T(8,128)(2,1)}, u32[]{:S(2)}, u32[]{:S(2)}) %collective-permute-start.26) | collective-permute-done | bytes 524320 | tf_op jit(solution)/shard_map/ppermute | solution.py:23
  289.1 10.5 %collective-permute-done.29 = bf16[128,2048]{1,0:T(8,128)(2,1)S(1)} collective-permute-done((bf16[128,2048]{1,0:T(8,128)(2,1)}, bf16[128,2048]{1,0:T(8,128)(2,1)S(1)}, u32[]{:S(2)}, u32[]{:S(2)}) %collective-permute-start.29) | collective-permute-done | bytes 524320 | tf_op jit(solution)/shard_map/ppermute | solution.py:23
  302.5 8.0 collective-permute-done.30
  319.6 4.0 collective-permute-done.37
  323.6 6.0 collective-permute-done.38
  335.5 14.5 %fusion.69 = f32[2048,1024]{1,0:T(8,128)} fusion(bf16[2048,2048]{1,0:T(8,128)(2,1)} %constant_dynamic-update-slice_fusion.18, bf16[1024,2048]{0,1:T(8,128)(2,1)} %all-gather.9.cloned.1.call-done), kind=kOutput, calls=%fused_computation.288 | convolution fusion | flops 8589934592 | bytes 20971520 | tf_op jit(solution)/shard_map/dot_general | solution.py:207
  350.0 17.0 %multiply_convert_fusion.2 = (bf16[2048,1024]{1,0:T(8,128)(2,1)}, f32[2048,1024]{1,0:T(8,128)}) fusion(f32[2048,1024]{1,0:T(8,128)} %fusion.69, bf16[2048,2048]{1,0:T(8,128)(2,1)} %constant_dynamic-update-slice_fusion.18, bf16[1024,2048]{0,1:T(8,128)(2,1)} %all-gather.11.cloned.1.call-done), kind=kOutput, calls=%fused_computation.7 | convolution fusion | flops 8602517504 | bytes 33554432 | tf_op jit(solution)/shard_map/dot_general | solution.py:208
  367.0 16.6 %all-gather.13.cloned.1.call-done = bf16[1024,2048]{1,0:T(8,128)(2,1)} async-done(((bf16[256,2048]{1,0:T(8,128)(2,1)}), bf16[1024,2048]{1,0:T(8,128)(2,1)}) %all-gather.13.cloned.1.call-update) | async-done | bytes 4194320 | tf_op jit(solution)/shard_map/all_gather | solution.py:167
  383.6 12.3 %convolution_convert_fusion.1 = bf16[2048,2048]{1,0:T(8,128)(2,1)S(1)} fusion(bf16[2048,1024]{1,0:T(8,128)(2,1)} %get-tuple-element.229, bf16[1024,2048]{1,0:T(8,128)(2,1)} %all-gather.13.cloned.1.call-done), kind=kOutput, calls=%fused_computation.11 | convolution fusion | flops 8594128896 | bytes 16777216 | tf_op jit(solution)/shard_map/dot_general | solution.py:212
  403.5 3.7 convert_add_fusion.6
  416.6 6.7 collective-permute-done.49
  432.1 4.0 collective-permute-done.43
  436.0 10.2 %collective-permute-done.50 = bf16[128,2048]{1,0:T(8,128)(2,1)} collective-permute-done((bf16[128,2048]{1,0:T(8,128)(2,1)}, bf16[128,2048]{1,0:T(8,128)(2,1)}, u32[]{:S(2)}, u32[]{:S(2)}) %collective-permute-start.50) | collective-permute-done | bytes 524320 | tf_op jit(solution)/shard_map/ppermute | solution.py:23
  459.2 10.5 %collective-permute-done.53 = bf16[128,2048]{1,0:T(8,128)(2,1)S(1)} collective-permute-done((bf16[128,2048]{1,0:T(8,128)(2,1)S(1)}, bf16[128,2048]{1,0:T(8,128)(2,1)S(1)}, u32[]{:S(2)}, u32[]{:S(2)}) %collective-permute-start.53) | collective-permute-done | bytes 524320 | tf_op jit(solution)/shard_map/ppermute | solution.py:23
  471.3 9.2 %collective-permute-done.54 = bf16[128,2048]{1,0:T(8,128)(2,1)S(1)} collective-permute-done((bf16[128,2048]{1,0:T(8,128)(2,1)S(1)}, bf16[128,2048]{1,0:T(8,128)(2,1)S(1)}, u32[]{:S(2)}, u32[]{:S(2)}) %collective-permute-start.54) | collective-permute-done | bytes 524320 | tf_op jit(solution)/shard_map/ppermute | solution.py:23
  484.2 9.3 %collective-permute-done.61 = bf16[128,2048]{1,0:T(8,128)(2,1)S(1)} collective-permute-done((bf16[128,2048]{1,0:T(8,128)(2,1)S(1)}, bf16[128,2048]{1,0:T(8,128)(2,1)S(1)}, u32[]{:S(2)}, u32[]{:S(2)}) %collective-permute-start.61) | collective-permute-done | bytes 524320 | tf_op jit(solution)/shard_map/ppermute | solution.py:23
  493.5 4.1 collective-permute-done.62
  499.6 3.4 copy-done.47
  502.9 11.1 %convolution_convert_fusion.5 = bf16[1024,2048]{1,0:T(8,128)(2,1)} fusion(bf16[2048,1024]{1,0:T(8,128)(2,1)S(1)} %copy-done.70, bf16[2048,2048]{1,0:T(8,128)(2,1)S(1)} %constant_dynamic-update-slice_fusion.33), kind=kOutput, calls=%fused_computation.15 | convolution fusion | flops 8592031744 | bytes 16777216 | tf_op jit(solution)/shard_map/dot_general | solution.py:225
  514.1 23.2 %multiply_convert_fusion = (bf16[2048,1024]{1,0:T(8,128)(2,1)}, bf16[2048,1024]{1,0:T(8,128)(2,1)}) fusion(f32[2048,1024]{1,0:T(8,128)} %fusion.69, f32[2048,1024]{1,0:T(8,128)} %get-tuple-element.230, bf16[2048,2048]{1,0:T(8,128)(2,1)} %copy-done.47, bf16[1024,2048]{1,0:T(8,128)(2,1)} %all-gather.13.cloned.1.call-done), kind=kOutput, calls=%fused_computation.5 | convolution fusion | flops 8617197568 | bytes 37748736 | tf_op jit(solution)/shard_map/dot_general | solution.py:229
  537.3 14.0 %fusion.70 = f32[2048,2048]{1,0:T(8,128)} fusion(bf16[2048,1024]{1,0:T(8,128)(2,1)} %get-tuple-element.121, bf16[1024,2048]{0,1:T(8,128)(2,1)S(1)} %copy-done.68), kind=kOutput, calls=%fused_computation.289 | convolution fusion | flops 8589934592 | bytes 25165824 | tf_op jit(solution)/shard_map/dot_general | solution.py:232
  551.3 14.7 %add_convert_fusion = bf16[2048,2048]{1,0:T(8,128)(2,1)S(1)} fusion(f32[2048,2048]{1,0:T(8,128)} %fusion.70, bf16[2048,1024]{1,0:T(8,128)(2,1)} %get-tuple-element.120, bf16[1024,2048]{0,1:T(8,128)(2,1)} %all-gather.11.cloned.1.call-done), kind=kOutput, calls=%fused_computation.4 | convolution fusion | flops 8598323200 | bytes 33554432 | tf_op jit(solution)/shard_map/dot_general | solution.py:232
  576.6 6.0 convert_add_fusion.3
  585.6 10.6 %convolution_convert_fusion.4 = bf16[1024,2048]{1,0:T(8,128)(2,1)} fusion(bf16[2048,1024]{1,0:T(8,128)(2,1)S(1)} %copy-done.71, bf16[2048,2048]{1,0:T(8,128)(2,1)S(1)} %bitcast.229), kind=kOutput, calls=%fused_computation.14 | convolution fusion | flops 8592031744 | bytes 16777216 | tf_op jit(solution)/shard_map/dot_general | solution.py:240
  609.3 14.4 %convolution_convert_fusion.3 = bf16[1024,2048]{1,0:T(8,128)(2,1)} fusion(bf16[2048,1024]{1,0:T(8,128)(2,1)} %get-tuple-element.120, bf16[2048,2048]{1,0:T(8,128)(2,1)} %constant_dynamic-update-slice_fusion.18), kind=kOutput, calls=%fused_computation.13 | convolution fusion | flops 8592031744 | bytes 16777216 | tf_op jit(solution)/shard_map/dot_general | solution.py:243
  635.4 10.5 %collective-permute-done.77 = bf16[128,2048]{1,0:T(8,128)(2,1)S(1)} collective-permute-done((bf16[128,2048]{1,0:T(8,128)(2,1)S(1)}, bf16[128,2048]{1,0:T(8,128)(2,1)S(1)}, u32[]{:S(2)}, u32[]{:S(2)}) %collective-permute-start.77) | collective-permute-done | bytes 524320 | tf_op jit(solution)/shard_map/ppermute | solution.py:23
  648.3 8.4 collective-permute-done.78
  664.5 5.4 collective-permute-done.85
  669.9 4.8 collective-permute-done.86
  685.0 7.3 convolution_convert_fusion.8
  713.7 5.6 fusion.3
  722.8 5.7 convolution_convert_fusion.7
  732.1 4.6 all_to_all.85
  743.0 9.2 %convolution_convert_fusion = bf16[2048,2048]{1,0:T(8,128)(2,1)} fusion(bf16[2048,768]{1,0:T(8,128)(2,1)S(1)} %bitcast.255, bf16[2048,256]{0,1:T(8,128)(2,1)S(1)} %bitcast.221, bf16[2048,256]{0,1:T(8,128)(2,1)S(1)} %get-tuple-element.155, bf16[2048,256]{0,1:T(8,128)(2,1)S(1)} %get-tuple-element.154), kind=kOutput, calls=%fused_computation.10 | convolution fusion | flops 6456082432 | bytes 14680064 | tf_op jit(solution)/shard_map/dot_general | solution.py:298
  752.2 4.3 reduce-scatter.10.cloned.1.call-done
  756.8 4.5 fusion.51
  762.3 10.4 %convolution_convert_fusion.6 = bf16[2048,768]{1,0:T(8,128)(2,1)} fusion(bf16[2048,2048]{1,0:T(8,128)(2,1)} %constant_dynamic-update-slice_fusion, bf16[2048,256]{0,1:T(8,128)(2,1)S(1)} %bitcast.222, bf16[2048,256]{0,1:T(8,128)(2,1)S(1)} %copy-done.32, bf16[2048,256]{0,1:T(8,128)(2,1)S(1)} %get-tuple-element.154), kind=kOutput, calls=%fused_computation.16 | convolution fusion | flops 6453460992 | bytes 14680064 | tf_op jit(solution)/shard_map/dot_general | solution.py:309
  772.7 13.8 %reduce-scatter.12.cloned.1.call-done = bf16[64,2048]{1,0:T(8,128)(2,1)} async-done(((bf16[256,2048]{1,0:T(8,128)(2,1)}), bf16[64,2048]{1,0:T(8,128)(2,1)}) %reduce-scatter.12.cloned.1.call-update) | async-done | bytes 262160 | tf_op jit(solution)/shard_map/reduce_scatter | solution.py:238
  786.6 6.7 convert_add_fusion
  799.2 9.1 %collective-permute-done.100 = bf16[128,2048]{1,0:T(8,128)(2,1)S(1)} collective-permute-done((bf16[128,2048]{1,0:T(8,128)(2,1)S(1)}, bf16[128,2048]{1,0:T(8,128)(2,1)S(1)}, u32[]{:S(2)}, u32[]{:S(2)}) %collective-permute-start.100) | collective-permute-done | bytes 524320 | tf_op jit(solution)/shard_map/ppermute | solution.py:23
  816.7 4.3 collective-permute-done.94
  821.0 10.0 %collective-permute-done.101 = bf16[128,2048]{1,0:T(8,128)(2,1)} collective-permute-done((bf16[128,2048]{1,0:T(8,128)(2,1)}, bf16[128,2048]{1,0:T(8,128)(2,1)}, u32[]{:S(2)}, u32[]{:S(2)}) %collective-permute-start.101) | collective-permute-done | bytes 524320 | tf_op jit(solution)/shard_map/ppermute | solution.py:23
  840.3 29.8 %all-to-all-done.4 = bf16[2,128,2048]{2,0,1:T(2,128)(2,1)S(1)} async-done(((bf16[2,128,2048]{2,0,1:T(2,128)(2,1)}), bf16[2,128,2048]{2,0,1:T(2,128)(2,1)S(1)}, u32[]{:S(2)}, u32[]{:S(2)}) %all-to-all-start.4) | async-done | bytes 1048608 | tf_op jit(solution)/shard_map/all_to_all | solution.py:300
  875.3 4.5 all-to-all-start.6
  887.2 5.2 all-to-all-done.6
  (590 shorter events, 299.0 us)
Async XLA Ops:
  7.2 142.2 %all-gather.7.cloned.1.call-start = ((), (), s32[]{:S(2)}) async-start(), calls=%async_computation.13 | async-start | bytes 3932160 | tf_op jit(solution)/shard_map/all_gather | solution.py:148
  31.2 54.2 %all-to-all-start = ((bf16[64,4,2048]{2,1,0:T(4,128)(2,1)}), bf16[64,4,2048]{2,1,0:T(4,128)(2,1)S(1)}, u32[]{:S(2)}, u32[]{:S(2)}) async-start(bf16[64,4,2048]{2,1,0:T(4,128)(2,1)} %broadcast_select_fusion), calls=%async_computation | async-start | bytes 2097152 | tf_op jit(solution)/shard_map/all_to_all | solution.py:142
  35.2 131.3 %all-gather.15.cloned.1.call-start = ((), (), s32[]{:S(2)}) async-start(), calls=%async_computation.22 | async-start | bytes 1310720 | tf_op jit(solution)/shard_map/all_gather | solution.py:161
  92.1 243.3 %all-gather.9.cloned.1.call-start = ((), (), s32[]{:S(2)}) async-start(), calls=%async_computation.14 | async-start | bytes 5242880 | tf_op jit(solution)/shard_map/all_gather | solution.py:165
  99.4 250.6 %all-gather.11.cloned.1.call-start = ((), (), s32[]{:S(2)}) async-start(), calls=%async_computation.15 | async-start | bytes 5242880 | tf_op jit(solution)/shard_map/all_gather | solution.py:166
  100.9 19.1 %collective-permute-start.3 = (bf16[128,2048]{1,0:T(8,128)(2,1)S(1)}, bf16[128,2048]{1,0:T(8,128)(2,1)S(1)}, u32[]{:S(2)}, u32[]{:S(2)}) collective-permute-start(bf16[128,2048]{1,0:T(8,128)(2,1)S(1)} %slice.335), channel_id=1, source_target_pairs={{0,2},{2,0},{1,3},{3,1},{4,6},{6,4},{5,7},{7,5},{8,10},{10,8},{9,1... | collective-permute-start | bytes 1572872 | tf_op jit(solution)/shard_map/ppermute | solution.py:23
  102.3 26.8 %collective-permute-start.6 = (bf16[128,2048]{1,0:T(8,128)(2,1)S(1)}, bf16[128,2048]{1,0:T(8,128)(2,1)S(1)}, u32[]{:S(2)}, u32[]{:S(2)}) collective-permute-start(bf16[128,2048]{1,0:T(8,128)(2,1)S(1)} %slice.333), channel_id=1, source_target_pairs={{0,4},{4,0},{1,5},{5,1},{2,6},{6,2},{3,7},{7,3},{8,12},{12,8},{9,1... | collective-permute-start | bytes 1572872 | tf_op jit(solution)/shard_map/ppermute | solution.py:23
  104.0 24.3 %collective-permute-start.7 = (bf16[128,2048]{1,0:T(8,128)(2,1)S(1)}, bf16[128,2048]{1,0:T(8,128)(2,1)S(1)}, u32[]{:S(2)}, u32[]{:S(2)}) collective-permute-start(bf16[128,2048]{1,0:T(8,128)(2,1)S(1)} %slice.335), channel_id=1, source_target_pairs={{0,4},{4,0},{1,5},{5,1},{2,6},{6,2},{3,7},{7,3},{8,12},{12,8},{9,1... | collective-permute-start | bytes 1572872 | tf_op jit(solution)/shard_map/ppermute | solution.py:23
  109.5 21.2 %collective-permute-start.4 = (bf16[128,2048]{1,0:T(8,128)(2,1)}, bf16[128,2048]{1,0:T(8,128)(2,1)S(1)}, u32[]{:S(2)}, u32[]{:S(2)}) collective-permute-start(bf16[128,2048]{1,0:T(8,128)(2,1)} %collective-permute-done.2), channel_id=1, source_target_pairs={{0,1},{1,0},{2,3},{3,2},{4,5},{5,4},{6,7},{7,6},{8,9},{9,8},{10,11... | collective-permute-start | bytes 1572872 | tf_op jit(solution)/shard_map/ppermute | solution.py:23
  111.4 27.4 %collective-permute-start.10 = (bf16[128,2048]{1,0:T(8,128)(2,1)}, bf16[128,2048]{1,0:T(8,128)(2,1)S(1)}, u32[]{:S(2)}, u32[]{:S(2)}) collective-permute-start(bf16[128,2048]{1,0:T(8,128)(2,1)} %collective-permute-done.2), channel_id=1, source_target_pairs={{0,4},{4,0},{1,5},{5,1},{2,6},{6,2},{3,7},{7,3},{8,12},{12,8},{9,1... | collective-permute-start | bytes 1572872 | tf_op jit(solution)/shard_map/ppermute | solution.py:23
  128.3 16.9 %collective-permute-start.9 = (bf16[128,2048]{1,0:T(8,128)(2,1)S(1)}, bf16[128,2048]{1,0:T(8,128)(2,1)S(1)}, u32[]{:S(2)}, u32[]{:S(2)}) collective-permute-start(bf16[128,2048]{1,0:T(8,128)(2,1)S(1)} %collective-permute-done.7), channel_id=1, source_target_pairs={{0,1},{1,0},{2,3},{3,2},{4,5},{5,4},{6,7},{7,6},{8,9},{9,8},{10,11... | collective-permute-start | bytes 1572872 | tf_op jit(solution)/shard_map/ppermute | solution.py:23
  219.9 163.7 %all-gather.13.cloned.1.call-start = ((), (), s32[]{:S(2)}) async-start(), calls=%async_computation.16 | async-start | bytes 5242880 | tf_op jit(solution)/shard_map/all_gather | solution.py:167
  240.4 16.3 %collective-permute-start.22 = (bf16[128,2048]{1,0:T(8,128)(2,1)S(1)}, bf16[128,2048]{1,0:T(8,128)(2,1)S(1)}, u32[]{:S(2)}, u32[]{:S(2)}) collective-permute-start(bf16[128,2048]{1,0:T(8,128)(2,1)S(1)} %get-tuple-element.195), channel_id=1, source_target_pairs={{0,4},{4,0},{1,5},{5,1},{2,6},{6,2},{3,7},{7,3},{8,12},{12,8},{9,1... | collective-permute-start | bytes 1572872 | tf_op jit(solution)/shard_map/ppermute | solution.py:23
  242.2 24.2 %collective-permute-start.19 = (bf16[128,2048]{1,0:T(8,128)(2,1)}, bf16[128,2048]{1,0:T(8,128)(2,1)S(1)}, u32[]{:S(2)}, u32[]{:S(2)}) collective-permute-start(bf16[128,2048]{1,0:T(8,128)(2,1)} %slice.649), channel_id=1, source_target_pairs={{0,4},{4,0},{1,5},{5,1},{2,6},{6,2},{3,7},{7,3},{8,12},{12,8},{9,1... | collective-permute-start | bytes 1572872 | tf_op jit(solution)/shard_map/ppermute | solution.py:23
  244.1 22.3 %collective-permute-start.24 = (bf16[128,2048]{1,0:T(8,128)(2,1)}, bf16[128,2048]{1,0:T(8,128)(2,1)S(1)}, u32[]{:S(2)}, u32[]{:S(2)}) collective-permute-start(bf16[128,2048]{1,0:T(8,128)(2,1)} %slice.648), channel_id=1, source_target_pairs={{0,2},{2,0},{1,3},{3,1},{4,6},{6,4},{5,7},{7,5},{8,10},{10,8},{9,1... | collective-permute-start | bytes 1572872 | tf_op jit(solution)/shard_map/ppermute | solution.py:23
  255.4 21.1 %collective-permute-start.26 = (bf16[128,2048]{1,0:T(8,128)(2,1)}, bf16[128,2048]{1,0:T(8,128)(2,1)}, u32[]{:S(2)}, u32[]{:S(2)}) collective-permute-start(bf16[128,2048]{1,0:T(8,128)(2,1)} %fusion.23), channel_id=1, source_target_pairs={{0,4},{4,0},{1,5},{5,1},{2,6},{6,2},{3,7},{7,3},{8,12},{12,8},{9,1... | collective-permute-start | bytes 1572872 | tf_op jit(solution)/shard_map/ppermute | solution.py:23
  257.5 19.0 %collective-permute-start.23 = (bf16[128,2048]{1,0:T(8,128)(2,1)}, bf16[128,2048]{1,0:T(8,128)(2,1)}, u32[]{:S(2)}, u32[]{:S(2)}) collective-permute-start(bf16[128,2048]{1,0:T(8,128)(2,1)} %fusion.25), channel_id=1, source_target_pairs={{0,2},{2,0},{1,3},{3,1},{4,6},{6,4},{5,7},{7,5},{8,10},{10,8},{9,1... | collective-permute-start | bytes 1572872 | tf_op jit(solution)/shard_map/ppermute | solution.py:23
  284.6 14.9 %collective-permute-start.29 = (bf16[128,2048]{1,0:T(8,128)(2,1)}, bf16[128,2048]{1,0:T(8,128)(2,1)S(1)}, u32[]{:S(2)}, u32[]{:S(2)}) collective-permute-start(bf16[128,2048]{1,0:T(8,128)(2,1)} %get-tuple-element.194), channel_id=1, source_target_pairs={{0,2},{2,0},{1,3},{3,1},{4,6},{6,4},{5,7},{7,5},{8,10},{10,8},{9,1... | collective-permute-start | bytes 1572872 | tf_op jit(solution)/shard_map/ppermute | solution.py:23
  285.9 15.6 %collective-permute-start.28 = (bf16[128,2048]{1,0:T(8,128)(2,1)}, bf16[128,2048]{1,0:T(8,128)(2,1)}, u32[]{:S(2)}, u32[]{:S(2)}) collective-permute-start(bf16[128,2048]{1,0:T(8,128)(2,1)} %get-tuple-element.193), channel_id=1, source_target_pairs={{0,1},{1,0},{2,3},{3,2},{4,5},{5,4},{6,7},{7,6},{8,9},{9,8},{10,11... | collective-permute-start | bytes 1572872 | tf_op jit(solution)/shard_map/ppermute | solution.py:23
  286.2 24.4 %collective-permute-start.30 = (bf16[128,2048]{1,0:T(8,128)(2,1)}, bf16[128,2048]{1,0:T(8,128)(2,1)}, u32[]{:S(2)}, u32[]{:S(2)}) collective-permute-start(bf16[128,2048]{1,0:T(8,128)(2,1)} %get-tuple-element.193), channel_id=1, source_target_pairs={{0,2},{2,0},{1,3},{3,1},{4,6},{6,4},{5,7},{7,5},{8,10},{10,8},{9,1... | collective-permute-start | bytes 1572872 | tf_op jit(solution)/shard_map/ppermute | solution.py:23
  286.9 315.5 %reduce-scatter.6.cloned.1.call-start = ((), (), s32[]{:S(2)}) async-start(), calls=%async_computation.17 | async-start | bytes 5242880 | tf_op jit(solution)/shard_map/reduce_scatter | solution.py:238
  287.0 28.7 %collective-permute-start.33 = (bf16[128,2048]{1,0:T(8,128)(2,1)}, bf16[128,2048]{1,0:T(8,128)(2,1)S(1)}, u32[]{:S(2)}, u32[]{:S(2)}) collective-permute-start(bf16[128,2048]{1,0:T(8,128)(2,1)} %get-tuple-element.194), channel_id=1, source_target_pairs={{0,4},{4,0},{1,5},{5,1},{2,6},{6,2},{3,7},{7,3},{8,12},{12,8},{9,1... | collective-permute-start | bytes 1572872 | tf_op jit(solution)/shard_map/ppermute | solution.py:23
  288.0 25.3 %collective-permute-start.34 = (bf16[128,2048]{1,0:T(8,128)(2,1)}, bf16[128,2048]{1,0:T(8,128)(2,1)S(1)}, u32[]{:S(2)}, u32[]{:S(2)}) collective-permute-start(bf16[128,2048]{1,0:T(8,128)(2,1)} %get-tuple-element.193), channel_id=1, source_target_pairs={{0,4},{4,0},{1,5},{5,1},{2,6},{6,2},{3,7},{7,3},{8,12},{12,8},{9,1... | collective-permute-start | bytes 1572872 | tf_op jit(solution)/shard_map/ppermute | solution.py:23
  299.6 17.5 %collective-permute-start.31 = (bf16[128,2048]{1,0:T(8,128)(2,1)S(1)}, bf16[128,2048]{1,0:T(8,128)(2,1)S(1)}, u32[]{:S(2)}, u32[]{:S(2)}) collective-permute-start(bf16[128,2048]{1,0:T(8,128)(2,1)S(1)} %collective-permute-done.29), channel_id=1, source_target_pairs={{0,1},{1,0},{2,3},{3,2},{4,5},{5,4},{6,7},{7,6},{8,9},{9,8},{10,11... | collective-permute-start | bytes 1572872 | tf_op jit(solution)/shard_map/ppermute | solution.py:23
  301.5 22.1 %collective-permute-start.37 = (bf16[128,2048]{1,0:T(8,128)(2,1)S(1)}, bf16[128,2048]{1,0:T(8,128)(2,1)S(1)}, u32[]{:S(2)}, u32[]{:S(2)}) collective-permute-start(bf16[128,2048]{1,0:T(8,128)(2,1)S(1)} %collective-permute-done.29), channel_id=1, source_target_pairs={{0,4},{4,0},{1,5},{5,1},{2,6},{6,2},{3,7},{7,3},{8,12},{12,8},{9,1... | collective-permute-start | bytes 1572872 | tf_op jit(solution)/shard_map/ppermute | solution.py:23
  313.3 17.9 %collective-permute-start.36 = (bf16[128,2048]{1,0:T(8,128)(2,1)S(1)}, bf16[128,2048]{1,0:T(8,128)(2,1)S(1)}, u32[]{:S(2)}, u32[]{:S(2)}) collective-permute-start(bf16[128,2048]{1,0:T(8,128)(2,1)S(1)} %collective-permute-done.34), channel_id=1, source_target_pairs={{0,1},{1,0},{2,3},{3,2},{4,5},{5,4},{6,7},{7,6},{8,9},{9,8},{10,11... | collective-permute-start | bytes 1572872 | tf_op jit(solution)/shard_map/ppermute | solution.py:23
  408.3 15.1 %collective-permute-start.49 = (bf16[128,2048]{1,0:T(8,128)(2,1)}, bf16[128,2048]{1,0:T(8,128)(2,1)}, u32[]{:S(2)}, u32[]{:S(2)}) collective-permute-start(bf16[128,2048]{1,0:T(8,128)(2,1)} %get-tuple-element.192), channel_id=1, source_target_pairs={{0,2},{2,0},{1,3},{3,1},{4,6},{6,4},{5,7},{7,5},{8,10},{10,8},{9,1... | collective-permute-start | bytes 1572872 | tf_op jit(solution)/shard_map/ppermute | solution.py:23
  409.8 17.3 %collective-permute-start.46 = (bf16[128,2048]{1,0:T(8,128)(2,1)}, bf16[128,2048]{1,0:T(8,128)(2,1)S(1)}, u32[]{:S(2)}, u32[]{:S(2)}) collective-permute-start(bf16[128,2048]{1,0:T(8,128)(2,1)} %get-tuple-element.191), channel_id=1, source_target_pairs={{0,4},{4,0},{1,5},{5,1},{2,6},{6,2},{3,7},{7,3},{8,12},{12,8},{9,1... | collective-permute-start | bytes 1572872 | tf_op jit(solution)/shard_map/ppermute | solution.py:23
  413.4 22.6 %collective-permute-start.43 = (bf16[128,2048]{1,0:T(8,128)(2,1)}, bf16[128,2048]{1,0:T(8,128)(2,1)S(1)}, u32[]{:S(2)}, u32[]{:S(2)}) collective-permute-start(bf16[128,2048]{1,0:T(8,128)(2,1)} %slice.647), channel_id=1, source_target_pairs={{0,4},{4,0},{1,5},{5,1},{2,6},{6,2},{3,7},{7,3},{8,12},{12,8},{9,1... | collective-permute-start | bytes 1572872 | tf_op jit(solution)/shard_map/ppermute | solution.py:23
  416.1 20.0 %collective-permute-start.48 = (bf16[128,2048]{1,0:T(8,128)(2,1)}, bf16[128,2048]{1,0:T(8,128)(2,1)}, u32[]{:S(2)}, u32[]{:S(2)}) collective-permute-start(bf16[128,2048]{1,0:T(8,128)(2,1)} %slice.646), channel_id=1, source_target_pairs={{0,2},{2,0},{1,3},{3,1},{4,6},{6,4},{5,7},{7,5},{8,10},{10,8},{9,1... | collective-permute-start | bytes 1572872 | tf_op jit(solution)/shard_map/ppermute | solution.py:23
  425.6 20.6 %collective-permute-start.50 = (bf16[128,2048]{1,0:T(8,128)(2,1)}, bf16[128,2048]{1,0:T(8,128)(2,1)}, u32[]{:S(2)}, u32[]{:S(2)}) collective-permute-start(bf16[128,2048]{1,0:T(8,128)(2,1)} %fusion.19), channel_id=1, source_target_pairs={{0,4},{4,0},{1,5},{5,1},{2,6},{6,2},{3,7},{7,3},{8,12},{12,8},{9,1... | collective-permute-start | bytes 1572872 | tf_op jit(solution)/shard_map/ppermute | solution.py:23
  428.0 18.2 %collective-permute-start.47 = (bf16[128,2048]{1,0:T(8,128)(2,1)}, bf16[128,2048]{1,0:T(8,128)(2,1)}, u32[]{:S(2)}, u32[]{:S(2)}) collective-permute-start(bf16[128,2048]{1,0:T(8,128)(2,1)} %fusion.21), channel_id=1, source_target_pairs={{0,2},{2,0},{1,3},{3,1},{4,6},{6,4},{5,7},{7,5},{8,10},{10,8},{9,1... | collective-permute-start | bytes 1572872 | tf_op jit(solution)/shard_map/ppermute | solution.py:23
  455.6 24.8 %collective-permute-start.54 = (bf16[128,2048]{1,0:T(8,128)(2,1)S(1)}, bf16[128,2048]{1,0:T(8,128)(2,1)S(1)}, u32[]{:S(2)}, u32[]{:S(2)}) collective-permute-start(bf16[128,2048]{1,0:T(8,128)(2,1)S(1)} %get-tuple-element.189), channel_id=1, source_target_pairs={{0,2},{2,0},{1,3},{3,1},{4,6},{6,4},{5,7},{7,5},{8,10},{10,8},{9,1... | collective-permute-start | bytes 1572872 | tf_op jit(solution)/shard_map/ppermute | solution.py:23
  457.1 26.1 %collective-permute-start.57 = (bf16[128,2048]{1,0:T(8,128)(2,1)S(1)}, bf16[128,2048]{1,0:T(8,128)(2,1)S(1)}, u32[]{:S(2)}, u32[]{:S(2)}) collective-permute-start(bf16[128,2048]{1,0:T(8,128)(2,1)S(1)} %get-tuple-element.190), channel_id=1, source_target_pairs={{0,4},{4,0},{1,5},{5,1},{2,6},{6,2},{3,7},{7,3},{8,12},{12,8},{9,1... | collective-permute-start | bytes 1572872 | tf_op jit(solution)/shard_map/ppermute | solution.py:23
  458.6 24.5 %collective-permute-start.58 = (bf16[128,2048]{1,0:T(8,128)(2,1)S(1)}, bf16[128,2048]{1,0:T(8,128)(2,1)S(1)}, u32[]{:S(2)}, u32[]{:S(2)}) collective-permute-start(bf16[128,2048]{1,0:T(8,128)(2,1)S(1)} %get-tuple-element.189), channel_id=1, source_target_pairs={{0,4},{4,0},{1,5},{5,1},{2,6},{6,2},{3,7},{7,3},{8,12},{12,8},{9,1... | collective-permute-start | bytes 1572872 | tf_op jit(solution)/shard_map/ppermute | solution.py:23
  469.7 23.8 %collective-permute-start.61 = (bf16[128,2048]{1,0:T(8,128)(2,1)S(1)}, bf16[128,2048]{1,0:T(8,128)(2,1)S(1)}, u32[]{:S(2)}, u32[]{:S(2)}) collective-permute-start(bf16[128,2048]{1,0:T(8,128)(2,1)S(1)} %collective-permute-done.53), channel_id=1, source_target_pairs={{0,4},{4,0},{1,5},{5,1},{2,6},{6,2},{3,7},{7,3},{8,12},{12,8},{9,1... | collective-permute-start | bytes 1572872 | tf_op jit(solution)/shard_map/ppermute | solution.py:23
  514.1 165.2 %reduce-scatter.8.cloned.1.call-start = ((), (), s32[]{:S(2)}) async-start(), calls=%async_computation.18 | async-start | bytes 5242880 | tf_op jit(solution)/shard_map/reduce_scatter | solution.py:238
  583.7 18.9 %collective-permute-start.73 = (bf16[128,2048]{1,0:T(8,128)(2,1)}, bf16[128,2048]{1,0:T(8,128)(2,1)}, u32[]{:S(2)}, u32[]{:S(2)}) collective-permute-start(bf16[128,2048]{1,0:T(8,128)(2,1)} %get-tuple-element.188), channel_id=1, source_target_pairs={{0,2},{2,0},{1,3},{3,1},{4,6},{6,4},{5,7},{7,5},{8,10},{10,8},{9,1... | collective-permute-start | bytes 1572872 | tf_op jit(solution)/shard_map/ppermute | solution.py:23
  584.1 22.2 %collective-permute-start.70 = (bf16[128,2048]{1,0:T(8,128)(2,1)}, bf16[128,2048]{1,0:T(8,128)(2,1)}, u32[]{:S(2)}, u32[]{:S(2)}) collective-permute-start(bf16[128,2048]{1,0:T(8,128)(2,1)} %get-tuple-element.187), channel_id=1, source_target_pairs={{0,4},{4,0},{1,5},{5,1},{2,6},{6,2},{3,7},{7,3},{8,12},{12,8},{9,1... | collective-permute-start | bytes 1572872 | tf_op jit(solution)/shard_map/ppermute | solution.py:23
  598.2 25.4 %collective-permute-start.67 = (bf16[128,2048]{1,0:T(8,128)(2,1)}, bf16[128,2048]{1,0:T(8,128)(2,1)S(1)}, u32[]{:S(2)}, u32[]{:S(2)}) collective-permute-start(bf16[128,2048]{1,0:T(8,128)(2,1)} %slice.645), channel_id=1, source_target_pairs={{0,4},{4,0},{1,5},{5,1},{2,6},{6,2},{3,7},{7,3},{8,12},{12,8},{9,1... | collective-permute-start | bytes 1572872 | tf_op jit(solution)/shard_map/ppermute | solution.py:23
  600.9 22.8 %collective-permute-start.72 = (bf16[128,2048]{1,0:T(8,128)(2,1)}, bf16[128,2048]{1,0:T(8,128)(2,1)S(1)}, u32[]{:S(2)}, u32[]{:S(2)}) collective-permute-start(bf16[128,2048]{1,0:T(8,128)(2,1)} %slice.644), channel_id=1, source_target_pairs={{0,2},{2,0},{1,3},{3,1},{4,6},{6,4},{5,7},{7,5},{8,10},{10,8},{9,1... | collective-permute-start | bytes 1572872 | tf_op jit(solution)/shard_map/ppermute | solution.py:23
  602.5 154.0 %reduce-scatter.10.cloned.1.call-start = ((), (), s32[]{:S(2)}) async-start(), calls=%async_computation.19 | async-start | bytes 5242880 | tf_op jit(solution)/shard_map/reduce_scatter | solution.py:238
  604.8 18.9 %collective-permute-start.74 = (bf16[128,2048]{1,0:T(8,128)(2,1)}, bf16[128,2048]{1,0:T(8,128)(2,1)}, u32[]{:S(2)}, u32[]{:S(2)}) collective-permute-start(bf16[128,2048]{1,0:T(8,128)(2,1)} %fusion.15), channel_id=1, source_target_pairs={{0,4},{4,0},{1,5},{5,1},{2,6},{6,2},{3,7},{7,3},{8,12},{12,8},{9,1... | collective-permute-start | bytes 1572872 | tf_op jit(solution)/shard_map/ppermute | solution.py:23
  608.7 16.9 %collective-permute-start.71 = (bf16[128,2048]{1,0:T(8,128)(2,1)}, bf16[128,2048]{1,0:T(8,128)(2,1)}, u32[]{:S(2)}, u32[]{:S(2)}) collective-permute-start(bf16[128,2048]{1,0:T(8,128)(2,1)} %fusion.17), channel_id=1, source_target_pairs={{0,2},{2,0},{1,3},{3,1},{4,6},{6,4},{5,7},{7,5},{8,10},{10,8},{9,1... | collective-permute-start | bytes 1572872 | tf_op jit(solution)/shard_map/ppermute | solution.py:23
  632.9 23.8 %collective-permute-start.78 = (bf16[128,2048]{1,0:T(8,128)(2,1)S(1)}, bf16[128,2048]{1,0:T(8,128)(2,1)S(1)}, u32[]{:S(2)}, u32[]{:S(2)}) collective-permute-start(bf16[128,2048]{1,0:T(8,128)(2,1)S(1)} %get-tuple-element.185), channel_id=1, source_target_pairs={{0,2},{2,0},{1,3},{3,1},{4,6},{6,4},{5,7},{7,5},{8,10},{10,8},{9,1... | collective-permute-start | bytes 1572872 | tf_op jit(solution)/shard_map/ppermute | solution.py:23
  633.4 26.9 %collective-permute-start.81 = (bf16[128,2048]{1,0:T(8,128)(2,1)S(1)}, bf16[128,2048]{1,0:T(8,128)(2,1)S(1)}, u32[]{:S(2)}, u32[]{:S(2)}) collective-permute-start(bf16[128,2048]{1,0:T(8,128)(2,1)S(1)} %get-tuple-element.186), channel_id=1, source_target_pairs={{0,4},{4,0},{1,5},{5,1},{2,6},{6,2},{3,7},{7,3},{8,12},{12,8},{9,1... | collective-permute-start | bytes 1572872 | tf_op jit(solution)/shard_map/ppermute | solution.py:23
  634.9 24.5 %collective-permute-start.82 = (bf16[128,2048]{1,0:T(8,128)(2,1)S(1)}, bf16[128,2048]{1,0:T(8,128)(2,1)S(1)}, u32[]{:S(2)}, u32[]{:S(2)}) collective-permute-start(bf16[128,2048]{1,0:T(8,128)(2,1)S(1)} %get-tuple-element.185), channel_id=1, source_target_pairs={{0,4},{4,0},{1,5},{5,1},{2,6},{6,2},{3,7},{7,3},{8,12},{12,8},{9,1... | collective-permute-start | bytes 1572872 | tf_op jit(solution)/shard_map/ppermute | solution.py:23
  645.9 15.8 %collective-permute-start.79 = (bf16[128,2048]{1,0:T(8,128)(2,1)S(1)}, bf16[128,2048]{1,0:T(8,128)(2,1)S(1)}, u32[]{:S(2)}, u32[]{:S(2)}) collective-permute-start(bf16[128,2048]{1,0:T(8,128)(2,1)S(1)} %collective-permute-done.77), channel_id=1, source_target_pairs={{0,1},{1,0},{2,3},{3,2},{4,5},{5,4},{6,7},{7,6},{8,9},{9,8},{10,11... | collective-permute-start | bytes 1572872 | tf_op jit(solution)/shard_map/ppermute | solution.py:23
  646.8 23.1 %collective-permute-start.85 = (bf16[128,2048]{1,0:T(8,128)(2,1)S(1)}, bf16[128,2048]{1,0:T(8,128)(2,1)}, u32[]{:S(2)}, u32[]{:S(2)}) collective-permute-start(bf16[128,2048]{1,0:T(8,128)(2,1)S(1)} %collective-permute-done.77), channel_id=1, source_target_pairs={{0,4},{4,0},{1,5},{5,1},{2,6},{6,2},{3,7},{7,3},{8,12},{12,8},{9,1... | collective-permute-start | bytes 1572872 | tf_op jit(solution)/shard_map/ppermute | solution.py:23
  659.4 17.0 %collective-permute-start.84 = (bf16[128,2048]{1,0:T(8,128)(2,1)S(1)}, bf16[128,2048]{1,0:T(8,128)(2,1)S(1)}, u32[]{:S(2)}, u32[]{:S(2)}) collective-permute-start(bf16[128,2048]{1,0:T(8,128)(2,1)S(1)} %collective-permute-done.82), channel_id=1, source_target_pairs={{0,1},{1,0},{2,3},{3,2},{4,5},{5,4},{6,7},{7,6},{8,9},{9,8},{10,11... | collective-permute-start | bytes 1572872 | tf_op jit(solution)/shard_map/ppermute | solution.py:23
  679.2 107.3 %reduce-scatter.12.cloned.1.call-start = ((), (), s32[]{:S(2)}) async-start(), calls=%async_computation.20 | async-start | bytes 1310720 | tf_op jit(solution)/shard_map/reduce_scatter | solution.py:238
  756.5 118.8 %reduce-scatter.14.cloned.1.call-start = ((), (), s32[]{:S(2)}) async-start(), calls=%async_computation.21 | async-start | bytes 3932160 | tf_op jit(solution)/shard_map/reduce_scatter | solution.py:238
  761.3 25.3 %collective-permute-start.92 = (bf16[256,2048]{1,0:T(8,128)(2,1)}, bf16[256,2048]{1,0:T(8,128)(2,1)}, u32[]{:S(2)}, u32[]{:S(2)}) collective-permute-start(bf16[256,2048]{1,0:T(8,128)(2,1)} %get-tuple-element.129), channel_id=1, source_target_pairs={{0,1},{1,0},{2,3},{3,2},{4,5},{5,4},{6,7},{7,6},{8,9},{9,8},{10,11... | collective-permute-start | bytes 3145736 | tf_op jit(solution)/shard_map/ppermute | solution.py:23
  761.3 25.3 %collective-permute-start.93 = (bf16[256,2048]{1,0:T(8,128)(2,1)}, bf16[256,2048]{1,0:T(8,128)(2,1)}, u32[]{:S(2)}, u32[]{:S(2)}) collective-permute-start(bf16[256,2048]{1,0:T(8,128)(2,1)} %get-tuple-element.128), channel_id=1, source_target_pairs={{0,1},{1,0},{2,3},{3,2},{4,5},{5,4},{6,7},{7,6},{8,9},{9,8},{10,11... | collective-permute-start | bytes 3145736 | tf_op jit(solution)/shard_map/ppermute | solution.py:23
  761.8 24.8 %collective-permute-start.95 = (bf16[256,2048]{1,0:T(8,128)(2,1)}, bf16[256,2048]{1,0:T(8,128)(2,1)}, u32[]{:S(2)}, u32[]{:S(2)}) collective-permute-start(bf16[256,2048]{1,0:T(8,128)(2,1)} %get-tuple-element.126), channel_id=1, source_target_pairs={{0,1},{1,0},{2,3},{3,2},{4,5},{5,4},{6,7},{7,6},{8,9},{9,8},{10,11... | collective-permute-start | bytes 3145736 | tf_op jit(solution)/shard_map/ppermute | solution.py:23
  761.8 24.8 %collective-permute-start.96 = (bf16[256,2048]{1,0:T(8,128)(2,1)}, bf16[256,2048]{1,0:T(8,128)(2,1)}, u32[]{:S(2)}, u32[]{:S(2)}) collective-permute-start(bf16[256,2048]{1,0:T(8,128)(2,1)} %get-tuple-element.127), channel_id=1, source_target_pairs={{0,1},{1,0},{2,3},{3,2},{4,5},{5,4},{6,7},{7,6},{8,9},{9,8},{10,11... | collective-permute-start | bytes 3145736 | tf_op jit(solution)/shard_map/ppermute | solution.py:23
  794.9 15.8 %collective-permute-start.97 = (bf16[128,2048]{1,0:T(8,128)(2,1)S(1)}, bf16[128,2048]{1,0:T(8,128)(2,1)S(1)}, u32[]{:S(2)}, u32[]{:S(2)}) collective-permute-start(bf16[128,2048]{1,0:T(8,128)(2,1)S(1)} %get-tuple-element.183), channel_id=1, source_target_pairs={{0,4},{4,0},{1,5},{5,1},{2,6},{6,2},{3,7},{7,3},{8,12},{12,8},{9,1... | collective-permute-start | bytes 1572872 | tf_op jit(solution)/shard_map/ppermute | solution.py:23
  797.2 23.7 %collective-permute-start.94 = (bf16[128,2048]{1,0:T(8,128)(2,1)}, bf16[128,2048]{1,0:T(8,128)(2,1)S(1)}, u32[]{:S(2)}, u32[]{:S(2)}) collective-permute-start(bf16[128,2048]{1,0:T(8,128)(2,1)} %slice.643), channel_id=1, source_target_pairs={{0,4},{4,0},{1,5},{5,1},{2,6},{6,2},{3,7},{7,3},{8,12},{12,8},{9,1... | collective-permute-start | bytes 1572872 | tf_op jit(solution)/shard_map/ppermute | solution.py:23
  798.6 22.4 %collective-permute-start.99 = (bf16[128,2048]{1,0:T(8,128)(2,1)}, bf16[128,2048]{1,0:T(8,128)(2,1)S(1)}, u32[]{:S(2)}, u32[]{:S(2)}) collective-permute-start(bf16[128,2048]{1,0:T(8,128)(2,1)} %slice.642), channel_id=1, source_target_pairs={{0,2},{2,0},{1,3},{3,1},{4,6},{6,4},{5,7},{7,5},{8,10},{10,8},{9,1... | collective-permute-start | bytes 1572872 | tf_op jit(solution)/shard_map/ppermute | solution.py:23
  809.2 21.9 %collective-permute-start.101 = (bf16[128,2048]{1,0:T(8,128)(2,1)}, bf16[128,2048]{1,0:T(8,128)(2,1)}, u32[]{:S(2)}, u32[]{:S(2)}) collective-permute-start(bf16[128,2048]{1,0:T(8,128)(2,1)} %fusion.11), channel_id=1, source_target_pairs={{0,4},{4,0},{1,5},{5,1},{2,6},{6,2},{3,7},{7,3},{8,12},{12,8},{9,1... | collective-permute-start | bytes 1572872 | tf_op jit(solution)/shard_map/ppermute | solution.py:23
  811.6 19.5 %collective-permute-start.98 = (bf16[128,2048]{1,0:T(8,128)(2,1)}, bf16[128,2048]{1,0:T(8,128)(2,1)}, u32[]{:S(2)}, u32[]{:S(2)}) collective-permute-start(bf16[128,2048]{1,0:T(8,128)(2,1)} %fusion.13), channel_id=1, source_target_pairs={{0,2},{2,0},{1,3},{3,1},{4,6},{6,4},{5,7},{7,5},{8,10},{10,8},{9,1... | collective-permute-start | bytes 1572872 | tf_op jit(solution)/shard_map/ppermute | solution.py:23
  814.1 21.6 %all-to-all-start.7 = ((f32[32,1,256]{2,1,0:T(1,128)}), f32[32,1,256]{2,1,0:T(1,128)S(1)}, u32[]{:S(2)}, u32[]{:S(2)}) async-start(f32[32,1,256]{2,1,0:T(1,128)} %reshape.459), calls=%async_computation.12 | async-start | bytes 65536 | tf_op jit(solution)/shard_map/all_to_all | solution.py:329
  835.7 34.3 %all-to-all-start.4 = ((bf16[2,128,2048]{2,0,1:T(2,128)(2,1)}), bf16[2,128,2048]{2,0,1:T(2,128)(2,1)S(1)}, u32[]{:S(2)}, u32[]{:S(2)}) async-start(bf16[2,128,2048]{2,0,1:T(2,128)(2,1)} %copy.179), calls=%async_computation.4 | async-start | bytes 2097152 | tf_op jit(solution)/shard_map/all_to_all | solution.py:300
  875.3 17.1 %all-to-all-start.6 = ((bf16[8,64,768]{2,1,0:T(8,128)(2,1)}), bf16[8,64,768]{2,1,0:T(8,128)(2,1)}, u32[]{:S(2)}, u32[]{:S(2)}) async-start(bf16[8,64,768]{2,1,0:T(8,128)(2,1)} %bitcast.227), calls=%async_computation.11 | async-start | bytes 1572864 | tf_op jit(solution)/shard_map/all_to_all | solution.py:311
  (129 other events, 1170.8 us)
Sparse Core Ops, SparseCore 0:
  31.3 81.3 all-gather.6
  114.2 27.0 all-gather.14
  142.9 80.0 all-gather.8
  224.4 78.7 all-gather.10
  304.6 78.9 all-gather.12
  514.2 74.3 reduce-scatter.5
  602.6 74.2 reduce-scatter.7
  679.4 77.0 reduce-scatter.9
  758.9 27.6 reduce-scatter.11
  788.7 62.7 reduce-scatter.13

commit v3 on v2

v3 whole, which is shorter than its diff:
```python
import math

import jax
import jax.numpy as jnp
from jax import lax
from jax.experimental import pallas as pl
from jax.experimental.pallas import tpu as pltpu
from jax.sharding import Mesh
from jax.sharding import PartitionSpec as P

HEADS = 16
PLANE = 8
BF = jnp.bfloat16
F32 = jnp.float32

norm_eps = 1e-06
rope_base = 500000.0

ALL = ("z", "m", "y", "x", "c")
GROUP = ("y", "x", "c")
REST = ("z", "m")
LINE = 4
SWAP = [(0, 1), (1, 0)]


def swap(value, axis):
    return lax.ppermute(value, axis, SWAP)


def rotary_tables(length, head_dim):
    half_dim = head_dim // 2
    exponents = jnp.arange(half_dim, dtype=F32) * (2.0 / head_dim)
    frequency = jnp.power(F32(rope_base), -exponents)
    angles = jnp.arange(length, dtype=F32)[:, None] * frequency[None, :]
    return (jnp.cos(angles), jnp.sin(angles))


def wide_tables(length, head_dim):
    cosines, sines = rotary_tables(length, head_dim)
    return (
        jnp.concatenate([cosines, cosines], axis=1),
        jnp.concatenate([-sines, sines], axis=1),
    )


def by_rows(vector, columns):
    return jnp.broadcast_to(vector, (columns, vector.shape[1])).T


def row_sums(values):
    return jnp.sum(values.T, axis=0, keepdims=True)


def matmul(left, right, left_dim=1, right_dim=0):
    return lax.dot_general(left, right, (((left_dim,), (right_dim,)), ((), ())), preferred_element_type=F32)


def turn(values, cosines, sines):
    return values * cosines + pltpu.roll(values, values.shape[1] // 2, 1) * sines


def project_kernel(parts, x_ref, w_ref, raw_ref, squares_ref):
    raw = matmul(x_ref[...], w_ref[...])
    raw_ref[...] = raw
    width = raw.shape[1] // 3
    step = raw.shape[0] // parts
    for part in range(parts):
        rows = slice(part * step, (part + 1) * step)
        for kind in range(2):
            piece = raw[rows, kind * width : (kind + 1) * width]
            squares_ref[kind : kind + 1, rows] = row_sums(piece * piece)


def project(x_wide, weight, seq_len):
    wide, width = x_wide.shape
    out = weight.shape[1]
    block = 2 * seq_len
    return pl.pallas_call(
        lambda *refs: project_kernel(2, *refs),
        grid=(wide // block,),
        in_specs=[pl.BlockSpec((block, width), lambda i: (i, 0)), pl.BlockSpec((width, out), lambda i: (0, 0))],
        out_specs=[pl.BlockSpec((block, out), lambda i: (i, 0)), pl.BlockSpec((2, block), lambda i: (0, i))],
        out_shape=[jax.ShapeDtypeStruct((wide, out), F32), jax.ShapeDtypeStruct((2, wide), F32)],
        cost_estimate=pl.CostEstimate(
            flops=2 * wide * width * out, bytes_accessed=2 * wide * width + 2 * width * out + 4 * wide * out, transcendentals=0
        ),
        name="project",
    )(x_wide, weight)


def soften(scores, causal):
    scores = jnp.where(causal, scores, -1e30)
    exps = jnp.exp(scores - jnp.max(scores, axis=1, keepdims=True))
    return exps * (1.0 / jnp.sum(exps, axis=1, keepdims=True))


def causal_mask(length):
    rows = lax.broadcasted_iota(jnp.int32, (length, length), 0)
    return lax.broadcasted_iota(jnp.int32, (length, length), 1) <= rows


def heads_of(raw_ref, inverses, gain_ref, cosines, sines, rows, head, heads):
    dim = cosines.shape[1]
    out = []
    for kind in range(2):
        at = (kind * heads + head) * dim
        normed = raw_ref[rows, at : at + dim] * inverses[kind]
        gain = gain_ref[kind : kind + 1, head * dim : (head + 1) * dim]
        out += [normed, turn(normed * gain, cosines, sines).astype(BF), gain]
    at = (2 * heads + head) * dim
    return out + [raw_ref[rows, at : at + dim].astype(BF)]


def attend_kernel(heads, parts, scale, raw_ref, inv_ref, gain_ref, cos_ref, sin_ref, out_ref):
    cosines, sines = cos_ref[...], sin_ref[...]
    length, dim = cosines.shape
    causal = causal_mask(length)
    for part in range(parts):
        rows = slice(part * length, (part + 1) * length)
        inverses = [by_rows(inv_ref[kind : kind + 1, rows], dim) for kind in range(2)]
        for head in range(heads):
            _, query, _, _, key, _, value = heads_of(raw_ref, inverses, gain_ref, cosines, sines, rows, head, heads)
            soft = soften(matmul(query, key, 1, 1) * scale, causal)
            out_ref[rows, head * dim : (head + 1) * dim] = matmul(soft.astype(BF), value).astype(BF)


def attend_back_kernel(
    heads, parts, scale, raw_ref, inv_ref, gain_ref, cos_ref, sin_ref, grad_ref, scaled_ref, value_ref, dots_ref, gains_ref
):
    cosines, sines = cos_ref[...], sin_ref[...]
    length, dim = cosines.shape
    causal = causal_mask(length)

    @pl.when(pl.program_id(0) == 0)
    def _():
        gains_ref[...] = jnp.zeros_like(gains_ref)

    for part in range(parts):
        rows = slice(part * length, (part + 1) * length)
        inverses = [by_rows(inv_ref[kind : kind + 1, rows], dim) for kind in range(2)]
        dots = [0.0, 0.0]
        for head in range(heads):
            query_normed, query, query_gain, key_normed, key, key_gain, value = heads_of(
                raw_ref, inverses, gain_ref, cosines, sines, rows, head, heads
            )
            columns = slice(head * dim, (head + 1) * dim)
            soft = soften(matmul(query, key, 1, 1) * scale, causal)
            grad = grad_ref[rows, columns]
            grad_soft = matmul(grad, value, 1, 1)
            delta = jnp.sum(soft * grad_soft, axis=1, keepdims=True)
            grad_scores = (soft * (grad_soft - delta)).astype(BF)
            value_ref[rows, columns] = matmul(soft.astype(BF), grad, 0, 0).astype(BF)
            turned = (matmul(grad_scores, key) * scale, matmul(grad_scores, query, 0, 0) * scale)
            for kind, normed, gain in ((0, query_normed, query_gain), (1, key_normed, key_gain)):
                back = turn(turned[kind], cosines, -sines)
                gains_ref[kind : kind + 1, columns] += jnp.sum(normed * back, axis=0, keepdims=True)
                scaled = back * gain
                scaled_ref[rows, (kind * heads + head) * dim : (kind * heads + head + 1) * dim] = scaled
                dots[kind] = dots[kind] + scaled * normed
        for kind in range(2):
            dots_ref[kind : kind + 1, rows] = row_sums(dots[kind])


def finish_kernel(heads, parts, length, raw_ref, inv_ref, means_ref, scaled_ref, value_ref, out_ref):
    width = value_ref.shape[1]
    for part in range(parts):
        rows = slice(part * length, (part + 1) * length)
        for kind in range(2):
            columns = slice(kind * width, (kind + 1) * width)
            inverse = by_rows(inv_ref[kind : kind + 1, rows], width)
            mean = by_rows(means_ref[kind : kind + 1, rows], width)
            normed = raw_ref[rows, columns] * inverse
            out_ref[rows, columns] = (inverse * (scaled_ref[rows, columns] - normed * mean)).astype(BF)
        out_ref[rows, 2 * width :] = value_ref[rows, :]


def block_specs(block, heads, dim, length):
    own = heads * dim
    rows = lambda columns: pl.BlockSpec((block, columns), lambda i: (i, 0))
    lanes = pl.BlockSpec((2, block), lambda i: (0, i))
    fixed = lambda shape: pl.BlockSpec(shape, lambda i: (0, 0))
    return own, rows, lanes, [rows(3 * own), lanes, fixed((2, own)), fixed((length, dim)), fixed((length, dim))]


def attend(raw, inverses, gains, tables, heads):
    length, dim = tables[0].shape
    wide = raw.shape[0]
    block = 2 * length
    own, rows, _, specs = block_specs(block, heads, dim, length)
    return pl.pallas_call(
        lambda *refs: attend_kernel(heads, 2, 1.0 / math.sqrt(dim), *refs),
        grid=(wide // block,),
        in_specs=specs,
        out_specs=rows(own),
        out_shape=jax.ShapeDtypeStruct((wide, own), BF),
        cost_estimate=pl.CostEstimate(
            flops=4 * wide * length * own, bytes_accessed=14 * wide * own, transcendentals=wide * length * heads
        ),
        name="attend",
    )(raw, inverses, gains, *tables)


def attend_back(raw, inverses, gains, tables, heads, grad):
    length, dim = tables[0].shape
    wide = raw.shape[0]
    block = 2 * length
    own, rows, lanes, specs = block_specs(block, heads, dim, length)
    return pl.pallas_call(
        lambda *refs: attend_back_kernel(heads, 2, 1.0 / math.sqrt(dim), *refs),
        grid=(wide // block,),
        in_specs=specs + [rows(own)],
        out_specs=[rows(2 * own), rows(own), lanes, pl.BlockSpec((2, own), lambda i: (0, 0))],
        out_shape=[
            jax.ShapeDtypeStruct((wide, 2 * own), F32),
            jax.ShapeDtypeStruct((wide, own), BF),
            jax.ShapeDtypeStruct((2, wide), F32),
            jax.ShapeDtypeStruct((2, own), F32),
        ],
        cost_estimate=pl.CostEstimate(
            flops=10 * wide * length * own, bytes_accessed=26 * wide * own, transcendentals=wide * length * heads
        ),
        name="attend_back",
    )(raw, inverses, gains, *tables, grad)


def finish(raw, inverses, means, scaled, value, length, heads):
    wide, own = value.shape
    block = 2 * length
    rows = lambda columns: pl.BlockSpec((block, columns), lambda i: (i, 0))
    lanes = pl.BlockSpec((2, block), lambda i: (0, i))
    return pl.pallas_call(
        lambda *refs: finish_kernel(heads, 2, length, *refs),
        grid=(wide // block,),
        in_specs=[rows(3 * own), lanes, lanes, rows(2 * own), rows(own)],
        out_specs=rows(3 * own),
        out_shape=jax.ShapeDtypeStruct((wide, 3 * own), BF),
        cost_estimate=pl.CostEstimate(flops=8 * wide * own, bytes_accessed=28 * wide * own, transcendentals=0),
        name="finish",
    )(raw, inverses, means, scaled, value)


def after(value, *earlier):
    return lax.optimization_barrier((value,) + earlier)[0]


def group_gather(block, meanwhile=None):
    half = block.shape[0] // 2
    over_x, over_y = swap(block, "x"), swap(block, "y")
    near_x, near_y = over_x[:half], over_y[half:]
    done = None
    if meanwhile is not None:
        done = meanwhile(block)
        near_x, near_y, _ = lax.optimization_barrier((near_x, near_y, done))
    pieces = [block, over_x, over_y, swap(near_x, "y"), swap(near_y, "x")]
    return jnp.concatenate(pieces + [swap(piece, "c") for piece in pieces], axis=0), over_x, done


def group_scatter(partial, meanwhile=None):
    wide = partial.shape[0] // 2
    rows = wide // 4
    half = rows // 2

    def both(i):
        away = swap(partial[wide + i * rows : wide + (i + 1) * rows], "c")
        return partial[i * rows : (i + 1) * rows].astype(F32) + away.astype(F32)

    def move(value, axis):
        return swap(value.astype(BF), axis).astype(F32)

    far, over_x, over_y, own = both(3), both(1), both(2), both(0)
    far_low, far_high = far[:half].astype(BF), far[half:].astype(BF)
    far_x, far_y = swap(far_low, "x"), swap(far_high, "y")
    done = None
    if meanwhile is not None:
        done = meanwhile(far_low)
        far_x, far_y, _ = lax.optimization_barrier((far_x, far_y, done))
    over_y = jnp.concatenate([over_y[:half] + far_x.astype(F32), over_y[half:]])
    over_x = jnp.concatenate([over_x[:half], over_x[half:] + far_y.astype(F32)])
    return own + move(over_x, "x") + move(over_y, "y"), done


def ring(ahead):
    return [(i, (i + ahead) % LINE) for i in range(LINE)]


def line_gather(block, at):
    out = jnp.zeros((LINE,) + block.shape, block.dtype)
    out = lax.dynamic_update_index_in_dim(out, block, at, 0)
    for ahead in range(1, LINE):
        moved = lax.ppermute(block, "z", ring(ahead))
        out = lax.dynamic_update_index_in_dim(out, moved, (at - ahead) % LINE, 0)
    return out


def line_sum(blocks, at):
    total = lax.dynamic_index_in_dim(blocks, at, 0, keepdims=False).astype(F32)
    for ahead in range(1, LINE):
        block = lax.dynamic_index_in_dim(blocks, (at + ahead) % LINE, 0, keepdims=False)
        total = total + lax.ppermute(block, "z", ring(ahead)).astype(F32)
    return total


def group_total(value):
    kinds, wide = value.shape
    split = value.reshape(kinds, 2, 2, 2, wide // PLANE)
    for axis, dim in (("c", 1), ("x", 3), ("y", 2)):
        split = split + jnp.flip(swap(split, axis), dim)
    return split.reshape(kinds, wide)


def per_device(
    tokens,
    lengths,
    dealing,
    w_query,
    w_key,
    w_value,
    w_output,
    query_gain,
    key_gain,
    attn_gain,
    w_gate,
    w_up,
    w_down,
    mlp_gain,
    cotangent,
):
    groups = lax.axis_size(REST)
    total = groups * PLANE
    rank = lax.axis_index(ALL)
    place = lax.axis_index(GROUP)
    at = lax.axis_index("z")
    along = lax.axis_size("m")
    micro_count, seq_len, width = cotangent.shape
    rows = micro_count * seq_len
    wide = rows * PLANE
    shard = width // total
    head_dim = width // HEADS
    own_heads = HEADS // PLANE
    own_width = own_heads * head_dim
    spread = head_dim // shard
    head_axes = GROUP[3 - (spread.bit_length() - 1) :]
    fan = PLANE // spread
    lead, lane = place // spread, place % spread

    tables = wide_tables(seq_len, head_dim)
    positions = jnp.arange(seq_len, dtype=jnp.int32)

    def heads_out(weight):
        split = weight.reshape(shard, spread, own_heads, fan, head_dim)
        return split.transpose(3, 1, 0, 2, 4).reshape(PLANE, shard, own_width)

    outgoing = jnp.take(tokens, dealing, axis=0)
    arrived = lax.all_to_all(outgoing, ALL, split_axis=0, concat_axis=1, tiled=True)
    x_low = arrived.reshape(rows, width)

    w_query, w_key, w_value, outgoing = lax.optimization_barrier((w_query, w_key, w_value, outgoing))
    qkv_out = jnp.concatenate([heads_out(w_query), heads_out(w_key), heads_out(w_value)], axis=2)
    qkv_in = lax.all_to_all(qkv_out, GROUP, split_axis=0, concat_axis=0, tiled=True)

    gains = jnp.stack([query_gain, key_gain, attn_gain, mlp_gain])
    gains = lax.all_to_all(
        jnp.broadcast_to(gains[None], (total, 4, shard)), ALL, split_axis=0, concat_axis=0, tiled=True
    )
    gains = gains.transpose(1, 0, 2).reshape(4, width).astype(F32)
    by_head = gains[:2].reshape(2, spread, own_heads, fan, head_dim)
    by_head = lax.dynamic_index_in_dim(by_head, lane, 1, keepdims=False)
    by_head = lax.dynamic_index_in_dim(by_head, lead, 2, keepdims=False)
    gain_heads = by_head.reshape(2, own_width)
    gain_attn, gain_mlp = gains[2], gains[3]

    out_all = w_output
    if along > 1:
        out_all = lax.all_gather(out_all, "m", axis=0, tiled=True)
    out_all = line_gather(out_all, at).reshape(groups, shard, width)
    qkv_in = after(qkv_in, out_all)
    w_qkv = lax.all_gather(qkv_in, REST, axis=0, tiled=True).reshape(width, 3 * own_width)
    w_out = lax.all_to_all(out_all, head_axes, split_axis=0, concat_axis=1, tiled=True)
    w_out = w_out.reshape(own_width, width)

    gate = lax.all_gather(after(w_gate.T, qkv_in), REST, axis=0, tiled=True)
    up = lax.all_gather(after(w_up.T, qkv_in), REST, axis=0, tiled=True)
    down = lax.all_gather(after(w_down, qkv_in), REST, axis=0, tiled=True)

    own_seqs = lax.dynamic_slice_in_dim(dealing, rank * micro_count, micro_count)
    own_lengths = jnp.take(lengths, own_seqs)
    valid_mask = (positions[None, :] < own_lengths[:, None]).astype(F32).reshape(rows, 1)

    x_wide, _, _ = group_gather(x_low)
    qkv_raw, squares = project(x_wide, w_qkv, seq_len)
    inverses = lax.rsqrt(group_total(squares) * (1.0 / width) + norm_eps)
    attended_low = attend(qkv_raw, inverses, gain_heads, tables, own_heads)
    out_raw, _ = group_scatter(jnp.dot(attended_low, w_out, preferred_element_type=F32).astype(BF))
    out_inv = lax.rsqrt(jnp.mean(out_raw * out_raw, axis=-1, keepdims=True) + norm_eps)
    out_normed = out_raw * out_inv
    hidden = x_low.astype(F32) + out_normed * gain_attn

    hidden_wide, _, _ = group_gather(hidden.astype(BF))
    contract_last = (((1,), (1,)), ((), ()))
    contract_rows = (((0,), (0,)), ((), ()))
    gate_proj = lax.dot_general(hidden_wide, gate, contract_last, preferred_element_type=F32)
    up_proj = lax.dot_general(hidden_wide, up, contract_last, preferred_element_type=F32)
    sigma_gate = jax.nn.sigmoid(gate_proj)
    act_value = gate_proj * sigma_gate
    act_low = (act_value * up_proj).astype(BF)
    down_raw, _ = group_scatter(jnp.dot(act_low, down, preferred_element_type=F32).astype(BF))
    down_inv = lax.rsqrt(jnp.mean(down_raw * down_raw, axis=-1, keepdims=True) + norm_eps)
    down_normed = down_raw * down_inv
    block_out = (
        (valid_mask * (hidden + down_normed * gain_mlp)).astype(BF).reshape(micro_count, seq_len, width)
    )

    grad_out = valid_mask * cotangent.reshape(rows, width).astype(F32)
    grad_gain_mlp = jnp.sum(down_normed * grad_out, axis=0)
    scaled = grad_out * gain_mlp
    grad_down = down_inv * (scaled - down_normed * jnp.mean(scaled * down_normed, axis=-1, keepdims=True))
    grad_down_wide, _, _ = group_gather(grad_down.astype(BF))

    down_term = lax.dot_general(
        act_low, grad_down_wide, contract_rows, preferred_element_type=F32
    ).astype(BF)
    grad_act = lax.dot_general(grad_down_wide, down, contract_last, preferred_element_type=F32)
    grad_gate_low = (grad_act * up_proj * sigma_gate * (1.0 + gate_proj * (1.0 - sigma_gate))).astype(BF)
    grad_up_low = (grad_act * act_value).astype(BF)
    grad_gate_low = after(grad_gate_low, down_term)
    grad_hidden = jnp.dot(grad_gate_low, gate, preferred_element_type=F32) + jnp.dot(
        grad_up_low, up, preferred_element_type=F32
    )
    hidden_term = grad_hidden.astype(BF)

    def weight_term(left, right):
        return lambda token: lax.dot_general(
            after(left, token), right, contract_rows, preferred_element_type=F32
        ).astype(BF)

    moved, gate_term = group_scatter(hidden_term, weight_term(grad_gate_low, hidden_wide))
    grad_hidden = grad_out + moved

    def owners(term):
        return lax.psum_scatter(term, REST, scatter_dimension=0, tiled=True)

    down_part = owners(down_term)

    grad_gain_attn = jnp.sum(out_normed * grad_hidden, axis=0)
    scaled = grad_hidden * gain_attn
    grad_out_raw = out_inv * (scaled - out_normed * jnp.mean(scaled * out_normed, axis=-1, keepdims=True))
    grad_out_low = grad_out_raw.astype(BF)
    grad_out_wide, grad_out_near, up_term = group_gather(grad_out_low, weight_term(grad_up_low, hidden_wide))

    output_term = lax.dot_general(
        attended_low, grad_out_wide, contract_rows, preferred_element_type=F32
    ).astype(BF)
    grad_out_wide = after(grad_out_wide, output_term)
    output_term = lax.all_to_all(
        output_term.reshape(own_heads, head_dim, width),
        head_axes,
        split_axis=1,
        concat_axis=0,
        tiled=True,
    )

    grad_att = lax.dot_general(grad_out_wide, w_out, contract_last, preferred_element_type=F32).astype(BF)
    scaled, grad_value, dots, gain_term = attend_back(qkv_raw, inverses, gain_heads, tables, own_heads, grad_att)
    means = group_total(dots) * (1.0 / width)
    grad_qkv = finish(qkv_raw, inverses, means, scaled, grad_value, seq_len, own_heads)

    grad_input = lax.dot_general(grad_qkv, w_qkv, contract_last, preferred_element_type=F32)
    grad_input = after(grad_input.astype(BF), output_term)
    moved, qkv_term = group_scatter(grad_input, weight_term(x_wide, grad_qkv))
    grad_input = grad_hidden + moved
    output_part = line_sum(output_term.reshape(LINE, along * shard, width), at)
    if along > 1:
        output_part = lax.psum_scatter(output_part.astype(BF), "m", scatter_dimension=0, tiled=True)
    returned = lax.all_to_all(
        after(grad_input.astype(BF), output_part).reshape(micro_count, seq_len, width),
        ALL,
        split_axis=1,
        concat_axis=0,
        tiled=True,
    )
    input_grad = jnp.zeros_like(tokens).at[dealing].set(returned)

    gate_part = owners(after(gate_term, down_part, hidden_term))
    up_part = owners(after(up_term, gate_part, grad_out_near))
    qkv_rows = owners(after(qkv_term, up_part))
    qkv_back = lax.all_to_all(
        qkv_rows.reshape(PLANE, shard, 3 * own_width), GROUP, split_axis=0, concat_axis=0, tiled=True
    )

    def heads_in(columns):
        split = columns.reshape(fan, spread, shard, own_heads, head_dim)
        return split.transpose(2, 1, 3, 0, 4).reshape(shard, width).astype(F32)

    query_part = heads_in(qkv_back[:, :, :own_width])
    key_part = heads_in(qkv_back[:, :, own_width : 2 * own_width])
    value_part = heads_in(qkv_back[:, :, 2 * own_width :])

    placed = jnp.zeros((2, spread, own_heads, fan, head_dim), F32)
    own = gain_term.reshape(2, 1, own_heads, 1, head_dim)
    placed = lax.dynamic_update_slice(placed, own, (0, lane, 0, lead, 0)).reshape(2, width)
    gain_terms = jnp.concatenate([placed, jnp.stack([grad_gain_attn, grad_gain_mlp])])
    gain_terms = gain_terms.reshape(4, total, shard).transpose(1, 0, 2)
    gain_part = jnp.sum(
        lax.all_to_all(gain_terms, ALL, split_axis=0, concat_axis=0, tiled=True), axis=0
    )
    return (
        block_out,
        input_grad,
        query_part,
        key_part,
        value_part,
        output_part.astype(F32),
        gain_part[0],
        gain_part[1],
        gain_part[2],
        gate_part.astype(F32).T,
        up_part.astype(F32).T,
        down_part.astype(F32),
        gain_part[3],
    )


def solution(mesh):
    count = mesh.devices.size
    inner = Mesh(mesh.devices.reshape(LINE, count // (LINE * PLANE), 2, 2, 2), ALL)
    first, second = P(ALL, None), P(None, ALL)
    vector = P(ALL)
    placed = (
        P(None, ALL, None),
        P(),
        P(),
        first,
        first,
        first,
        first,
        vector,
        vector,
        vector,
        second,
        second,
        first,
        vector,
        P(ALL, None, None),
    )
    return jax.shard_map(
        per_device,
        mesh=inner,
        in_specs=placed,
        out_specs=(
            P(ALL, None, None),
            P(None, ALL, None),
            first,
            first,
            first,
            first,
            vector,
            vector,
            vector,
            second,
            second,
            first,
            vector,
        ),
        check_vma=False,
    )
```

time: 912 us -> 890 us (0.976)
  local copies, waits for them, and re-layouts: 151 us -> 90.2 us
  Pallas kernels: 0 us -> 57.5 us
  blocking collectives: 27.9 us -> 64.4 us
  other arithmetic: 90.6 us -> 55.7 us
  matrix products: 191 us -> 164 us
  waiting for transfers between devices: 330 us -> 344 us
    pallas_call x0 -> x4, Pallas kernels: none -> 57.5 us  [the longest x1 20.8 us: attend_back(): pl.pallas_call(lambda *refs: attend_back_kernel(heads, 2, 1.0 / math.sqrt...]
    all_to_all x2, waiting for transfers between devices: 77.5 us -> 25.8 us  [the longest x1 21.5 us: per_device(): lax.all_to_all(after(grad_input.astype(BF), output_part).reshape(micro_co...]
    ppermute x0 -> x6, waiting for transfers between devices: none -> 43.7 us  [the longest x3 38.7 us: line_sum(): total = total + lax.ppermute(block, 'z', ring(ahead)).astype(F32)]
    unnamed x227 -> x142, local copies, waits for them, and re-layouts: 83.1 us -> 43.8 us
    all_to_all x2, blocking collectives: 22.2 us -> 59.6 us  [the longest x1 55.1 us: per_device(): lax.all_to_all(outgoing, ALL, split_axis=0, concat_axis=1, tiled=True)]
    dot_general x9 -> x3, matrix products: 54.2 us -> 32.7 us  [weight_term(): lax.dot_general(after(left, token), right, contract_rows, preferred_eleme...]
    all_gather x5 -> x4, waiting for transfers between devices: 16.7 us -> 37.7 us  [the longest x1 37.7 us: per_device(): down = lax.all_gather(after(w_down, qkv_in), REST, axis=0, tiled=True)]
    ppermute x102 -> x74, waiting for transfers between devices: 209 us -> 230 us  [swap(): return lax.ppermute(value, axis, SWAP)]
  transfers between devices with their start and end apart: 117 -> 93, of which waited for: 47 -> 49; matrix products, arithmetic and copies ran while one was open for 40% -> 30% of each run, Pallas kernels for 0% -> 7%
where the time goes in v3:
time: 890 us; the launch traced here: 882 us
  waiting for transfers between devices  344 us (39%)
  matrix products  164 us (18%)
  starting transfers between devices  91.3 us (10%)
  local copies, waits for them, and re-layouts  90.2 us (10%)
  blocking collectives  64.4 us (7%)
  Pallas kernels  57.5 us (6%)
  other arithmetic  55.7 us (6%)
  between operations  16 us (2%)
    ppermute x74, waiting for transfers between devices, swap(): return lax.ppermute(value, axis, SWAP)  230 us
    all_to_all x1, blocking collectives, per_device(): lax.all_to_all(outgoing, ALL, split_axis=0, concat_axis=1, tiled=True)  55.1 us
    ppermute x74, starting transfers between devices, swap(): return lax.ppermute(value, axis, SWAP)  53.8 us
    unnamed x142, local copies, waits for them, and re-layouts  43.8 us
    ppermute x3, waiting for transfers between devices, line_sum(): total = total + lax.ppermute(block, 'z', ring(ahead)).astype(F32)  38.7 us
    all_gather x1, waiting for transfers between devices, per_device(): down = lax.all_gather(after(w_down, qkv_in), REST, axis=0, tiled=True)  37.7 us
    dot_general x3, matrix products, weight_term(): lax.dot_general(after(left, token), right, contract_rows, preferred_eleme...  32.7 us
    dot_general x1, matrix products, per_device(): lax.dot_general(grad_down_wide, down, contract_last, preferred_element_ty...  23.2 us
  transfers between devices with their start and end apart: 93, of which 49 were waited for; matrix products, arithmetic and copies ran while one was open for 30% of the time, Pallas kernels for 7%

profile of v3, /device:TPU:0, one launch (start us, length us, event | category | flops | bytes accessed | tf_op | source)
XLA Modules:
  0.0 882.3 jit_solution(5678787844299318365)
XLA Ops:
  7.2 3.1 collective-permute-start.9
  10.3 2.6 collective-permute-start.10
  20.2 3.7 all-to-all-start.1
  25.3 5.0 collective-permute-done.10
  32.3 4.3 all-to-all-done.1
  37.5 55.1 %all_to_all.86 = bf16[64,4,2048]{2,1,0:T(4,128)(2,1)S(1)} all-to-all(bf16[64,4,2048]{2,1,0:T(4,128)(2,1)S(1)} %broadcast_select_fusion), channel_id=1, replica_groups=mesh['z'=4,'m'=1,'y'=2,'x'=2,'c'=2] {'z','m','y','x','c'}, dimensions={0} | all-to-all | bytes 2097152 | tf_op jit(solution)/shard_map/all_to_all | solution.py:354
  97.2 4.8 all-to-all-start.2
  103.2 12.3 %collective-permute-done = bf16[256,2048]{1,0:T(8,128)(2,1)} collective-permute-done((bf16[256,2048]{1,0:T(8,128)(2,1)S(1)}, bf16[256,2048]{1,0:T(8,128)(2,1)}, u32[]{:S(2)}, u32[]{:S(2)}) %collective-permute-start) | collective-permute-done | bytes 1048608 | tf_op jit(solution)/shard_map/ppermute | solution.py:27
  116.5 3.6 collective-permute-start.2
  127.0 2.8 collective-permute-done.2
  138.4 12.9 %project.1 = (f32[2048,768]{1,0:T(8,128)}, f32[2,2048]{1,0:T(2,128)}) custom-call(bf16[2048,2048]{1,0:T(8,128)(2,1)} %constant_dynamic-update-slice_fusion.refs_0_, bf16[2048,768]{1,0:T(8,128)(2,1)} %bitcast.154), custom_call_target="tpu_custom_call" | custom-call | flops 6442450944 | bytes 17825792 | tf_op jit(solution)/shard_map/project/pallas_call | solution.py:78
  158.5 4.8 all_to_all.87
  164.1 15.3 %attend.1 = bf16[2048,256]{1,0:T(8,128)(2,1)} custom-call(f32[2048,768]{1,0:T(8,128)} %get-tuple-element.46.refs_0_, f32[2,2048]{1,0:T(2,128)} %rsqrt.22.refs_1_, f32[2,256]{1,0:T(2,128)} %bitcast.146, f32[128,128]{1,0:T(8,128)} %get-tuple-element.194.refs_3_, f32[128,128]{1,0:T(8,128)} %get-tuple-element.195.refs_4_), custom_call_target="tpu_custom_call" | custom-call | flops 268435456 | bytes 7340032 | tf_op jit(solution)/shard_map/attend/pallas_call | solution.py:190
  179.4 3.6 convolution_convert_fusion.2
  190.4 2.8 collective-permute-done.20
  193.2 3.7 convert_add_fusion.9
  200.8 10.6 %collective-permute-done.21 = bf16[128,2048]{1,0:T(8,128)(2,1)S(1)} collective-permute-done((bf16[128,2048]{1,0:T(8,128)(2,1)S(1)}, bf16[128,2048]{1,0:T(8,128)(2,1)S(1)}, u32[]{:S(2)}, u32[]{:S(2)}) %collective-permute-start.21) | collective-permute-done | bytes 524320 | tf_op jit(solution)/shard_map/ppermute | solution.py:27
  215.4 21.1 %collective-permute-done.22 = bf16[256,2048]{1,0:T(8,128)(2,1)} collective-permute-done((bf16[256,2048]{1,0:T(8,128)(2,1)S(1)}, bf16[256,2048]{1,0:T(8,128)(2,1)}, u32[]{:S(2)}, u32[]{:S(2)}) %collective-permute-start.22) | collective-permute-done | bytes 1048608 | tf_op jit(solution)/shard_map/ppermute | solution.py:27
  238.8 2.9 multiply_reduce_fusion.3
  246.5 22.4 %collective-permute-done.23 = bf16[256,2048]{1,0:T(8,128)(2,1)S(1)} collective-permute-done((bf16[256,2048]{1,0:T(8,128)(2,1)}, bf16[256,2048]{1,0:T(8,128)(2,1)S(1)}, u32[]{:S(2)}, u32[]{:S(2)}) %collective-permute-start.23) | collective-permute-done | bytes 1048608 | tf_op jit(solution)/shard_map/ppermute | solution.py:27
  275.7 6.4 collective-permute-done.25
  292.9 14.5 %fusion.36 = f32[2048,1024]{1,0:T(8,128)} fusion(bf16[2048,2048]{1,0:T(8,128)(2,1)} %constant_dynamic-update-slice_fusion.10, bf16[1024,2048]{0,1:T(8,128)(2,1)} %all-gather.7.cloned.1.call-done), kind=kOutput, calls=%fused_computation.190 | convolution fusion | flops 8589934592 | bytes 20971520 | tf_op jit(solution)/shard_map/dot_general | solution.py:401
  307.4 16.9 %multiply_convert_fusion.2 = (bf16[2048,1024]{1,0:T(8,128)(2,1)}, f32[2048,1024]{1,0:T(8,128)}) fusion(f32[2048,1024]{1,0:T(8,128)} %fusion.36, bf16[2048,2048]{1,0:T(8,128)(2,1)} %constant_dynamic-update-slice_fusion.10, bf16[1024,2048]{0,1:T(8,128)(2,1)} %all-gather.9.cloned.1.call-done), kind=kOutput, calls=%fused_computation.6 | convolution fusion | flops 8602517504 | bytes 33554432 | tf_op jit(solution)/shard_map/dot_general | solution.py:402
  324.3 37.7 %all-gather.11.cloned.1.call-done = bf16[1024,2048]{1,0:T(8,128)(2,1)} async-done(((bf16[256,2048]{1,0:T(8,128)(2,1)}), bf16[1024,2048]{1,0:T(8,128)(2,1)}) %all-gather.11.cloned.1.call-update) | async-done | bytes 4194320 | tf_op jit(solution)/shard_map/all_gather | solution.py:383
  361.9 12.1 %convolution_convert_fusion.1 = bf16[2048,2048]{1,0:T(8,128)(2,1)S(1)} fusion(bf16[2048,1024]{1,0:T(8,128)(2,1)} %get-tuple-element.190, bf16[1024,2048]{1,0:T(8,128)(2,1)} %all-gather.11.cloned.1.call-done), kind=kOutput, calls=%fused_computation.10 | convolution fusion | flops 8594128896 | bytes 16777216 | tf_op jit(solution)/shard_map/dot_general | solution.py:406
  386.2 10.8 %collective-permute-done.38 = bf16[128,2048]{1,0:T(8,128)(2,1)S(1)} collective-permute-done((bf16[128,2048]{1,0:T(8,128)(2,1)S(1)}, bf16[128,2048]{1,0:T(8,128)(2,1)S(1)}, u32[]{:S(2)}, u32[]{:S(2)}) %collective-permute-start.38) | collective-permute-done | bytes 524320 | tf_op jit(solution)/shard_map/ppermute | solution.py:27
  401.4 20.3 %collective-permute-done.39 = bf16[256,2048]{1,0:T(8,128)(2,1)} collective-permute-done((bf16[256,2048]{1,0:T(8,128)(2,1)S(1)}, bf16[256,2048]{1,0:T(8,128)(2,1)}, u32[]{:S(2)}, u32[]{:S(2)}) %collective-permute-start.39) | collective-permute-done | bytes 1048608 | tf_op jit(solution)/shard_map/ppermute | solution.py:27
  424.1 2.9 multiply_reduce_fusion.2
  427.0 2.6 fusion.9
  432.2 21.9 %collective-permute-done.40 = bf16[256,2048]{1,0:T(8,128)(2,1)S(1)} collective-permute-done((bf16[256,2048]{1,0:T(8,128)(2,1)S(1)}, bf16[256,2048]{1,0:T(8,128)(2,1)S(1)}, u32[]{:S(2)}, u32[]{:S(2)}) %collective-permute-start.40) | collective-permute-done | bytes 1048608 | tf_op jit(solution)/shard_map/ppermute | solution.py:27
  457.4 8.6 collective-permute-done.42
  469.2 3.4 copy-done.29
  472.6 11.0 %convolution_convert_fusion.5 = bf16[1024,2048]{1,0:T(8,128)(2,1)} fusion(bf16[2048,1024]{1,0:T(8,128)(2,1)S(1)} %copy-done.44, bf16[2048,2048]{1,0:T(8,128)(2,1)S(1)} %constant_dynamic-update-slice_fusion.20), kind=kOutput, calls=%fused_computation.14 | convolution fusion | flops 8592031744 | bytes 16777216 | tf_op jit(solution)/shard_map/dot_general | solution.py:419
  483.7 23.2 %multiply_convert_fusion = (bf16[2048,1024]{1,0:T(8,128)(2,1)}, bf16[2048,1024]{1,0:T(8,128)(2,1)}) fusion(f32[2048,1024]{1,0:T(8,128)} %fusion.36, f32[2048,1024]{1,0:T(8,128)} %get-tuple-element.191, bf16[2048,2048]{1,0:T(8,128)(2,1)} %copy-done.29, bf16[1024,2048]{1,0:T(8,128)(2,1)} %all-gather.11.cloned.1.call-done), kind=kOutput, calls=%fused_computation.4 | convolution fusion | flops 8617197568 | bytes 37748736 | tf_op jit(solution)/shard_map/dot_general | solution.py:422
  506.9 14.1 %fusion.37 = f32[2048,2048]{1,0:T(8,128)} fusion(bf16[2048,1024]{1,0:T(8,128)(2,1)} %get-tuple-element.52, bf16[1024,2048]{0,1:T(8,128)(2,1)S(1)} %copy-done.43), kind=kOutput, calls=%fused_computation.191 | convolution fusion | flops 8589934592 | bytes 25165824 | tf_op jit(solution)/shard_map/dot_general | solution.py:426
  521.0 16.9 %add_convert_fusion = bf16[2048,2048]{1,0:T(8,128)(2,1)} fusion(f32[2048,2048]{1,0:T(8,128)} %fusion.37, bf16[2048,1024]{1,0:T(8,128)(2,1)} %get-tuple-element.55, bf16[1024,2048]{0,1:T(8,128)(2,1)} %all-gather.9.cloned.1.call-done), kind=kOutput, calls=%fused_computation.3 | convolution fusion | flops 8598323200 | bytes 33554432 | tf_op jit(solution)/shard_map/dot_general | solution.py:426
  537.9 3.9 fusion.29
  547.4 5.1 convert_add_fusion.3
  555.7 11.0 %convolution_convert_fusion.4 = bf16[1024,2048]{1,0:T(8,128)(2,1)} fusion(bf16[2048,1024]{1,0:T(8,128)(2,1)S(1)} %copy-done.46, bf16[2048,2048]{1,0:T(8,128)(2,1)S(1)} %bitcast.143), kind=kOutput, calls=%fused_computation.13 | convolution fusion | flops 8592031744 | bytes 16777216 | tf_op jit(solution)/shard_map/dot_general | solution.py:432
  575.6 21.8 %collective-permute-done.56 = bf16[256,2048]{1,0:T(8,128)(2,1)S(1)} collective-permute-done((bf16[256,2048]{1,0:T(8,128)(2,1)S(1)}, bf16[256,2048]{1,0:T(8,128)(2,1)S(1)}, u32[]{:S(2)}, u32[]{:S(2)}) %collective-permute-start.56) | collective-permute-done | bytes 1048608 | tf_op jit(solution)/shard_map/ppermute | solution.py:27
  599.1 4.2 multiply_reduce_fusion
  608.1 11.0 %convolution_convert_fusion.3 = bf16[1024,2048]{1,0:T(8,128)(2,1)} fusion(bf16[2048,1024]{1,0:T(8,128)(2,1)S(1)} %copy-done.45, bf16[2048,2048]{1,0:T(8,128)(2,1)S(1)} %bitcast.145), kind=kOutput, calls=%fused_computation.12 | convolution fusion | flops 8592031744 | bytes 16777216 | tf_op jit(solution)/shard_map/dot_general | solution.py:432
  619.2 11.0 %collective-permute-done.57 = bf16[256,2048]{1,0:T(8,128)(2,1)S(1)} collective-permute-done((bf16[256,2048]{1,0:T(8,128)(2,1)}, bf16[256,2048]{1,0:T(8,128)(2,1)S(1)}, u32[]{:S(2)}, u32[]{:S(2)}) %collective-permute-start.57) | collective-permute-done | bytes 1048608 | tf_op jit(solution)/shard_map/ppermute | solution.py:27
  636.4 7.2 collective-permute-done.59
  651.3 5.9 convolution_convert_fusion.8
  658.1 3.4 convolution_convert_fusion.7.refs_5_
  661.5 20.8 %attend_back.1 = (f32[2048,512]{1,0:T(8,128)}, bf16[2048,256]{1,0:T(8,128)(2,1)}, f32[2,2048]{1,0:T(2,128)}, f32[2,256]{1,0:T(2,128)}) custom-call(f32[2048,768]{1,0:T(8,128)} %get-tuple-element.46.refs_0_, f32[2,2048]{1,0:T(2,128)} %rsqrt.22.refs_1_, f32[2,256]{1,0:T(2,128)} %bitcast.147, f32[128,128]{1,0:T(8,128)} %get-tuple-element.194.refs_3_, ...), custom_call_target="tpu_custom_call" | custom-call | flops 671088640 | bytes 13631488 | tf_op jit(solution)/shard_map/attend_back/pallas_call | solution.py:208
  690.4 4.6 all_to_all.88
  696.0 8.4 finish.1
  704.5 9.3 %convolution_convert_fusion = bf16[2048,2048]{1,0:T(8,128)(2,1)S(1)} fusion(bf16[2048,768]{1,0:T(8,128)(2,1)} %finish.1, bf16[2048,768]{1,0:T(8,128)(2,1)} %bitcast.155), kind=kOutput, calls=%fused_computation.9 | convolution fusion | flops 6446645248 | bytes 14680064 | tf_op jit(solution)/shard_map/dot_general | solution.py:467
  721.0 2.6 convert_add_fusion.1
  724.7 10.7 %convolution_convert_fusion.6 = bf16[2048,768]{1,0:T(8,128)(2,1)} fusion(bf16[2048,2048]{1,0:T(8,128)(2,1)} %constant_dynamic-update-slice_fusion.refs_0_, bf16[2048,768]{1,0:T(8,128)(2,1)S(1)} %copy-done.22), kind=kOutput, calls=%fused_computation.15 | convolution fusion | flops 6444023808 | bytes 14680064 | tf_op jit(solution)/shard_map/dot_general | solution.py:432
  739.4 10.4 %collective-permute-done.72 = bf16[128,2048]{1,0:T(8,128)(2,1)} collective-permute-done((bf16[128,2048]{1,0:T(8,128)(2,1)}, bf16[128,2048]{1,0:T(8,128)(2,1)}, u32[]{:S(2)}, u32[]{:S(2)}) %collective-permute-start.72) | collective-permute-done | bytes 524320 | tf_op jit(solution)/shard_map/ppermute | solution.py:27
  759.9 16.2 %collective-permute-done.79 = bf16[64,2048]{1,0:T(8,128)(2,1)S(1)} collective-permute-done((bf16[64,2048]{1,0:T(8,128)(2,1)S(1)}, bf16[64,2048]{1,0:T(8,128)(2,1)S(1)}, u32[]{:S(2)}, u32[]{:S(2)}) %collective-permute-start.79) | collective-permute-done | bytes 262176 | tf_op jit(solution)/shard_map/ppermute | solution.py:299
  776.2 9.1 %collective-permute-start.77 = (bf16[64,2048]{1,0:T(8,128)(2,1)S(1)}, bf16[64,2048]{1,0:T(8,128)(2,1)}, u32[]{:S(2)}, u32[]{:S(2)}) collective-permute-start(bf16[64,2048]{1,0:T(8,128)(2,1)S(1)} %get-tuple-element.169), channel_id=1, source_target_pairs={{0,8},{8,16},{16,24},{24,0},{1,9},{9,17},{17,25},{25,1},{2,10},{10... | collective-permute-start | bytes 786440 | tf_op jit(solution)/shard_map/ppermute | solution.py:299
  786.3 2.8 all-to-all-start.7
  789.1 22.4 %collective-permute-done.78 = bf16[64,2048]{1,0:T(8,128)(2,1)} collective-permute-done((bf16[64,2048]{1,0:T(8,128)(2,1)}, bf16[64,2048]{1,0:T(8,128)(2,1)}, u32[]{:S(2)}, u32[]{:S(2)}) %collective-permute-start.78) | collective-permute-done | bytes 262176 | tf_op jit(solution)/shard_map/ppermute | solution.py:299
  813.6 3.0 add_convert_fusion.1
  818.7 3.5 all-to-all-start.5
  824.1 2.8 convert_element_type.386
  826.9 21.5 %all-to-all-done.5 = bf16[2,128,2048]{2,0,1:T(2,128)(2,1)S(1)} async-done(((bf16[2,128,2048]{2,0,1:T(2,128)(2,1)}), bf16[2,128,2048]{2,0,1:T(2,128)(2,1)S(1)}, u32[]{:S(2)}, u32[]{:S(2)}) %all-to-all-start.5) | async-done | bytes 1048608 | tf_op jit(solution)/shard_map/all_to_all | solution.py:474
  849.5 2.5 scatter_fusion
  852.0 4.2 all-to-all-start.6
  862.8 6.1 all-to-all-done.6
  (441 shorter events, 200.2 us)
Async XLA Ops:
  7.2 17.0 %collective-permute-start.9 = (bf16[64,2048]{1,0:T(8,128)(2,1)}, bf16[64,2048]{1,0:T(8,128)(2,1)}, u32[]{:S(2)}, u32[]{:S(2)}) collective-permute-start(bf16[64,2048]{1,0:T(8,128)(2,1)} %param.21), channel_id=1, source_target_pairs={{0,8},{8,16},{16,24},{24,0},{1,9},{9,17},{17,25},{25,1},{2,10},{10... | collective-permute-start | bytes 786440 | tf_op jit(solution)/shard_map/ppermute | solution.py:290
  10.3 20.0 %collective-permute-start.10 = (bf16[64,2048]{1,0:T(8,128)(2,1)}, bf16[64,2048]{1,0:T(8,128)(2,1)}, u32[]{:S(2)}, u32[]{:S(2)}) collective-permute-start(bf16[64,2048]{1,0:T(8,128)(2,1)} %param.21), channel_id=1, source_target_pairs={{0,16},{8,24},{16,0},{24,8},{1,17},{9,25},{17,1},{25,9},{2,18},{10... | collective-permute-start | bytes 786440 | tf_op jit(solution)/shard_map/ppermute | solution.py:290
  12.9 18.4 %collective-permute-start.11 = (bf16[64,2048]{1,0:T(8,128)(2,1)}, bf16[64,2048]{1,0:T(8,128)(2,1)}, u32[]{:S(2)}, u32[]{:S(2)}) collective-permute-start(bf16[64,2048]{1,0:T(8,128)(2,1)} %param.21), channel_id=1, source_target_pairs={{0,24},{8,0},{16,8},{24,16},{1,25},{9,1},{17,9},{25,17},{2,26},{10... | collective-permute-start | bytes 786440 | tf_op jit(solution)/shard_map/ppermute | solution.py:290
  20.2 16.3 %all-to-all-start.1 = ((bf16[8,64,768]{2,1,0:T(8,128)(2,1)}), bf16[8,64,768]{2,1,0:T(8,128)(2,1)S(1)}, u32[]{:S(2)}, u32[]{:S(2)}) async-start(bf16[8,64,768]{2,1,0:T(8,128)(2,1)} %pad_maximum_fusion.8), calls=%async_computation.1 | async-start | bytes 1572864 | tf_op jit(solution)/shard_map/all_to_all | solution.py:359
  24.0 114.4 %all-gather.5.cloned.1.call-start = ((), (), s32[]{:S(2)}) async-start(), calls=%async_computation.12 | async-start | bytes 3932160 | tf_op jit(solution)/shard_map/all_gather | solution.py:377
  93.3 22.2 %collective-permute-start = (bf16[256,2048]{1,0:T(8,128)(2,1)S(1)}, bf16[256,2048]{1,0:T(8,128)(2,1)}, u32[]{:S(2)}, u32[]{:S(2)}) collective-permute-start(bf16[256,2048]{1,0:T(8,128)(2,1)S(1)} %reshape.194), channel_id=1, source_target_pairs={{0,2},{2,0},{1,3},{3,1},{4,6},{6,4},{5,7},{7,5},{8,10},{10,8},{9,1... | collective-permute-start | bytes 3145736 | tf_op jit(solution)/shard_map/ppermute | solution.py:27
  95.2 25.0 %collective-permute-start.1 = (bf16[256,2048]{1,0:T(8,128)(2,1)S(1)}, bf16[256,2048]{1,0:T(8,128)(2,1)S(1)}, u32[]{:S(2)}, u32[]{:S(2)}) collective-permute-start(bf16[256,2048]{1,0:T(8,128)(2,1)S(1)} %reshape.194), channel_id=1, source_target_pairs={{0,4},{4,0},{1,5},{5,1},{2,6},{6,2},{3,7},{7,3},{8,12},{12,8},{9,1... | collective-permute-start | bytes 3145736 | tf_op jit(solution)/shard_map/ppermute | solution.py:27
  97.2 58.9 %all-to-all-start.2 = ((bf16[32,2,128]{2,1,0:T(2,128)(2,1)}), bf16[32,2,128]{2,1,0:T(2,128)(2,1)S(1)}, u32[]{:S(2)}, u32[]{:S(2)}) async-start(bf16[32,2,128]{2,1,0:T(2,128)(2,1)} %reshape.265), calls=%async_computation.2 | async-start | bytes 32768 | tf_op jit(solution)/shard_map/all_to_all | solution.py:362
  102.0 190.8 %all-gather.7.cloned.1.call-start = ((), (), s32[]{:S(2)}) async-start(), calls=%async_computation.13 | async-start | bytes 5242880 | tf_op jit(solution)/shard_map/all_gather | solution.py:381
  102.8 204.6 %all-gather.9.cloned.1.call-start = ((), (), s32[]{:S(2)}) async-start(), calls=%async_computation.14 | async-start | bytes 5242880 | tf_op jit(solution)/shard_map/all_gather | solution.py:382
  102.8 30.6 %collective-permute-start.4 = (bf16[256,2048]{1,0:T(8,128)(2,1)S(1)}, bf16[256,2048]{1,0:T(8,128)(2,1)S(1)}, u32[]{:S(2)}, u32[]{:S(2)}) collective-permute-start(bf16[256,2048]{1,0:T(8,128)(2,1)S(1)} %reshape.194), channel_id=1, source_target_pairs={{0,1},{1,0},{2,3},{3,2},{4,5},{5,4},{6,7},{7,6},{8,9},{9,8},{10,11... | collective-permute-start | bytes 3145736 | tf_op jit(solution)/shard_map/ppermute | solution.py:27
  116.5 13.3 %collective-permute-start.2 = (bf16[128,2048]{1,0:T(8,128)(2,1)S(1)}, bf16[128,2048]{1,0:T(8,128)(2,1)S(1)}, u32[]{:S(2)}, u32[]{:S(2)}) collective-permute-start(bf16[128,2048]{1,0:T(8,128)(2,1)S(1)} %slice.319), channel_id=1, source_target_pairs={{0,4},{4,0},{1,5},{5,1},{2,6},{6,2},{3,7},{7,3},{8,12},{12,8},{9,1... | collective-permute-start | bytes 1572872 | tf_op jit(solution)/shard_map/ppermute | solution.py:27
  120.2 11.6 %collective-permute-start.3 = (bf16[128,2048]{1,0:T(8,128)(2,1)S(1)}, bf16[128,2048]{1,0:T(8,128)(2,1)S(1)}, u32[]{:S(2)}, u32[]{:S(2)}) collective-permute-start(bf16[128,2048]{1,0:T(8,128)(2,1)S(1)} %slice.320), channel_id=1, source_target_pairs={{0,2},{2,0},{1,3},{3,1},{4,6},{6,4},{5,7},{7,5},{8,10},{10,8},{9,1... | collective-permute-start | bytes 1572872 | tf_op jit(solution)/shard_map/ppermute | solution.py:27
  123.1 11.5 %collective-permute-start.5 = (bf16[256,2048]{1,0:T(8,128)(2,1)}, bf16[256,2048]{1,0:T(8,128)(2,1)S(1)}, u32[]{:S(2)}, u32[]{:S(2)}) collective-permute-start(bf16[256,2048]{1,0:T(8,128)(2,1)} %collective-permute-done), channel_id=1, source_target_pairs={{0,1},{1,0},{2,3},{3,2},{4,5},{5,4},{6,7},{7,6},{8,9},{9,8},{10,11... | collective-permute-start | bytes 3145736 | tf_op jit(solution)/shard_map/ppermute | solution.py:27
  123.1 12.6 %collective-permute-start.6 = (bf16[256,2048]{1,0:T(8,128)(2,1)S(1)}, bf16[256,2048]{1,0:T(8,128)(2,1)S(1)}, u32[]{:S(2)}, u32[]{:S(2)}) collective-permute-start(bf16[256,2048]{1,0:T(8,128)(2,1)S(1)} %collective-permute-done.1), channel_id=1, source_target_pairs={{0,1},{1,0},{2,3},{3,2},{4,5},{5,4},{6,7},{7,6},{8,9},{9,8},{10,11... | collective-permute-start | bytes 3145736 | tf_op jit(solution)/shard_map/ppermute | solution.py:27
  188.0 173.9 %all-gather.11.cloned.1.call-start = ((), (), s32[]{:S(2)}) async-start(), calls=%async_computation.15 | async-start | bytes 5242880 | tf_op jit(solution)/shard_map/all_gather | solution.py:383
  197.0 14.4 %collective-permute-start.21 = (bf16[128,2048]{1,0:T(8,128)(2,1)S(1)}, bf16[128,2048]{1,0:T(8,128)(2,1)S(1)}, u32[]{:S(2)}, u32[]{:S(2)}) collective-permute-start(bf16[128,2048]{1,0:T(8,128)(2,1)S(1)} %get-tuple-element.179), channel_id=1, source_target_pairs={{0,2},{2,0},{1,3},{3,1},{4,6},{6,4},{5,7},{7,5},{8,10},{10,8},{9,1... | collective-permute-start | bytes 1572872 | tf_op jit(solution)/shard_map/ppermute | solution.py:27
  199.0 16.4 %collective-permute-start.15 = (bf16[256,2048]{1,0:T(8,128)(2,1)}, bf16[256,2048]{1,0:T(8,128)(2,1)}, u32[]{:S(2)}, u32[]{:S(2)}) collective-permute-start(bf16[256,2048]{1,0:T(8,128)(2,1)} %get-tuple-element.161), channel_id=1, source_target_pairs={{0,1},{1,0},{2,3},{3,2},{4,5},{5,4},{6,7},{7,6},{8,9},{9,8},{10,11... | collective-permute-start | bytes 3145736 | tf_op jit(solution)/shard_map/ppermute | solution.py:27
  199.1 14.4 %collective-permute-start.18 = (bf16[128,2048]{1,0:T(8,128)(2,1)S(1)}, bf16[128,2048]{1,0:T(8,128)(2,1)S(1)}, u32[]{:S(2)}, u32[]{:S(2)}) collective-permute-start(bf16[128,2048]{1,0:T(8,128)(2,1)S(1)} %get-tuple-element.178), channel_id=1, source_target_pairs={{0,4},{4,0},{1,5},{5,1},{2,6},{6,2},{3,7},{7,3},{8,12},{12,8},{9,1... | collective-permute-start | bytes 1572872 | tf_op jit(solution)/shard_map/ppermute | solution.py:27
  211.6 24.9 %collective-permute-start.22 = (bf16[256,2048]{1,0:T(8,128)(2,1)S(1)}, bf16[256,2048]{1,0:T(8,128)(2,1)}, u32[]{:S(2)}, u32[]{:S(2)}) collective-permute-start(bf16[256,2048]{1,0:T(8,128)(2,1)S(1)} %pad_maximum_fusion.1), channel_id=1, source_target_pairs={{0,4},{4,0},{1,5},{5,1},{2,6},{6,2},{3,7},{7,3},{8,12},{12,8},{9,1... | collective-permute-start | bytes 3145736 | tf_op jit(solution)/shard_map/ppermute | solution.py:27
  213.7 25.1 %collective-permute-start.19 = (bf16[256,2048]{1,0:T(8,128)(2,1)S(1)}, bf16[256,2048]{1,0:T(8,128)(2,1)}, u32[]{:S(2)}, u32[]{:S(2)}) collective-permute-start(bf16[256,2048]{1,0:T(8,128)(2,1)S(1)} %pad_maximum_fusion), channel_id=1, source_target_pairs={{0,2},{2,0},{1,3},{3,1},{4,6},{6,4},{5,7},{7,5},{8,10},{10,8},{9,1... | collective-permute-start | bytes 3145736 | tf_op jit(solution)/shard_map/ppermute | solution.py:27
  244.7 24.2 %collective-permute-start.23 = (bf16[256,2048]{1,0:T(8,128)(2,1)}, bf16[256,2048]{1,0:T(8,128)(2,1)S(1)}, u32[]{:S(2)}, u32[]{:S(2)}) collective-permute-start(bf16[256,2048]{1,0:T(8,128)(2,1)} %get-tuple-element.135), channel_id=1, source_target_pairs={{0,2},{2,0},{1,3},{3,1},{4,6},{6,4},{5,7},{7,5},{8,10},{10,8},{9,1... | collective-permute-start | bytes 3145736 | tf_op jit(solution)/shard_map/ppermute | solution.py:27
  245.5 25.8 %collective-permute-start.24 = (bf16[256,2048]{1,0:T(8,128)(2,1)}, bf16[256,2048]{1,0:T(8,128)(2,1)S(1)}, u32[]{:S(2)}, u32[]{:S(2)}) collective-permute-start(bf16[256,2048]{1,0:T(8,128)(2,1)} %get-tuple-element.135), channel_id=1, source_target_pairs={{0,4},{4,0},{1,5},{5,1},{2,6},{6,2},{3,7},{7,3},{8,12},{12,8},{9,1... | collective-permute-start | bytes 3145736 | tf_op jit(solution)/shard_map/ppermute | solution.py:27
  246.5 41.4 %collective-permute-start.27 = (bf16[256,2048]{1,0:T(8,128)(2,1)}, bf16[256,2048]{1,0:T(8,128)(2,1)S(1)}, u32[]{:S(2)}, u32[]{:S(2)}) collective-permute-start(bf16[256,2048]{1,0:T(8,128)(2,1)} %get-tuple-element.135), channel_id=1, source_target_pairs={{0,1},{1,0},{2,3},{3,2},{4,5},{5,4},{6,7},{7,6},{8,9},{9,8},{10,11... | collective-permute-start | bytes 3145736 | tf_op jit(solution)/shard_map/ppermute | solution.py:27
  269.8 12.3 %collective-permute-start.25 = (bf16[128,2048]{1,0:T(8,128)(2,1)}, bf16[128,2048]{1,0:T(8,128)(2,1)}, u32[]{:S(2)}, u32[]{:S(2)}) collective-permute-start(bf16[128,2048]{1,0:T(8,128)(2,1)} %slice.337), channel_id=1, source_target_pairs={{0,4},{4,0},{1,5},{5,1},{2,6},{6,2},{3,7},{7,3},{8,12},{12,8},{9,1... | collective-permute-start | bytes 1572872 | tf_op jit(solution)/shard_map/ppermute | solution.py:27
  272.2 12.0 %collective-permute-start.26 = (bf16[128,2048]{1,0:T(8,128)(2,1)}, bf16[128,2048]{1,0:T(8,128)(2,1)}, u32[]{:S(2)}, u32[]{:S(2)}) collective-permute-start(bf16[128,2048]{1,0:T(8,128)(2,1)} %slice.338), channel_id=1, source_target_pairs={{0,2},{2,0},{1,3},{3,1},{4,6},{6,4},{5,7},{7,5},{8,10},{10,8},{9,1... | collective-permute-start | bytes 1572872 | tf_op jit(solution)/shard_map/ppermute | solution.py:27
  272.5 294.2 %reduce-scatter.5.cloned.1.call-start = ((), (), s32[]{:S(2)}) async-start(), calls=%async_computation.16 | async-start | bytes 5242880 | tf_op jit(solution)/shard_map/reduce_scatter | solution.py:440
  272.9 16.1 %collective-permute-start.28 = (bf16[256,2048]{1,0:T(8,128)(2,1)S(1)}, bf16[256,2048]{1,0:T(8,128)(2,1)S(1)}, u32[]{:S(2)}, u32[]{:S(2)}) collective-permute-start(bf16[256,2048]{1,0:T(8,128)(2,1)S(1)} %collective-permute-done.23), channel_id=1, source_target_pairs={{0,1},{1,0},{2,3},{3,2},{4,5},{5,4},{6,7},{7,6},{8,9},{9,8},{10,11... | collective-permute-start | bytes 3145736 | tf_op jit(solution)/shard_map/ppermute | solution.py:27
  273.0 17.1 %collective-permute-start.29 = (bf16[256,2048]{1,0:T(8,128)(2,1)S(1)}, bf16[256,2048]{1,0:T(8,128)(2,1)S(1)}, u32[]{:S(2)}, u32[]{:S(2)}) collective-permute-start(bf16[256,2048]{1,0:T(8,128)(2,1)S(1)} %collective-permute-done.24), channel_id=1, source_target_pairs={{0,1},{1,0},{2,3},{3,2},{4,5},{5,4},{6,7},{7,6},{8,9},{9,8},{10,11... | collective-permute-start | bytes 3145736 | tf_op jit(solution)/shard_map/ppermute | solution.py:27
  382.9 14.0 %collective-permute-start.38 = (bf16[128,2048]{1,0:T(8,128)(2,1)S(1)}, bf16[128,2048]{1,0:T(8,128)(2,1)S(1)}, u32[]{:S(2)}, u32[]{:S(2)}) collective-permute-start(bf16[128,2048]{1,0:T(8,128)(2,1)S(1)} %get-tuple-element.177), channel_id=1, source_target_pairs={{0,2},{2,0},{1,3},{3,1},{4,6},{6,4},{5,7},{7,5},{8,10},{10,8},{9,1... | collective-permute-start | bytes 1572872 | tf_op jit(solution)/shard_map/ppermute | solution.py:27
  384.5 16.9 %collective-permute-start.32 = (bf16[256,2048]{1,0:T(8,128)(2,1)}, bf16[256,2048]{1,0:T(8,128)(2,1)}, u32[]{:S(2)}, u32[]{:S(2)}) collective-permute-start(bf16[256,2048]{1,0:T(8,128)(2,1)} %get-tuple-element.154), channel_id=1, source_target_pairs={{0,1},{1,0},{2,3},{3,2},{4,5},{5,4},{6,7},{7,6},{8,9},{9,8},{10,11... | collective-permute-start | bytes 3145736 | tf_op jit(solution)/shard_map/ppermute | solution.py:27
  384.5 14.4 %collective-permute-start.35 = (bf16[128,2048]{1,0:T(8,128)(2,1)S(1)}, bf16[128,2048]{1,0:T(8,128)(2,1)S(1)}, u32[]{:S(2)}, u32[]{:S(2)}) collective-permute-start(bf16[128,2048]{1,0:T(8,128)(2,1)S(1)} %get-tuple-element.176), channel_id=1, source_target_pairs={{0,4},{4,0},{1,5},{5,1},{2,6},{6,2},{3,7},{7,3},{8,12},{12,8},{9,1... | collective-permute-start | bytes 1572872 | tf_op jit(solution)/shard_map/ppermute | solution.py:27
  397.1 24.5 %collective-permute-start.39 = (bf16[256,2048]{1,0:T(8,128)(2,1)S(1)}, bf16[256,2048]{1,0:T(8,128)(2,1)}, u32[]{:S(2)}, u32[]{:S(2)}) collective-permute-start(bf16[256,2048]{1,0:T(8,128)(2,1)S(1)} %pad_maximum_fusion.3), channel_id=1, source_target_pairs={{0,4},{4,0},{1,5},{5,1},{2,6},{6,2},{3,7},{7,3},{8,12},{12,8},{9,1... | collective-permute-start | bytes 3145736 | tf_op jit(solution)/shard_map/ppermute | solution.py:27
  399.1 25.0 %collective-permute-start.36 = (bf16[256,2048]{1,0:T(8,128)(2,1)S(1)}, bf16[256,2048]{1,0:T(8,128)(2,1)}, u32[]{:S(2)}, u32[]{:S(2)}) collective-permute-start(bf16[256,2048]{1,0:T(8,128)(2,1)S(1)} %pad_maximum_fusion.2), channel_id=1, source_target_pairs={{0,2},{2,0},{1,3},{3,1},{4,6},{6,4},{5,7},{7,5},{8,10},{10,8},{9,1... | collective-permute-start | bytes 3145736 | tf_op jit(solution)/shard_map/ppermute | solution.py:27
  430.1 24.0 %collective-permute-start.40 = (bf16[256,2048]{1,0:T(8,128)(2,1)S(1)}, bf16[256,2048]{1,0:T(8,128)(2,1)S(1)}, u32[]{:S(2)}, u32[]{:S(2)}) collective-permute-start(bf16[256,2048]{1,0:T(8,128)(2,1)S(1)} %get-tuple-element.193), channel_id=1, source_target_pairs={{0,2},{2,0},{1,3},{3,1},{4,6},{6,4},{5,7},{7,5},{8,10},{10,8},{9,1... | collective-permute-start | bytes 3145736 | tf_op jit(solution)/shard_map/ppermute | solution.py:27
  430.8 24.9 %collective-permute-start.41 = (bf16[256,2048]{1,0:T(8,128)(2,1)S(1)}, bf16[256,2048]{1,0:T(8,128)(2,1)S(1)}, u32[]{:S(2)}, u32[]{:S(2)}) collective-permute-start(bf16[256,2048]{1,0:T(8,128)(2,1)S(1)} %get-tuple-element.193), channel_id=1, source_target_pairs={{0,4},{4,0},{1,5},{5,1},{2,6},{6,2},{3,7},{7,3},{8,12},{12,8},{9,1... | collective-permute-start | bytes 3145736 | tf_op jit(solution)/shard_map/ppermute | solution.py:27
  432.2 35.1 %collective-permute-start.44 = (bf16[256,2048]{1,0:T(8,128)(2,1)S(1)}, bf16[256,2048]{1,0:T(8,128)(2,1)S(1)}, u32[]{:S(2)}, u32[]{:S(2)}) collective-permute-start(bf16[256,2048]{1,0:T(8,128)(2,1)S(1)} %get-tuple-element.193), channel_id=1, source_target_pairs={{0,1},{1,0},{2,3},{3,2},{4,5},{5,4},{6,7},{7,6},{8,9},{9,8},{10,11... | collective-permute-start | bytes 3145736 | tf_op jit(solution)/shard_map/ppermute | solution.py:27
  454.2 11.8 %collective-permute-start.42 = (bf16[128,2048]{1,0:T(8,128)(2,1)S(1)}, bf16[128,2048]{1,0:T(8,128)(2,1)S(1)}, u32[]{:S(2)}, u32[]{:S(2)}) collective-permute-start(bf16[128,2048]{1,0:T(8,128)(2,1)S(1)} %slice.354), channel_id=1, source_target_pairs={{0,4},{4,0},{1,5},{5,1},{2,6},{6,2},{3,7},{7,3},{8,12},{12,8},{9,1... | collective-permute-start | bytes 1572872 | tf_op jit(solution)/shard_map/ppermute | solution.py:27
  455.7 11.5 %collective-permute-start.43 = (bf16[128,2048]{1,0:T(8,128)(2,1)S(1)}, bf16[128,2048]{1,0:T(8,128)(2,1)S(1)}, u32[]{:S(2)}, u32[]{:S(2)}) collective-permute-start(bf16[128,2048]{1,0:T(8,128)(2,1)S(1)} %slice.355), channel_id=1, source_target_pairs={{0,2},{2,0},{1,3},{3,1},{4,6},{6,4},{5,7},{7,5},{8,10},{10,8},{9,1... | collective-permute-start | bytes 1572872 | tf_op jit(solution)/shard_map/ppermute | solution.py:27
  483.7 167.5 %reduce-scatter.7.cloned.1.call-start = ((), (), s32[]{:S(2)}) async-start(), calls=%async_computation.17 | async-start | bytes 5242880 | tf_op jit(solution)/shard_map/reduce_scatter | solution.py:440
  553.6 16.0 %collective-permute-start.52 = (bf16[128,2048]{1,0:T(8,128)(2,1)}, bf16[128,2048]{1,0:T(8,128)(2,1)}, u32[]{:S(2)}, u32[]{:S(2)}) collective-permute-start(bf16[128,2048]{1,0:T(8,128)(2,1)} %get-tuple-element.175), channel_id=1, source_target_pairs={{0,2},{2,0},{1,3},{3,1},{4,6},{6,4},{5,7},{7,5},{8,10},{10,8},{9,1... | collective-permute-start | bytes 1572872 | tf_op jit(solution)/shard_map/ppermute | solution.py:27
  554.2 15.5 %collective-permute-start.53 = (bf16[128,2048]{1,0:T(8,128)(2,1)}, bf16[128,2048]{1,0:T(8,128)(2,1)}, u32[]{:S(2)}, u32[]{:S(2)}) collective-permute-start(bf16[128,2048]{1,0:T(8,128)(2,1)} %get-tuple-element.174), channel_id=1, source_target_pairs={{0,4},{4,0},{1,5},{5,1},{2,6},{6,2},{3,7},{7,3},{8,12},{12,8},{9,1... | collective-permute-start | bytes 1572872 | tf_op jit(solution)/shard_map/ppermute | solution.py:27
  566.7 168.7 %reduce-scatter.9.cloned.1.call-start = ((), (), s32[]{:S(2)}) async-start(), calls=%async_computation.18 | async-start | bytes 5242880 | tf_op jit(solution)/shard_map/reduce_scatter | solution.py:440
  571.9 25.5 %collective-permute-start.56 = (bf16[256,2048]{1,0:T(8,128)(2,1)S(1)}, bf16[256,2048]{1,0:T(8,128)(2,1)S(1)}, u32[]{:S(2)}, u32[]{:S(2)}) collective-permute-start(bf16[256,2048]{1,0:T(8,128)(2,1)S(1)} %pad_maximum_fusion.5), channel_id=1, source_target_pairs={{0,4},{4,0},{1,5},{5,1},{2,6},{6,2},{3,7},{7,3},{8,12},{12,8},{9,1... | collective-permute-start | bytes 3145736 | tf_op jit(solution)/shard_map/ppermute | solution.py:27
  573.8 25.3 %collective-permute-start.54 = (bf16[256,2048]{1,0:T(8,128)(2,1)S(1)}, bf16[256,2048]{1,0:T(8,128)(2,1)S(1)}, u32[]{:S(2)}, u32[]{:S(2)}) collective-permute-start(bf16[256,2048]{1,0:T(8,128)(2,1)S(1)} %pad_maximum_fusion.4), channel_id=1, source_target_pairs={{0,2},{2,0},{1,3},{3,1},{4,6},{6,4},{5,7},{7,5},{8,10},{10,8},{9,1... | collective-permute-start | bytes 3145736 | tf_op jit(solution)/shard_map/ppermute | solution.py:27
  605.4 24.7 %collective-permute-start.57 = (bf16[256,2048]{1,0:T(8,128)(2,1)}, bf16[256,2048]{1,0:T(8,128)(2,1)S(1)}, u32[]{:S(2)}, u32[]{:S(2)}) collective-permute-start(bf16[256,2048]{1,0:T(8,128)(2,1)} %get-tuple-element.130), channel_id=1, source_target_pairs={{0,2},{2,0},{1,3},{3,1},{4,6},{6,4},{5,7},{7,5},{8,10},{10,8},{9,1... | collective-permute-start | bytes 3145736 | tf_op jit(solution)/shard_map/ppermute | solution.py:27
  607.1 24.4 %collective-permute-start.58 = (bf16[256,2048]{1,0:T(8,128)(2,1)}, bf16[256,2048]{1,0:T(8,128)(2,1)S(1)}, u32[]{:S(2)}, u32[]{:S(2)}) collective-permute-start(bf16[256,2048]{1,0:T(8,128)(2,1)} %get-tuple-element.130), channel_id=1, source_target_pairs={{0,4},{4,0},{1,5},{5,1},{2,6},{6,2},{3,7},{7,3},{8,12},{12,8},{9,1... | collective-permute-start | bytes 3145736 | tf_op jit(solution)/shard_map/ppermute | solution.py:27
  608.1 38.1 %collective-permute-start.61 = (bf16[256,2048]{1,0:T(8,128)(2,1)}, bf16[256,2048]{1,0:T(8,128)(2,1)S(1)}, u32[]{:S(2)}, u32[]{:S(2)}) collective-permute-start(bf16[256,2048]{1,0:T(8,128)(2,1)} %get-tuple-element.130), channel_id=1, source_target_pairs={{0,1},{1,0},{2,3},{3,2},{4,5},{5,4},{6,7},{7,6},{8,9},{9,8},{10,11... | collective-permute-start | bytes 3145736 | tf_op jit(solution)/shard_map/ppermute | solution.py:27
  631.5 12.2 %collective-permute-start.59 = (bf16[128,2048]{1,0:T(8,128)(2,1)S(1)}, bf16[128,2048]{1,0:T(8,128)(2,1)S(1)}, u32[]{:S(2)}, u32[]{:S(2)}) collective-permute-start(bf16[128,2048]{1,0:T(8,128)(2,1)S(1)} %slice.370), channel_id=1, source_target_pairs={{0,4},{4,0},{1,5},{5,1},{2,6},{6,2},{3,7},{7,3},{8,12},{12,8},{9,1... | collective-permute-start | bytes 1572872 | tf_op jit(solution)/shard_map/ppermute | solution.py:27
  632.6 11.9 %collective-permute-start.60 = (bf16[128,2048]{1,0:T(8,128)(2,1)S(1)}, bf16[128,2048]{1,0:T(8,128)(2,1)S(1)}, u32[]{:S(2)}, u32[]{:S(2)}) collective-permute-start(bf16[128,2048]{1,0:T(8,128)(2,1)S(1)} %slice.371), channel_id=1, source_target_pairs={{0,2},{2,0},{1,3},{3,1},{4,6},{6,4},{5,7},{7,5},{8,10},{10,8},{9,1... | collective-permute-start | bytes 1572872 | tf_op jit(solution)/shard_map/ppermute | solution.py:27
  633.7 13.5 %collective-permute-start.62 = (bf16[256,2048]{1,0:T(8,128)(2,1)S(1)}, bf16[256,2048]{1,0:T(8,128)(2,1)S(1)}, u32[]{:S(2)}, u32[]{:S(2)}) collective-permute-start(bf16[256,2048]{1,0:T(8,128)(2,1)S(1)} %collective-permute-done.57), channel_id=1, source_target_pairs={{0,1},{1,0},{2,3},{3,2},{4,5},{5,4},{6,7},{7,6},{8,9},{9,8},{10,11... | collective-permute-start | bytes 3145736 | tf_op jit(solution)/shard_map/ppermute | solution.py:27
  633.8 14.6 %collective-permute-start.63 = (bf16[256,2048]{1,0:T(8,128)(2,1)S(1)}, bf16[256,2048]{1,0:T(8,128)(2,1)S(1)}, u32[]{:S(2)}, u32[]{:S(2)}) collective-permute-start(bf16[256,2048]{1,0:T(8,128)(2,1)S(1)} %collective-permute-done.58), channel_id=1, source_target_pairs={{0,1},{1,0},{2,3},{3,2},{4,5},{5,4},{6,7},{7,6},{8,9},{9,8},{10,11... | collective-permute-start | bytes 3145736 | tf_op jit(solution)/shard_map/ppermute | solution.py:27
  651.2 200.8 %reduce-scatter.11.cloned.1.call-start = ((), (), s32[]{:S(2)}) async-start(), calls=%async_computation.19 | async-start | bytes 3932160 | tf_op jit(solution)/shard_map/reduce_scatter | solution.py:440
  735.4 14.4 %collective-permute-start.72 = (bf16[128,2048]{1,0:T(8,128)(2,1)}, bf16[128,2048]{1,0:T(8,128)(2,1)}, u32[]{:S(2)}, u32[]{:S(2)}) collective-permute-start(bf16[128,2048]{1,0:T(8,128)(2,1)} %get-tuple-element.173), channel_id=1, source_target_pairs={{0,2},{2,0},{1,3},{3,1},{4,6},{6,4},{5,7},{7,5},{8,10},{10,8},{9,1... | collective-permute-start | bytes 1572872 | tf_op jit(solution)/shard_map/ppermute | solution.py:27
  736.5 14.0 %collective-permute-start.73 = (bf16[128,2048]{1,0:T(8,128)(2,1)}, bf16[128,2048]{1,0:T(8,128)(2,1)}, u32[]{:S(2)}, u32[]{:S(2)}) collective-permute-start(bf16[128,2048]{1,0:T(8,128)(2,1)} %get-tuple-element.172), channel_id=1, source_target_pairs={{0,4},{4,0},{1,5},{5,1},{2,6},{6,2},{3,7},{7,3},{8,12},{12,8},{9,1... | collective-permute-start | bytes 1572872 | tf_op jit(solution)/shard_map/ppermute | solution.py:27
  738.0 75.6 %collective-permute-start.69 = (bf16[256,2048]{1,0:T(8,128)(2,1)}, bf16[256,2048]{1,0:T(8,128)(2,1)}, u32[]{:S(2)}, u32[]{:S(2)}) collective-permute-start(bf16[256,2048]{1,0:T(8,128)(2,1)} %get-tuple-element.140), channel_id=1, source_target_pairs={{0,1},{1,0},{2,3},{3,2},{4,5},{5,4},{6,7},{7,6},{8,9},{9,8},{10,11... | collective-permute-start | bytes 3145736 | tf_op jit(solution)/shard_map/ppermute | solution.py:27
  753.1 60.5 %collective-permute-start.76 = (bf16[256,2048]{1,0:T(8,128)(2,1)}, bf16[256,2048]{1,0:T(8,128)(2,1)}, u32[]{:S(2)}, u32[]{:S(2)}) collective-permute-start(bf16[256,2048]{1,0:T(8,128)(2,1)} %pad_maximum_fusion.7), channel_id=1, source_target_pairs={{0,4},{4,0},{1,5},{5,1},{2,6},{6,2},{3,7},{7,3},{8,12},{12,8},{9,1... | collective-permute-start | bytes 3145736 | tf_op jit(solution)/shard_map/ppermute | solution.py:27
  756.9 56.7 %collective-permute-start.74 = (bf16[256,2048]{1,0:T(8,128)(2,1)}, bf16[256,2048]{1,0:T(8,128)(2,1)}, u32[]{:S(2)}, u32[]{:S(2)}) collective-permute-start(bf16[256,2048]{1,0:T(8,128)(2,1)} %pad_maximum_fusion.6), channel_id=1, source_target_pairs={{0,2},{2,0},{1,3},{3,1},{4,6},{6,4},{5,7},{7,5},{8,10},{10,8},{9,1... | collective-permute-start | bytes 3145736 | tf_op jit(solution)/shard_map/ppermute | solution.py:27
  758.3 17.8 %collective-permute-start.79 = (bf16[64,2048]{1,0:T(8,128)(2,1)S(1)}, bf16[64,2048]{1,0:T(8,128)(2,1)S(1)}, u32[]{:S(2)}, u32[]{:S(2)}) collective-permute-start(bf16[64,2048]{1,0:T(8,128)(2,1)S(1)} %get-tuple-element.170), channel_id=1, source_target_pairs={{0,24},{8,0},{16,8},{24,16},{1,25},{9,1},{17,9},{25,17},{2,26},{10... | collective-permute-start | bytes 786440 | tf_op jit(solution)/shard_map/ppermute | solution.py:299
  758.3 53.2 %collective-permute-start.78 = (bf16[64,2048]{1,0:T(8,128)(2,1)}, bf16[64,2048]{1,0:T(8,128)(2,1)}, u32[]{:S(2)}, u32[]{:S(2)}) collective-permute-start(bf16[64,2048]{1,0:T(8,128)(2,1)} %get-tuple-element.171), channel_id=1, source_target_pairs={{0,16},{8,24},{16,0},{24,8},{1,17},{9,25},{17,1},{25,9},{2,18},{10... | collective-permute-start | bytes 786440 | tf_op jit(solution)/shard_map/ppermute | solution.py:299
  776.2 35.4 %collective-permute-start.77 = (bf16[64,2048]{1,0:T(8,128)(2,1)S(1)}, bf16[64,2048]{1,0:T(8,128)(2,1)}, u32[]{:S(2)}, u32[]{:S(2)}) collective-permute-start(bf16[64,2048]{1,0:T(8,128)(2,1)S(1)} %get-tuple-element.169), channel_id=1, source_target_pairs={{0,8},{8,16},{16,24},{24,0},{1,9},{9,17},{17,25},{25,1},{2,10},{10... | collective-permute-start | bytes 786440 | tf_op jit(solution)/shard_map/ppermute | solution.py:299
  786.3 32.4 %all-to-all-start.7 = ((f32[32,1,256]{2,1,0:T(1,128)}), f32[32,1,256]{2,1,0:T(1,128)S(1)}, u32[]{:S(2)}, u32[]{:S(2)}) async-start(f32[32,1,256]{2,1,0:T(1,128)} %reshape.267), calls=%async_computation.11 | async-start | bytes 65536 | tf_op jit(solution)/shard_map/all_to_all | solution.py:504
  818.7 29.7 %all-to-all-start.5 = ((bf16[2,128,2048]{2,0,1:T(2,128)(2,1)}), bf16[2,128,2048]{2,0,1:T(2,128)(2,1)S(1)}, u32[]{:S(2)}, u32[]{:S(2)}) async-start(bf16[2,128,2048]{2,0,1:T(2,128)(2,1)} %copy.72), calls=%async_computation.5 | async-start | bytes 2097152 | tf_op jit(solution)/shard_map/all_to_all | solution.py:474
  852.0 16.8 %all-to-all-start.6 = ((bf16[8,64,768]{2,1,0:T(8,128)(2,1)}), bf16[8,64,768]{2,1,0:T(8,128)(2,1)}, u32[]{:S(2)}, u32[]{:S(2)}) async-start(bf16[8,64,768]{2,1,0:T(8,128)(2,1)} %bitcast.141), calls=%async_computation.10 | async-start | bytes 1572864 | tf_op jit(solution)/shard_map/all_to_all | solution.py:486
  (80 other events, 1329.6 us)
Sparse Core Ops, SparseCore 0:
  37.6 82.2 all-gather.4
  121.4 79.7 all-gather.6
  202.8 78.7 all-gather.8
  283.0 78.9 all-gather.10
  483.8 74.3 reduce-scatter.4
  566.9 74.2 reduce-scatter.6
  651.3 74.7 reduce-scatter.8
  735.5 75.4 reduce-scatter.10

commit v4 on v3

--- a/solution.py
+++ b/solution.py
@@ -255,7 +255,7 @@
     return jnp.concatenate(pieces + [swap(piece, "c") for piece in pieces], axis=0), over_x, done
 
 
-def group_scatter(partial, meanwhile=None):
+def group_scatter(partial, meanwhile=None, until=()):
     wide = partial.shape[0] // 2
     rows = wide // 4
     half = rows // 2
@@ -273,10 +273,76 @@
     done = None
     if meanwhile is not None:
         done = meanwhile(far_low)
-        far_x, far_y, _ = lax.optimization_barrier((far_x, far_y, done))
+        far_x, far_y = lax.optimization_barrier((far_x, far_y, done) + until)[:2]
     over_y = jnp.concatenate([over_y[:half] + far_x.astype(F32), over_y[half:]])
     over_x = jnp.concatenate([over_x[:half], over_x[half:] + far_y.astype(F32)])
     return own + move(over_x, "x") + move(over_y, "y"), done
+
+
+def gated_kernel(groups, hidden_ref, weight_ref, raw_ref, act_ref):
+    raw = matmul(hidden_ref[...], weight_ref[...], 1, 1)
+    raw_ref[...] = raw
+    step = raw.shape[1] // (2 * groups)
+    for i in range(groups):
+        gate = raw[:, 2 * i * step : (2 * i + 1) * step]
+        up = raw[:, (2 * i + 1) * step : (2 * i + 2) * step]
+        act_ref[:, i * step : (i + 1) * step] = (gate * jax.nn.sigmoid(gate) * up).astype(BF)
+
+
+def gated(hidden, weight, groups):
+    wide, width = hidden.shape
+    units = weight.shape[0]
+    block = 256
+    rows = lambda columns: pl.BlockSpec((block, columns), lambda i: (i, 0))
+    return pl.pallas_call(
+        lambda *refs: gated_kernel(groups, *refs),
+        grid=(wide // block,),
+        in_specs=[rows(width), pl.BlockSpec((units, width), lambda i: (0, 0))],
+        out_specs=[rows(units), rows(units // 2)],
+        out_shape=[jax.ShapeDtypeStruct((wide, units), F32), jax.ShapeDtypeStruct((wide, units // 2), BF)],
+        cost_estimate=pl.CostEstimate(
+            flops=2 * wide * width * units,
+            bytes_accessed=2 * wide * width + 2 * units * width + 5 * wide * units,
+            transcendentals=wide * units // 2,
+        ),
+        name="gated",
+    )(hidden, weight)
+
+
+def gated_back_kernel(groups, grad_ref, down_ref, raw_ref, weight_ref, units_ref, hidden_ref):
+    grad_act = matmul(grad_ref[...], down_ref[...], 1, 1)
+    step = grad_act.shape[1] // groups
+    for i in range(groups):
+        gate = raw_ref[:, 2 * i * step : (2 * i + 1) * step]
+        up = raw_ref[:, (2 * i + 1) * step : (2 * i + 2) * step]
+        grad = grad_act[:, i * step : (i + 1) * step]
+        sigma = jax.nn.sigmoid(gate)
+        units_ref[:, 2 * i * step : (2 * i + 1) * step] = (
+            grad * up * sigma * (1.0 + gate * (1.0 - sigma))
+        ).astype(BF)
+        units_ref[:, (2 * i + 1) * step : (2 * i + 2) * step] = (grad * (gate * sigma)).astype(BF)
+    hidden_ref[...] = matmul(units_ref[...], weight_ref[...]).astype(BF)
+
+
+def gated_back(grad, down, raw, weight, groups):
+    wide, width = grad.shape
+    units = weight.shape[0]
+    block = 256
+    rows = lambda columns: pl.BlockSpec((block, columns), lambda i: (i, 0))
+    fixed = lambda count: pl.BlockSpec((count, width), lambda i: (0, 0))
+    return pl.pallas_call(
+        lambda *refs: gated_back_kernel(groups, *refs),
+        grid=(wide // block,),
+        in_specs=[rows(width), fixed(units // 2), rows(units), fixed(units)],
+        out_specs=[rows(units), rows(width)],
+        out_shape=[jax.ShapeDtypeStruct((wide, units), BF), jax.ShapeDtypeStruct((wide, width), BF)],
+        cost_estimate=pl.CostEstimate(
+            flops=3 * wide * width * units,
+            bytes_accessed=4 * wide * width + 3 * units * width + 6 * wide * units,
+            transcendentals=wide * units // 2,
+        ),
+        name="gated_back",
+    )(grad, down, raw, weight)
 
 
 def ring(ahead):
@@ -290,14 +356,6 @@
         moved = lax.ppermute(block, "z", ring(ahead))
         out = lax.dynamic_update_index_in_dim(out, moved, (at - ahead) % LINE, 0)
     return out
-
-
-def line_sum(blocks, at):
-    total = lax.dynamic_index_in_dim(blocks, at, 0, keepdims=False).astype(F32)
-    for ahead in range(1, LINE):
-        block = lax.dynamic_index_in_dim(blocks, (at + ahead) % LINE, 0, keepdims=False)
-        total = total + lax.ppermute(block, "z", ring(ahead)).astype(F32)
-    return total
 
 
 def group_total(value):
@@ -378,8 +436,9 @@
     w_out = lax.all_to_all(out_all, head_axes, split_axis=0, concat_axis=1, tiled=True)
     w_out = w_out.reshape(own_width, width)
 
-    gate = lax.all_gather(after(w_gate.T, qkv_in), REST, axis=0, tiled=True)
-    up = lax.all_gather(after(w_up.T, qkv_in), REST, axis=0, tiled=True)
+    units = w_gate.shape[1]
+    gate_up = jnp.concatenate([w_gate.T, w_up.T])
+    gate_up = lax.all_gather(after(gate_up, qkv_in), REST, axis=0, tiled=True)
     down = lax.all_gather(after(w_down, qkv_in), REST, axis=0, tiled=True)
 
     own_seqs = lax.dynamic_slice_in_dim(dealing, rank * micro_count, micro_count)
@@ -398,11 +457,7 @@
     hidden_wide, _, _ = group_gather(hidden.astype(BF))
     contract_last = (((1,), (1,)), ((), ()))
     contract_rows = (((0,), (0,)), ((), ()))
-    gate_proj = lax.dot_general(hidden_wide, gate, contract_last, preferred_element_type=F32)
-    up_proj = lax.dot_general(hidden_wide, up, contract_last, preferred_element_type=F32)
-    sigma_gate = jax.nn.sigmoid(gate_proj)
-    act_value = gate_proj * sigma_gate
-    act_low = (act_value * up_proj).astype(BF)
+    unit_raw, act_low = gated(hidden_wide, gate_up, groups)
     down_raw, _ = group_scatter(jnp.dot(act_low, down, preferred_element_type=F32).astype(BF))
     down_inv = lax.rsqrt(jnp.mean(down_raw * down_raw, axis=-1, keepdims=True) + norm_eps)
     down_normed = down_raw * down_inv
@@ -419,33 +474,26 @@
     down_term = lax.dot_general(
         act_low, grad_down_wide, contract_rows, preferred_element_type=F32
     ).astype(BF)
-    grad_act = lax.dot_general(grad_down_wide, down, contract_last, preferred_element_type=F32)
-    grad_gate_low = (grad_act * up_proj * sigma_gate * (1.0 + gate_proj * (1.0 - sigma_gate))).astype(BF)
-    grad_up_low = (grad_act * act_value).astype(BF)
-    grad_gate_low = after(grad_gate_low, down_term)
-    grad_hidden = jnp.dot(grad_gate_low, gate, preferred_element_type=F32) + jnp.dot(
-        grad_up_low, up, preferred_element_type=F32
-    )
-    hidden_term = grad_hidden.astype(BF)
+    grad_units, hidden_term = gated_back(after(grad_down_wide, down_term), down, unit_raw, gate_up, groups)
 
     def weight_term(left, right):
         return lambda token: lax.dot_general(
             after(left, token), right, contract_rows, preferred_element_type=F32
         ).astype(BF)
 
-    moved, gate_term = group_scatter(hidden_term, weight_term(grad_gate_low, hidden_wide))
-    grad_hidden = grad_out + moved
-
     def owners(term):
         return lax.psum_scatter(term, REST, scatter_dimension=0, tiled=True)
 
     down_part = owners(down_term)
+    moved, unit_term = group_scatter(hidden_term, weight_term(grad_units, hidden_wide), (down_part,))
+    grad_hidden = grad_out + moved
+    unit_part = owners(after(unit_term, down_part))
 
     grad_gain_attn = jnp.sum(out_normed * grad_hidden, axis=0)
     scaled = grad_hidden * gain_attn
     grad_out_raw = out_inv * (scaled - out_normed * jnp.mean(scaled * out_normed, axis=-1, keepdims=True))
     grad_out_low = grad_out_raw.astype(BF)
-    grad_out_wide, grad_out_near, up_term = group_gather(grad_out_low, weight_term(grad_up_low, hidden_wide))
+    grad_out_wide, _, _ = group_gather(grad_out_low)
 
     output_term = lax.dot_general(
         attended_low, grad_out_wide, contract_rows, preferred_element_type=F32
@@ -461,6 +509,7 @@
 
     grad_att = lax.dot_general(grad_out_wide, w_out, contract_last, preferred_element_type=F32).astype(BF)
     scaled, grad_value, dots, gain_term = attend_back(qkv_raw, inverses, gain_heads, tables, own_heads, grad_att)
+    scaled = after(scaled, output_term)
     means = group_total(dots) * (1.0 / width)
     grad_qkv = finish(qkv_raw, inverses, means, scaled, grad_value, seq_len, own_heads)
 
@@ -468,11 +517,8 @@
     grad_input = after(grad_input.astype(BF), output_term)
     moved, qkv_term = group_scatter(grad_input, weight_term(x_wide, grad_qkv))
     grad_input = grad_hidden + moved
-    output_part = line_sum(output_term.reshape(LINE, along * shard, width), at)
-    if along > 1:
-        output_part = lax.psum_scatter(output_part.astype(BF), "m", scatter_dimension=0, tiled=True)
     returned = lax.all_to_all(
-        after(grad_input.astype(BF), output_part).reshape(micro_count, seq_len, width),
+        grad_input.astype(BF).reshape(micro_count, seq_len, width),
         ALL,
         split_axis=1,
         concat_axis=0,
@@ -480,9 +526,8 @@
     )
     input_grad = jnp.zeros_like(tokens).at[dealing].set(returned)
 
-    gate_part = owners(after(gate_term, down_part, hidden_term))
-    up_part = owners(after(up_term, gate_part, grad_out_near))
-    qkv_rows = owners(after(qkv_term, up_part))
+    qkv_rows = owners(after(qkv_term, unit_part))
+    output_part = owners(after(output_term.reshape(groups * shard, width), qkv_term))
     qkv_back = lax.all_to_all(
         qkv_rows.reshape(PLANE, shard, 3 * own_width), GROUP, split_axis=0, concat_axis=0, tiled=True
     )
@@ -513,8 +558,8 @@
         gain_part[0],
         gain_part[1],
         gain_part[2],
-        gate_part.astype(F32).T,
-        up_part.astype(F32).T,
+        unit_part[:units].astype(F32).T,
+        unit_part[units:].astype(F32).T,
         down_part.astype(F32),
         gain_part[3],
     )

time: 890 us -> 848 us (0.953)
  matrix products: 164 us -> 74.4 us
  waiting for transfers between devices: 344 us -> 414 us
  Pallas kernels: 57.5 us -> 119 us
  blocking collectives: 64.4 us -> 9.84 us
  starting transfers between devices: 91.3 us -> 76.8 us
  local copies, waits for them, and re-layouts: 90.2 us -> 77.4 us
    dot_general x5 -> x0, matrix products: 85.6 us -> none  [the longest x1 23.2 us: per_device(): lax.dot_general(grad_down_wide, down, contract_last, preferred_element_ty...]
    pallas_call x0 -> x2, Pallas kernels: none -> 62.1 us  [the longest x1 37.8 us: gated_back(): pl.pallas_call(lambda *refs: gated_back_kernel(groups, *refs), grid=(wide...]
    all_to_all x1 -> x2, waiting for transfers between devices: 21.5 us -> 81.5 us  [the longest x1 43.6 us: per_device(): lax.all_to_all(outgoing, ALL, split_axis=0, concat_axis=1, tiled=True)]
    all_to_all x1 -> x0, blocking collectives: 55.1 us -> none  [per_device(): lax.all_to_all(outgoing, ALL, split_axis=0, concat_axis=1, tiled=True)]
    ppermute x74, waiting for transfers between devices: 230 us -> 274 us  [swap(): return lax.ppermute(value, axis, SWAP)]
    ppermute x3 -> x0, waiting for transfers between devices: 38.7 us -> none  [line_sum(): total = total + lax.ppermute(block, 'z', ring(ahead)).astype(F32)]
    ppermute x3 -> x0, starting transfers between devices: 10.7 us -> none  [line_sum(): total = total + lax.ppermute(block, 'z', ring(ahead)).astype(F32)]
    unnamed x142 -> x126, local copies, waits for them, and re-layouts: 43.8 us -> 35.9 us
  transfers between devices with their start and end apart: 93 -> 90, of which waited for: 49 -> 54; matrix products, arithmetic and copies ran while one was open for 30% -> 19% of each run, Pallas kernels for 7% -> 14%
where the time goes in v4:
time: 848 us; the launch traced here: 839 us
  waiting for transfers between devices  414 us (49%)
  Pallas kernels  119 us (14%)
  local copies, waits for them, and re-layouts  77.4 us (9%)
  starting transfers between devices  76.8 us (9%)
  matrix products  74.4 us (9%)
  other arithmetic  51.7 us (6%)
  between operations  16 us (2%)
  blocking collectives  9.84 us (1%)
    ppermute x74, waiting for transfers between devices, swap(): return lax.ppermute(value, axis, SWAP)  274 us
    ppermute x74, starting transfers between devices, swap(): return lax.ppermute(value, axis, SWAP)  48.7 us
    all_gather x1, waiting for transfers between devices, per_device(): down = lax.all_gather(after(w_down, qkv_in), REST, axis=0, tiled=True)  45.1 us
    all_to_all x1, waiting for transfers between devices, per_device(): lax.all_to_all(outgoing, ALL, split_axis=0, concat_axis=1, tiled=True)  43.6 us
    all_to_all x1, waiting for transfers between devices, per_device(): lax.all_to_all(grad_input.astype(BF).reshape(micro_count, seq_len, width)...  38 us
    pallas_call x1, Pallas kernels, gated_back(): pl.pallas_call(lambda *refs: gated_back_kernel(groups, *refs), grid=(wide...  37.8 us
    unnamed x126, local copies, waits for them, and re-layouts  35.9 us
    dot_general x2, matrix products, weight_term(): lax.dot_general(after(left, token), right, contract_rows, preferred_eleme...  32.7 us
  transfers between devices with their start and end apart: 90, of which 54 were waited for; matrix products, arithmetic and copies ran while one was open for 19% of the time, Pallas kernels for 14%

profile of v4, /device:TPU:0, one launch (start us, length us, event | category | flops | bytes accessed | tf_op | source)
XLA Modules:
  0.0 839.4 jit_solution(15724632451417334100)
XLA Ops:
  7.2 3.1 collective-permute-start.9
  10.3 2.6 collective-permute-start.10
  21.2 3.7 all-to-all-start.1
  25.3 5.0 collective-permute-done.10
  30.3 7.3 all-to-all-done.1
  38.4 2.7 all-to-all-start
  42.7 2.3 copy.134
  45.0 2.8 pad_maximum_fusion
  47.8 43.6 %all-to-all-done = bf16[64,4,2048]{2,1,0:T(4,128)(2,1)S(1)} async-done(((bf16[64,4,2048]{2,1,0:T(4,128)(2,1)}), bf16[64,4,2048]{2,1,0:T(4,128)(2,1)S(1)}, u32[]{:S(2)}, u32[]{:S(2)}) %all-to-all-start) | async-done | bytes 1048608 | tf_op jit(solution)/shard_map/all_to_all | solution.py:412
  96.2 4.5 all-to-all-start.2
  101.1 15.4 %collective-permute-done = bf16[256,2048]{1,0:T(8,128)(2,1)} collective-permute-done((bf16[256,2048]{1,0:T(8,128)(2,1)S(1)}, bf16[256,2048]{1,0:T(8,128)(2,1)}, u32[]{:S(2)}, u32[]{:S(2)}) %collective-permute-start) | collective-permute-done | bytes 1048608 | tf_op jit(solution)/shard_map/ppermute | solution.py:27
  122.5 2.4 constant_dynamic-update-slice_fusion.8
  125.9 3.5 collective-permute-done.2
  137.2 13.0 %project.1 = (f32[2048,768]{1,0:T(8,128)}, f32[2,2048]{1,0:T(2,128)}) custom-call(bf16[2048,2048]{1,0:T(8,128)(2,1)} %constant_dynamic-update-slice_fusion.refs_0_, bf16[2048,768]{1,0:T(8,128)(2,1)} %bitcast.129), custom_call_target="tpu_custom_call" | custom-call | flops 6442450944 | bytes 17825792 | tf_op jit(solution)/shard_map/project/pallas_call | solution.py:78
  157.7 5.1 all_to_all.86
  163.7 15.3 %attend.1 = bf16[2048,256]{1,0:T(8,128)(2,1)} custom-call(f32[2048,768]{1,0:T(8,128)} %get-tuple-element.46.refs_0_, f32[2,2048]{1,0:T(2,128)} %rsqrt.22.refs_1_, f32[2,256]{1,0:T(2,128)} %bitcast.121, f32[128,128]{1,0:T(8,128)} %get-tuple-element.228.refs_3_, f32[128,128]{1,0:T(8,128)} %get-tuple-element.229.refs_4_), custom_call_target="tpu_custom_call" | custom-call | flops 268435456 | bytes 7340032 | tf_op jit(solution)/shard_map/attend/pallas_call | solution.py:190
  179.0 3.6 convolution_convert_fusion.3
  194.8 10.6 %collective-permute-done.18 = bf16[128,2048]{1,0:T(8,128)(2,1)S(1)} collective-permute-done((bf16[128,2048]{1,0:T(8,128)(2,1)S(1)}, bf16[128,2048]{1,0:T(8,128)(2,1)S(1)}, u32[]{:S(2)}, u32[]{:S(2)}) %collective-permute-start.18) | collective-permute-done | bytes 524320 | tf_op jit(solution)/shard_map/ppermute | solution.py:27
  209.5 20.7 %collective-permute-done.19 = bf16[256,2048]{1,0:T(8,128)(2,1)} collective-permute-done((bf16[256,2048]{1,0:T(8,128)(2,1)S(1)}, bf16[256,2048]{1,0:T(8,128)(2,1)}, u32[]{:S(2)}, u32[]{:S(2)}) %collective-permute-start.19) | collective-permute-done | bytes 1048608 | tf_op jit(solution)/shard_map/ppermute | solution.py:27
  230.3 2.3 collective-permute-done.22
  232.6 2.9 multiply_reduce_fusion.3
  239.1 21.8 %collective-permute-done.23 = bf16[256,2048]{1,0:T(8,128)(2,1)S(1)} collective-permute-done((bf16[256,2048]{1,0:T(8,128)(2,1)S(1)}, bf16[256,2048]{1,0:T(8,128)(2,1)S(1)}, u32[]{:S(2)}, u32[]{:S(2)}) %collective-permute-start.23) | collective-permute-done | bytes 1048608 | tf_op jit(solution)/shard_map/ppermute | solution.py:27
  265.9 7.6 collective-permute-done.25
  280.7 24.3 %gated.1 = (f32[2048,2048]{1,0:T(8,128)}, bf16[2048,1024]{1,0:T(8,128)(2,1)}) custom-call(bf16[2048,2048]{1,0:T(8,128)(2,1)} %constant_dynamic-update-slice_fusion.10.refs_0_, bf16[2048,2048]{1,0:T(8,128)(2,1)} %all-gather.6.cloned.1.call-done.refs_1_.refs_3_), custom_call_target="tpu_custom_call" | custom-call | flops 17179869184 | bytes 37748736 | tf_op jit(solution)/shard_map/gated/pallas_call | solution.py:297
  305.0 45.1 %all-gather.8.cloned.1.call-done.refs_1_ = bf16[1024,2048]{1,0:T(8,128)(2,1)} async-done(((bf16[256,2048]{1,0:T(8,128)(2,1)}), bf16[1024,2048]{1,0:T(8,128)(2,1)}) %all-gather.8.cloned.1.call-update) | async-done | bytes 4194320 | tf_op jit(solution)/shard_map/all_gather | solution.py:442
  350.1 12.1 %convolution_convert_fusion.2 = bf16[2048,2048]{1,0:T(8,128)(2,1)S(1)} fusion(bf16[2048,1024]{1,0:T(8,128)(2,1)} %get-tuple-element.49, bf16[1024,2048]{1,0:T(8,128)(2,1)} %all-gather.8.cloned.1.call-done.refs_1_), kind=kOutput, calls=%fused_computation.5 | convolution fusion | flops 8594128896 | bytes 16777216 | tf_op jit(solution)/shard_map/dot_general | solution.py:461
  364.7 2.1 collective-permute-done.33
  374.4 10.8 %collective-permute-done.35 = bf16[128,2048]{1,0:T(8,128)(2,1)S(1)} collective-permute-done((bf16[128,2048]{1,0:T(8,128)(2,1)S(1)}, bf16[128,2048]{1,0:T(8,128)(2,1)S(1)}, u32[]{:S(2)}, u32[]{:S(2)}) %collective-permute-start.35) | collective-permute-done | bytes 524320 | tf_op jit(solution)/shard_map/ppermute | solution.py:27
  391.5 19.6 %collective-permute-done.36 = bf16[256,2048]{1,0:T(8,128)(2,1)} collective-permute-done((bf16[256,2048]{1,0:T(8,128)(2,1)}, bf16[256,2048]{1,0:T(8,128)(2,1)}, u32[]{:S(2)}, u32[]{:S(2)}) %collective-permute-start.36) | collective-permute-done | bytes 1048608 | tf_op jit(solution)/shard_map/ppermute | solution.py:27
  411.1 2.4 collective-permute-done.39
  413.5 2.9 multiply_reduce_fusion.2
  420.0 21.6 %collective-permute-done.40 = bf16[256,2048]{1,0:T(8,128)(2,1)S(1)} collective-permute-done((bf16[256,2048]{1,0:T(8,128)(2,1)S(1)}, bf16[256,2048]{1,0:T(8,128)(2,1)S(1)}, u32[]{:S(2)}, u32[]{:S(2)}) %collective-permute-start.40) | collective-permute-done | bytes 1048608 | tf_op jit(solution)/shard_map/ppermute | solution.py:27
  444.9 9.4 %collective-permute-done.42 = bf16[128,2048]{1,0:T(8,128)(2,1)S(1)} collective-permute-done((bf16[128,2048]{1,0:T(8,128)(2,1)S(1)}, bf16[128,2048]{1,0:T(8,128)(2,1)S(1)}, u32[]{:S(2)}, u32[]{:S(2)}) %collective-permute-start.42) | collective-permute-done | bytes 524320 | tf_op jit(solution)/shard_map/ppermute | solution.py:27
  457.0 3.3 copy-done.30
  460.3 11.0 %convolution_convert_fusion.4 = bf16[1024,2048]{1,0:T(8,128)(2,1)} fusion(bf16[2048,1024]{1,0:T(8,128)(2,1)S(1)} %copy-done.39, bf16[2048,2048]{1,0:T(8,128)(2,1)S(1)} %constant_dynamic-update-slice_fusion.20.refs_0_), kind=kOutput, calls=%fused_computation.7 | convolution fusion | flops 8592031744 | bytes 16777216 | tf_op jit(solution)/shard_map/dot_general | solution.py:474
  471.4 37.8 %gated_back.1 = (bf16[2048,2048]{1,0:T(8,128)(2,1)}, bf16[2048,2048]{1,0:T(8,128)(2,1)}) custom-call(bf16[2048,2048]{1,0:T(8,128)(2,1)} %copy-done.30, bf16[1024,2048]{1,0:T(8,128)(2,1)} %all-gather.8.cloned.1.call-done.refs_1_, f32[2048,2048]{1,0:T(8,128)} %get-tuple-element.52.refs_2_, bf16[2048,2048]{1,0:T(8,128)(2,1)} %all-gather.6.cloned.1.call-done.refs_1_.refs_3_), custom_call_target="tpu_custom_call" | custom-call | flops 25769803776 | bytes 54525952 | tf_op jit(solution)/shard_map/gated_back/pallas_call | solution.py:333
  509.2 3.9 fusion.25
  518.7 5.1 convert_add_fusion.3
  524.9 22.1 %convolution_convert_fusion.1 = bf16[2048,2048]{1,0:T(8,128)(2,1)} fusion(bf16[2048,2048]{1,0:T(8,128)(2,1)S(1)} %bitcast.132, bf16[2048,2048]{1,0:T(8,128)(2,1)} %constant_dynamic-update-slice_fusion.10.refs_0_), kind=kOutput, calls=%fused_computation.4 | convolution fusion | flops 17184063488 | bytes 25165824 | tf_op jit(solution)/shard_map/dot_general | solution.py:480
  552.8 9.2 %collective-permute-done.52 = bf16[128,2048]{1,0:T(8,128)(2,1)S(1)} collective-permute-done((bf16[128,2048]{1,0:T(8,128)(2,1)S(1)}, bf16[128,2048]{1,0:T(8,128)(2,1)S(1)}, u32[]{:S(2)}, u32[]{:S(2)}) %collective-permute-start.52) | collective-permute-done | bytes 524320 | tf_op jit(solution)/shard_map/ppermute | solution.py:27
  566.1 22.3 %collective-permute-done.54 = bf16[256,2048]{1,0:T(8,128)(2,1)S(1)} collective-permute-done((bf16[256,2048]{1,0:T(8,128)(2,1)S(1)}, bf16[256,2048]{1,0:T(8,128)(2,1)S(1)}, u32[]{:S(2)}, u32[]{:S(2)}) %collective-permute-start.54) | collective-permute-done | bytes 1048608 | tf_op jit(solution)/shard_map/ppermute | solution.py:27
  589.5 4.2 multiply_reduce_fusion
  597.1 20.9 %collective-permute-done.57 = bf16[256,2048]{1,0:T(8,128)(2,1)S(1)} collective-permute-done((bf16[256,2048]{1,0:T(8,128)(2,1)S(1)}, bf16[256,2048]{1,0:T(8,128)(2,1)S(1)}, u32[]{:S(2)}, u32[]{:S(2)}) %collective-permute-start.57) | collective-permute-done | bytes 1048608 | tf_op jit(solution)/shard_map/ppermute | solution.py:27
  621.5 8.5 %collective-permute-done.59 = bf16[128,2048]{1,0:T(8,128)(2,1)S(1)} collective-permute-done((bf16[128,2048]{1,0:T(8,128)(2,1)S(1)}, bf16[128,2048]{1,0:T(8,128)(2,1)S(1)}, u32[]{:S(2)}, u32[]{:S(2)}) %collective-permute-start.59) | collective-permute-done | bytes 524320 | tf_op jit(solution)/shard_map/ppermute | solution.py:27
  632.7 2.3 convolution_convert_fusion.7
  635.1 3.4 convolution_convert_fusion.6.refs_5_
  638.5 20.6 %attend_back.1 = (f32[2048,512]{1,0:T(8,128)}, bf16[2048,256]{1,0:T(8,128)(2,1)}, f32[2,2048]{1,0:T(2,128)}, f32[2,256]{1,0:T(2,128)}) custom-call(f32[2048,768]{1,0:T(8,128)} %get-tuple-element.46.refs_0_, f32[2,2048]{1,0:T(2,128)} %rsqrt.22.refs_1_, f32[2,256]{1,0:T(2,128)} %bitcast.122, f32[128,128]{1,0:T(8,128)} %get-tuple-element.228.refs_3_, ...), custom_call_target="tpu_custom_call" | custom-call | flops 671088640 | bytes 13631488 | tf_op jit(solution)/shard_map/attend_back/pallas_call | solution.py:208
  662.2 2.7 collective-permute-done.67
  667.3 4.8 all_to_all.87
  674.2 8.4 %finish.1 = bf16[2048,768]{1,0:T(8,128)(2,1)} custom-call(f32[2048,768]{1,0:T(8,128)} %get-tuple-element.46.refs_0_, f32[2,2048]{1,0:T(2,128)} %rsqrt.22.refs_1_, f32[2,2048]{1,0:T(2,128)} %mul.215.refs_2_, f32[2048,512]{1,0:T(8,128)} %get-tuple-element.61.refs_3_, bf16[2048,256]{1,0:T(8,128)(2,1)} %get-tuple-element.62.refs_4_), custom_call_target="tpu_custom_call" | custom-call | flops 4194304 | bytes 14680064 | tf_op jit(solution)/shard_map/finish/pallas_call | solution.py:231
  682.7 9.3 %convolution_convert_fusion = bf16[2048,2048]{1,0:T(8,128)(2,1)S(1)} fusion(bf16[2048,768]{1,0:T(8,128)(2,1)} %finish.1, bf16[2048,768]{1,0:T(8,128)(2,1)} %bitcast.130), kind=kOutput, calls=%fused_computation.3 | convolution fusion | flops 6446645248 | bytes 14680064 | tf_op jit(solution)/shard_map/dot_general | solution.py:516
  699.2 2.6 convert_add_fusion.1
  703.0 10.6 %convolution_convert_fusion.5 = bf16[2048,768]{1,0:T(8,128)(2,1)} fusion(bf16[2048,2048]{1,0:T(8,128)(2,1)} %constant_dynamic-update-slice_fusion.refs_0_, bf16[2048,768]{1,0:T(8,128)(2,1)S(1)} %copy-done.21), kind=kOutput, calls=%fused_computation.8 | convolution fusion | flops 6444023808 | bytes 14680064 | tf_op jit(solution)/shard_map/dot_general | solution.py:480
  717.0 10.9 %collective-permute-done.72 = bf16[128,2048]{1,0:T(8,128)(2,1)S(1)} collective-permute-done((bf16[128,2048]{1,0:T(8,128)(2,1)}, bf16[128,2048]{1,0:T(8,128)(2,1)S(1)}, u32[]{:S(2)}, u32[]{:S(2)}) %collective-permute-start.72) | collective-permute-done | bytes 524320 | tf_op jit(solution)/shard_map/ppermute | solution.py:27
  735.2 2.8 all-to-all-start.7
  738.1 17.7 %collective-permute-done.74 = bf16[256,2048]{1,0:T(8,128)(2,1)} collective-permute-done((bf16[256,2048]{1,0:T(8,128)(2,1)}, bf16[256,2048]{1,0:T(8,128)(2,1)}, u32[]{:S(2)}, u32[]{:S(2)}) %collective-permute-start.74) | collective-permute-done | bytes 1048608 | tf_op jit(solution)/shard_map/ppermute | solution.py:27
  755.7 2.1 collective-permute-done.76
  757.9 3.1 add_convert_fusion
  763.0 2.6 all-to-all-start.5
  769.4 38.0 %all-to-all-done.5 = bf16[2,128,2048]{2,0,1:T(2,128)(2,1)S(1)} async-done(((bf16[2,128,2048]{2,0,1:T(2,128)(2,1)}), bf16[2,128,2048]{2,0,1:T(2,128)(2,1)S(1)}, u32[]{:S(2)}, u32[]{:S(2)}) %all-to-all-start.5) | async-done | bytes 1048608 | tf_op jit(solution)/shard_map/all_to_all | solution.py:520
  807.3 4.2 all-to-all-start.6
  814.9 2.5 scatter_fusion
  817.4 3.8 convert_bitcast_fusion
  821.2 2.9 copy.146
  (412 shorter events, 167.9 us)
Async XLA Ops:
  7.2 18.0 %collective-permute-start.9 = (bf16[64,2048]{1,0:T(8,128)(2,1)}, bf16[64,2048]{1,0:T(8,128)(2,1)S(1)}, u32[]{:S(2)}, u32[]{:S(2)}) collective-permute-start(bf16[64,2048]{1,0:T(8,128)(2,1)} %param.21), channel_id=1, source_target_pairs={{0,8},{8,16},{16,24},{24,0},{1,9},{9,17},{17,25},{25,1},{2,10},{10... | collective-permute-start | bytes 786440 | tf_op jit(solution)/shard_map/ppermute | solution.py:356
  10.3 19.9 %collective-permute-start.10 = (bf16[64,2048]{1,0:T(8,128)(2,1)}, bf16[64,2048]{1,0:T(8,128)(2,1)S(1)}, u32[]{:S(2)}, u32[]{:S(2)}) collective-permute-start(bf16[64,2048]{1,0:T(8,128)(2,1)} %param.21), channel_id=1, source_target_pairs={{0,16},{8,24},{16,0},{24,8},{1,17},{9,25},{17,1},{25,9},{2,18},{10... | collective-permute-start | bytes 786440 | tf_op jit(solution)/shard_map/ppermute | solution.py:356
  12.9 17.4 %collective-permute-start.11 = (bf16[64,2048]{1,0:T(8,128)(2,1)}, bf16[64,2048]{1,0:T(8,128)(2,1)S(1)}, u32[]{:S(2)}, u32[]{:S(2)}) collective-permute-start(bf16[64,2048]{1,0:T(8,128)(2,1)} %param.21), channel_id=1, source_target_pairs={{0,24},{8,0},{16,8},{24,16},{1,25},{9,1},{17,9},{25,17},{2,26},{10... | collective-permute-start | bytes 786440 | tf_op jit(solution)/shard_map/ppermute | solution.py:356
  21.2 16.3 %all-to-all-start.1 = ((bf16[8,64,768]{2,1,0:T(8,128)(2,1)}), bf16[8,64,768]{2,1,0:T(8,128)(2,1)S(1)}, u32[]{:S(2)}, u32[]{:S(2)}) async-start(bf16[8,64,768]{2,1,0:T(8,128)(2,1)} %pad_maximum_fusion.9), calls=%async_computation.1 | async-start | bytes 1572864 | tf_op jit(solution)/shard_map/all_to_all | solution.py:417
  24.9 112.3 %all-gather.4.cloned.1.call-start = ((), (), s32[]{:S(2)}) async-start(), calls=%async_computation.12 | async-start | bytes 3932160 | tf_op jit(solution)/shard_map/all_gather | solution.py:435
  38.4 53.0 %all-to-all-start = ((bf16[64,4,2048]{2,1,0:T(4,128)(2,1)}), bf16[64,4,2048]{2,1,0:T(4,128)(2,1)S(1)}, u32[]{:S(2)}, u32[]{:S(2)}) async-start(bf16[64,4,2048]{2,1,0:T(4,128)(2,1)} %broadcast_select_fusion), calls=%async_computation | async-start | bytes 2097152 | tf_op jit(solution)/shard_map/all_to_all | solution.py:412
  41.1 239.6 %all-gather.6.cloned.1.call-start = ((), (), s32[]{:S(2)}) async-start(), calls=%async_computation.13 | async-start | bytes 10485760 | tf_op jit(solution)/shard_map/all_gather | solution.py:441
  92.2 24.3 %collective-permute-start = (bf16[256,2048]{1,0:T(8,128)(2,1)S(1)}, bf16[256,2048]{1,0:T(8,128)(2,1)}, u32[]{:S(2)}, u32[]{:S(2)}) collective-permute-start(bf16[256,2048]{1,0:T(8,128)(2,1)S(1)} %reshape.196), channel_id=1, source_target_pairs={{0,2},{2,0},{1,3},{3,1},{4,6},{6,4},{5,7},{7,5},{8,10},{10,8},{9,1... | collective-permute-start | bytes 3145736 | tf_op jit(solution)/shard_map/ppermute | solution.py:27
  94.1 25.0 %collective-permute-start.1 = (bf16[256,2048]{1,0:T(8,128)(2,1)S(1)}, bf16[256,2048]{1,0:T(8,128)(2,1)S(1)}, u32[]{:S(2)}, u32[]{:S(2)}) collective-permute-start(bf16[256,2048]{1,0:T(8,128)(2,1)S(1)} %reshape.196), channel_id=1, source_target_pairs={{0,4},{4,0},{1,5},{5,1},{2,6},{6,2},{3,7},{7,3},{8,12},{12,8},{9,1... | collective-permute-start | bytes 3145736 | tf_op jit(solution)/shard_map/ppermute | solution.py:27
  96.2 58.7 %all-to-all-start.2 = ((bf16[32,2,128]{2,1,0:T(2,128)(2,1)}), bf16[32,2,128]{2,1,0:T(2,128)(2,1)S(1)}, u32[]{:S(2)}, u32[]{:S(2)}) async-start(bf16[32,2,128]{2,1,0:T(2,128)(2,1)} %reshape.267), calls=%async_computation.2 | async-start | bytes 32768 | tf_op jit(solution)/shard_map/all_to_all | solution.py:420
  100.7 249.4 %all-gather.8.cloned.1.call-start = ((), (), s32[]{:S(2)}) async-start(), calls=%async_computation.14 | async-start | bytes 5242880 | tf_op jit(solution)/shard_map/all_gather | solution.py:442
  100.8 31.5 %collective-permute-start.4 = (bf16[256,2048]{1,0:T(8,128)(2,1)S(1)}, bf16[256,2048]{1,0:T(8,128)(2,1)S(1)}, u32[]{:S(2)}, u32[]{:S(2)}) collective-permute-start(bf16[256,2048]{1,0:T(8,128)(2,1)S(1)} %reshape.196), channel_id=1, source_target_pairs={{0,1},{1,0},{2,3},{3,2},{4,5},{5,4},{6,7},{7,6},{8,9},{9,8},{10,11... | collective-permute-start | bytes 3145736 | tf_op jit(solution)/shard_map/ppermute | solution.py:27
  117.6 11.9 %collective-permute-start.2 = (bf16[128,2048]{1,0:T(8,128)(2,1)S(1)}, bf16[128,2048]{1,0:T(8,128)(2,1)S(1)}, u32[]{:S(2)}, u32[]{:S(2)}) collective-permute-start(bf16[128,2048]{1,0:T(8,128)(2,1)S(1)} %slice.327), channel_id=1, source_target_pairs={{0,4},{4,0},{1,5},{5,1},{2,6},{6,2},{3,7},{7,3},{8,12},{12,8},{9,1... | collective-permute-start | bytes 1572872 | tf_op jit(solution)/shard_map/ppermute | solution.py:27
  119.1 11.5 %collective-permute-start.3 = (bf16[128,2048]{1,0:T(8,128)(2,1)S(1)}, bf16[128,2048]{1,0:T(8,128)(2,1)S(1)}, u32[]{:S(2)}, u32[]{:S(2)}) collective-permute-start(bf16[128,2048]{1,0:T(8,128)(2,1)S(1)} %slice.328), channel_id=1, source_target_pairs={{0,2},{2,0},{1,3},{3,1},{4,6},{6,4},{5,7},{7,5},{8,10},{10,8},{9,1... | collective-permute-start | bytes 1572872 | tf_op jit(solution)/shard_map/ppermute | solution.py:27
  122.0 11.4 %collective-permute-start.5 = (bf16[256,2048]{1,0:T(8,128)(2,1)}, bf16[256,2048]{1,0:T(8,128)(2,1)S(1)}, u32[]{:S(2)}, u32[]{:S(2)}) collective-permute-start(bf16[256,2048]{1,0:T(8,128)(2,1)} %collective-permute-done), channel_id=1, source_target_pairs={{0,1},{1,0},{2,3},{3,2},{4,5},{5,4},{6,7},{7,6},{8,9},{9,8},{10,11... | collective-permute-start | bytes 3145736 | tf_op jit(solution)/shard_map/ppermute | solution.py:27
  122.0 12.5 %collective-permute-start.6 = (bf16[256,2048]{1,0:T(8,128)(2,1)S(1)}, bf16[256,2048]{1,0:T(8,128)(2,1)S(1)}, u32[]{:S(2)}, u32[]{:S(2)}) collective-permute-start(bf16[256,2048]{1,0:T(8,128)(2,1)S(1)} %collective-permute-done.1), channel_id=1, source_target_pairs={{0,1},{1,0},{2,3},{3,2},{4,5},{5,4},{6,7},{7,6},{8,9},{9,8},{10,11... | collective-permute-start | bytes 3145736 | tf_op jit(solution)/shard_map/ppermute | solution.py:27
  191.4 14.0 %collective-permute-start.18 = (bf16[128,2048]{1,0:T(8,128)(2,1)S(1)}, bf16[128,2048]{1,0:T(8,128)(2,1)S(1)}, u32[]{:S(2)}, u32[]{:S(2)}) collective-permute-start(bf16[128,2048]{1,0:T(8,128)(2,1)S(1)} %get-tuple-element.214), channel_id=1, source_target_pairs={{0,4},{4,0},{1,5},{5,1},{2,6},{6,2},{3,7},{7,3},{8,12},{12,8},{9,1... | collective-permute-start | bytes 1572872 | tf_op jit(solution)/shard_map/ppermute | solution.py:27
  192.8 16.7 %collective-permute-start.15 = (bf16[256,2048]{1,0:T(8,128)(2,1)}, bf16[256,2048]{1,0:T(8,128)(2,1)}, u32[]{:S(2)}, u32[]{:S(2)}) collective-permute-start(bf16[256,2048]{1,0:T(8,128)(2,1)} %get-tuple-element.198), channel_id=1, source_target_pairs={{0,1},{1,0},{2,3},{3,2},{4,5},{5,4},{6,7},{7,6},{8,9},{9,8},{10,11... | collective-permute-start | bytes 3145736 | tf_op jit(solution)/shard_map/ppermute | solution.py:27
  192.9 14.4 %collective-permute-start.21 = (bf16[128,2048]{1,0:T(8,128)(2,1)S(1)}, bf16[128,2048]{1,0:T(8,128)(2,1)S(1)}, u32[]{:S(2)}, u32[]{:S(2)}) collective-permute-start(bf16[128,2048]{1,0:T(8,128)(2,1)S(1)} %get-tuple-element.215), channel_id=1, source_target_pairs={{0,2},{2,0},{1,3},{3,1},{4,6},{6,4},{5,7},{7,5},{8,10},{10,8},{9,1... | collective-permute-start | bytes 1572872 | tf_op jit(solution)/shard_map/ppermute | solution.py:27
  205.6 24.6 %collective-permute-start.19 = (bf16[256,2048]{1,0:T(8,128)(2,1)S(1)}, bf16[256,2048]{1,0:T(8,128)(2,1)}, u32[]{:S(2)}, u32[]{:S(2)}) collective-permute-start(bf16[256,2048]{1,0:T(8,128)(2,1)S(1)} %pad_maximum_fusion.1), channel_id=1, source_target_pairs={{0,2},{2,0},{1,3},{3,1},{4,6},{6,4},{5,7},{7,5},{8,10},{10,8},{9,1... | collective-permute-start | bytes 3145736 | tf_op jit(solution)/shard_map/ppermute | solution.py:27
  207.5 25.1 %collective-permute-start.22 = (bf16[256,2048]{1,0:T(8,128)(2,1)S(1)}, bf16[256,2048]{1,0:T(8,128)(2,1)}, u32[]{:S(2)}, u32[]{:S(2)}) collective-permute-start(bf16[256,2048]{1,0:T(8,128)(2,1)S(1)} %pad_maximum_fusion.2), channel_id=1, source_target_pairs={{0,4},{4,0},{1,5},{5,1},{2,6},{6,2},{3,7},{7,3},{8,12},{12,8},{9,1... | collective-permute-start | bytes 3145736 | tf_op jit(solution)/shard_map/ppermute | solution.py:27
  209.1 337.9 %reduce-scatter.5.cloned.1.call-start = ((), (), s32[]{:S(2)}) async-start(), calls=%async_computation.15 | async-start | bytes 5242880 | tf_op jit(solution)/shard_map/reduce_scatter | solution.py:485
  236.8 24.0 %collective-permute-start.23 = (bf16[256,2048]{1,0:T(8,128)(2,1)S(1)}, bf16[256,2048]{1,0:T(8,128)(2,1)S(1)}, u32[]{:S(2)}, u32[]{:S(2)}) collective-permute-start(bf16[256,2048]{1,0:T(8,128)(2,1)S(1)} %get-tuple-element.174), channel_id=1, source_target_pairs={{0,2},{2,0},{1,3},{3,1},{4,6},{6,4},{5,7},{7,5},{8,10},{10,8},{9,1... | collective-permute-start | bytes 3145736 | tf_op jit(solution)/shard_map/ppermute | solution.py:27
  238.6 24.3 %collective-permute-start.24 = (bf16[256,2048]{1,0:T(8,128)(2,1)S(1)}, bf16[256,2048]{1,0:T(8,128)(2,1)S(1)}, u32[]{:S(2)}, u32[]{:S(2)}) collective-permute-start(bf16[256,2048]{1,0:T(8,128)(2,1)S(1)} %get-tuple-element.174), channel_id=1, source_target_pairs={{0,4},{4,0},{1,5},{5,1},{2,6},{6,2},{3,7},{7,3},{8,12},{12,8},{9,1... | collective-permute-start | bytes 3145736 | tf_op jit(solution)/shard_map/ppermute | solution.py:27
  239.1 36.7 %collective-permute-start.27 = (bf16[256,2048]{1,0:T(8,128)(2,1)S(1)}, bf16[256,2048]{1,0:T(8,128)(2,1)S(1)}, u32[]{:S(2)}, u32[]{:S(2)}) collective-permute-start(bf16[256,2048]{1,0:T(8,128)(2,1)S(1)} %get-tuple-element.174), channel_id=1, source_target_pairs={{0,1},{1,0},{2,3},{3,2},{4,5},{5,4},{6,7},{7,6},{8,9},{9,8},{10,11... | collective-permute-start | bytes 3145736 | tf_op jit(solution)/shard_map/ppermute | solution.py:27
  260.9 12.6 %collective-permute-start.25 = (bf16[128,2048]{1,0:T(8,128)(2,1)S(1)}, bf16[128,2048]{1,0:T(8,128)(2,1)S(1)}, u32[]{:S(2)}, u32[]{:S(2)}) collective-permute-start(bf16[128,2048]{1,0:T(8,128)(2,1)S(1)} %slice.345), channel_id=1, source_target_pairs={{0,4},{4,0},{1,5},{5,1},{2,6},{6,2},{3,7},{7,3},{8,12},{12,8},{9,1... | collective-permute-start | bytes 1572872 | tf_op jit(solution)/shard_map/ppermute | solution.py:27
  262.9 11.2 %collective-permute-start.26 = (bf16[128,2048]{1,0:T(8,128)(2,1)S(1)}, bf16[128,2048]{1,0:T(8,128)(2,1)S(1)}, u32[]{:S(2)}, u32[]{:S(2)}) collective-permute-start(bf16[128,2048]{1,0:T(8,128)(2,1)S(1)} %slice.346), channel_id=1, source_target_pairs={{0,2},{2,0},{1,3},{3,1},{4,6},{6,4},{5,7},{7,5},{8,10},{10,8},{9,1... | collective-permute-start | bytes 1572872 | tf_op jit(solution)/shard_map/ppermute | solution.py:27
  263.3 13.6 %collective-permute-start.28 = (bf16[256,2048]{1,0:T(8,128)(2,1)S(1)}, bf16[256,2048]{1,0:T(8,128)(2,1)S(1)}, u32[]{:S(2)}, u32[]{:S(2)}) collective-permute-start(bf16[256,2048]{1,0:T(8,128)(2,1)S(1)} %collective-permute-done.23), channel_id=1, source_target_pairs={{0,1},{1,0},{2,3},{3,2},{4,5},{5,4},{6,7},{7,6},{8,9},{9,8},{10,11... | collective-permute-start | bytes 3145736 | tf_op jit(solution)/shard_map/ppermute | solution.py:27
  263.3 14.6 %collective-permute-start.29 = (bf16[256,2048]{1,0:T(8,128)(2,1)S(1)}, bf16[256,2048]{1,0:T(8,128)(2,1)S(1)}, u32[]{:S(2)}, u32[]{:S(2)}) collective-permute-start(bf16[256,2048]{1,0:T(8,128)(2,1)S(1)} %collective-permute-done.24), channel_id=1, source_target_pairs={{0,1},{1,0},{2,3},{3,2},{4,5},{5,4},{6,7},{7,6},{8,9},{9,8},{10,11... | collective-permute-start | bytes 3145736 | tf_op jit(solution)/shard_map/ppermute | solution.py:27
  371.2 14.0 %collective-permute-start.35 = (bf16[128,2048]{1,0:T(8,128)(2,1)S(1)}, bf16[128,2048]{1,0:T(8,128)(2,1)S(1)}, u32[]{:S(2)}, u32[]{:S(2)}) collective-permute-start(bf16[128,2048]{1,0:T(8,128)(2,1)S(1)} %get-tuple-element.212), channel_id=1, source_target_pairs={{0,4},{4,0},{1,5},{5,1},{2,6},{6,2},{3,7},{7,3},{8,12},{12,8},{9,1... | collective-permute-start | bytes 1572872 | tf_op jit(solution)/shard_map/ppermute | solution.py:27
  372.8 18.8 %collective-permute-start.32 = (bf16[256,2048]{1,0:T(8,128)(2,1)}, bf16[256,2048]{1,0:T(8,128)(2,1)}, u32[]{:S(2)}, u32[]{:S(2)}) collective-permute-start(bf16[256,2048]{1,0:T(8,128)(2,1)} %get-tuple-element.191), channel_id=1, source_target_pairs={{0,1},{1,0},{2,3},{3,2},{4,5},{5,4},{6,7},{7,6},{8,9},{9,8},{10,11... | collective-permute-start | bytes 3145736 | tf_op jit(solution)/shard_map/ppermute | solution.py:27
  372.8 15.1 %collective-permute-start.38 = (bf16[128,2048]{1,0:T(8,128)(2,1)S(1)}, bf16[128,2048]{1,0:T(8,128)(2,1)S(1)}, u32[]{:S(2)}, u32[]{:S(2)}) collective-permute-start(bf16[128,2048]{1,0:T(8,128)(2,1)S(1)} %get-tuple-element.213), channel_id=1, source_target_pairs={{0,2},{2,0},{1,3},{3,1},{4,6},{6,4},{5,7},{7,5},{8,10},{10,8},{9,1... | collective-permute-start | bytes 1572872 | tf_op jit(solution)/shard_map/ppermute | solution.py:27
  386.4 24.7 %collective-permute-start.36 = (bf16[256,2048]{1,0:T(8,128)(2,1)}, bf16[256,2048]{1,0:T(8,128)(2,1)}, u32[]{:S(2)}, u32[]{:S(2)}) collective-permute-start(bf16[256,2048]{1,0:T(8,128)(2,1)} %pad_maximum_fusion.3), channel_id=1, source_target_pairs={{0,2},{2,0},{1,3},{3,1},{4,6},{6,4},{5,7},{7,5},{8,10},{10,8},{9,1... | collective-permute-start | bytes 3145736 | tf_op jit(solution)/shard_map/ppermute | solution.py:27
  389.1 24.4 %collective-permute-start.39 = (bf16[256,2048]{1,0:T(8,128)(2,1)}, bf16[256,2048]{1,0:T(8,128)(2,1)}, u32[]{:S(2)}, u32[]{:S(2)}) collective-permute-start(bf16[256,2048]{1,0:T(8,128)(2,1)} %pad_maximum_fusion.4), channel_id=1, source_target_pairs={{0,4},{4,0},{1,5},{5,1},{2,6},{6,2},{3,7},{7,3},{8,12},{12,8},{9,1... | collective-permute-start | bytes 3145736 | tf_op jit(solution)/shard_map/ppermute | solution.py:27
  417.9 23.7 %collective-permute-start.40 = (bf16[256,2048]{1,0:T(8,128)(2,1)S(1)}, bf16[256,2048]{1,0:T(8,128)(2,1)S(1)}, u32[]{:S(2)}, u32[]{:S(2)}) collective-permute-start(bf16[256,2048]{1,0:T(8,128)(2,1)S(1)} %get-tuple-element.227), channel_id=1, source_target_pairs={{0,2},{2,0},{1,3},{3,1},{4,6},{6,4},{5,7},{7,5},{8,10},{10,8},{9,1... | collective-permute-start | bytes 3145736 | tf_op jit(solution)/shard_map/ppermute | solution.py:27
  419.4 24.7 %collective-permute-start.41 = (bf16[256,2048]{1,0:T(8,128)(2,1)S(1)}, bf16[256,2048]{1,0:T(8,128)(2,1)S(1)}, u32[]{:S(2)}, u32[]{:S(2)}) collective-permute-start(bf16[256,2048]{1,0:T(8,128)(2,1)S(1)} %get-tuple-element.227), channel_id=1, source_target_pairs={{0,4},{4,0},{1,5},{5,1},{2,6},{6,2},{3,7},{7,3},{8,12},{12,8},{9,1... | collective-permute-start | bytes 3145736 | tf_op jit(solution)/shard_map/ppermute | solution.py:27
  420.0 34.9 %collective-permute-start.44 = (bf16[256,2048]{1,0:T(8,128)(2,1)S(1)}, bf16[256,2048]{1,0:T(8,128)(2,1)S(1)}, u32[]{:S(2)}, u32[]{:S(2)}) collective-permute-start(bf16[256,2048]{1,0:T(8,128)(2,1)S(1)} %get-tuple-element.227), channel_id=1, source_target_pairs={{0,1},{1,0},{2,3},{3,2},{4,5},{5,4},{6,7},{7,6},{8,9},{9,8},{10,11... | collective-permute-start | bytes 3145736 | tf_op jit(solution)/shard_map/ppermute | solution.py:27
  441.6 12.6 %collective-permute-start.42 = (bf16[128,2048]{1,0:T(8,128)(2,1)S(1)}, bf16[128,2048]{1,0:T(8,128)(2,1)S(1)}, u32[]{:S(2)}, u32[]{:S(2)}) collective-permute-start(bf16[128,2048]{1,0:T(8,128)(2,1)S(1)} %slice.362), channel_id=1, source_target_pairs={{0,4},{4,0},{1,5},{5,1},{2,6},{6,2},{3,7},{7,3},{8,12},{12,8},{9,1... | collective-permute-start | bytes 1572872 | tf_op jit(solution)/shard_map/ppermute | solution.py:27
  444.1 10.5 %collective-permute-start.43 = (bf16[128,2048]{1,0:T(8,128)(2,1)S(1)}, bf16[128,2048]{1,0:T(8,128)(2,1)S(1)}, u32[]{:S(2)}, u32[]{:S(2)}) collective-permute-start(bf16[128,2048]{1,0:T(8,128)(2,1)S(1)} %slice.363), channel_id=1, source_target_pairs={{0,2},{2,0},{1,3},{3,1},{4,6},{6,4},{5,7},{7,5},{8,10},{10,8},{9,1... | collective-permute-start | bytes 1572872 | tf_op jit(solution)/shard_map/ppermute | solution.py:27
  444.2 10.8 %collective-permute-start.45 = (bf16[256,2048]{1,0:T(8,128)(2,1)S(1)}, bf16[256,2048]{1,0:T(8,128)(2,1)S(1)}, u32[]{:S(2)}, u32[]{:S(2)}) collective-permute-start(bf16[256,2048]{1,0:T(8,128)(2,1)S(1)} %collective-permute-done.40), channel_id=1, source_target_pairs={{0,1},{1,0},{2,3},{3,2},{4,5},{5,4},{6,7},{7,6},{8,9},{9,8},{10,11... | collective-permute-start | bytes 3145736 | tf_op jit(solution)/shard_map/ppermute | solution.py:27
  444.3 10.8 %collective-permute-start.46 = (bf16[256,2048]{1,0:T(8,128)(2,1)S(1)}, bf16[256,2048]{1,0:T(8,128)(2,1)S(1)}, u32[]{:S(2)}, u32[]{:S(2)}) collective-permute-start(bf16[256,2048]{1,0:T(8,128)(2,1)S(1)} %collective-permute-done.41), channel_id=1, source_target_pairs={{0,1},{1,0},{2,3},{3,2},{4,5},{5,4},{6,7},{7,6},{8,9},{9,8},{10,11... | collective-permute-start | bytes 3145736 | tf_op jit(solution)/shard_map/ppermute | solution.py:27
  471.3 242.2 %reduce-scatter.7.cloned.1.call-start = ((), (), s32[]{:S(2)}) async-start(), calls=%async_computation.16 | async-start | bytes 10485760 | tf_op jit(solution)/shard_map/reduce_scatter | solution.py:485
  547.1 260.3 %reduce-scatter.9.cloned.1.call-start = ((), (), s32[]{:S(2)}) async-start(), calls=%async_computation.17 | async-start | bytes 3932160 | tf_op jit(solution)/shard_map/reduce_scatter | solution.py:485
  548.1 14.0 %collective-permute-start.52 = (bf16[128,2048]{1,0:T(8,128)(2,1)S(1)}, bf16[128,2048]{1,0:T(8,128)(2,1)S(1)}, u32[]{:S(2)}, u32[]{:S(2)}) collective-permute-start(bf16[128,2048]{1,0:T(8,128)(2,1)S(1)} %copy-done.25), channel_id=1, source_target_pairs={{0,2},{2,0},{1,3},{3,1},{4,6},{6,4},{5,7},{7,5},{8,10},{10,8},{9,1... | collective-permute-start | bytes 1572872 | tf_op jit(solution)/shard_map/ppermute | solution.py:27
  549.0 13.7 %collective-permute-start.53 = (bf16[128,2048]{1,0:T(8,128)(2,1)S(1)}, bf16[128,2048]{1,0:T(8,128)(2,1)S(1)}, u32[]{:S(2)}, u32[]{:S(2)}) collective-permute-start(bf16[128,2048]{1,0:T(8,128)(2,1)S(1)} %copy-done.24), channel_id=1, source_target_pairs={{0,4},{4,0},{1,5},{5,1},{2,6},{6,2},{3,7},{7,3},{8,12},{12,8},{9,1... | collective-permute-start | bytes 1572872 | tf_op jit(solution)/shard_map/ppermute | solution.py:27
  550.1 16.0 %collective-permute-start.49 = (bf16[256,2048]{1,0:T(8,128)(2,1)}, bf16[256,2048]{1,0:T(8,128)(2,1)S(1)}, u32[]{:S(2)}, u32[]{:S(2)}) collective-permute-start(bf16[256,2048]{1,0:T(8,128)(2,1)} %get-tuple-element.184), channel_id=1, source_target_pairs={{0,1},{1,0},{2,3},{3,2},{4,5},{5,4},{6,7},{7,6},{8,9},{9,8},{10,11... | collective-permute-start | bytes 3145736 | tf_op jit(solution)/shard_map/ppermute | solution.py:27
  564.2 24.2 %collective-permute-start.54 = (bf16[256,2048]{1,0:T(8,128)(2,1)S(1)}, bf16[256,2048]{1,0:T(8,128)(2,1)S(1)}, u32[]{:S(2)}, u32[]{:S(2)}) collective-permute-start(bf16[256,2048]{1,0:T(8,128)(2,1)S(1)} %pad_maximum_fusion.5), channel_id=1, source_target_pairs={{0,2},{2,0},{1,3},{3,1},{4,6},{6,4},{5,7},{7,5},{8,10},{10,8},{9,1... | collective-permute-start | bytes 3145736 | tf_op jit(solution)/shard_map/ppermute | solution.py:27
  565.6 23.9 %collective-permute-start.56 = (bf16[256,2048]{1,0:T(8,128)(2,1)S(1)}, bf16[256,2048]{1,0:T(8,128)(2,1)S(1)}, u32[]{:S(2)}, u32[]{:S(2)}) collective-permute-start(bf16[256,2048]{1,0:T(8,128)(2,1)S(1)} %pad_maximum_fusion.6), channel_id=1, source_target_pairs={{0,4},{4,0},{1,5},{5,1},{2,6},{6,2},{3,7},{7,3},{8,12},{12,8},{9,1... | collective-permute-start | bytes 3145736 | tf_op jit(solution)/shard_map/ppermute | solution.py:27
  595.0 23.1 %collective-permute-start.57 = (bf16[256,2048]{1,0:T(8,128)(2,1)S(1)}, bf16[256,2048]{1,0:T(8,128)(2,1)S(1)}, u32[]{:S(2)}, u32[]{:S(2)}) collective-permute-start(bf16[256,2048]{1,0:T(8,128)(2,1)S(1)} %get-tuple-element.169), channel_id=1, source_target_pairs={{0,2},{2,0},{1,3},{3,1},{4,6},{6,4},{5,7},{7,5},{8,10},{10,8},{9,1... | collective-permute-start | bytes 3145736 | tf_op jit(solution)/shard_map/ppermute | solution.py:27
  596.0 23.5 %collective-permute-start.58 = (bf16[256,2048]{1,0:T(8,128)(2,1)S(1)}, bf16[256,2048]{1,0:T(8,128)(2,1)S(1)}, u32[]{:S(2)}, u32[]{:S(2)}) collective-permute-start(bf16[256,2048]{1,0:T(8,128)(2,1)S(1)} %get-tuple-element.169), channel_id=1, source_target_pairs={{0,4},{4,0},{1,5},{5,1},{2,6},{6,2},{3,7},{7,3},{8,12},{12,8},{9,1... | collective-permute-start | bytes 3145736 | tf_op jit(solution)/shard_map/ppermute | solution.py:27
  597.1 33.5 %collective-permute-start.61 = (bf16[256,2048]{1,0:T(8,128)(2,1)S(1)}, bf16[256,2048]{1,0:T(8,128)(2,1)S(1)}, u32[]{:S(2)}, u32[]{:S(2)}) collective-permute-start(bf16[256,2048]{1,0:T(8,128)(2,1)S(1)} %get-tuple-element.169), channel_id=1, source_target_pairs={{0,1},{1,0},{2,3},{3,2},{4,5},{5,4},{6,7},{7,6},{8,9},{9,8},{10,11... | collective-permute-start | bytes 3145736 | tf_op jit(solution)/shard_map/ppermute | solution.py:27
  618.1 11.9 %collective-permute-start.59 = (bf16[128,2048]{1,0:T(8,128)(2,1)S(1)}, bf16[128,2048]{1,0:T(8,128)(2,1)S(1)}, u32[]{:S(2)}, u32[]{:S(2)}) collective-permute-start(bf16[128,2048]{1,0:T(8,128)(2,1)S(1)} %slice.370), channel_id=1, source_target_pairs={{0,4},{4,0},{1,5},{5,1},{2,6},{6,2},{3,7},{7,3},{8,12},{12,8},{9,1... | collective-permute-start | bytes 1572872 | tf_op jit(solution)/shard_map/ppermute | solution.py:27
  619.6 10.7 %collective-permute-start.60 = (bf16[128,2048]{1,0:T(8,128)(2,1)S(1)}, bf16[128,2048]{1,0:T(8,128)(2,1)S(1)}, u32[]{:S(2)}, u32[]{:S(2)}) collective-permute-start(bf16[128,2048]{1,0:T(8,128)(2,1)S(1)} %slice.371), channel_id=1, source_target_pairs={{0,2},{2,0},{1,3},{3,1},{4,6},{6,4},{5,7},{7,5},{8,10},{10,8},{9,1... | collective-permute-start | bytes 1572872 | tf_op jit(solution)/shard_map/ppermute | solution.py:27
  620.8 10.0 %collective-permute-start.62 = (bf16[256,2048]{1,0:T(8,128)(2,1)S(1)}, bf16[256,2048]{1,0:T(8,128)(2,1)S(1)}, u32[]{:S(2)}, u32[]{:S(2)}) collective-permute-start(bf16[256,2048]{1,0:T(8,128)(2,1)S(1)} %collective-permute-done.57), channel_id=1, source_target_pairs={{0,1},{1,0},{2,3},{3,2},{4,5},{5,4},{6,7},{7,6},{8,9},{9,8},{10,11... | collective-permute-start | bytes 3145736 | tf_op jit(solution)/shard_map/ppermute | solution.py:27
  620.8 10.1 %collective-permute-start.63 = (bf16[256,2048]{1,0:T(8,128)(2,1)S(1)}, bf16[256,2048]{1,0:T(8,128)(2,1)S(1)}, u32[]{:S(2)}, u32[]{:S(2)}) collective-permute-start(bf16[256,2048]{1,0:T(8,128)(2,1)S(1)} %collective-permute-done.58), channel_id=1, source_target_pairs={{0,1},{1,0},{2,3},{3,2},{4,5},{5,4},{6,7},{7,6},{8,9},{9,8},{10,11... | collective-permute-start | bytes 3145736 | tf_op jit(solution)/shard_map/ppermute | solution.py:27
  713.6 14.3 %collective-permute-start.72 = (bf16[128,2048]{1,0:T(8,128)(2,1)}, bf16[128,2048]{1,0:T(8,128)(2,1)S(1)}, u32[]{:S(2)}, u32[]{:S(2)}) collective-permute-start(bf16[128,2048]{1,0:T(8,128)(2,1)} %get-tuple-element.209), channel_id=1, source_target_pairs={{0,2},{2,0},{1,3},{3,1},{4,6},{6,4},{5,7},{7,5},{8,10},{10,8},{9,1... | collective-permute-start | bytes 1572872 | tf_op jit(solution)/shard_map/ppermute | solution.py:27
  714.5 13.9 %collective-permute-start.73 = (bf16[128,2048]{1,0:T(8,128)(2,1)}, bf16[128,2048]{1,0:T(8,128)(2,1)S(1)}, u32[]{:S(2)}, u32[]{:S(2)}) collective-permute-start(bf16[128,2048]{1,0:T(8,128)(2,1)} %get-tuple-element.208), channel_id=1, source_target_pairs={{0,4},{4,0},{1,5},{5,1},{2,6},{6,2},{3,7},{7,3},{8,12},{12,8},{9,1... | collective-permute-start | bytes 1572872 | tf_op jit(solution)/shard_map/ppermute | solution.py:27
  715.6 22.5 %collective-permute-start.69 = (bf16[256,2048]{1,0:T(8,128)(2,1)}, bf16[256,2048]{1,0:T(8,128)(2,1)}, u32[]{:S(2)}, u32[]{:S(2)}) collective-permute-start(bf16[256,2048]{1,0:T(8,128)(2,1)} %get-tuple-element.177), channel_id=1, source_target_pairs={{0,1},{1,0},{2,3},{3,2},{4,5},{5,4},{6,7},{7,6},{8,9},{9,8},{10,11... | collective-permute-start | bytes 3145736 | tf_op jit(solution)/shard_map/ppermute | solution.py:27
  730.9 24.8 %collective-permute-start.74 = (bf16[256,2048]{1,0:T(8,128)(2,1)}, bf16[256,2048]{1,0:T(8,128)(2,1)}, u32[]{:S(2)}, u32[]{:S(2)}) collective-permute-start(bf16[256,2048]{1,0:T(8,128)(2,1)} %pad_maximum_fusion.7), channel_id=1, source_target_pairs={{0,2},{2,0},{1,3},{3,1},{4,6},{6,4},{5,7},{7,5},{8,10},{10,8},{9,1... | collective-permute-start | bytes 3145736 | tf_op jit(solution)/shard_map/ppermute | solution.py:27
  733.3 24.5 %collective-permute-start.76 = (bf16[256,2048]{1,0:T(8,128)(2,1)}, bf16[256,2048]{1,0:T(8,128)(2,1)}, u32[]{:S(2)}, u32[]{:S(2)}) collective-permute-start(bf16[256,2048]{1,0:T(8,128)(2,1)} %pad_maximum_fusion.8), channel_id=1, source_target_pairs={{0,4},{4,0},{1,5},{5,1},{2,6},{6,2},{3,7},{7,3},{8,12},{12,8},{9,1... | collective-permute-start | bytes 3145736 | tf_op jit(solution)/shard_map/ppermute | solution.py:27
  735.2 27.8 %all-to-all-start.7 = ((f32[32,1,256]{2,1,0:T(1,128)}), f32[32,1,256]{2,1,0:T(1,128)S(1)}, u32[]{:S(2)}, u32[]{:S(2)}) async-start(f32[32,1,256]{2,1,0:T(1,128)} %reshape.269), calls=%async_computation.11 | async-start | bytes 65536 | tf_op jit(solution)/shard_map/all_to_all | solution.py:549
  763.0 44.3 %all-to-all-start.5 = ((bf16[2,128,2048]{2,0,1:T(2,128)(2,1)}), bf16[2,128,2048]{2,0,1:T(2,128)(2,1)S(1)}, u32[]{:S(2)}, u32[]{:S(2)}) async-start(bf16[2,128,2048]{2,0,1:T(2,128)(2,1)} %copy.138), calls=%async_computation.6 | async-start | bytes 2097152 | tf_op jit(solution)/shard_map/all_to_all | solution.py:520
  765.7 46.4 %reduce-scatter.11.cloned.1.call-start = ((), (), s32[]{:S(2)}) async-start(), calls=%async_computation.18 | async-start | bytes 1310720 | tf_op jit(solution)/shard_map/reduce_scatter | solution.py:485
  807.3 18.5 %all-to-all-start.6 = ((bf16[8,64,768]{2,1,0:T(8,128)(2,1)}), bf16[8,64,768]{2,1,0:T(8,128)(2,1)}, u32[]{:S(2)}, u32[]{:S(2)}) async-start(bf16[8,64,768]{2,1,0:T(8,128)(2,1)} %bitcast.120), calls=%async_computation.9 | async-start | bytes 1572864 | tf_op jit(solution)/shard_map/all_to_all | solution.py:531
  (68 other events, 820.9 us)
Sparse Core Ops, SparseCore 0:
  38.6 80.0 all-gather.3
  120.8 148.7 all-gather.5
  271.1 78.9 all-gather.7
  471.5 74.2 reduce-scatter.4
  548.1 144.9 reduce-scatter.6
  713.7 58.1 reduce-scatter.8
  774.3 37.0 reduce-scatter.10

commit v5 on v4

--- a/solution.py
+++ b/solution.py
@@ -161,7 +161,7 @@
             dots_ref[kind : kind + 1, rows] = row_sums(dots[kind])
 
 
-def finish_kernel(heads, parts, length, raw_ref, inv_ref, means_ref, scaled_ref, value_ref, out_ref):
+def finish_kernel(heads, parts, length, raw_ref, inv_ref, means_ref, scaled_ref, value_ref, weight_ref, out_ref, input_ref):
     width = value_ref.shape[1]
     for part in range(parts):
         rows = slice(part * length, (part + 1) * length)
@@ -172,6 +172,7 @@
             normed = raw_ref[rows, columns] * inverse
             out_ref[rows, columns] = (inverse * (scaled_ref[rows, columns] - normed * mean)).astype(BF)
         out_ref[rows, 2 * width :] = value_ref[rows, :]
+    input_ref[...] = matmul(out_ref[...], weight_ref[...], 1, 1).astype(BF)
 
 
 def block_specs(block, heads, dim, length):
@@ -223,7 +224,7 @@
     )(raw, inverses, gains, *tables, grad)
 
 
-def finish(raw, inverses, means, scaled, value, length, heads):
+def finish(raw, inverses, means, scaled, value, length, heads, weight):
     wide, own = value.shape
     block = 2 * length
     rows = lambda columns: pl.BlockSpec((block, columns), lambda i: (i, 0))
@@ -231,12 +232,14 @@
     return pl.pallas_call(
         lambda *refs: finish_kernel(heads, 2, length, *refs),
         grid=(wide // block,),
-        in_specs=[rows(3 * own), lanes, lanes, rows(2 * own), rows(own)],
-        out_specs=rows(3 * own),
-        out_shape=jax.ShapeDtypeStruct((wide, 3 * own), BF),
-        cost_estimate=pl.CostEstimate(flops=8 * wide * own, bytes_accessed=28 * wide * own, transcendentals=0),
+        in_specs=[rows(3 * own), lanes, lanes, rows(2 * own), rows(own), pl.BlockSpec(weight.shape, lambda i: (0, 0))],
+        out_specs=[rows(3 * own), rows(weight.shape[0])],
+        out_shape=[jax.ShapeDtypeStruct((wide, 3 * own), BF), jax.ShapeDtypeStruct((wide, weight.shape[0]), BF)],
+        cost_estimate=pl.CostEstimate(
+            flops=2 * wide * weight.size, bytes_accessed=28 * wide * own + 2 * wide * weight.shape[0], transcendentals=0
+        ),
         name="finish",
-    )(raw, inverses, means, scaled, value)
+    )(raw, inverses, means, scaled, value, weight)
 
 
 def after(value, *earlier):
@@ -255,7 +258,7 @@
     return jnp.concatenate(pieces + [swap(piece, "c") for piece in pieces], axis=0), over_x, done
 
 
-def group_scatter(partial, meanwhile=None, until=()):
+def group_scatter(partial, meanwhile=None):
     wide = partial.shape[0] // 2
     rows = wide // 4
     half = rows // 2
@@ -273,7 +276,7 @@
     done = None
     if meanwhile is not None:
         done = meanwhile(far_low)
-        far_x, far_y = lax.optimization_barrier((far_x, far_y, done) + until)[:2]
+        far_x, far_y, done = lax.optimization_barrier((far_x, far_y, done))
     over_y = jnp.concatenate([over_y[:half] + far_x.astype(F32), over_y[half:]])
     over_x = jnp.concatenate([over_x[:half], over_x[half:] + far_y.astype(F32)])
     return own + move(over_x, "x") + move(over_y, "y"), done
@@ -355,6 +358,16 @@
     for ahead in range(1, LINE):
         moved = lax.ppermute(block, "z", ring(ahead))
         out = lax.dynamic_update_index_in_dim(out, moved, (at - ahead) % LINE, 0)
+    return out
+
+
+def group_exchange(blocks, place):
+    out = jnp.zeros_like(blocks)
+    out = lax.dynamic_update_index_in_dim(out, lax.dynamic_index_in_dim(blocks, place, 0), place, 0)
+    for apart in range(1, PLANE):
+        block = lax.dynamic_index_in_dim(blocks, place ^ apart, 0)
+        moved = lax.ppermute(block, GROUP, [(i, i ^ apart) for i in range(PLANE)])
+        out = lax.dynamic_update_index_in_dim(out, moved, place ^ apart, 0)
     return out
 
 
@@ -478,14 +491,14 @@
 
     def weight_term(left, right):
         return lambda token: lax.dot_general(
-            after(left, token), right, contract_rows, preferred_element_type=F32
+            after(left, *(token if isinstance(token, tuple) else (token,))), right, contract_rows, preferred_element_type=F32
         ).astype(BF)
 
     def owners(term):
         return lax.psum_scatter(term, REST, scatter_dimension=0, tiled=True)
 
     down_part = owners(down_term)
-    moved, unit_term = group_scatter(hidden_term, weight_term(grad_units, hidden_wide), (down_part,))
+    moved, unit_term = group_scatter(hidden_term, weight_term(grad_units, hidden_wide))
     grad_hidden = grad_out + moved
     unit_part = owners(after(unit_term, down_part))
 
@@ -511,11 +524,10 @@
     scaled, grad_value, dots, gain_term = attend_back(qkv_raw, inverses, gain_heads, tables, own_heads, grad_att)
     scaled = after(scaled, output_term)
     means = group_total(dots) * (1.0 / width)
-    grad_qkv = finish(qkv_raw, inverses, means, scaled, grad_value, seq_len, own_heads)
-
-    grad_input = lax.dot_general(grad_qkv, w_qkv, contract_last, preferred_element_type=F32)
-    grad_input = after(grad_input.astype(BF), output_term)
-    moved, qkv_term = group_scatter(grad_input, weight_term(x_wide, grad_qkv))
+    grad_qkv, grad_input = finish(qkv_raw, inverses, means, scaled, grad_value, seq_len, own_heads, w_qkv)
+
+    qkv_term = weight_term(x_wide, grad_qkv)((output_term,))
+    moved, _ = group_scatter(after(grad_input, qkv_term))
     grad_input = grad_hidden + moved
     returned = lax.all_to_all(
         grad_input.astype(BF).reshape(micro_count, seq_len, width),
@@ -527,10 +539,9 @@
     input_grad = jnp.zeros_like(tokens).at[dealing].set(returned)
 
     qkv_rows = owners(after(qkv_term, unit_part))
-    output_part = owners(after(output_term.reshape(groups * shard, width), qkv_term))
-    qkv_back = lax.all_to_all(
-        qkv_rows.reshape(PLANE, shard, 3 * own_width), GROUP, split_axis=0, concat_axis=0, tiled=True
-    )
+    qkv_back = group_exchange(qkv_rows.reshape(PLANE, shard, 3 * own_width), place)
+
+    output_part = owners(after(output_term.reshape(groups * shard, width), qkv_back))
 
     def heads_in(columns):
         split = columns.reshape(fan, spread, shard, own_heads, head_dim)

time: 848 us -> 835 us (0.985)
  waiting for transfers between devices: 414 us -> 393 us
  matrix products: 74.4 us -> 65.9 us
    all_to_all x1, waiting for transfers between devices: 38 us -> 5.67 us  [per_device(): lax.all_to_all(grad_input.astype(BF).reshape(micro_count, seq_len, width)...]
    reduce_scatter x4, waiting for transfers between devices: 0.01 us -> 28.4 us  [owners(): return lax.psum_scatter(term, REST, scatter_dimension=0, tiled=True)]
    ppermute x74, waiting for transfers between devices: 274 us -> 246 us  [swap(): return lax.ppermute(value, axis, SWAP)]
    ppermute x0 -> x7, waiting for transfers between devices: none -> 11.1 us  [group_exchange(): moved = lax.ppermute(block, GROUP, [(i, i ^ apart) for i in range(PLANE)])]
    dot_general x3 -> x2, matrix products: 42 us -> 33.5 us  [weight_term(): lax.dot_general(after(left, *(token if isinstance(token, tuple) else (tok...]
  transfers between devices with their start and end apart: 90 -> 96, of which waited for: 54 -> 52; matrix products, arithmetic and copies ran while one was open for 19% -> 19% of each run, Pallas kernels for 14% -> 15%
where the time goes in v5:
time: 835 us; the launch traced here: 827 us
  waiting for transfers between devices  393 us (47%)
  Pallas kernels  125 us (15%)
  starting transfers between devices  84.9 us (10%)
  local copies, waits for them, and re-layouts  82.7 us (10%)
  matrix products  65.9 us (8%)
  other arithmetic  49.8 us (6%)
  between operations  16 us (2%)
  blocking collectives  9.84 us (1%)
    ppermute x74, waiting for transfers between devices, swap(): return lax.ppermute(value, axis, SWAP)  246 us
    ppermute x74, starting transfers between devices, swap(): return lax.ppermute(value, axis, SWAP)  51.7 us
    all_gather x1, waiting for transfers between devices, per_device(): down = lax.all_gather(after(w_down, qkv_in), REST, axis=0, tiled=True)  45.1 us
    all_to_all x1, waiting for transfers between devices, per_device(): lax.all_to_all(outgoing, ALL, split_axis=0, concat_axis=1, tiled=True)  43.6 us
    pallas_call x1, Pallas kernels, gated_back(): pl.pallas_call(lambda *refs: gated_back_kernel(groups, *refs), grid=(wide...  37.7 us
    unnamed x126, local copies, waits for them, and re-layouts  36.5 us
    dot_general x2, matrix products, weight_term(): lax.dot_general(after(left, *(token if isinstance(token, tuple) else (tok...  33.5 us
    reduce_scatter x4, waiting for transfers between devices, owners(): return lax.psum_scatter(term, REST, scatter_dimension=0, tiled=True)  28.4 us
  transfers between devices with their start and end apart: 96, of which 52 were waited for; matrix products, arithmetic and copies ran while one was open for 19% of the time, Pallas kernels for 15%

profile of v5, /device:TPU:0, one launch (start us, length us, event | category | flops | bytes accessed | tf_op | source)
XLA Modules:
  0.0 827.1 jit_solution(17947207074268932931)
XLA Ops:
  7.2 3.1 collective-permute-start.9
  10.3 2.6 collective-permute-start.10
  21.2 3.7 all-to-all-start.1
  25.3 5.0 collective-permute-done.10
  30.3 7.3 all-to-all-done.1
  38.4 2.7 all-to-all-start
  42.7 2.3 copy.128
  45.0 2.8 pad_maximum_fusion
  47.8 43.6 %all-to-all-done = bf16[64,4,2048]{2,1,0:T(4,128)(2,1)S(1)} async-done(((bf16[64,4,2048]{2,1,0:T(4,128)(2,1)}), bf16[64,4,2048]{2,1,0:T(4,128)(2,1)S(1)}, u32[]{:S(2)}, u32[]{:S(2)}) %all-to-all-start) | async-done | bytes 1048608 | tf_op jit(solution)/shard_map/all_to_all | solution.py:425
  96.2 4.5 all-to-all-start.2
  101.1 15.4 %collective-permute-done = bf16[256,2048]{1,0:T(8,128)(2,1)} collective-permute-done((bf16[256,2048]{1,0:T(8,128)(2,1)S(1)}, bf16[256,2048]{1,0:T(8,128)(2,1)}, u32[]{:S(2)}, u32[]{:S(2)}) %collective-permute-start) | collective-permute-done | bytes 1048608 | tf_op jit(solution)/shard_map/ppermute | solution.py:27
  122.5 2.4 constant_dynamic-update-slice_fusion.8
  125.9 3.5 collective-permute-done.2
  137.2 13.0 %project.1 = (f32[2048,768]{1,0:T(8,128)}, f32[2,2048]{1,0:T(2,128)}) custom-call(bf16[2048,2048]{1,0:T(8,128)(2,1)} %constant_dynamic-update-slice_fusion.refs_0_, bf16[2048,768]{1,0:T(8,128)(2,1)} %bitcast.121), custom_call_target="tpu_custom_call" | custom-call | flops 6442450944 | bytes 17825792 | tf_op jit(solution)/shard_map/project/pallas_call | solution.py:78
  157.8 5.1 all_to_all.81
  163.7 15.3 %attend.1 = bf16[2048,256]{1,0:T(8,128)(2,1)} custom-call(f32[2048,768]{1,0:T(8,128)} %get-tuple-element.47.refs_0_, f32[2,2048]{1,0:T(2,128)} %rsqrt.22.refs_1_, f32[2,256]{1,0:T(2,128)} %bitcast.113, f32[128,128]{1,0:T(8,128)} %get-tuple-element.238.refs_3_, f32[128,128]{1,0:T(8,128)} %get-tuple-element.239.refs_4_), custom_call_target="tpu_custom_call" | custom-call | flops 268435456 | bytes 7340032 | tf_op jit(solution)/shard_map/attend/pallas_call | solution.py:191
  179.0 3.6 convolution_convert_fusion.2
  194.9 10.6 %collective-permute-done.18 = bf16[128,2048]{1,0:T(8,128)(2,1)S(1)} collective-permute-done((bf16[128,2048]{1,0:T(8,128)(2,1)S(1)}, bf16[128,2048]{1,0:T(8,128)(2,1)S(1)}, u32[]{:S(2)}, u32[]{:S(2)}) %collective-permute-start.18) | collective-permute-done | bytes 524320 | tf_op jit(solution)/shard_map/ppermute | solution.py:27
  209.6 20.7 %collective-permute-done.19 = bf16[256,2048]{1,0:T(8,128)(2,1)} collective-permute-done((bf16[256,2048]{1,0:T(8,128)(2,1)S(1)}, bf16[256,2048]{1,0:T(8,128)(2,1)}, u32[]{:S(2)}, u32[]{:S(2)}) %collective-permute-start.19) | collective-permute-done | bytes 1048608 | tf_op jit(solution)/shard_map/ppermute | solution.py:27
  230.3 2.3 collective-permute-done.22
  232.7 2.9 multiply_reduce_fusion.3
  239.1 21.8 %collective-permute-done.23 = bf16[256,2048]{1,0:T(8,128)(2,1)S(1)} collective-permute-done((bf16[256,2048]{1,0:T(8,128)(2,1)S(1)}, bf16[256,2048]{1,0:T(8,128)(2,1)S(1)}, u32[]{:S(2)}, u32[]{:S(2)}) %collective-permute-start.23) | collective-permute-done | bytes 1048608 | tf_op jit(solution)/shard_map/ppermute | solution.py:27
  266.0 7.6 collective-permute-done.25
  280.7 24.3 %gated.1 = (f32[2048,2048]{1,0:T(8,128)}, bf16[2048,1024]{1,0:T(8,128)(2,1)}) custom-call(bf16[2048,2048]{1,0:T(8,128)(2,1)} %constant_dynamic-update-slice_fusion.10.refs_0_, bf16[2048,2048]{1,0:T(8,128)(2,1)} %all-gather.6.cloned.1.call-done.refs_1_.refs_3_), custom_call_target="tpu_custom_call" | custom-call | flops 17179869184 | bytes 37748736 | tf_op jit(solution)/shard_map/gated/pallas_call | solution.py:300
  305.0 45.1 %all-gather.8.cloned.1.call-done.refs_1_ = bf16[1024,2048]{1,0:T(8,128)(2,1)} async-done(((bf16[256,2048]{1,0:T(8,128)(2,1)}), bf16[1024,2048]{1,0:T(8,128)(2,1)}) %all-gather.8.cloned.1.call-update) | async-done | bytes 4194320 | tf_op jit(solution)/shard_map/all_gather | solution.py:455
  350.1 12.1 %convolution_convert_fusion.1 = bf16[2048,2048]{1,0:T(8,128)(2,1)S(1)} fusion(bf16[2048,1024]{1,0:T(8,128)(2,1)} %get-tuple-element.50, bf16[1024,2048]{1,0:T(8,128)(2,1)} %all-gather.8.cloned.1.call-done.refs_1_), kind=kOutput, calls=%fused_computation.4 | convolution fusion | flops 8594128896 | bytes 16777216 | tf_op jit(solution)/shard_map/dot_general | solution.py:474
  364.7 2.1 collective-permute-done.33
  374.4 10.8 %collective-permute-done.35 = bf16[128,2048]{1,0:T(8,128)(2,1)S(1)} collective-permute-done((bf16[128,2048]{1,0:T(8,128)(2,1)S(1)}, bf16[128,2048]{1,0:T(8,128)(2,1)S(1)}, u32[]{:S(2)}, u32[]{:S(2)}) %collective-permute-start.35) | collective-permute-done | bytes 524320 | tf_op jit(solution)/shard_map/ppermute | solution.py:27
  391.5 19.6 %collective-permute-done.36 = bf16[256,2048]{1,0:T(8,128)(2,1)} collective-permute-done((bf16[256,2048]{1,0:T(8,128)(2,1)}, bf16[256,2048]{1,0:T(8,128)(2,1)}, u32[]{:S(2)}, u32[]{:S(2)}) %collective-permute-start.36) | collective-permute-done | bytes 1048608 | tf_op jit(solution)/shard_map/ppermute | solution.py:27
  411.1 2.4 collective-permute-done.39
  413.5 2.9 multiply_reduce_fusion.2
  420.0 21.6 %collective-permute-done.40 = bf16[256,2048]{1,0:T(8,128)(2,1)S(1)} collective-permute-done((bf16[256,2048]{1,0:T(8,128)(2,1)S(1)}, bf16[256,2048]{1,0:T(8,128)(2,1)S(1)}, u32[]{:S(2)}, u32[]{:S(2)}) %collective-permute-start.40) | collective-permute-done | bytes 1048608 | tf_op jit(solution)/shard_map/ppermute | solution.py:27
  444.9 9.4 %collective-permute-done.42 = bf16[128,2048]{1,0:T(8,128)(2,1)S(1)} collective-permute-done((bf16[128,2048]{1,0:T(8,128)(2,1)S(1)}, bf16[128,2048]{1,0:T(8,128)(2,1)S(1)}, u32[]{:S(2)}, u32[]{:S(2)}) %collective-permute-start.42) | collective-permute-done | bytes 524320 | tf_op jit(solution)/shard_map/ppermute | solution.py:27
  457.0 3.3 copy-done.30
  460.3 11.0 %convolution_convert_fusion.3 = bf16[1024,2048]{1,0:T(8,128)(2,1)} fusion(bf16[2048,1024]{1,0:T(8,128)(2,1)S(1)} %copy-done.39, bf16[2048,2048]{1,0:T(8,128)(2,1)S(1)} %constant_dynamic-update-slice_fusion.20.refs_0_), kind=kOutput, calls=%fused_computation.6 | convolution fusion | flops 8592031744 | bytes 16777216 | tf_op jit(solution)/shard_map/dot_general | solution.py:487
  471.4 37.7 %gated_back.1 = (bf16[2048,2048]{1,0:T(8,128)(2,1)}, bf16[2048,2048]{1,0:T(8,128)(2,1)}) custom-call(bf16[2048,2048]{1,0:T(8,128)(2,1)} %copy-done.30, bf16[1024,2048]{1,0:T(8,128)(2,1)} %all-gather.8.cloned.1.call-done.refs_1_, f32[2048,2048]{1,0:T(8,128)} %get-tuple-element.53.refs_2_, bf16[2048,2048]{1,0:T(8,128)(2,1)} %all-gather.6.cloned.1.call-done.refs_1_.refs_3_), custom_call_target="tpu_custom_call" | custom-call | flops 25769803776 | bytes 54525952 | tf_op jit(solution)/shard_map/gated_back/pallas_call | solution.py:336
  509.1 3.9 fusion.26
  518.7 5.1 convert_add_fusion.3
  526.9 22.1 %convolution_convert_fusion = bf16[2048,2048]{1,0:T(8,128)(2,1)} fusion(bf16[2048,2048]{1,0:T(8,128)(2,1)S(1)} %bitcast.124, bf16[2048,2048]{1,0:T(8,128)(2,1)} %constant_dynamic-update-slice_fusion.10.refs_0_), kind=kOutput, calls=%fused_computation.3 | convolution fusion | flops 17184063488 | bytes 25165824 | tf_op jit(solution)/shard_map/dot_general | solution.py:493
  556.5 23.2 %collective-permute-done.54 = bf16[256,2048]{1,0:T(8,128)(2,1)S(1)} collective-permute-done((bf16[256,2048]{1,0:T(8,128)(2,1)S(1)}, bf16[256,2048]{1,0:T(8,128)(2,1)S(1)}, u32[]{:S(2)}, u32[]{:S(2)}) %collective-permute-start.54) | collective-permute-done | bytes 1048608 | tf_op jit(solution)/shard_map/ppermute | solution.py:27
  580.0 4.2 multiply_reduce_fusion
  588.2 22.0 %collective-permute-done.57 = bf16[256,2048]{1,0:T(8,128)(2,1)S(1)} collective-permute-done((bf16[256,2048]{1,0:T(8,128)(2,1)S(1)}, bf16[256,2048]{1,0:T(8,128)(2,1)S(1)}, u32[]{:S(2)}, u32[]{:S(2)}) %collective-permute-start.57) | collective-permute-done | bytes 1048608 | tf_op jit(solution)/shard_map/ppermute | solution.py:27
  613.7 9.1 %collective-permute-done.59 = bf16[128,2048]{1,0:T(8,128)(2,1)S(1)} collective-permute-done((bf16[128,2048]{1,0:T(8,128)(2,1)S(1)}, bf16[128,2048]{1,0:T(8,128)(2,1)S(1)}, u32[]{:S(2)}, u32[]{:S(2)}) %collective-permute-start.59) | collective-permute-done | bytes 524320 | tf_op jit(solution)/shard_map/ppermute | solution.py:27
  626.3 2.3 convolution_convert_fusion.6
  628.6 3.4 convolution_convert_fusion.5.refs_5_
  632.0 20.6 %attend_back.1 = (f32[2048,512]{1,0:T(8,128)}, bf16[2048,256]{1,0:T(8,128)(2,1)}, f32[2,2048]{1,0:T(2,128)}, f32[2,256]{1,0:T(2,128)}) custom-call(f32[2048,768]{1,0:T(8,128)} %get-tuple-element.47.refs_0_, f32[2,2048]{1,0:T(2,128)} %rsqrt.22.refs_1_, f32[2,256]{1,0:T(2,128)} %bitcast.114, f32[128,128]{1,0:T(8,128)} %get-tuple-element.238.refs_3_, ...), custom_call_target="tpu_custom_call" | custom-call | flops 671088640 | bytes 13631488 | tf_op jit(solution)/shard_map/attend_back/pallas_call | solution.py:209
  655.6 2.8 collective-permute-done.67
  660.6 4.8 all_to_all.82
  667.5 14.4 %finish.1 = (bf16[2048,768]{1,0:T(8,128)(2,1)}, bf16[2048,2048]{1,0:T(8,128)(2,1)}) custom-call(f32[2048,768]{1,0:T(8,128)} %get-tuple-element.47.refs_0_, f32[2,2048]{1,0:T(2,128)} %rsqrt.22.refs_1_, f32[2,2048]{1,0:T(2,128)} %mul.215.refs_2_, f32[2048,512]{1,0:T(8,128)} %get-tuple-element.62.refs_3_, bf16[2048,256]{1,0:T(8,128)(2,1)} %get-tuple-element.63.refs_4_, ...), custom_call_target="tpu_custom_call" | custom-call | flops 6442450944 | bytes 23068672 | tf_op jit(solution)/shard_map/finish/pallas_call | solution.py:232
  681.9 11.4 %convolution_convert_fusion.4 = bf16[2048,768]{1,0:T(8,128)(2,1)} fusion(bf16[2048,2048]{1,0:T(8,128)(2,1)} %constant_dynamic-update-slice_fusion.refs_0_, bf16[2048,768]{1,0:T(8,128)(2,1)} %get-tuple-element.66), kind=kOutput, calls=%fused_computation.7 | convolution fusion | flops 6444023808 | bytes 14680064 | tf_op jit(solution)/shard_map/dot_general | solution.py:493
  693.3 3.7 fusion.25
  702.7 3.1 convert_add_fusion.1
  709.1 10.9 %collective-permute-done.72 = bf16[128,2048]{1,0:T(8,128)(2,1)S(1)} collective-permute-done((bf16[128,2048]{1,0:T(8,128)(2,1)S(1)}, bf16[128,2048]{1,0:T(8,128)(2,1)S(1)}, u32[]{:S(2)}, u32[]{:S(2)}) %collective-permute-start.72) | collective-permute-done | bytes 524320 | tf_op jit(solution)/shard_map/ppermute | solution.py:27
  726.4 3.7 all-to-all-start.6
  730.1 26.9 %reduce-scatter.9.cloned.1.call-done = bf16[512,768]{1,0:T(8,128)(2,1)} async-done(((bf16[2048,768]{1,0:T(8,128)(2,1)}), bf16[512,768]{1,0:T(8,128)(2,1)}) %reduce-scatter.9.cloned.1.call-update) | async-done | bytes 786448 | tf_op jit(solution)/shard_map/reduce_scatter | solution.py:498
  759.9 3.0 add_convert_fusion
  762.9 2.0 copy.132
  768.5 4.6 all-to-all-start.5
  773.4 2.7 collective-permute-start.82
  779.0 9.1 %collective-permute-done.82 = bf16[1,64,768]{2,1,0:T(8,128)(2,1)S(1)} collective-permute-done((bf16[1,64,768]{2,1,0:T(8,128)(2,1)S(1)}, bf16[1,64,768]{2,1,0:T(8,128)(2,1)S(1)}, u32[]{:S(2)}, u32[]{:S(2)}) %collective-permute-start.82) | collective-permute-done | bytes 98336 | tf_op jit(solution)/shard_map/ppermute | solution.py:369
  793.7 5.7 all-to-all-done.5
  800.5 2.5 scatter_fusion
  803.0 3.8 convert_bitcast_fusion
  806.7 2.9 copy.140
  (432 shorter events, 173.4 us)
Async XLA Ops:
  7.2 18.0 %collective-permute-start.9 = (bf16[64,2048]{1,0:T(8,128)(2,1)}, bf16[64,2048]{1,0:T(8,128)(2,1)S(1)}, u32[]{:S(2)}, u32[]{:S(2)}) collective-permute-start(bf16[64,2048]{1,0:T(8,128)(2,1)} %param.21), channel_id=1, source_target_pairs={{0,8},{8,16},{16,24},{24,0},{1,9},{9,17},{17,25},{25,1},{2,10},{10... | collective-permute-start | bytes 786440 | tf_op jit(solution)/shard_map/ppermute | solution.py:359
  10.3 19.9 %collective-permute-start.10 = (bf16[64,2048]{1,0:T(8,128)(2,1)}, bf16[64,2048]{1,0:T(8,128)(2,1)S(1)}, u32[]{:S(2)}, u32[]{:S(2)}) collective-permute-start(bf16[64,2048]{1,0:T(8,128)(2,1)} %param.21), channel_id=1, source_target_pairs={{0,16},{8,24},{16,0},{24,8},{1,17},{9,25},{17,1},{25,9},{2,18},{10... | collective-permute-start | bytes 786440 | tf_op jit(solution)/shard_map/ppermute | solution.py:359
  12.9 17.4 %collective-permute-start.11 = (bf16[64,2048]{1,0:T(8,128)(2,1)}, bf16[64,2048]{1,0:T(8,128)(2,1)S(1)}, u32[]{:S(2)}, u32[]{:S(2)}) collective-permute-start(bf16[64,2048]{1,0:T(8,128)(2,1)} %param.21), channel_id=1, source_target_pairs={{0,24},{8,0},{16,8},{24,16},{1,25},{9,1},{17,9},{25,17},{2,26},{10... | collective-permute-start | bytes 786440 | tf_op jit(solution)/shard_map/ppermute | solution.py:359
  21.2 16.3 %all-to-all-start.1 = ((bf16[8,64,768]{2,1,0:T(8,128)(2,1)}), bf16[8,64,768]{2,1,0:T(8,128)(2,1)S(1)}, u32[]{:S(2)}, u32[]{:S(2)}) async-start(bf16[8,64,768]{2,1,0:T(8,128)(2,1)} %pad_maximum_fusion.9), calls=%async_computation.1 | async-start | bytes 1572864 | tf_op jit(solution)/shard_map/all_to_all | solution.py:430
  24.9 112.3 %all-gather.4.cloned.1.call-start = ((), (), s32[]{:S(2)}) async-start(), calls=%async_computation.11 | async-start | bytes 3932160 | tf_op jit(solution)/shard_map/all_gather | solution.py:448
  38.4 53.0 %all-to-all-start = ((bf16[64,4,2048]{2,1,0:T(4,128)(2,1)}), bf16[64,4,2048]{2,1,0:T(4,128)(2,1)S(1)}, u32[]{:S(2)}, u32[]{:S(2)}) async-start(bf16[64,4,2048]{2,1,0:T(4,128)(2,1)} %broadcast_select_fusion), calls=%async_computation | async-start | bytes 2097152 | tf_op jit(solution)/shard_map/all_to_all | solution.py:425
  41.1 239.6 %all-gather.6.cloned.1.call-start = ((), (), s32[]{:S(2)}) async-start(), calls=%async_computation.12 | async-start | bytes 10485760 | tf_op jit(solution)/shard_map/all_gather | solution.py:454
  92.2 24.3 %collective-permute-start = (bf16[256,2048]{1,0:T(8,128)(2,1)S(1)}, bf16[256,2048]{1,0:T(8,128)(2,1)}, u32[]{:S(2)}, u32[]{:S(2)}) collective-permute-start(bf16[256,2048]{1,0:T(8,128)(2,1)S(1)} %reshape.196), channel_id=1, source_target_pairs={{0,2},{2,0},{1,3},{3,1},{4,6},{6,4},{5,7},{7,5},{8,10},{10,8},{9,1... | collective-permute-start | bytes 3145736 | tf_op jit(solution)/shard_map/ppermute | solution.py:27
  94.1 25.0 %collective-permute-start.1 = (bf16[256,2048]{1,0:T(8,128)(2,1)S(1)}, bf16[256,2048]{1,0:T(8,128)(2,1)S(1)}, u32[]{:S(2)}, u32[]{:S(2)}) collective-permute-start(bf16[256,2048]{1,0:T(8,128)(2,1)S(1)} %reshape.196), channel_id=1, source_target_pairs={{0,4},{4,0},{1,5},{5,1},{2,6},{6,2},{3,7},{7,3},{8,12},{12,8},{9,1... | collective-permute-start | bytes 3145736 | tf_op jit(solution)/shard_map/ppermute | solution.py:27
  96.2 58.8 %all-to-all-start.2 = ((bf16[32,2,128]{2,1,0:T(2,128)(2,1)}), bf16[32,2,128]{2,1,0:T(2,128)(2,1)S(1)}, u32[]{:S(2)}, u32[]{:S(2)}) async-start(bf16[32,2,128]{2,1,0:T(2,128)(2,1)} %reshape.267), calls=%async_computation.2 | async-start | bytes 32768 | tf_op jit(solution)/shard_map/all_to_all | solution.py:433
  100.7 249.4 %all-gather.8.cloned.1.call-start = ((), (), s32[]{:S(2)}) async-start(), calls=%async_computation.13 | async-start | bytes 5242880 | tf_op jit(solution)/shard_map/all_gather | solution.py:455
  100.8 31.5 %collective-permute-start.4 = (bf16[256,2048]{1,0:T(8,128)(2,1)S(1)}, bf16[256,2048]{1,0:T(8,128)(2,1)S(1)}, u32[]{:S(2)}, u32[]{:S(2)}) collective-permute-start(bf16[256,2048]{1,0:T(8,128)(2,1)S(1)} %reshape.196), channel_id=1, source_target_pairs={{0,1},{1,0},{2,3},{3,2},{4,5},{5,4},{6,7},{7,6},{8,9},{9,8},{10,11... | collective-permute-start | bytes 3145736 | tf_op jit(solution)/shard_map/ppermute | solution.py:27
  117.6 11.9 %collective-permute-start.2 = (bf16[128,2048]{1,0:T(8,128)(2,1)S(1)}, bf16[128,2048]{1,0:T(8,128)(2,1)S(1)}, u32[]{:S(2)}, u32[]{:S(2)}) collective-permute-start(bf16[128,2048]{1,0:T(8,128)(2,1)S(1)} %slice.327), channel_id=1, source_target_pairs={{0,4},{4,0},{1,5},{5,1},{2,6},{6,2},{3,7},{7,3},{8,12},{12,8},{9,1... | collective-permute-start | bytes 1572872 | tf_op jit(solution)/shard_map/ppermute | solution.py:27
  119.1 11.5 %collective-permute-start.3 = (bf16[128,2048]{1,0:T(8,128)(2,1)S(1)}, bf16[128,2048]{1,0:T(8,128)(2,1)S(1)}, u32[]{:S(2)}, u32[]{:S(2)}) collective-permute-start(bf16[128,2048]{1,0:T(8,128)(2,1)S(1)} %slice.328), channel_id=1, source_target_pairs={{0,2},{2,0},{1,3},{3,1},{4,6},{6,4},{5,7},{7,5},{8,10},{10,8},{9,1... | collective-permute-start | bytes 1572872 | tf_op jit(solution)/shard_map/ppermute | solution.py:27
  122.0 11.4 %collective-permute-start.5 = (bf16[256,2048]{1,0:T(8,128)(2,1)}, bf16[256,2048]{1,0:T(8,128)(2,1)S(1)}, u32[]{:S(2)}, u32[]{:S(2)}) collective-permute-start(bf16[256,2048]{1,0:T(8,128)(2,1)} %collective-permute-done), channel_id=1, source_target_pairs={{0,1},{1,0},{2,3},{3,2},{4,5},{5,4},{6,7},{7,6},{8,9},{9,8},{10,11... | collective-permute-start | bytes 3145736 | tf_op jit(solution)/shard_map/ppermute | solution.py:27
  122.0 12.5 %collective-permute-start.6 = (bf16[256,2048]{1,0:T(8,128)(2,1)S(1)}, bf16[256,2048]{1,0:T(8,128)(2,1)S(1)}, u32[]{:S(2)}, u32[]{:S(2)}) collective-permute-start(bf16[256,2048]{1,0:T(8,128)(2,1)S(1)} %collective-permute-done.1), channel_id=1, source_target_pairs={{0,1},{1,0},{2,3},{3,2},{4,5},{5,4},{6,7},{7,6},{8,9},{9,8},{10,11... | collective-permute-start | bytes 3145736 | tf_op jit(solution)/shard_map/ppermute | solution.py:27
  191.4 14.0 %collective-permute-start.18 = (bf16[128,2048]{1,0:T(8,128)(2,1)S(1)}, bf16[128,2048]{1,0:T(8,128)(2,1)S(1)}, u32[]{:S(2)}, u32[]{:S(2)}) collective-permute-start(bf16[128,2048]{1,0:T(8,128)(2,1)S(1)} %get-tuple-element.216), channel_id=1, source_target_pairs={{0,4},{4,0},{1,5},{5,1},{2,6},{6,2},{3,7},{7,3},{8,12},{12,8},{9,1... | collective-permute-start | bytes 1572872 | tf_op jit(solution)/shard_map/ppermute | solution.py:27
  192.9 16.7 %collective-permute-start.15 = (bf16[256,2048]{1,0:T(8,128)(2,1)}, bf16[256,2048]{1,0:T(8,128)(2,1)}, u32[]{:S(2)}, u32[]{:S(2)}) collective-permute-start(bf16[256,2048]{1,0:T(8,128)(2,1)} %get-tuple-element.200), channel_id=1, source_target_pairs={{0,1},{1,0},{2,3},{3,2},{4,5},{5,4},{6,7},{7,6},{8,9},{9,8},{10,11... | collective-permute-start | bytes 3145736 | tf_op jit(solution)/shard_map/ppermute | solution.py:27
  193.0 14.4 %collective-permute-start.21 = (bf16[128,2048]{1,0:T(8,128)(2,1)S(1)}, bf16[128,2048]{1,0:T(8,128)(2,1)S(1)}, u32[]{:S(2)}, u32[]{:S(2)}) collective-permute-start(bf16[128,2048]{1,0:T(8,128)(2,1)S(1)} %get-tuple-element.217), channel_id=1, source_target_pairs={{0,2},{2,0},{1,3},{3,1},{4,6},{6,4},{5,7},{7,5},{8,10},{10,8},{9,1... | collective-permute-start | bytes 1572872 | tf_op jit(solution)/shard_map/ppermute | solution.py:27
  205.7 24.6 %collective-permute-start.19 = (bf16[256,2048]{1,0:T(8,128)(2,1)S(1)}, bf16[256,2048]{1,0:T(8,128)(2,1)}, u32[]{:S(2)}, u32[]{:S(2)}) collective-permute-start(bf16[256,2048]{1,0:T(8,128)(2,1)S(1)} %pad_maximum_fusion.1), channel_id=1, source_target_pairs={{0,2},{2,0},{1,3},{3,1},{4,6},{6,4},{5,7},{7,5},{8,10},{10,8},{9,1... | collective-permute-start | bytes 3145736 | tf_op jit(solution)/shard_map/ppermute | solution.py:27
  207.6 25.1 %collective-permute-start.22 = (bf16[256,2048]{1,0:T(8,128)(2,1)S(1)}, bf16[256,2048]{1,0:T(8,128)(2,1)}, u32[]{:S(2)}, u32[]{:S(2)}) collective-permute-start(bf16[256,2048]{1,0:T(8,128)(2,1)S(1)} %pad_maximum_fusion.2), channel_id=1, source_target_pairs={{0,4},{4,0},{1,5},{5,1},{2,6},{6,2},{3,7},{7,3},{8,12},{12,8},{9,1... | collective-permute-start | bytes 3145736 | tf_op jit(solution)/shard_map/ppermute | solution.py:27
  209.2 339.8 %reduce-scatter.5.cloned.1.call-start = ((), (), s32[]{:S(2)}) async-start(), calls=%async_computation.14 | async-start | bytes 5242880 | tf_op jit(solution)/shard_map/reduce_scatter | solution.py:498
  236.9 24.0 %collective-permute-start.23 = (bf16[256,2048]{1,0:T(8,128)(2,1)S(1)}, bf16[256,2048]{1,0:T(8,128)(2,1)S(1)}, u32[]{:S(2)}, u32[]{:S(2)}) collective-permute-start(bf16[256,2048]{1,0:T(8,128)(2,1)S(1)} %get-tuple-element.176), channel_id=1, source_target_pairs={{0,2},{2,0},{1,3},{3,1},{4,6},{6,4},{5,7},{7,5},{8,10},{10,8},{9,1... | collective-permute-start | bytes 3145736 | tf_op jit(solution)/shard_map/ppermute | solution.py:27
  238.6 24.3 %collective-permute-start.24 = (bf16[256,2048]{1,0:T(8,128)(2,1)S(1)}, bf16[256,2048]{1,0:T(8,128)(2,1)S(1)}, u32[]{:S(2)}, u32[]{:S(2)}) collective-permute-start(bf16[256,2048]{1,0:T(8,128)(2,1)S(1)} %get-tuple-element.176), channel_id=1, source_target_pairs={{0,4},{4,0},{1,5},{5,1},{2,6},{6,2},{3,7},{7,3},{8,12},{12,8},{9,1... | collective-permute-start | bytes 3145736 | tf_op jit(solution)/shard_map/ppermute | solution.py:27
  239.1 36.7 %collective-permute-start.27 = (bf16[256,2048]{1,0:T(8,128)(2,1)S(1)}, bf16[256,2048]{1,0:T(8,128)(2,1)S(1)}, u32[]{:S(2)}, u32[]{:S(2)}) collective-permute-start(bf16[256,2048]{1,0:T(8,128)(2,1)S(1)} %get-tuple-element.176), channel_id=1, source_target_pairs={{0,1},{1,0},{2,3},{3,2},{4,5},{5,4},{6,7},{7,6},{8,9},{9,8},{10,11... | collective-permute-start | bytes 3145736 | tf_op jit(solution)/shard_map/ppermute | solution.py:27
  261.0 12.6 %collective-permute-start.25 = (bf16[128,2048]{1,0:T(8,128)(2,1)S(1)}, bf16[128,2048]{1,0:T(8,128)(2,1)S(1)}, u32[]{:S(2)}, u32[]{:S(2)}) collective-permute-start(bf16[128,2048]{1,0:T(8,128)(2,1)S(1)} %slice.345), channel_id=1, source_target_pairs={{0,4},{4,0},{1,5},{5,1},{2,6},{6,2},{3,7},{7,3},{8,12},{12,8},{9,1... | collective-permute-start | bytes 1572872 | tf_op jit(solution)/shard_map/ppermute | solution.py:27
  263.4 13.5 %collective-permute-start.28 = (bf16[256,2048]{1,0:T(8,128)(2,1)S(1)}, bf16[256,2048]{1,0:T(8,128)(2,1)S(1)}, u32[]{:S(2)}, u32[]{:S(2)}) collective-permute-start(bf16[256,2048]{1,0:T(8,128)(2,1)S(1)} %collective-permute-done.23), channel_id=1, source_target_pairs={{0,1},{1,0},{2,3},{3,2},{4,5},{5,4},{6,7},{7,6},{8,9},{9,8},{10,11... | collective-permute-start | bytes 3145736 | tf_op jit(solution)/shard_map/ppermute | solution.py:27
  263.4 14.6 %collective-permute-start.29 = (bf16[256,2048]{1,0:T(8,128)(2,1)S(1)}, bf16[256,2048]{1,0:T(8,128)(2,1)S(1)}, u32[]{:S(2)}, u32[]{:S(2)}) collective-permute-start(bf16[256,2048]{1,0:T(8,128)(2,1)S(1)} %collective-permute-done.24), channel_id=1, source_target_pairs={{0,1},{1,0},{2,3},{3,2},{4,5},{5,4},{6,7},{7,6},{8,9},{9,8},{10,11... | collective-permute-start | bytes 3145736 | tf_op jit(solution)/shard_map/ppermute | solution.py:27
  371.2 14.0 %collective-permute-start.35 = (bf16[128,2048]{1,0:T(8,128)(2,1)S(1)}, bf16[128,2048]{1,0:T(8,128)(2,1)S(1)}, u32[]{:S(2)}, u32[]{:S(2)}) collective-permute-start(bf16[128,2048]{1,0:T(8,128)(2,1)S(1)} %get-tuple-element.214), channel_id=1, source_target_pairs={{0,4},{4,0},{1,5},{5,1},{2,6},{6,2},{3,7},{7,3},{8,12},{12,8},{9,1... | collective-permute-start | bytes 1572872 | tf_op jit(solution)/shard_map/ppermute | solution.py:27
  372.8 18.8 %collective-permute-start.32 = (bf16[256,2048]{1,0:T(8,128)(2,1)}, bf16[256,2048]{1,0:T(8,128)(2,1)}, u32[]{:S(2)}, u32[]{:S(2)}) collective-permute-start(bf16[256,2048]{1,0:T(8,128)(2,1)} %get-tuple-element.193), channel_id=1, source_target_pairs={{0,1},{1,0},{2,3},{3,2},{4,5},{5,4},{6,7},{7,6},{8,9},{9,8},{10,11... | collective-permute-start | bytes 3145736 | tf_op jit(solution)/shard_map/ppermute | solution.py:27
  372.8 15.1 %collective-permute-start.38 = (bf16[128,2048]{1,0:T(8,128)(2,1)S(1)}, bf16[128,2048]{1,0:T(8,128)(2,1)S(1)}, u32[]{:S(2)}, u32[]{:S(2)}) collective-permute-start(bf16[128,2048]{1,0:T(8,128)(2,1)S(1)} %get-tuple-element.215), channel_id=1, source_target_pairs={{0,2},{2,0},{1,3},{3,1},{4,6},{6,4},{5,7},{7,5},{8,10},{10,8},{9,1... | collective-permute-start | bytes 1572872 | tf_op jit(solution)/shard_map/ppermute | solution.py:27
  386.4 24.7 %collective-permute-start.36 = (bf16[256,2048]{1,0:T(8,128)(2,1)}, bf16[256,2048]{1,0:T(8,128)(2,1)}, u32[]{:S(2)}, u32[]{:S(2)}) collective-permute-start(bf16[256,2048]{1,0:T(8,128)(2,1)} %pad_maximum_fusion.3), channel_id=1, source_target_pairs={{0,2},{2,0},{1,3},{3,1},{4,6},{6,4},{5,7},{7,5},{8,10},{10,8},{9,1... | collective-permute-start | bytes 3145736 | tf_op jit(solution)/shard_map/ppermute | solution.py:27
  389.1 24.4 %collective-permute-start.39 = (bf16[256,2048]{1,0:T(8,128)(2,1)}, bf16[256,2048]{1,0:T(8,128)(2,1)}, u32[]{:S(2)}, u32[]{:S(2)}) collective-permute-start(bf16[256,2048]{1,0:T(8,128)(2,1)} %pad_maximum_fusion.4), channel_id=1, source_target_pairs={{0,4},{4,0},{1,5},{5,1},{2,6},{6,2},{3,7},{7,3},{8,12},{12,8},{9,1... | collective-permute-start | bytes 3145736 | tf_op jit(solution)/shard_map/ppermute | solution.py:27
  417.9 23.7 %collective-permute-start.40 = (bf16[256,2048]{1,0:T(8,128)(2,1)S(1)}, bf16[256,2048]{1,0:T(8,128)(2,1)S(1)}, u32[]{:S(2)}, u32[]{:S(2)}) collective-permute-start(bf16[256,2048]{1,0:T(8,128)(2,1)S(1)} %get-tuple-element.237), channel_id=1, source_target_pairs={{0,2},{2,0},{1,3},{3,1},{4,6},{6,4},{5,7},{7,5},{8,10},{10,8},{9,1... | collective-permute-start | bytes 3145736 | tf_op jit(solution)/shard_map/ppermute | solution.py:27
  419.4 24.7 %collective-permute-start.41 = (bf16[256,2048]{1,0:T(8,128)(2,1)S(1)}, bf16[256,2048]{1,0:T(8,128)(2,1)S(1)}, u32[]{:S(2)}, u32[]{:S(2)}) collective-permute-start(bf16[256,2048]{1,0:T(8,128)(2,1)S(1)} %get-tuple-element.237), channel_id=1, source_target_pairs={{0,4},{4,0},{1,5},{5,1},{2,6},{6,2},{3,7},{7,3},{8,12},{12,8},{9,1... | collective-permute-start | bytes 3145736 | tf_op jit(solution)/shard_map/ppermute | solution.py:27
  420.0 34.9 %collective-permute-start.44 = (bf16[256,2048]{1,0:T(8,128)(2,1)S(1)}, bf16[256,2048]{1,0:T(8,128)(2,1)S(1)}, u32[]{:S(2)}, u32[]{:S(2)}) collective-permute-start(bf16[256,2048]{1,0:T(8,128)(2,1)S(1)} %get-tuple-element.237), channel_id=1, source_target_pairs={{0,1},{1,0},{2,3},{3,2},{4,5},{5,4},{6,7},{7,6},{8,9},{9,8},{10,11... | collective-permute-start | bytes 3145736 | tf_op jit(solution)/shard_map/ppermute | solution.py:27
  441.6 12.6 %collective-permute-start.42 = (bf16[128,2048]{1,0:T(8,128)(2,1)S(1)}, bf16[128,2048]{1,0:T(8,128)(2,1)S(1)}, u32[]{:S(2)}, u32[]{:S(2)}) collective-permute-start(bf16[128,2048]{1,0:T(8,128)(2,1)S(1)} %slice.362), channel_id=1, source_target_pairs={{0,4},{4,0},{1,5},{5,1},{2,6},{6,2},{3,7},{7,3},{8,12},{12,8},{9,1... | collective-permute-start | bytes 1572872 | tf_op jit(solution)/shard_map/ppermute | solution.py:27
  471.3 221.9 %reduce-scatter.7.cloned.1.call-start = ((), (), s32[]{:S(2)}) async-start(), calls=%async_computation.15 | async-start | bytes 10485760 | tf_op jit(solution)/shard_map/reduce_scatter | solution.py:498
  524.9 24.1 %collective-permute-start.52 = (bf16[128,2048]{1,0:T(8,128)(2,1)}, bf16[128,2048]{1,0:T(8,128)(2,1)S(1)}, u32[]{:S(2)}, u32[]{:S(2)}) collective-permute-start(bf16[128,2048]{1,0:T(8,128)(2,1)} %get-tuple-element.213), channel_id=1, source_target_pairs={{0,2},{2,0},{1,3},{3,1},{4,6},{6,4},{5,7},{7,5},{8,10},{10,8},{9,1... | collective-permute-start | bytes 1572872 | tf_op jit(solution)/shard_map/ppermute | solution.py:27
  525.8 23.2 %collective-permute-start.53 = (bf16[128,2048]{1,0:T(8,128)(2,1)}, bf16[128,2048]{1,0:T(8,128)(2,1)S(1)}, u32[]{:S(2)}, u32[]{:S(2)}) collective-permute-start(bf16[128,2048]{1,0:T(8,128)(2,1)} %get-tuple-element.212), channel_id=1, source_target_pairs={{0,4},{4,0},{1,5},{5,1},{2,6},{6,2},{3,7},{7,3},{8,12},{12,8},{9,1... | collective-permute-start | bytes 1572872 | tf_op jit(solution)/shard_map/ppermute | solution.py:27
  549.8 207.1 %reduce-scatter.9.cloned.1.call-start = ((), (), s32[]{:S(2)}) async-start(), calls=%async_computation.16 | async-start | bytes 3932160 | tf_op jit(solution)/shard_map/reduce_scatter | solution.py:498
  554.0 25.6 %collective-permute-start.54 = (bf16[256,2048]{1,0:T(8,128)(2,1)S(1)}, bf16[256,2048]{1,0:T(8,128)(2,1)S(1)}, u32[]{:S(2)}, u32[]{:S(2)}) collective-permute-start(bf16[256,2048]{1,0:T(8,128)(2,1)S(1)} %pad_maximum_fusion.5), channel_id=1, source_target_pairs={{0,2},{2,0},{1,3},{3,1},{4,6},{6,4},{5,7},{7,5},{8,10},{10,8},{9,1... | collective-permute-start | bytes 3145736 | tf_op jit(solution)/shard_map/ppermute | solution.py:27
  554.6 25.4 %collective-permute-start.56 = (bf16[256,2048]{1,0:T(8,128)(2,1)S(1)}, bf16[256,2048]{1,0:T(8,128)(2,1)S(1)}, u32[]{:S(2)}, u32[]{:S(2)}) collective-permute-start(bf16[256,2048]{1,0:T(8,128)(2,1)S(1)} %pad_maximum_fusion.6), channel_id=1, source_target_pairs={{0,4},{4,0},{1,5},{5,1},{2,6},{6,2},{3,7},{7,3},{8,12},{12,8},{9,1... | collective-permute-start | bytes 3145736 | tf_op jit(solution)/shard_map/ppermute | solution.py:27
  585.5 24.6 %collective-permute-start.57 = (bf16[256,2048]{1,0:T(8,128)(2,1)S(1)}, bf16[256,2048]{1,0:T(8,128)(2,1)S(1)}, u32[]{:S(2)}, u32[]{:S(2)}) collective-permute-start(bf16[256,2048]{1,0:T(8,128)(2,1)S(1)} %get-tuple-element.171), channel_id=1, source_target_pairs={{0,2},{2,0},{1,3},{3,1},{4,6},{6,4},{5,7},{7,5},{8,10},{10,8},{9,1... | collective-permute-start | bytes 3145736 | tf_op jit(solution)/shard_map/ppermute | solution.py:27
  587.2 24.7 %collective-permute-start.58 = (bf16[256,2048]{1,0:T(8,128)(2,1)S(1)}, bf16[256,2048]{1,0:T(8,128)(2,1)S(1)}, u32[]{:S(2)}, u32[]{:S(2)}) collective-permute-start(bf16[256,2048]{1,0:T(8,128)(2,1)S(1)} %get-tuple-element.171), channel_id=1, source_target_pairs={{0,4},{4,0},{1,5},{5,1},{2,6},{6,2},{3,7},{7,3},{8,12},{12,8},{9,1... | collective-permute-start | bytes 3145736 | tf_op jit(solution)/shard_map/ppermute | solution.py:27
  588.2 36.2 %collective-permute-start.61 = (bf16[256,2048]{1,0:T(8,128)(2,1)S(1)}, bf16[256,2048]{1,0:T(8,128)(2,1)S(1)}, u32[]{:S(2)}, u32[]{:S(2)}) collective-permute-start(bf16[256,2048]{1,0:T(8,128)(2,1)S(1)} %get-tuple-element.171), channel_id=1, source_target_pairs={{0,1},{1,0},{2,3},{3,2},{4,5},{5,4},{6,7},{7,6},{8,9},{9,8},{10,11... | collective-permute-start | bytes 3145736 | tf_op jit(solution)/shard_map/ppermute | solution.py:27
  610.2 12.7 %collective-permute-start.59 = (bf16[128,2048]{1,0:T(8,128)(2,1)S(1)}, bf16[128,2048]{1,0:T(8,128)(2,1)S(1)}, u32[]{:S(2)}, u32[]{:S(2)}) collective-permute-start(bf16[128,2048]{1,0:T(8,128)(2,1)S(1)} %slice.370), channel_id=1, source_target_pairs={{0,4},{4,0},{1,5},{5,1},{2,6},{6,2},{3,7},{7,3},{8,12},{12,8},{9,1... | collective-permute-start | bytes 1572872 | tf_op jit(solution)/shard_map/ppermute | solution.py:27
  612.0 12.3 %collective-permute-start.60 = (bf16[128,2048]{1,0:T(8,128)(2,1)S(1)}, bf16[128,2048]{1,0:T(8,128)(2,1)S(1)}, u32[]{:S(2)}, u32[]{:S(2)}) collective-permute-start(bf16[128,2048]{1,0:T(8,128)(2,1)S(1)} %slice.371), channel_id=1, source_target_pairs={{0,2},{2,0},{1,3},{3,1},{4,6},{6,4},{5,7},{7,5},{8,10},{10,8},{9,1... | collective-permute-start | bytes 1572872 | tf_op jit(solution)/shard_map/ppermute | solution.py:27
  613.0 11.5 %collective-permute-start.62 = (bf16[256,2048]{1,0:T(8,128)(2,1)S(1)}, bf16[256,2048]{1,0:T(8,128)(2,1)S(1)}, u32[]{:S(2)}, u32[]{:S(2)}) collective-permute-start(bf16[256,2048]{1,0:T(8,128)(2,1)S(1)} %collective-permute-done.57), channel_id=1, source_target_pairs={{0,1},{1,0},{2,3},{3,2},{4,5},{5,4},{6,7},{7,6},{8,9},{9,8},{10,11... | collective-permute-start | bytes 3145736 | tf_op jit(solution)/shard_map/ppermute | solution.py:27
  613.0 11.6 %collective-permute-start.63 = (bf16[256,2048]{1,0:T(8,128)(2,1)S(1)}, bf16[256,2048]{1,0:T(8,128)(2,1)S(1)}, u32[]{:S(2)}, u32[]{:S(2)}) collective-permute-start(bf16[256,2048]{1,0:T(8,128)(2,1)S(1)} %collective-permute-done.58), channel_id=1, source_target_pairs={{0,1},{1,0},{2,3},{3,2},{4,5},{5,4},{6,7},{7,6},{8,9},{9,8},{10,11... | collective-permute-start | bytes 3145736 | tf_op jit(solution)/shard_map/ppermute | solution.py:27
  705.9 14.1 %collective-permute-start.72 = (bf16[128,2048]{1,0:T(8,128)(2,1)S(1)}, bf16[128,2048]{1,0:T(8,128)(2,1)S(1)}, u32[]{:S(2)}, u32[]{:S(2)}) collective-permute-start(bf16[128,2048]{1,0:T(8,128)(2,1)S(1)} %get-tuple-element.210), channel_id=1, source_target_pairs={{0,4},{4,0},{1,5},{5,1},{2,6},{6,2},{3,7},{7,3},{8,12},{12,8},{9,1... | collective-permute-start | bytes 1572872 | tf_op jit(solution)/shard_map/ppermute | solution.py:27
  707.4 51.6 %collective-permute-start.69 = (bf16[256,2048]{1,0:T(8,128)(2,1)}, bf16[256,2048]{1,0:T(8,128)(2,1)}, u32[]{:S(2)}, u32[]{:S(2)}) collective-permute-start(bf16[256,2048]{1,0:T(8,128)(2,1)} %get-tuple-element.179), channel_id=1, source_target_pairs={{0,1},{1,0},{2,3},{3,2},{4,5},{5,4},{6,7},{7,6},{8,9},{9,8},{10,11... | collective-permute-start | bytes 3145736 | tf_op jit(solution)/shard_map/ppermute | solution.py:27
  707.5 15.2 %collective-permute-start.75 = (bf16[128,2048]{1,0:T(8,128)(2,1)S(1)}, bf16[128,2048]{1,0:T(8,128)(2,1)S(1)}, u32[]{:S(2)}, u32[]{:S(2)}) collective-permute-start(bf16[128,2048]{1,0:T(8,128)(2,1)S(1)} %get-tuple-element.211), channel_id=1, source_target_pairs={{0,2},{2,0},{1,3},{3,1},{4,6},{6,4},{5,7},{7,5},{8,10},{10,8},{9,1... | collective-permute-start | bytes 1572872 | tf_op jit(solution)/shard_map/ppermute | solution.py:27
  721.2 37.8 %collective-permute-start.73 = (bf16[256,2048]{1,0:T(8,128)(2,1)}, bf16[256,2048]{1,0:T(8,128)(2,1)}, u32[]{:S(2)}, u32[]{:S(2)}) collective-permute-start(bf16[256,2048]{1,0:T(8,128)(2,1)} %pad_maximum_fusion.7), channel_id=1, source_target_pairs={{0,2},{2,0},{1,3},{3,1},{4,6},{6,4},{5,7},{7,5},{8,10},{10,8},{9,1... | collective-permute-start | bytes 3145736 | tf_op jit(solution)/shard_map/ppermute | solution.py:27
  723.9 36.0 %collective-permute-start.76 = (bf16[256,2048]{1,0:T(8,128)(2,1)}, bf16[256,2048]{1,0:T(8,128)(2,1)}, u32[]{:S(2)}, u32[]{:S(2)}) collective-permute-start(bf16[256,2048]{1,0:T(8,128)(2,1)} %pad_maximum_fusion.8), channel_id=1, source_target_pairs={{0,4},{4,0},{1,5},{5,1},{2,6},{6,2},{3,7},{7,3},{8,12},{12,8},{9,1... | collective-permute-start | bytes 3145736 | tf_op jit(solution)/shard_map/ppermute | solution.py:27
  726.4 42.1 %all-to-all-start.6 = ((f32[32,1,256]{2,1,0:T(1,128)}), f32[32,1,256]{2,1,0:T(1,128)S(1)}, u32[]{:S(2)}, u32[]{:S(2)}) async-start(f32[32,1,256]{2,1,0:T(1,128)} %reshape.269), calls=%async_computation.10 | async-start | bytes 65536 | tf_op jit(solution)/shard_map/all_to_all | solution.py:560
  759.0 14.4 %collective-permute-start.77 = (bf16[1,64,768]{2,1,0:T(8,128)(2,1)}, bf16[1,64,768]{2,1,0:T(8,128)(2,1)}, u32[]{:S(2)}, u32[]{:S(2)}) collective-permute-start(bf16[1,64,768]{2,1,0:T(8,128)(2,1)} %get-tuple-element.227), channel_id=1, source_target_pairs={{0,1},{1,0},{2,3},{3,2},{4,5},{5,4},{6,7},{7,6},{8,9},{9,8},{10,11... | collective-permute-start | bytes 294920 | tf_op jit(solution)/shard_map/ppermute | solution.py:369
  765.0 12.1 %collective-permute-start.78 = (bf16[1,64,768]{2,1,0:T(8,128)(2,1)}, bf16[1,64,768]{2,1,0:T(8,128)(2,1)}, u32[]{:S(2)}, u32[]{:S(2)}) collective-permute-start(bf16[1,64,768]{2,1,0:T(8,128)(2,1)} %get-tuple-element.226), channel_id=1, source_target_pairs={{0,2},{1,3},{2,0},{3,1},{4,6},{5,7},{6,4},{7,5},{8,10},{9,11},{10,... | collective-permute-start | bytes 294920 | tf_op jit(solution)/shard_map/ppermute | solution.py:369
  766.4 11.6 %collective-permute-start.79 = (bf16[1,64,768]{2,1,0:T(8,128)(2,1)}, bf16[1,64,768]{2,1,0:T(8,128)(2,1)}, u32[]{:S(2)}, u32[]{:S(2)}) collective-permute-start(bf16[1,64,768]{2,1,0:T(8,128)(2,1)} %get-tuple-element.225), channel_id=1, source_target_pairs={{0,3},{1,2},{2,1},{3,0},{4,7},{5,6},{6,5},{7,4},{8,11},{9,10},{10,... | collective-permute-start | bytes 294920 | tf_op jit(solution)/shard_map/ppermute | solution.py:369
  766.5 12.5 %collective-permute-start.80 = (bf16[1,64,768]{2,1,0:T(8,128)(2,1)}, bf16[1,64,768]{2,1,0:T(8,128)(2,1)S(1)}, u32[]{:S(2)}, u32[]{:S(2)}) collective-permute-start(bf16[1,64,768]{2,1,0:T(8,128)(2,1)} %get-tuple-element.224), channel_id=1, source_target_pairs={{0,4},{1,5},{2,6},{3,7},{4,0},{5,1},{6,2},{7,3},{8,12},{9,13},{10,... | collective-permute-start | bytes 294920 | tf_op jit(solution)/shard_map/ppermute | solution.py:369
  768.5 30.9 %all-to-all-start.5 = ((bf16[2,128,2048]{2,0,1:T(2,128)(2,1)}), bf16[2,128,2048]{2,0,1:T(2,128)(2,1)S(1)}, u32[]{:S(2)}, u32[]{:S(2)}) async-start(bf16[2,128,2048]{2,0,1:T(2,128)(2,1)} %copy.132), calls=%async_computation.5 | async-start | bytes 2097152 | tf_op jit(solution)/shard_map/all_to_all | solution.py:532
  773.1 44.9 %reduce-scatter.11.cloned.1.call-start = ((), (), s32[]{:S(2)}) async-start(), calls=%async_computation.17 | async-start | bytes 1310720 | tf_op jit(solution)/shard_map/reduce_scatter | solution.py:498
  773.4 14.7 %collective-permute-start.82 = (bf16[1,64,768]{2,1,0:T(8,128)(2,1)S(1)}, bf16[1,64,768]{2,1,0:T(8,128)(2,1)S(1)}, u32[]{:S(2)}, u32[]{:S(2)}) collective-permute-start(bf16[1,64,768]{2,1,0:T(8,128)(2,1)S(1)} %get-tuple-element.222), channel_id=1, source_target_pairs={{0,6},{1,7},{2,4},{3,5},{4,2},{5,3},{6,0},{7,1},{8,14},{9,15},{10,... | collective-permute-start | bytes 294920 | tf_op jit(solution)/shard_map/ppermute | solution.py:369
  777.1 13.1 %collective-permute-start.83 = (bf16[1,64,768]{2,1,0:T(8,128)(2,1)S(1)}, bf16[1,64,768]{2,1,0:T(8,128)(2,1)S(1)}, u32[]{:S(2)}, u32[]{:S(2)}) collective-permute-start(bf16[1,64,768]{2,1,0:T(8,128)(2,1)S(1)} %get-tuple-element.221), channel_id=1, source_target_pairs={{0,7},{1,6},{2,5},{3,4},{4,3},{5,2},{6,1},{7,0},{8,15},{9,14},{10,... | collective-permute-start | bytes 294920 | tf_op jit(solution)/shard_map/ppermute | solution.py:369
  (74 other events, 857.4 us)
Sparse Core Ops, SparseCore 0:
  38.6 80.0 all-gather.3
  120.8 148.7 all-gather.5
  271.1 78.9 all-gather.7
  471.5 74.3 reduce-scatter.4
  549.2 143.9 reduce-scatter.6
  695.4 61.4 reduce-scatter.8
  790.3 27.7 reduce-scatter.10

commit v6 on v5

--- a/solution.py
+++ b/solution.py
@@ -312,8 +312,9 @@
     )(hidden, weight)
 
 
-def gated_back_kernel(groups, grad_ref, down_ref, raw_ref, weight_ref, units_ref, hidden_ref):
-    grad_act = matmul(grad_ref[...], down_ref[...], 1, 1)
+def gated_back_kernel(groups, grad_ref, first_ref, second_ref, raw_ref, weight_ref, units_ref, hidden_ref):
+    split = first_ref.shape[1]
+    grad_act = matmul(grad_ref[:, :split], first_ref[...], 1, 1) + matmul(grad_ref[:, split:], second_ref[...], 1, 1)
     step = grad_act.shape[1] // groups
     for i in range(groups):
         gate = raw_ref[:, 2 * i * step : (2 * i + 1) * step]
@@ -327,16 +328,16 @@
     hidden_ref[...] = matmul(units_ref[...], weight_ref[...]).astype(BF)
 
 
-def gated_back(grad, down, raw, weight, groups):
+def gated_back(grad, downs, raw, weight, groups):
     wide, width = grad.shape
     units = weight.shape[0]
     block = 256
     rows = lambda columns: pl.BlockSpec((block, columns), lambda i: (i, 0))
-    fixed = lambda count: pl.BlockSpec((count, width), lambda i: (0, 0))
+    fixed = lambda array: pl.BlockSpec(array.shape, lambda i: (0, 0))
     return pl.pallas_call(
         lambda *refs: gated_back_kernel(groups, *refs),
         grid=(wide // block,),
-        in_specs=[rows(width), fixed(units // 2), rows(units), fixed(units)],
+        in_specs=[rows(width), fixed(downs[0]), fixed(downs[1]), rows(units), fixed(weight)],
         out_specs=[rows(units), rows(width)],
         out_shape=[jax.ShapeDtypeStruct((wide, units), BF), jax.ShapeDtypeStruct((wide, width), BF)],
         cost_estimate=pl.CostEstimate(
@@ -345,7 +346,7 @@
             transcendentals=wide * units // 2,
         ),
         name="gated_back",
-    )(grad, down, raw, weight)
+    )(grad, *downs, raw, weight)
 
 
 def ring(ahead):
@@ -452,7 +453,11 @@
     units = w_gate.shape[1]
     gate_up = jnp.concatenate([w_gate.T, w_up.T])
     gate_up = lax.all_gather(after(gate_up, qkv_in), REST, axis=0, tiled=True)
-    down = lax.all_gather(after(w_down, qkv_in), REST, axis=0, tiled=True)
+    split = width // 2
+    downs = [
+        lax.all_gather(after(part, qkv_in), REST, axis=0, tiled=True)
+        for part in (w_down[:, :split], w_down[:, split:])
+    ]
 
     own_seqs = lax.dynamic_slice_in_dim(dealing, rank * micro_count, micro_count)
     own_lengths = jnp.take(lengths, own_seqs)
@@ -471,7 +476,11 @@
     contract_last = (((1,), (1,)), ((), ()))
     contract_rows = (((0,), (0,)), ((), ()))
     unit_raw, act_low = gated(hidden_wide, gate_up, groups)
-    down_raw, _ = group_scatter(jnp.dot(act_low, down, preferred_element_type=F32).astype(BF))
+    down_raws = []
+    for part in downs:
+        rows_in = after(act_low, *down_raws)
+        down_raws.append(group_scatter(jnp.dot(rows_in, part, preferred_element_type=F32).astype(BF))[0])
+    down_raw = jnp.concatenate(down_raws, axis=1)
     down_inv = lax.rsqrt(jnp.mean(down_raw * down_raw, axis=-1, keepdims=True) + norm_eps)
     down_normed = down_raw * down_inv
     block_out = (
@@ -487,7 +496,7 @@
     down_term = lax.dot_general(
         act_low, grad_down_wide, contract_rows, preferred_element_type=F32
     ).astype(BF)
-    grad_units, hidden_term = gated_back(after(grad_down_wide, down_term), down, unit_raw, gate_up, groups)
+    grad_units, hidden_term = gated_back(after(grad_down_wide, down_term), downs, unit_raw, gate_up, groups)
 
     def weight_term(left, right):
         return lambda token: lax.dot_general(

time: 835 us -> 830 us (level)
  waiting for transfers between devices: 393 us -> 362 us
  other arithmetic: 49.8 us -> 58.4 us
    all_gather x1 -> x2, waiting for transfers between devices: 45.1 us -> 14.4 us  [per_device(): lax.all_gather(after(part, qkv_in), REST, axis=0, tiled=True)]
    ppermute x74 -> x82, starting transfers between devices: 51.7 us -> 58.5 us  [swap(): return lax.ppermute(value, axis, SWAP)]
    unnamed x126 -> x128, local copies, waits for them, and re-layouts: 36.5 us -> 39.7 us
    ppermute x74 -> x82, waiting for transfers between devices: 246 us -> 244 us  [swap(): return lax.ppermute(value, axis, SWAP)]
  transfers between devices with their start and end apart: 96 -> 105, of which waited for: 52 -> 62; matrix products, arithmetic and copies ran while one was open for 19% -> 22% of each run, Pallas kernels for 15% -> 15%
where the time goes in v6:
time: 830 us; the launch traced here: 821 us
  waiting for transfers between devices  362 us (44%)
  Pallas kernels  125 us (15%)
  starting transfers between devices  91.5 us (11%)
  local copies, waits for them, and re-layouts  91 us (11%)
  matrix products  67.2 us (8%)
  other arithmetic  58.4 us (7%)
  between operations  16.2 us (2%)
  blocking collectives  9.78 us (1%)
    ppermute x82, waiting for transfers between devices, swap(): return lax.ppermute(value, axis, SWAP)  244 us
    ppermute x82, starting transfers between devices, swap(): return lax.ppermute(value, axis, SWAP)  58.5 us
    all_to_all x1, waiting for transfers between devices, per_device(): lax.all_to_all(outgoing, ALL, split_axis=0, concat_axis=1, tiled=True)  44 us
    unnamed x128, local copies, waits for them, and re-layouts  39.7 us
    pallas_call x1, Pallas kernels, gated_back(): pl.pallas_call(lambda *refs: gated_back_kernel(groups, *refs), grid=(wide...  37.4 us
    dot_general x2, matrix products, weight_term(): lax.dot_general(after(left, *(token if isinstance(token, tuple) else (tok...  32.1 us
    reduce_scatter x4, waiting for transfers between devices, owners(): return lax.psum_scatter(term, REST, scatter_dimension=0, tiled=True)  30.7 us
    pallas_call x1, Pallas kernels, gated(): pl.pallas_call(lambda *refs: gated_kernel(groups, *refs), grid=(wide // b...  24.5 us
  transfers between devices with their start and end apart: 105, of which 62 were waited for; matrix products, arithmetic and copies ran while one was open for 22% of the time, Pallas kernels for 15%

profile of v6, /device:TPU:0, one launch (start us, length us, event | category | flops | bytes accessed | tf_op | source)
XLA Modules:
  0.0 821.1 jit_solution(2505034738021850998)
XLA Ops:
  7.2 3.1 collective-permute-start.9
  10.3 2.6 collective-permute-start.10
  22.1 3.7 all-to-all-start.1
  26.2 4.0 collective-permute-done.10
  30.3 8.2 all-to-all-done.1
  39.4 2.7 all-to-all-start
  45.9 2.7 pad_maximum_fusion
  48.7 44.0 %all-to-all-done = bf16[64,4,2048]{2,1,0:T(4,128)(2,1)S(1)} async-done(((bf16[64,4,2048]{2,1,0:T(4,128)(2,1)}), bf16[64,4,2048]{2,1,0:T(4,128)(2,1)S(1)}, u32[]{:S(2)}, u32[]{:S(2)}) %all-to-all-start) | async-done | bytes 1048608 | tf_op jit(solution)/shard_map/all_to_all | solution.py:426
  97.8 4.5 all-to-all-start.2
  102.6 15.0 %collective-permute-done = bf16[256,2048]{1,0:T(8,128)(2,1)} collective-permute-done((bf16[256,2048]{1,0:T(8,128)(2,1)S(1)}, bf16[256,2048]{1,0:T(8,128)(2,1)}, u32[]{:S(2)}, u32[]{:S(2)}) %collective-permute-start) | collective-permute-done | bytes 1048608 | tf_op jit(solution)/shard_map/ppermute | solution.py:27
  127.4 3.4 collective-permute-done.2
  138.9 13.0 %project.1 = (f32[2048,768]{1,0:T(8,128)}, f32[2,2048]{1,0:T(2,128)}) custom-call(bf16[2048,2048]{1,0:T(8,128)(2,1)} %constant_dynamic-update-slice_fusion.refs_0_, bf16[2048,768]{1,0:T(8,128)(2,1)} %bitcast.133), custom_call_target="tpu_custom_call" | custom-call | flops 6442450944 | bytes 17825792 | tf_op jit(solution)/shard_map/project/pallas_call | solution.py:78
  159.2 5.0 all_to_all.81
  165.1 15.3 %attend.1 = bf16[2048,256]{1,0:T(8,128)(2,1)} custom-call(f32[2048,768]{1,0:T(8,128)} %get-tuple-element.49.refs_0_, f32[2,2048]{1,0:T(2,128)} %rsqrt.26.refs_1_, f32[2,256]{1,0:T(2,128)} %bitcast.125, f32[128,128]{1,0:T(8,128)} %get-tuple-element.255.refs_3_, f32[128,128]{1,0:T(8,128)} %get-tuple-element.256.refs_4_), custom_call_target="tpu_custom_call" | custom-call | flops 268435456 | bytes 7340032 | tf_op jit(solution)/shard_map/attend/pallas_call | solution.py:191
  180.4 3.6 convolution_convert_fusion.1
  196.2 10.7 %collective-permute-done.18 = bf16[128,2048]{1,0:T(8,128)(2,1)S(1)} collective-permute-done((bf16[128,2048]{1,0:T(8,128)(2,1)S(1)}, bf16[128,2048]{1,0:T(8,128)(2,1)S(1)}, u32[]{:S(2)}, u32[]{:S(2)}) %collective-permute-start.18) | collective-permute-done | bytes 524320 | tf_op jit(solution)/shard_map/ppermute | solution.py:27
  211.8 20.0 %collective-permute-done.19 = bf16[256,2048]{1,0:T(8,128)(2,1)} collective-permute-done((bf16[256,2048]{1,0:T(8,128)(2,1)S(1)}, bf16[256,2048]{1,0:T(8,128)(2,1)}, u32[]{:S(2)}, u32[]{:S(2)}) %collective-permute-start.19) | collective-permute-done | bytes 1048608 | tf_op jit(solution)/shard_map/ppermute | solution.py:27
  231.8 2.5 collective-permute-done.22
  234.3 2.9 multiply_reduce_fusion.5
  240.8 22.3 %collective-permute-done.23 = bf16[256,2048]{1,0:T(8,128)(2,1)S(1)} collective-permute-done((bf16[256,2048]{1,0:T(8,128)(2,1)}, bf16[256,2048]{1,0:T(8,128)(2,1)S(1)}, u32[]{:S(2)}, u32[]{:S(2)}) %collective-permute-start.23) | collective-permute-done | bytes 1048608 | tf_op jit(solution)/shard_map/ppermute | solution.py:27
  270.9 5.4 collective-permute-done.25
  287.3 24.5 %gated.1 = (f32[2048,2048]{1,0:T(8,128)}, bf16[2048,1024]{1,0:T(8,128)(2,1)}) custom-call(bf16[2048,2048]{1,0:T(8,128)(2,1)} %constant_dynamic-update-slice_fusion.10.refs_0_, bf16[2048,2048]{1,0:T(8,128)(2,1)} %all-gather.7.cloned.1.call-done.refs_1_.refs_4_), custom_call_target="tpu_custom_call" | custom-call | flops 17179869184 | bytes 37748736 | tf_op jit(solution)/shard_map/gated/pallas_call | solution.py:300
  311.9 4.9 all-gather.9.cloned.1.call-done.refs_1_
  316.8 7.4 convolution_convert_fusion.4
  331.6 5.3 collective-permute-done.35
  340.2 10.1 %collective-permute-done.36 = bf16[256,1024]{1,0:T(8,128)(2,1)S(1)} collective-permute-done((bf16[256,1024]{1,0:T(8,128)(2,1)S(1)}, bf16[256,1024]{1,0:T(8,128)(2,1)S(1)}, u32[]{:S(2)}, u32[]{:S(2)}) %collective-permute-start.36) | collective-permute-done | bytes 524320 | tf_op jit(solution)/shard_map/ppermute | solution.py:27
  350.3 2.4 collective-permute-done.39
  354.0 9.5 %all-gather.11.cloned.1.call-done.refs_2_ = bf16[1024,1024]{1,0:T(8,128)(2,1)} async-done(((bf16[256,1024]{1,0:T(8,128)(2,1)}), bf16[1024,1024]{1,0:T(8,128)(2,1)}) %all-gather.11.cloned.1.call-update) | async-done | bytes 2097168 | tf_op jit(solution)/shard_map/all_gather | solution.py:458
  363.5 7.4 convolution_convert_fusion.3
  383.0 3.0 collective-permute-done.43
  394.1 7.3 collective-permute-done.44
  401.4 3.6 collective-permute-done.47
  413.7 21.8 %collective-permute-done.48 = bf16[256,2048]{1,0:T(8,128)(2,1)S(1)} collective-permute-done((bf16[256,2048]{1,0:T(8,128)(2,1)S(1)}, bf16[256,2048]{1,0:T(8,128)(2,1)S(1)}, u32[]{:S(2)}, u32[]{:S(2)}) %collective-permute-start.48) | collective-permute-done | bytes 1048608 | tf_op jit(solution)/shard_map/ppermute | solution.py:27
  438.7 9.5 %collective-permute-done.50 = bf16[128,2048]{1,0:T(8,128)(2,1)S(1)} collective-permute-done((bf16[128,2048]{1,0:T(8,128)(2,1)S(1)}, bf16[128,2048]{1,0:T(8,128)(2,1)S(1)}, u32[]{:S(2)}, u32[]{:S(2)}) %collective-permute-start.50) | collective-permute-done | bytes 524320 | tf_op jit(solution)/shard_map/ppermute | solution.py:27
  450.9 3.3 copy-done.30
  454.2 11.0 %convolution_convert_fusion.2 = bf16[1024,2048]{1,0:T(8,128)(2,1)} fusion(bf16[2048,1024]{1,0:T(8,128)(2,1)S(1)} %copy-done.39, bf16[2048,2048]{1,0:T(8,128)(2,1)S(1)} %constant_dynamic-update-slice_fusion.20.refs_0_), kind=kOutput, calls=%fused_computation.5 | convolution fusion | flops 8592031744 | bytes 16777216 | tf_op jit(solution)/shard_map/dot_general | solution.py:496
  465.3 37.4 %gated_back.1 = (bf16[2048,2048]{1,0:T(8,128)(2,1)}, bf16[2048,2048]{1,0:T(8,128)(2,1)}) custom-call(bf16[2048,2048]{1,0:T(8,128)(2,1)} %copy-done.30, bf16[1024,1024]{1,0:T(8,128)(2,1)} %all-gather.9.cloned.1.call-done.refs_1_, bf16[1024,1024]{1,0:T(8,128)(2,1)} %all-gather.11.cloned.1.call-done.refs_2_, f32[2048,2048]{1,0:T(8,128)} %get-tuple-element.57.refs_3_, ...), custom_call_target="tpu_custom_call" | custom-call | flops 25769803776 | bytes 54525952 | tf_op jit(solution)/shard_map/gated_back/pallas_call | solution.py:337
  502.7 4.0 fusion.19
  512.3 5.1 convert_add_fusion.3
  520.4 20.6 %convolution_convert_fusion = bf16[2048,2048]{1,0:T(8,128)(2,1)} fusion(bf16[2048,2048]{1,0:T(8,128)(2,1)S(1)} %copy-done.40, bf16[2048,2048]{1,0:T(8,128)(2,1)S(1)} %bitcast.124), kind=kOutput, calls=%fused_computation.3 | convolution fusion | flops 17184063488 | bytes 25165824 | tf_op jit(solution)/shard_map/dot_general | solution.py:502
  549.3 21.9 %collective-permute-done.62 = bf16[256,2048]{1,0:T(8,128)(2,1)S(1)} collective-permute-done((bf16[256,2048]{1,0:T(8,128)(2,1)S(1)}, bf16[256,2048]{1,0:T(8,128)(2,1)S(1)}, u32[]{:S(2)}, u32[]{:S(2)}) %collective-permute-start.62) | collective-permute-done | bytes 1048608 | tf_op jit(solution)/shard_map/ppermute | solution.py:27
  572.7 4.2 multiply_reduce_fusion.1
  580.0 22.0 %collective-permute-done.65 = bf16[256,2048]{1,0:T(8,128)(2,1)S(1)} collective-permute-done((bf16[256,2048]{1,0:T(8,128)(2,1)S(1)}, bf16[256,2048]{1,0:T(8,128)(2,1)S(1)}, u32[]{:S(2)}, u32[]{:S(2)}) %collective-permute-start.65) | collective-permute-done | bytes 1048608 | tf_op jit(solution)/shard_map/ppermute | solution.py:27
  605.4 9.2 %collective-permute-done.67 = bf16[128,2048]{1,0:T(8,128)(2,1)S(1)} collective-permute-done((bf16[128,2048]{1,0:T(8,128)(2,1)S(1)}, bf16[128,2048]{1,0:T(8,128)(2,1)S(1)}, u32[]{:S(2)}, u32[]{:S(2)}) %collective-permute-start.67) | collective-permute-done | bytes 524320 | tf_op jit(solution)/shard_map/ppermute | solution.py:27
  617.8 2.3 convolution_convert_fusion.7
  620.2 3.4 convolution_convert_fusion.6.refs_5_
  623.5 20.6 %attend_back.1 = (f32[2048,512]{1,0:T(8,128)}, bf16[2048,256]{1,0:T(8,128)(2,1)}, f32[2,2048]{1,0:T(2,128)}, f32[2,256]{1,0:T(2,128)}) custom-call(f32[2048,768]{1,0:T(8,128)} %get-tuple-element.49.refs_0_, f32[2,2048]{1,0:T(2,128)} %rsqrt.26.refs_1_, f32[2,256]{1,0:T(2,128)} %bitcast.126, f32[128,128]{1,0:T(8,128)} %get-tuple-element.255.refs_3_, ...), custom_call_target="tpu_custom_call" | custom-call | flops 671088640 | bytes 13631488 | tf_op jit(solution)/shard_map/attend_back/pallas_call | solution.py:209
  647.1 2.9 collective-permute-done.75
  652.2 4.8 all_to_all.82
  659.0 14.3 %finish.1 = (bf16[2048,768]{1,0:T(8,128)(2,1)}, bf16[2048,2048]{1,0:T(8,128)(2,1)}) custom-call(f32[2048,768]{1,0:T(8,128)} %get-tuple-element.49.refs_0_, f32[2,2048]{1,0:T(2,128)} %rsqrt.26.refs_1_, f32[2,2048]{1,0:T(2,128)} %mul.240.refs_2_, f32[2048,512]{1,0:T(8,128)} %get-tuple-element.66.refs_3_, bf16[2048,256]{1,0:T(8,128)(2,1)} %get-tuple-element.67.refs_4_, ...), custom_call_target="tpu_custom_call" | custom-call | flops 6442450944 | bytes 23068672 | tf_op jit(solution)/shard_map/finish/pallas_call | solution.py:232
  673.3 11.5 %convolution_convert_fusion.5 = bf16[2048,768]{1,0:T(8,128)(2,1)} fusion(bf16[2048,2048]{1,0:T(8,128)(2,1)} %constant_dynamic-update-slice_fusion.refs_0_, bf16[2048,768]{1,0:T(8,128)(2,1)} %get-tuple-element.70), kind=kOutput, calls=%fused_computation.8 | convolution fusion | flops 6444023808 | bytes 14680064 | tf_op jit(solution)/shard_map/dot_general | solution.py:502
  687.1 3.7 fusion.18
  696.4 3.1 convert_add_fusion.1
  703.0 10.7 %collective-permute-done.80 = bf16[128,2048]{1,0:T(8,128)(2,1)S(1)} collective-permute-done((bf16[128,2048]{1,0:T(8,128)(2,1)S(1)}, bf16[128,2048]{1,0:T(8,128)(2,1)S(1)}, u32[]{:S(2)}, u32[]{:S(2)}) %collective-permute-start.80) | collective-permute-done | bytes 524320 | tf_op jit(solution)/shard_map/ppermute | solution.py:27
  720.3 3.7 all-to-all-start.6
  724.0 26.9 %reduce-scatter.9.cloned.1.call-done = bf16[512,768]{1,0:T(8,128)(2,1)} async-done(((bf16[2048,768]{1,0:T(8,128)(2,1)}), bf16[512,768]{1,0:T(8,128)(2,1)}) %reduce-scatter.9.cloned.1.call-update) | async-done | bytes 786448 | tf_op jit(solution)/shard_map/reduce_scatter | solution.py:507
  753.9 3.0 add_convert_fusion
  762.5 4.6 all-to-all-start.5
  767.4 2.7 collective-permute-start.90
  773.0 9.0 %collective-permute-done.90 = bf16[1,64,768]{2,1,0:T(8,128)(2,1)S(1)} collective-permute-done((bf16[1,64,768]{2,1,0:T(8,128)(2,1)S(1)}, bf16[1,64,768]{2,1,0:T(8,128)(2,1)S(1)}, u32[]{:S(2)}, u32[]{:S(2)}) %collective-permute-start.90) | collective-permute-done | bytes 98336 | tf_op jit(solution)/shard_map/ppermute | solution.py:370
  787.7 5.7 all-to-all-done.5
  794.4 2.5 scatter_fusion
  796.9 3.8 convert_bitcast_fusion
  800.7 2.9 copy.140
  (466 shorter events, 213.1 us)
Async XLA Ops:
  7.2 18.9 %collective-permute-start.9 = (bf16[64,2048]{1,0:T(8,128)(2,1)}, bf16[64,2048]{1,0:T(8,128)(2,1)S(1)}, u32[]{:S(2)}, u32[]{:S(2)}) collective-permute-start(bf16[64,2048]{1,0:T(8,128)(2,1)} %param.21), channel_id=1, source_target_pairs={{0,8},{8,16},{16,24},{24,0},{1,9},{9,17},{17,25},{25,1},{2,10},{10... | collective-permute-start | bytes 786440 | tf_op jit(solution)/shard_map/ppermute | solution.py:360
  10.3 19.9 %collective-permute-start.10 = (bf16[64,2048]{1,0:T(8,128)(2,1)}, bf16[64,2048]{1,0:T(8,128)(2,1)S(1)}, u32[]{:S(2)}, u32[]{:S(2)}) collective-permute-start(bf16[64,2048]{1,0:T(8,128)(2,1)} %param.21), channel_id=1, source_target_pairs={{0,16},{8,24},{16,0},{24,8},{1,17},{9,25},{17,1},{25,9},{2,18},{10... | collective-permute-start | bytes 786440 | tf_op jit(solution)/shard_map/ppermute | solution.py:360
  12.9 17.4 %collective-permute-start.11 = (bf16[64,2048]{1,0:T(8,128)(2,1)}, bf16[64,2048]{1,0:T(8,128)(2,1)S(1)}, u32[]{:S(2)}, u32[]{:S(2)}) collective-permute-start(bf16[64,2048]{1,0:T(8,128)(2,1)} %param.21), channel_id=1, source_target_pairs={{0,24},{8,0},{16,8},{24,16},{1,25},{9,1},{17,9},{25,17},{2,26},{10... | collective-permute-start | bytes 786440 | tf_op jit(solution)/shard_map/ppermute | solution.py:360
  22.1 16.3 %all-to-all-start.1 = ((bf16[8,64,768]{2,1,0:T(8,128)(2,1)}), bf16[8,64,768]{2,1,0:T(8,128)(2,1)S(1)}, u32[]{:S(2)}, u32[]{:S(2)}) async-start(bf16[8,64,768]{2,1,0:T(8,128)(2,1)} %pad_maximum_fusion.8), calls=%async_computation.1 | async-start | bytes 1572864 | tf_op jit(solution)/shard_map/all_to_all | solution.py:431
  25.9 113.0 %all-gather.5.cloned.1.call-start = ((), (), s32[]{:S(2)}) async-start(), calls=%async_computation.11 | async-start | bytes 3932160 | tf_op jit(solution)/shard_map/all_gather | solution.py:449
  39.4 53.3 %all-to-all-start = ((bf16[64,4,2048]{2,1,0:T(4,128)(2,1)}), bf16[64,4,2048]{2,1,0:T(4,128)(2,1)S(1)}, u32[]{:S(2)}, u32[]{:S(2)}) async-start(bf16[64,4,2048]{2,1,0:T(4,128)(2,1)} %broadcast_select_fusion), calls=%async_computation | async-start | bytes 2097152 | tf_op jit(solution)/shard_map/all_to_all | solution.py:426
  42.0 245.3 %all-gather.7.cloned.1.call-start = ((), (), s32[]{:S(2)}) async-start(), calls=%async_computation.12 | async-start | bytes 10485760 | tf_op jit(solution)/shard_map/all_gather | solution.py:455
  93.5 24.2 %collective-permute-start = (bf16[256,2048]{1,0:T(8,128)(2,1)S(1)}, bf16[256,2048]{1,0:T(8,128)(2,1)}, u32[]{:S(2)}, u32[]{:S(2)}) collective-permute-start(bf16[256,2048]{1,0:T(8,128)(2,1)S(1)} %reshape.237), channel_id=1, source_target_pairs={{0,2},{2,0},{1,3},{3,1},{4,6},{6,4},{5,7},{7,5},{8,10},{10,8},{9,1... | collective-permute-start | bytes 3145736 | tf_op jit(solution)/shard_map/ppermute | solution.py:27
  95.2 25.6 %collective-permute-start.1 = (bf16[256,2048]{1,0:T(8,128)(2,1)S(1)}, bf16[256,2048]{1,0:T(8,128)(2,1)S(1)}, u32[]{:S(2)}, u32[]{:S(2)}) collective-permute-start(bf16[256,2048]{1,0:T(8,128)(2,1)S(1)} %reshape.237), channel_id=1, source_target_pairs={{0,4},{4,0},{1,5},{5,1},{2,6},{6,2},{3,7},{7,3},{8,12},{12,8},{9,1... | collective-permute-start | bytes 3145736 | tf_op jit(solution)/shard_map/ppermute | solution.py:27
  97.8 58.6 %all-to-all-start.2 = ((bf16[32,2,128]{2,1,0:T(2,128)(2,1)}), bf16[32,2,128]{2,1,0:T(2,128)(2,1)S(1)}, u32[]{:S(2)}, u32[]{:S(2)}) async-start(bf16[32,2,128]{2,1,0:T(2,128)(2,1)} %reshape.308), calls=%async_computation.2 | async-start | bytes 32768 | tf_op jit(solution)/shard_map/all_to_all | solution.py:434
  102.3 214.5 %all-gather.9.cloned.1.call-start = ((), (), s32[]{:S(2)}) async-start(), calls=%async_computation.13 | async-start | bytes 2621440 | tf_op jit(solution)/shard_map/all_gather | solution.py:458
  102.3 31.7 %collective-permute-start.4 = (bf16[256,2048]{1,0:T(8,128)(2,1)S(1)}, bf16[256,2048]{1,0:T(8,128)(2,1)S(1)}, u32[]{:S(2)}, u32[]{:S(2)}) collective-permute-start(bf16[256,2048]{1,0:T(8,128)(2,1)S(1)} %reshape.237), channel_id=1, source_target_pairs={{0,1},{1,0},{2,3},{3,2},{4,5},{5,4},{6,7},{7,6},{8,9},{9,8},{10,11... | collective-permute-start | bytes 3145736 | tf_op jit(solution)/shard_map/ppermute | solution.py:27
  118.7 12.0 %collective-permute-start.2 = (bf16[128,2048]{1,0:T(8,128)(2,1)S(1)}, bf16[128,2048]{1,0:T(8,128)(2,1)S(1)}, u32[]{:S(2)}, u32[]{:S(2)}) collective-permute-start(bf16[128,2048]{1,0:T(8,128)(2,1)S(1)} %slice.395), channel_id=1, source_target_pairs={{0,4},{4,0},{1,5},{5,1},{2,6},{6,2},{3,7},{7,3},{8,12},{12,8},{9,1... | collective-permute-start | bytes 1572872 | tf_op jit(solution)/shard_map/ppermute | solution.py:27
  123.5 11.6 %collective-permute-start.5 = (bf16[256,2048]{1,0:T(8,128)(2,1)}, bf16[256,2048]{1,0:T(8,128)(2,1)S(1)}, u32[]{:S(2)}, u32[]{:S(2)}) collective-permute-start(bf16[256,2048]{1,0:T(8,128)(2,1)} %collective-permute-done), channel_id=1, source_target_pairs={{0,1},{1,0},{2,3},{3,2},{4,5},{5,4},{6,7},{7,6},{8,9},{9,8},{10,11... | collective-permute-start | bytes 3145736 | tf_op jit(solution)/shard_map/ppermute | solution.py:27
  123.5 12.6 %collective-permute-start.6 = (bf16[256,2048]{1,0:T(8,128)(2,1)S(1)}, bf16[256,2048]{1,0:T(8,128)(2,1)S(1)}, u32[]{:S(2)}, u32[]{:S(2)}) collective-permute-start(bf16[256,2048]{1,0:T(8,128)(2,1)S(1)} %collective-permute-done.1), channel_id=1, source_target_pairs={{0,1},{1,0},{2,3},{3,2},{4,5},{5,4},{6,7},{7,6},{8,9},{9,8},{10,11... | collective-permute-start | bytes 3145736 | tf_op jit(solution)/shard_map/ppermute | solution.py:27
  192.9 14.0 %collective-permute-start.18 = (bf16[128,2048]{1,0:T(8,128)(2,1)S(1)}, bf16[128,2048]{1,0:T(8,128)(2,1)S(1)}, u32[]{:S(2)}, u32[]{:S(2)}) collective-permute-start(bf16[128,2048]{1,0:T(8,128)(2,1)S(1)} %get-tuple-element.225), channel_id=1, source_target_pairs={{0,4},{4,0},{1,5},{5,1},{2,6},{6,2},{3,7},{7,3},{8,12},{12,8},{9,1... | collective-permute-start | bytes 1572872 | tf_op jit(solution)/shard_map/ppermute | solution.py:27
  194.5 17.3 %collective-permute-start.15 = (bf16[256,2048]{1,0:T(8,128)(2,1)}, bf16[256,2048]{1,0:T(8,128)(2,1)}, u32[]{:S(2)}, u32[]{:S(2)}) collective-permute-start(bf16[256,2048]{1,0:T(8,128)(2,1)} %get-tuple-element.195), channel_id=1, source_target_pairs={{0,1},{1,0},{2,3},{3,2},{4,5},{5,4},{6,7},{7,6},{8,9},{9,8},{10,11... | collective-permute-start | bytes 3145736 | tf_op jit(solution)/shard_map/ppermute | solution.py:27
  194.6 14.4 %collective-permute-start.21 = (bf16[128,2048]{1,0:T(8,128)(2,1)S(1)}, bf16[128,2048]{1,0:T(8,128)(2,1)S(1)}, u32[]{:S(2)}, u32[]{:S(2)}) collective-permute-start(bf16[128,2048]{1,0:T(8,128)(2,1)S(1)} %get-tuple-element.226), channel_id=1, source_target_pairs={{0,2},{2,0},{1,3},{3,1},{4,6},{6,4},{5,7},{7,5},{8,10},{10,8},{9,1... | collective-permute-start | bytes 1572872 | tf_op jit(solution)/shard_map/ppermute | solution.py:27
  207.1 24.6 %collective-permute-start.19 = (bf16[256,2048]{1,0:T(8,128)(2,1)S(1)}, bf16[256,2048]{1,0:T(8,128)(2,1)}, u32[]{:S(2)}, u32[]{:S(2)}) collective-permute-start(bf16[256,2048]{1,0:T(8,128)(2,1)S(1)} %pad_maximum_fusion.2), channel_id=1, source_target_pairs={{0,2},{2,0},{1,3},{3,1},{4,6},{6,4},{5,7},{7,5},{8,10},{10,8},{9,1... | collective-permute-start | bytes 3145736 | tf_op jit(solution)/shard_map/ppermute | solution.py:27
  209.2 25.1 %collective-permute-start.22 = (bf16[256,2048]{1,0:T(8,128)(2,1)S(1)}, bf16[256,2048]{1,0:T(8,128)(2,1)}, u32[]{:S(2)}, u32[]{:S(2)}) collective-permute-start(bf16[256,2048]{1,0:T(8,128)(2,1)S(1)} %pad_maximum_fusion.3), channel_id=1, source_target_pairs={{0,4},{4,0},{1,5},{5,1},{2,6},{6,2},{3,7},{7,3},{8,12},{12,8},{9,1... | collective-permute-start | bytes 3145736 | tf_op jit(solution)/shard_map/ppermute | solution.py:27
  211.6 151.9 %all-gather.11.cloned.1.call-start = ((), (), s32[]{:S(2)}) async-start(), calls=%async_computation.14 | async-start | bytes 2621440 | tf_op jit(solution)/shard_map/all_gather | solution.py:458
  238.8 24.2 %collective-permute-start.23 = (bf16[256,2048]{1,0:T(8,128)(2,1)}, bf16[256,2048]{1,0:T(8,128)(2,1)S(1)}, u32[]{:S(2)}, u32[]{:S(2)}) collective-permute-start(bf16[256,2048]{1,0:T(8,128)(2,1)} %get-tuple-element.178), channel_id=1, source_target_pairs={{0,2},{2,0},{1,3},{3,1},{4,6},{6,4},{5,7},{7,5},{8,10},{10,8},{9,1... | collective-permute-start | bytes 3145736 | tf_op jit(solution)/shard_map/ppermute | solution.py:27
  240.3 24.0 %collective-permute-start.24 = (bf16[256,2048]{1,0:T(8,128)(2,1)}, bf16[256,2048]{1,0:T(8,128)(2,1)S(1)}, u32[]{:S(2)}, u32[]{:S(2)}) collective-permute-start(bf16[256,2048]{1,0:T(8,128)(2,1)} %get-tuple-element.178), channel_id=1, source_target_pairs={{0,4},{4,0},{1,5},{5,1},{2,6},{6,2},{3,7},{7,3},{8,12},{12,8},{9,1... | collective-permute-start | bytes 3145736 | tf_op jit(solution)/shard_map/ppermute | solution.py:27
  240.8 40.4 %collective-permute-start.27 = (bf16[256,2048]{1,0:T(8,128)(2,1)}, bf16[256,2048]{1,0:T(8,128)(2,1)}, u32[]{:S(2)}, u32[]{:S(2)}) collective-permute-start(bf16[256,2048]{1,0:T(8,128)(2,1)} %get-tuple-element.178), channel_id=1, source_target_pairs={{0,1},{1,0},{2,3},{3,2},{4,5},{5,4},{6,7},{7,6},{8,9},{9,8},{10,11... | collective-permute-start | bytes 3145736 | tf_op jit(solution)/shard_map/ppermute | solution.py:27
  264.0 12.3 %collective-permute-start.25 = (bf16[128,2048]{1,0:T(8,128)(2,1)}, bf16[128,2048]{1,0:T(8,128)(2,1)}, u32[]{:S(2)}, u32[]{:S(2)}) collective-permute-start(bf16[128,2048]{1,0:T(8,128)(2,1)} %slice.413), channel_id=1, source_target_pairs={{0,4},{4,0},{1,5},{5,1},{2,6},{6,2},{3,7},{7,3},{8,12},{12,8},{9,1... | collective-permute-start | bytes 1572872 | tf_op jit(solution)/shard_map/ppermute | solution.py:27
  265.1 12.2 %collective-permute-start.26 = (bf16[128,2048]{1,0:T(8,128)(2,1)}, bf16[128,2048]{1,0:T(8,128)(2,1)}, u32[]{:S(2)}, u32[]{:S(2)}) collective-permute-start(bf16[128,2048]{1,0:T(8,128)(2,1)} %slice.414), channel_id=1, source_target_pairs={{0,2},{2,0},{1,3},{3,1},{4,6},{6,4},{5,7},{7,5},{8,10},{10,8},{9,1... | collective-permute-start | bytes 1572872 | tf_op jit(solution)/shard_map/ppermute | solution.py:27
  266.8 274.2 %reduce-scatter.5.cloned.1.call-start = ((), (), s32[]{:S(2)}) async-start(), calls=%async_computation.15 | async-start | bytes 5242880 | tf_op jit(solution)/shard_map/reduce_scatter | solution.py:507
  266.9 16.7 %collective-permute-start.28 = (bf16[256,2048]{1,0:T(8,128)(2,1)}, bf16[256,2048]{1,0:T(8,128)(2,1)S(1)}, u32[]{:S(2)}, u32[]{:S(2)}) collective-permute-start(bf16[256,2048]{1,0:T(8,128)(2,1)} %copy-done.24), channel_id=1, source_target_pairs={{0,1},{1,0},{2,3},{3,2},{4,5},{5,4},{6,7},{7,6},{8,9},{9,8},{10,11... | collective-permute-start | bytes 3145736 | tf_op jit(solution)/shard_map/ppermute | solution.py:27
  266.9 17.7 %collective-permute-start.29 = (bf16[256,2048]{1,0:T(8,128)(2,1)S(1)}, bf16[256,2048]{1,0:T(8,128)(2,1)S(1)}, u32[]{:S(2)}, u32[]{:S(2)}) collective-permute-start(bf16[256,2048]{1,0:T(8,128)(2,1)S(1)} %collective-permute-done.24), channel_id=1, source_target_pairs={{0,1},{1,0},{2,3},{3,2},{4,5},{5,4},{6,7},{7,6},{8,9},{9,8},{10,11... | collective-permute-start | bytes 3145736 | tf_op jit(solution)/shard_map/ppermute | solution.py:27
  337.0 13.3 %collective-permute-start.36 = (bf16[256,1024]{1,0:T(8,128)(2,1)S(1)}, bf16[256,1024]{1,0:T(8,128)(2,1)S(1)}, u32[]{:S(2)}, u32[]{:S(2)}) collective-permute-start(bf16[256,1024]{1,0:T(8,128)(2,1)S(1)} %pad_maximum_fusion.9), channel_id=1, source_target_pairs={{0,2},{2,0},{1,3},{3,1},{4,6},{6,4},{5,7},{7,5},{8,10},{10,8},{9,1... | collective-permute-start | bytes 1572872 | tf_op jit(solution)/shard_map/ppermute | solution.py:27
  339.0 13.7 %collective-permute-start.39 = (bf16[256,1024]{1,0:T(8,128)(2,1)S(1)}, bf16[256,1024]{1,0:T(8,128)(2,1)S(1)}, u32[]{:S(2)}, u32[]{:S(2)}) collective-permute-start(bf16[256,1024]{1,0:T(8,128)(2,1)S(1)} %pad_maximum_fusion.10), channel_id=1, source_target_pairs={{0,4},{4,0},{1,5},{5,1},{2,6},{6,2},{3,7},{7,3},{8,12},{12,8},{9,1... | collective-permute-start | bytes 1572872 | tf_op jit(solution)/shard_map/ppermute | solution.py:27
  379.1 15.0 %collective-permute-start.40 = (bf16[256,1024]{1,0:T(8,128)(2,1)}, bf16[256,1024]{1,0:T(8,128)(2,1)}, u32[]{:S(2)}, u32[]{:S(2)}) collective-permute-start(bf16[256,1024]{1,0:T(8,128)(2,1)} %get-tuple-element.202), channel_id=1, source_target_pairs={{0,1},{1,0},{2,3},{3,2},{4,5},{5,4},{6,7},{7,6},{8,9},{9,8},{10,11... | collective-permute-start | bytes 1572872 | tf_op jit(solution)/shard_map/ppermute | solution.py:27
  388.0 13.5 %collective-permute-start.44 = (bf16[256,1024]{1,0:T(8,128)(2,1)}, bf16[256,1024]{1,0:T(8,128)(2,1)}, u32[]{:S(2)}, u32[]{:S(2)}) collective-permute-start(bf16[256,1024]{1,0:T(8,128)(2,1)} %pad_maximum_fusion.11), channel_id=1, source_target_pairs={{0,2},{2,0},{1,3},{3,1},{4,6},{6,4},{5,7},{7,5},{8,10},{10,8},{9,1... | collective-permute-start | bytes 1572872 | tf_op jit(solution)/shard_map/ppermute | solution.py:27
  391.6 13.4 %collective-permute-start.47 = (bf16[256,1024]{1,0:T(8,128)(2,1)}, bf16[256,1024]{1,0:T(8,128)(2,1)}, u32[]{:S(2)}, u32[]{:S(2)}) collective-permute-start(bf16[256,1024]{1,0:T(8,128)(2,1)} %pad_maximum_fusion.12), channel_id=1, source_target_pairs={{0,4},{4,0},{1,5},{5,1},{2,6},{6,2},{3,7},{7,3},{8,12},{12,8},{9,1... | collective-permute-start | bytes 1572872 | tf_op jit(solution)/shard_map/ppermute | solution.py:27
  411.6 23.8 %collective-permute-start.48 = (bf16[256,2048]{1,0:T(8,128)(2,1)S(1)}, bf16[256,2048]{1,0:T(8,128)(2,1)S(1)}, u32[]{:S(2)}, u32[]{:S(2)}) collective-permute-start(bf16[256,2048]{1,0:T(8,128)(2,1)S(1)} %get-tuple-element.254), channel_id=1, source_target_pairs={{0,2},{2,0},{1,3},{3,1},{4,6},{6,4},{5,7},{7,5},{8,10},{10,8},{9,1... | collective-permute-start | bytes 3145736 | tf_op jit(solution)/shard_map/ppermute | solution.py:27
  413.3 24.5 %collective-permute-start.49 = (bf16[256,2048]{1,0:T(8,128)(2,1)S(1)}, bf16[256,2048]{1,0:T(8,128)(2,1)S(1)}, u32[]{:S(2)}, u32[]{:S(2)}) collective-permute-start(bf16[256,2048]{1,0:T(8,128)(2,1)S(1)} %get-tuple-element.254), channel_id=1, source_target_pairs={{0,4},{4,0},{1,5},{5,1},{2,6},{6,2},{3,7},{7,3},{8,12},{12,8},{9,1... | collective-permute-start | bytes 3145736 | tf_op jit(solution)/shard_map/ppermute | solution.py:27
  413.7 35.1 %collective-permute-start.52 = (bf16[256,2048]{1,0:T(8,128)(2,1)S(1)}, bf16[256,2048]{1,0:T(8,128)(2,1)S(1)}, u32[]{:S(2)}, u32[]{:S(2)}) collective-permute-start(bf16[256,2048]{1,0:T(8,128)(2,1)S(1)} %get-tuple-element.254), channel_id=1, source_target_pairs={{0,1},{1,0},{2,3},{3,2},{4,5},{5,4},{6,7},{7,6},{8,9},{9,8},{10,11... | collective-permute-start | bytes 3145736 | tf_op jit(solution)/shard_map/ppermute | solution.py:27
  435.5 12.6 %collective-permute-start.50 = (bf16[128,2048]{1,0:T(8,128)(2,1)S(1)}, bf16[128,2048]{1,0:T(8,128)(2,1)S(1)}, u32[]{:S(2)}, u32[]{:S(2)}) collective-permute-start(bf16[128,2048]{1,0:T(8,128)(2,1)S(1)} %slice.444), channel_id=1, source_target_pairs={{0,4},{4,0},{1,5},{5,1},{2,6},{6,2},{3,7},{7,3},{8,12},{12,8},{9,1... | collective-permute-start | bytes 1572872 | tf_op jit(solution)/shard_map/ppermute | solution.py:27
  465.2 221.8 %reduce-scatter.7.cloned.1.call-start = ((), (), s32[]{:S(2)}) async-start(), calls=%async_computation.16 | async-start | bytes 10485760 | tf_op jit(solution)/shard_map/reduce_scatter | solution.py:507
  518.5 22.6 %collective-permute-start.60 = (bf16[128,2048]{1,0:T(8,128)(2,1)}, bf16[128,2048]{1,0:T(8,128)(2,1)}, u32[]{:S(2)}, u32[]{:S(2)}) collective-permute-start(bf16[128,2048]{1,0:T(8,128)(2,1)} %get-tuple-element.222), channel_id=1, source_target_pairs={{0,2},{2,0},{1,3},{3,1},{4,6},{6,4},{5,7},{7,5},{8,10},{10,8},{9,1... | collective-permute-start | bytes 1572872 | tf_op jit(solution)/shard_map/ppermute | solution.py:27
  519.3 21.7 %collective-permute-start.61 = (bf16[128,2048]{1,0:T(8,128)(2,1)}, bf16[128,2048]{1,0:T(8,128)(2,1)}, u32[]{:S(2)}, u32[]{:S(2)}) collective-permute-start(bf16[128,2048]{1,0:T(8,128)(2,1)} %get-tuple-element.221), channel_id=1, source_target_pairs={{0,4},{4,0},{1,5},{5,1},{2,6},{6,2},{3,7},{7,3},{8,12},{12,8},{9,1... | collective-permute-start | bytes 1572872 | tf_op jit(solution)/shard_map/ppermute | solution.py:27
  541.1 209.8 %reduce-scatter.9.cloned.1.call-start = ((), (), s32[]{:S(2)}) async-start(), calls=%async_computation.17 | async-start | bytes 3932160 | tf_op jit(solution)/shard_map/reduce_scatter | solution.py:507
  545.7 25.5 %collective-permute-start.62 = (bf16[256,2048]{1,0:T(8,128)(2,1)S(1)}, bf16[256,2048]{1,0:T(8,128)(2,1)S(1)}, u32[]{:S(2)}, u32[]{:S(2)}) collective-permute-start(bf16[256,2048]{1,0:T(8,128)(2,1)S(1)} %pad_maximum_fusion.4), channel_id=1, source_target_pairs={{0,2},{2,0},{1,3},{3,1},{4,6},{6,4},{5,7},{7,5},{8,10},{10,8},{9,1... | collective-permute-start | bytes 3145736 | tf_op jit(solution)/shard_map/ppermute | solution.py:27
  547.3 25.3 %collective-permute-start.64 = (bf16[256,2048]{1,0:T(8,128)(2,1)S(1)}, bf16[256,2048]{1,0:T(8,128)(2,1)S(1)}, u32[]{:S(2)}, u32[]{:S(2)}) collective-permute-start(bf16[256,2048]{1,0:T(8,128)(2,1)S(1)} %pad_maximum_fusion.5), channel_id=1, source_target_pairs={{0,4},{4,0},{1,5},{5,1},{2,6},{6,2},{3,7},{7,3},{8,12},{12,8},{9,1... | collective-permute-start | bytes 3145736 | tf_op jit(solution)/shard_map/ppermute | solution.py:27
  577.4 24.6 %collective-permute-start.65 = (bf16[256,2048]{1,0:T(8,128)(2,1)S(1)}, bf16[256,2048]{1,0:T(8,128)(2,1)S(1)}, u32[]{:S(2)}, u32[]{:S(2)}) collective-permute-start(bf16[256,2048]{1,0:T(8,128)(2,1)S(1)} %get-tuple-element.175), channel_id=1, source_target_pairs={{0,2},{2,0},{1,3},{3,1},{4,6},{6,4},{5,7},{7,5},{8,10},{10,8},{9,1... | collective-permute-start | bytes 3145736 | tf_op jit(solution)/shard_map/ppermute | solution.py:27
  579.0 24.6 %collective-permute-start.66 = (bf16[256,2048]{1,0:T(8,128)(2,1)S(1)}, bf16[256,2048]{1,0:T(8,128)(2,1)S(1)}, u32[]{:S(2)}, u32[]{:S(2)}) collective-permute-start(bf16[256,2048]{1,0:T(8,128)(2,1)S(1)} %get-tuple-element.175), channel_id=1, source_target_pairs={{0,4},{4,0},{1,5},{5,1},{2,6},{6,2},{3,7},{7,3},{8,12},{12,8},{9,1... | collective-permute-start | bytes 3145736 | tf_op jit(solution)/shard_map/ppermute | solution.py:27
  580.0 35.9 %collective-permute-start.69 = (bf16[256,2048]{1,0:T(8,128)(2,1)S(1)}, bf16[256,2048]{1,0:T(8,128)(2,1)S(1)}, u32[]{:S(2)}, u32[]{:S(2)}) collective-permute-start(bf16[256,2048]{1,0:T(8,128)(2,1)S(1)} %get-tuple-element.175), channel_id=1, source_target_pairs={{0,1},{1,0},{2,3},{3,2},{4,5},{5,4},{6,7},{7,6},{8,9},{9,8},{10,11... | collective-permute-start | bytes 3145736 | tf_op jit(solution)/shard_map/ppermute | solution.py:27
  602.0 12.6 %collective-permute-start.67 = (bf16[128,2048]{1,0:T(8,128)(2,1)S(1)}, bf16[128,2048]{1,0:T(8,128)(2,1)S(1)}, u32[]{:S(2)}, u32[]{:S(2)}) collective-permute-start(bf16[128,2048]{1,0:T(8,128)(2,1)S(1)} %slice.452), channel_id=1, source_target_pairs={{0,4},{4,0},{1,5},{5,1},{2,6},{6,2},{3,7},{7,3},{8,12},{12,8},{9,1... | collective-permute-start | bytes 1572872 | tf_op jit(solution)/shard_map/ppermute | solution.py:27
  603.7 12.1 %collective-permute-start.68 = (bf16[128,2048]{1,0:T(8,128)(2,1)S(1)}, bf16[128,2048]{1,0:T(8,128)(2,1)S(1)}, u32[]{:S(2)}, u32[]{:S(2)}) collective-permute-start(bf16[128,2048]{1,0:T(8,128)(2,1)S(1)} %slice.453), channel_id=1, source_target_pairs={{0,2},{2,0},{1,3},{3,1},{4,6},{6,4},{5,7},{7,5},{8,10},{10,8},{9,1... | collective-permute-start | bytes 1572872 | tf_op jit(solution)/shard_map/ppermute | solution.py:27
  604.6 11.6 %collective-permute-start.71 = (bf16[256,2048]{1,0:T(8,128)(2,1)S(1)}, bf16[256,2048]{1,0:T(8,128)(2,1)S(1)}, u32[]{:S(2)}, u32[]{:S(2)}) collective-permute-start(bf16[256,2048]{1,0:T(8,128)(2,1)S(1)} %collective-permute-done.66), channel_id=1, source_target_pairs={{0,1},{1,0},{2,3},{3,2},{4,5},{5,4},{6,7},{7,6},{8,9},{9,8},{10,11... | collective-permute-start | bytes 3145736 | tf_op jit(solution)/shard_map/ppermute | solution.py:27
  699.7 14.1 %collective-permute-start.80 = (bf16[128,2048]{1,0:T(8,128)(2,1)S(1)}, bf16[128,2048]{1,0:T(8,128)(2,1)S(1)}, u32[]{:S(2)}, u32[]{:S(2)}) collective-permute-start(bf16[128,2048]{1,0:T(8,128)(2,1)S(1)} %get-tuple-element.219), channel_id=1, source_target_pairs={{0,4},{4,0},{1,5},{5,1},{2,6},{6,2},{3,7},{7,3},{8,12},{12,8},{9,1... | collective-permute-start | bytes 1572872 | tf_op jit(solution)/shard_map/ppermute | solution.py:27
  701.3 51.7 %collective-permute-start.77 = (bf16[256,2048]{1,0:T(8,128)(2,1)}, bf16[256,2048]{1,0:T(8,128)(2,1)}, u32[]{:S(2)}, u32[]{:S(2)}) collective-permute-start(bf16[256,2048]{1,0:T(8,128)(2,1)} %get-tuple-element.181), channel_id=1, source_target_pairs={{0,1},{1,0},{2,3},{3,2},{4,5},{5,4},{6,7},{7,6},{8,9},{9,8},{10,11... | collective-permute-start | bytes 3145736 | tf_op jit(solution)/shard_map/ppermute | solution.py:27
  701.4 15.1 %collective-permute-start.83 = (bf16[128,2048]{1,0:T(8,128)(2,1)S(1)}, bf16[128,2048]{1,0:T(8,128)(2,1)S(1)}, u32[]{:S(2)}, u32[]{:S(2)}) collective-permute-start(bf16[128,2048]{1,0:T(8,128)(2,1)S(1)} %get-tuple-element.220), channel_id=1, source_target_pairs={{0,2},{2,0},{1,3},{3,1},{4,6},{6,4},{5,7},{7,5},{8,10},{10,8},{9,1... | collective-permute-start | bytes 1572872 | tf_op jit(solution)/shard_map/ppermute | solution.py:27
  715.0 38.0 %collective-permute-start.81 = (bf16[256,2048]{1,0:T(8,128)(2,1)}, bf16[256,2048]{1,0:T(8,128)(2,1)}, u32[]{:S(2)}, u32[]{:S(2)}) collective-permute-start(bf16[256,2048]{1,0:T(8,128)(2,1)} %pad_maximum_fusion.6), channel_id=1, source_target_pairs={{0,2},{2,0},{1,3},{3,1},{4,6},{6,4},{5,7},{7,5},{8,10},{10,8},{9,1... | collective-permute-start | bytes 3145736 | tf_op jit(solution)/shard_map/ppermute | solution.py:27
  717.8 36.1 %collective-permute-start.84 = (bf16[256,2048]{1,0:T(8,128)(2,1)}, bf16[256,2048]{1,0:T(8,128)(2,1)}, u32[]{:S(2)}, u32[]{:S(2)}) collective-permute-start(bf16[256,2048]{1,0:T(8,128)(2,1)} %pad_maximum_fusion.7), channel_id=1, source_target_pairs={{0,4},{4,0},{1,5},{5,1},{2,6},{6,2},{3,7},{7,3},{8,12},{12,8},{9,1... | collective-permute-start | bytes 3145736 | tf_op jit(solution)/shard_map/ppermute | solution.py:27
  720.3 42.1 %all-to-all-start.6 = ((f32[32,1,256]{2,1,0:T(1,128)}), f32[32,1,256]{2,1,0:T(1,128)S(1)}, u32[]{:S(2)}, u32[]{:S(2)}) async-start(f32[32,1,256]{2,1,0:T(1,128)} %reshape.310), calls=%async_computation.10 | async-start | bytes 65536 | tf_op jit(solution)/shard_map/all_to_all | solution.py:569
  753.0 14.4 %collective-permute-start.85 = (bf16[1,64,768]{2,1,0:T(8,128)(2,1)}, bf16[1,64,768]{2,1,0:T(8,128)(2,1)}, u32[]{:S(2)}, u32[]{:S(2)}) collective-permute-start(bf16[1,64,768]{2,1,0:T(8,128)(2,1)} %get-tuple-element.236), channel_id=1, source_target_pairs={{0,1},{1,0},{2,3},{3,2},{4,5},{5,4},{6,7},{7,6},{8,9},{9,8},{10,11... | collective-permute-start | bytes 294920 | tf_op jit(solution)/shard_map/ppermute | solution.py:370
  759.0 12.1 %collective-permute-start.86 = (bf16[1,64,768]{2,1,0:T(8,128)(2,1)}, bf16[1,64,768]{2,1,0:T(8,128)(2,1)}, u32[]{:S(2)}, u32[]{:S(2)}) collective-permute-start(bf16[1,64,768]{2,1,0:T(8,128)(2,1)} %get-tuple-element.235), channel_id=1, source_target_pairs={{0,2},{1,3},{2,0},{3,1},{4,6},{5,7},{6,4},{7,5},{8,10},{9,11},{10,... | collective-permute-start | bytes 294920 | tf_op jit(solution)/shard_map/ppermute | solution.py:370
  760.4 11.6 %collective-permute-start.87 = (bf16[1,64,768]{2,1,0:T(8,128)(2,1)}, bf16[1,64,768]{2,1,0:T(8,128)(2,1)}, u32[]{:S(2)}, u32[]{:S(2)}) collective-permute-start(bf16[1,64,768]{2,1,0:T(8,128)(2,1)} %get-tuple-element.234), channel_id=1, source_target_pairs={{0,3},{1,2},{2,1},{3,0},{4,7},{5,6},{6,5},{7,4},{8,11},{9,10},{10,... | collective-permute-start | bytes 294920 | tf_op jit(solution)/shard_map/ppermute | solution.py:370
  760.4 12.5 %collective-permute-start.88 = (bf16[1,64,768]{2,1,0:T(8,128)(2,1)}, bf16[1,64,768]{2,1,0:T(8,128)(2,1)S(1)}, u32[]{:S(2)}, u32[]{:S(2)}) collective-permute-start(bf16[1,64,768]{2,1,0:T(8,128)(2,1)} %get-tuple-element.233), channel_id=1, source_target_pairs={{0,4},{1,5},{2,6},{3,7},{4,0},{5,1},{6,2},{7,3},{8,12},{9,13},{10,... | collective-permute-start | bytes 294920 | tf_op jit(solution)/shard_map/ppermute | solution.py:370
  762.5 30.9 %all-to-all-start.5 = ((bf16[2,128,2048]{2,0,1:T(2,128)(2,1)}), bf16[2,128,2048]{2,0,1:T(2,128)(2,1)S(1)}, u32[]{:S(2)}, u32[]{:S(2)}) async-start(bf16[2,128,2048]{2,0,1:T(2,128)(2,1)} %copy.132), calls=%async_computation.5 | async-start | bytes 2097152 | tf_op jit(solution)/shard_map/all_to_all | solution.py:541
  767.1 44.9 %reduce-scatter.11.cloned.1.call-start = ((), (), s32[]{:S(2)}) async-start(), calls=%async_computation.18 | async-start | bytes 1310720 | tf_op jit(solution)/shard_map/reduce_scatter | solution.py:507
  767.4 14.7 %collective-permute-start.90 = (bf16[1,64,768]{2,1,0:T(8,128)(2,1)S(1)}, bf16[1,64,768]{2,1,0:T(8,128)(2,1)S(1)}, u32[]{:S(2)}, u32[]{:S(2)}) collective-permute-start(bf16[1,64,768]{2,1,0:T(8,128)(2,1)S(1)} %get-tuple-element.231), channel_id=1, source_target_pairs={{0,6},{1,7},{2,4},{3,5},{4,2},{5,3},{6,0},{7,1},{8,14},{9,15},{10,... | collective-permute-start | bytes 294920 | tf_op jit(solution)/shard_map/ppermute | solution.py:370
  771.0 13.1 %collective-permute-start.91 = (bf16[1,64,768]{2,1,0:T(8,128)(2,1)S(1)}, bf16[1,64,768]{2,1,0:T(8,128)(2,1)S(1)}, u32[]{:S(2)}, u32[]{:S(2)}) collective-permute-start(bf16[1,64,768]{2,1,0:T(8,128)(2,1)S(1)} %get-tuple-element.230), channel_id=1, source_target_pairs={{0,7},{1,6},{2,5},{3,4},{4,3},{5,2},{6,1},{7,0},{8,15},{9,14},{10,... | collective-permute-start | bytes 294920 | tf_op jit(solution)/shard_map/ppermute | solution.py:370
  (84 other events, 1044.1 us)
Sparse Core Ops, SparseCore 0:
  39.5 80.0 all-gather.4
  121.7 148.6 all-gather.6
  272.6 44.1 all-gather.8
  318.8 44.6 all-gather.10
  465.3 74.3 reduce-scatter.4
  542.0 144.9 reduce-scatter.6
  689.4 61.4 reduce-scatter.8
  784.3 27.7 reduce-scatter.10

commit v7 on v6

--- a/solution.py
+++ b/solution.py
@@ -368,8 +368,10 @@
     for apart in range(1, PLANE):
         block = lax.dynamic_index_in_dim(blocks, place ^ apart, 0)
         moved = lax.ppermute(block, GROUP, [(i, i ^ apart) for i in range(PLANE)])
+        if apart == 1:
+            token = moved
         out = lax.dynamic_update_index_in_dim(out, moved, place ^ apart, 0)
-    return out
+    return out, token
 
 
 def group_total(value):
@@ -538,8 +540,11 @@
     qkv_term = weight_term(x_wide, grad_qkv)((output_term,))
     moved, _ = group_scatter(after(grad_input, qkv_term))
     grad_input = grad_hidden + moved
+
+    qkv_rows = owners(after(qkv_term, unit_part))
+    qkv_back, sent = group_exchange(qkv_rows.reshape(PLANE, shard, 3 * own_width), place)
     returned = lax.all_to_all(
-        grad_input.astype(BF).reshape(micro_count, seq_len, width),
+        after(grad_input.astype(BF), sent).reshape(micro_count, seq_len, width),
         ALL,
         split_axis=1,
         concat_axis=0,
@@ -547,10 +552,7 @@
     )
     input_grad = jnp.zeros_like(tokens).at[dealing].set(returned)
 
-    qkv_rows = owners(after(qkv_term, unit_part))
-    qkv_back = group_exchange(qkv_rows.reshape(PLANE, shard, 3 * own_width), place)
-
-    output_part = owners(after(output_term.reshape(groups * shard, width), qkv_back))
+    output_part = owners(after(output_term.reshape(groups * shard, width), qkv_rows))
 
     def heads_in(columns):
         split = columns.reshape(fan, spread, shard, own_heads, head_dim)

time: 830 us -> 824 us (level)
  waiting for transfers between devices: 362 us -> 353 us
where the time goes in v7:
time: 824 us; the launch traced here: 815 us
  waiting for transfers between devices  353 us (43%)
  Pallas kernels  125 us (15%)
  local copies, waits for them, and re-layouts  92 us (11%)
  starting transfers between devices  91.8 us (11%)
  matrix products  67.2 us (8%)
  other arithmetic  59.2 us (7%)
  between operations  16.2 us (2%)
  blocking collectives  9.78 us (1%)
    ppermute x82, waiting for transfers between devices, swap(): return lax.ppermute(value, axis, SWAP)  244 us
    ppermute x82, starting transfers between devices, swap(): return lax.ppermute(value, axis, SWAP)  58.5 us
    all_to_all x1, waiting for transfers between devices, per_device(): lax.all_to_all(outgoing, ALL, split_axis=0, concat_axis=1, tiled=True)  44 us
    unnamed x128, local copies, waits for them, and re-layouts  41.4 us
    pallas_call x1, Pallas kernels, gated_back(): pl.pallas_call(lambda *refs: gated_back_kernel(groups, *refs), grid=(wide...  37.4 us
    dot_general x2, matrix products, weight_term(): lax.dot_general(after(left, *(token if isinstance(token, tuple) else (tok...  32.1 us
    reduce_scatter x4, waiting for transfers between devices, owners(): return lax.psum_scatter(term, REST, scatter_dimension=0, tiled=True)  29.1 us
    pallas_call x1, Pallas kernels, gated(): pl.pallas_call(lambda *refs: gated_kernel(groups, *refs), grid=(wide // b...  24.5 us
  transfers between devices with their start and end apart: 105, of which 62 were waited for; matrix products, arithmetic and copies ran while one was open for 22% of the time, Pallas kernels for 15%

profile of v7, /device:TPU:0, one launch (start us, length us, event | category | flops | bytes accessed | tf_op | source)
XLA Modules:
  0.0 814.7 jit_solution(7909812197770440091)
XLA Ops:
  7.2 3.1 collective-permute-start.9
  10.3 2.6 collective-permute-start.10
  22.1 3.7 all-to-all-start.1
  26.2 4.0 collective-permute-done.10
  30.3 8.2 %all-to-all-done.1 = bf16[8,64,768]{2,1,0:T(8,128)(2,1)S(1)} async-done(((bf16[8,64,768]{2,1,0:T(8,128)(2,1)}), bf16[8,64,768]{2,1,0:T(8,128)(2,1)S(1)}, u32[]{:S(2)}, u32[]{:S(2)}) %all-to-all-start.1) | async-done | bytes 786464 | tf_op jit(solution)/shard_map/all_to_all | solution.py:433
  39.4 2.7 all-to-all-start
  45.9 2.7 pad_maximum_fusion
  48.7 44.0 %all-to-all-done = bf16[64,4,2048]{2,1,0:T(4,128)(2,1)S(1)} async-done(((bf16[64,4,2048]{2,1,0:T(4,128)(2,1)}), bf16[64,4,2048]{2,1,0:T(4,128)(2,1)S(1)}, u32[]{:S(2)}, u32[]{:S(2)}) %all-to-all-start) | async-done | bytes 1048608 | tf_op jit(solution)/shard_map/all_to_all | solution.py:428
  97.8 4.5 all-to-all-start.2
  102.6 15.0 %collective-permute-done = bf16[256,2048]{1,0:T(8,128)(2,1)} collective-permute-done((bf16[256,2048]{1,0:T(8,128)(2,1)S(1)}, bf16[256,2048]{1,0:T(8,128)(2,1)}, u32[]{:S(2)}, u32[]{:S(2)}) %collective-permute-start) | collective-permute-done | bytes 1048608 | tf_op jit(solution)/shard_map/ppermute | solution.py:27
  127.4 3.4 collective-permute-done.2
  138.9 13.0 %project.1 = (f32[2048,768]{1,0:T(8,128)}, f32[2,2048]{1,0:T(2,128)}) custom-call(bf16[2048,2048]{1,0:T(8,128)(2,1)} %constant_dynamic-update-slice_fusion.refs_0_, bf16[2048,768]{1,0:T(8,128)(2,1)} %bitcast.132), custom_call_target="tpu_custom_call" | custom-call | flops 6442450944 | bytes 17825792 | tf_op jit(solution)/shard_map/project/pallas_call | solution.py:78
  159.2 5.0 all_to_all.81
  165.1 15.3 %attend.1 = bf16[2048,256]{1,0:T(8,128)(2,1)} custom-call(f32[2048,768]{1,0:T(8,128)} %get-tuple-element.50.refs_0_, f32[2,2048]{1,0:T(2,128)} %rsqrt.26.refs_1_, f32[2,256]{1,0:T(2,128)} %bitcast.124, f32[128,128]{1,0:T(8,128)} %get-tuple-element.257.refs_3_, f32[128,128]{1,0:T(8,128)} %get-tuple-element.258.refs_4_), custom_call_target="tpu_custom_call" | custom-call | flops 268435456 | bytes 7340032 | tf_op jit(solution)/shard_map/attend/pallas_call | solution.py:191
  180.4 3.6 convolution_convert_fusion.1
  196.2 10.7 %collective-permute-done.18 = bf16[128,2048]{1,0:T(8,128)(2,1)S(1)} collective-permute-done((bf16[128,2048]{1,0:T(8,128)(2,1)S(1)}, bf16[128,2048]{1,0:T(8,128)(2,1)S(1)}, u32[]{:S(2)}, u32[]{:S(2)}) %collective-permute-start.18) | collective-permute-done | bytes 524320 | tf_op jit(solution)/shard_map/ppermute | solution.py:27
  211.8 20.0 %collective-permute-done.19 = bf16[256,2048]{1,0:T(8,128)(2,1)} collective-permute-done((bf16[256,2048]{1,0:T(8,128)(2,1)S(1)}, bf16[256,2048]{1,0:T(8,128)(2,1)}, u32[]{:S(2)}, u32[]{:S(2)}) %collective-permute-start.19) | collective-permute-done | bytes 1048608 | tf_op jit(solution)/shard_map/ppermute | solution.py:27
  231.8 2.5 collective-permute-done.22
  234.3 2.9 multiply_reduce_fusion.5
  240.8 22.3 %collective-permute-done.23 = bf16[256,2048]{1,0:T(8,128)(2,1)S(1)} collective-permute-done((bf16[256,2048]{1,0:T(8,128)(2,1)}, bf16[256,2048]{1,0:T(8,128)(2,1)S(1)}, u32[]{:S(2)}, u32[]{:S(2)}) %collective-permute-start.23) | collective-permute-done | bytes 1048608 | tf_op jit(solution)/shard_map/ppermute | solution.py:27
  270.9 5.4 collective-permute-done.25
  287.3 24.5 %gated.1 = (f32[2048,2048]{1,0:T(8,128)}, bf16[2048,1024]{1,0:T(8,128)(2,1)}) custom-call(bf16[2048,2048]{1,0:T(8,128)(2,1)} %constant_dynamic-update-slice_fusion.10.refs_0_, bf16[2048,2048]{1,0:T(8,128)(2,1)} %all-gather.7.cloned.1.call-done.refs_1_.refs_4_), custom_call_target="tpu_custom_call" | custom-call | flops 17179869184 | bytes 37748736 | tf_op jit(solution)/shard_map/gated/pallas_call | solution.py:300
  311.9 4.9 all-gather.9.cloned.1.call-done.refs_1_
  316.8 7.4 convolution_convert_fusion.4
  331.6 5.3 collective-permute-done.35
  340.2 10.1 %collective-permute-done.36 = bf16[256,1024]{1,0:T(8,128)(2,1)S(1)} collective-permute-done((bf16[256,1024]{1,0:T(8,128)(2,1)S(1)}, bf16[256,1024]{1,0:T(8,128)(2,1)S(1)}, u32[]{:S(2)}, u32[]{:S(2)}) %collective-permute-start.36) | collective-permute-done | bytes 524320 | tf_op jit(solution)/shard_map/ppermute | solution.py:27
  350.3 2.4 collective-permute-done.39
  354.0 9.5 %all-gather.11.cloned.1.call-done.refs_2_ = bf16[1024,1024]{1,0:T(8,128)(2,1)} async-done(((bf16[256,1024]{1,0:T(8,128)(2,1)}), bf16[1024,1024]{1,0:T(8,128)(2,1)}) %all-gather.11.cloned.1.call-update) | async-done | bytes 2097168 | tf_op jit(solution)/shard_map/all_gather | solution.py:460
  363.5 7.4 convolution_convert_fusion.3
  383.0 3.0 collective-permute-done.43
  394.1 7.3 collective-permute-done.44
  401.4 3.6 collective-permute-done.47
  413.7 21.8 %collective-permute-done.48 = bf16[256,2048]{1,0:T(8,128)(2,1)S(1)} collective-permute-done((bf16[256,2048]{1,0:T(8,128)(2,1)S(1)}, bf16[256,2048]{1,0:T(8,128)(2,1)S(1)}, u32[]{:S(2)}, u32[]{:S(2)}) %collective-permute-start.48) | collective-permute-done | bytes 1048608 | tf_op jit(solution)/shard_map/ppermute | solution.py:27
  438.7 9.5 %collective-permute-done.50 = bf16[128,2048]{1,0:T(8,128)(2,1)S(1)} collective-permute-done((bf16[128,2048]{1,0:T(8,128)(2,1)S(1)}, bf16[128,2048]{1,0:T(8,128)(2,1)S(1)}, u32[]{:S(2)}, u32[]{:S(2)}) %collective-permute-start.50) | collective-permute-done | bytes 524320 | tf_op jit(solution)/shard_map/ppermute | solution.py:27
  450.9 3.3 copy-done.27
  454.2 11.0 %convolution_convert_fusion.2 = bf16[1024,2048]{1,0:T(8,128)(2,1)} fusion(bf16[2048,1024]{1,0:T(8,128)(2,1)S(1)} %copy-done.39, bf16[2048,2048]{1,0:T(8,128)(2,1)S(1)} %constant_dynamic-update-slice_fusion.20.refs_0_), kind=kOutput, calls=%fused_computation.5 | convolution fusion | flops 8592031744 | bytes 16777216 | tf_op jit(solution)/shard_map/dot_general | solution.py:498
  465.3 37.4 %gated_back.1 = (bf16[2048,2048]{1,0:T(8,128)(2,1)}, bf16[2048,2048]{1,0:T(8,128)(2,1)}) custom-call(bf16[2048,2048]{1,0:T(8,128)(2,1)} %copy-done.27, bf16[1024,1024]{1,0:T(8,128)(2,1)} %all-gather.9.cloned.1.call-done.refs_1_, bf16[1024,1024]{1,0:T(8,128)(2,1)} %all-gather.11.cloned.1.call-done.refs_2_, f32[2048,2048]{1,0:T(8,128)} %get-tuple-element.58.refs_3_, ...), custom_call_target="tpu_custom_call" | custom-call | flops 25769803776 | bytes 54525952 | tf_op jit(solution)/shard_map/gated_back/pallas_call | solution.py:337
  502.7 4.0 fusion.19
  512.3 5.1 convert_add_fusion.3
  520.4 20.6 %convolution_convert_fusion = bf16[2048,2048]{1,0:T(8,128)(2,1)} fusion(bf16[2048,2048]{1,0:T(8,128)(2,1)S(1)} %copy-done.40, bf16[2048,2048]{1,0:T(8,128)(2,1)S(1)} %bitcast.123), kind=kOutput, calls=%fused_computation.3 | convolution fusion | flops 17184063488 | bytes 25165824 | tf_op jit(solution)/shard_map/dot_general | solution.py:504
  549.3 21.9 %collective-permute-done.62 = bf16[256,2048]{1,0:T(8,128)(2,1)S(1)} collective-permute-done((bf16[256,2048]{1,0:T(8,128)(2,1)S(1)}, bf16[256,2048]{1,0:T(8,128)(2,1)S(1)}, u32[]{:S(2)}, u32[]{:S(2)}) %collective-permute-start.62) | collective-permute-done | bytes 1048608 | tf_op jit(solution)/shard_map/ppermute | solution.py:27
  572.7 4.2 multiply_reduce_fusion.1
  580.0 22.0 %collective-permute-done.65 = bf16[256,2048]{1,0:T(8,128)(2,1)S(1)} collective-permute-done((bf16[256,2048]{1,0:T(8,128)(2,1)S(1)}, bf16[256,2048]{1,0:T(8,128)(2,1)S(1)}, u32[]{:S(2)}, u32[]{:S(2)}) %collective-permute-start.65) | collective-permute-done | bytes 1048608 | tf_op jit(solution)/shard_map/ppermute | solution.py:27
  605.4 9.2 %collective-permute-done.67 = bf16[128,2048]{1,0:T(8,128)(2,1)S(1)} collective-permute-done((bf16[128,2048]{1,0:T(8,128)(2,1)S(1)}, bf16[128,2048]{1,0:T(8,128)(2,1)S(1)}, u32[]{:S(2)}, u32[]{:S(2)}) %collective-permute-start.67) | collective-permute-done | bytes 524320 | tf_op jit(solution)/shard_map/ppermute | solution.py:27
  617.8 2.3 convolution_convert_fusion.7
  620.2 3.4 convolution_convert_fusion.6.refs_5_
  623.5 20.6 %attend_back.1 = (f32[2048,512]{1,0:T(8,128)}, bf16[2048,256]{1,0:T(8,128)(2,1)}, f32[2,2048]{1,0:T(2,128)}, f32[2,256]{1,0:T(2,128)}) custom-call(f32[2048,768]{1,0:T(8,128)} %get-tuple-element.50.refs_0_, f32[2,2048]{1,0:T(2,128)} %rsqrt.26.refs_1_, f32[2,256]{1,0:T(2,128)} %bitcast.125, f32[128,128]{1,0:T(8,128)} %get-tuple-element.257.refs_3_, ...), custom_call_target="tpu_custom_call" | custom-call | flops 671088640 | bytes 13631488 | tf_op jit(solution)/shard_map/attend_back/pallas_call | solution.py:209
  647.1 2.9 collective-permute-done.75
  652.2 4.8 all_to_all.82
  659.0 14.3 %finish.1 = (bf16[2048,768]{1,0:T(8,128)(2,1)}, bf16[2048,2048]{1,0:T(8,128)(2,1)}) custom-call(f32[2048,768]{1,0:T(8,128)} %get-tuple-element.50.refs_0_, f32[2,2048]{1,0:T(2,128)} %rsqrt.26.refs_1_, f32[2,2048]{1,0:T(2,128)} %mul.240.refs_2_, f32[2048,512]{1,0:T(8,128)} %get-tuple-element.67.refs_3_, bf16[2048,256]{1,0:T(8,128)(2,1)} %get-tuple-element.68.refs_4_, ...), custom_call_target="tpu_custom_call" | custom-call | flops 6442450944 | bytes 23068672 | tf_op jit(solution)/shard_map/finish/pallas_call | solution.py:232
  673.3 11.5 %convolution_convert_fusion.5 = bf16[2048,768]{1,0:T(8,128)(2,1)} fusion(bf16[2048,2048]{1,0:T(8,128)(2,1)} %constant_dynamic-update-slice_fusion.refs_0_, bf16[2048,768]{1,0:T(8,128)(2,1)} %get-tuple-element.71), kind=kOutput, calls=%fused_computation.8 | convolution fusion | flops 6444023808 | bytes 14680064 | tf_op jit(solution)/shard_map/dot_general | solution.py:504
  687.1 3.7 fusion.18
  696.4 3.1 convert_add_fusion.1
  703.0 10.7 %collective-permute-done.80 = bf16[128,2048]{1,0:T(8,128)(2,1)S(1)} collective-permute-done((bf16[128,2048]{1,0:T(8,128)(2,1)S(1)}, bf16[128,2048]{1,0:T(8,128)(2,1)S(1)}, u32[]{:S(2)}, u32[]{:S(2)}) %collective-permute-start.80) | collective-permute-done | bytes 524320 | tf_op jit(solution)/shard_map/ppermute | solution.py:27
  720.3 3.7 all-to-all-start.6
  724.1 26.8 %reduce-scatter.9.cloned.1.call-done = bf16[512,768]{1,0:T(8,128)(2,1)} async-done(((bf16[2048,768]{1,0:T(8,128)(2,1)}), bf16[512,768]{1,0:T(8,128)(2,1)}) %reduce-scatter.9.cloned.1.call-update) | async-done | bytes 786448 | tf_op jit(solution)/shard_map/reduce_scatter | solution.py:509
  753.9 3.0 add_convert_fusion
  759.6 5.0 all-to-all-start.5
  766.5 2.8 convert_element_type.411
  769.3 3.4 convert_bitcast_fusion
  772.7 3.0 copy.140
  781.1 2.6 collective-permute-start.90
  787.8 6.2 collective-permute-done.89
  804.0 2.5 scatter_fusion
  (466 shorter events, 212.6 us)
Async XLA Ops:
  7.2 18.9 %collective-permute-start.9 = (bf16[64,2048]{1,0:T(8,128)(2,1)}, bf16[64,2048]{1,0:T(8,128)(2,1)S(1)}, u32[]{:S(2)}, u32[]{:S(2)}) collective-permute-start(bf16[64,2048]{1,0:T(8,128)(2,1)} %param.21), channel_id=1, source_target_pairs={{0,8},{8,16},{16,24},{24,0},{1,9},{9,17},{17,25},{25,1},{2,10},{10... | collective-permute-start | bytes 786440 | tf_op jit(solution)/shard_map/ppermute | solution.py:360
  10.3 19.9 %collective-permute-start.10 = (bf16[64,2048]{1,0:T(8,128)(2,1)}, bf16[64,2048]{1,0:T(8,128)(2,1)S(1)}, u32[]{:S(2)}, u32[]{:S(2)}) collective-permute-start(bf16[64,2048]{1,0:T(8,128)(2,1)} %param.21), channel_id=1, source_target_pairs={{0,16},{8,24},{16,0},{24,8},{1,17},{9,25},{17,1},{25,9},{2,18},{10... | collective-permute-start | bytes 786440 | tf_op jit(solution)/shard_map/ppermute | solution.py:360
  12.9 17.4 %collective-permute-start.11 = (bf16[64,2048]{1,0:T(8,128)(2,1)}, bf16[64,2048]{1,0:T(8,128)(2,1)S(1)}, u32[]{:S(2)}, u32[]{:S(2)}) collective-permute-start(bf16[64,2048]{1,0:T(8,128)(2,1)} %param.21), channel_id=1, source_target_pairs={{0,24},{8,0},{16,8},{24,16},{1,25},{9,1},{17,9},{25,17},{2,26},{10... | collective-permute-start | bytes 786440 | tf_op jit(solution)/shard_map/ppermute | solution.py:360
  22.1 16.3 %all-to-all-start.1 = ((bf16[8,64,768]{2,1,0:T(8,128)(2,1)}), bf16[8,64,768]{2,1,0:T(8,128)(2,1)S(1)}, u32[]{:S(2)}, u32[]{:S(2)}) async-start(bf16[8,64,768]{2,1,0:T(8,128)(2,1)} %pad_maximum_fusion.8), calls=%async_computation.1 | async-start | bytes 1572864 | tf_op jit(solution)/shard_map/all_to_all | solution.py:433
  25.9 113.0 %all-gather.5.cloned.1.call-start = ((), (), s32[]{:S(2)}) async-start(), calls=%async_computation.11 | async-start | bytes 3932160 | tf_op jit(solution)/shard_map/all_gather | solution.py:451
  39.4 53.3 %all-to-all-start = ((bf16[64,4,2048]{2,1,0:T(4,128)(2,1)}), bf16[64,4,2048]{2,1,0:T(4,128)(2,1)S(1)}, u32[]{:S(2)}, u32[]{:S(2)}) async-start(bf16[64,4,2048]{2,1,0:T(4,128)(2,1)} %broadcast_select_fusion), calls=%async_computation | async-start | bytes 2097152 | tf_op jit(solution)/shard_map/all_to_all | solution.py:428
  42.0 245.3 %all-gather.7.cloned.1.call-start = ((), (), s32[]{:S(2)}) async-start(), calls=%async_computation.12 | async-start | bytes 10485760 | tf_op jit(solution)/shard_map/all_gather | solution.py:457
  93.5 24.2 %collective-permute-start = (bf16[256,2048]{1,0:T(8,128)(2,1)S(1)}, bf16[256,2048]{1,0:T(8,128)(2,1)}, u32[]{:S(2)}, u32[]{:S(2)}) collective-permute-start(bf16[256,2048]{1,0:T(8,128)(2,1)S(1)} %reshape.237), channel_id=1, source_target_pairs={{0,2},{2,0},{1,3},{3,1},{4,6},{6,4},{5,7},{7,5},{8,10},{10,8},{9,1... | collective-permute-start | bytes 3145736 | tf_op jit(solution)/shard_map/ppermute | solution.py:27
  95.2 25.6 %collective-permute-start.1 = (bf16[256,2048]{1,0:T(8,128)(2,1)S(1)}, bf16[256,2048]{1,0:T(8,128)(2,1)S(1)}, u32[]{:S(2)}, u32[]{:S(2)}) collective-permute-start(bf16[256,2048]{1,0:T(8,128)(2,1)S(1)} %reshape.237), channel_id=1, source_target_pairs={{0,4},{4,0},{1,5},{5,1},{2,6},{6,2},{3,7},{7,3},{8,12},{12,8},{9,1... | collective-permute-start | bytes 3145736 | tf_op jit(solution)/shard_map/ppermute | solution.py:27
  97.8 58.6 %all-to-all-start.2 = ((bf16[32,2,128]{2,1,0:T(2,128)(2,1)}), bf16[32,2,128]{2,1,0:T(2,128)(2,1)S(1)}, u32[]{:S(2)}, u32[]{:S(2)}) async-start(bf16[32,2,128]{2,1,0:T(2,128)(2,1)} %reshape.308), calls=%async_computation.2 | async-start | bytes 32768 | tf_op jit(solution)/shard_map/all_to_all | solution.py:436
  102.3 214.5 %all-gather.9.cloned.1.call-start = ((), (), s32[]{:S(2)}) async-start(), calls=%async_computation.13 | async-start | bytes 2621440 | tf_op jit(solution)/shard_map/all_gather | solution.py:460
  102.3 31.7 %collective-permute-start.4 = (bf16[256,2048]{1,0:T(8,128)(2,1)S(1)}, bf16[256,2048]{1,0:T(8,128)(2,1)S(1)}, u32[]{:S(2)}, u32[]{:S(2)}) collective-permute-start(bf16[256,2048]{1,0:T(8,128)(2,1)S(1)} %reshape.237), channel_id=1, source_target_pairs={{0,1},{1,0},{2,3},{3,2},{4,5},{5,4},{6,7},{7,6},{8,9},{9,8},{10,11... | collective-permute-start | bytes 3145736 | tf_op jit(solution)/shard_map/ppermute | solution.py:27
  118.7 12.0 %collective-permute-start.2 = (bf16[128,2048]{1,0:T(8,128)(2,1)S(1)}, bf16[128,2048]{1,0:T(8,128)(2,1)S(1)}, u32[]{:S(2)}, u32[]{:S(2)}) collective-permute-start(bf16[128,2048]{1,0:T(8,128)(2,1)S(1)} %slice.395), channel_id=1, source_target_pairs={{0,4},{4,0},{1,5},{5,1},{2,6},{6,2},{3,7},{7,3},{8,12},{12,8},{9,1... | collective-permute-start | bytes 1572872 | tf_op jit(solution)/shard_map/ppermute | solution.py:27
  120.8 11.5 %collective-permute-start.3 = (bf16[128,2048]{1,0:T(8,128)(2,1)S(1)}, bf16[128,2048]{1,0:T(8,128)(2,1)S(1)}, u32[]{:S(2)}, u32[]{:S(2)}) collective-permute-start(bf16[128,2048]{1,0:T(8,128)(2,1)S(1)} %slice.396), channel_id=1, source_target_pairs={{0,2},{2,0},{1,3},{3,1},{4,6},{6,4},{5,7},{7,5},{8,10},{10,8},{9,1... | collective-permute-start | bytes 1572872 | tf_op jit(solution)/shard_map/ppermute | solution.py:27
  123.5 11.6 %collective-permute-start.5 = (bf16[256,2048]{1,0:T(8,128)(2,1)}, bf16[256,2048]{1,0:T(8,128)(2,1)S(1)}, u32[]{:S(2)}, u32[]{:S(2)}) collective-permute-start(bf16[256,2048]{1,0:T(8,128)(2,1)} %collective-permute-done), channel_id=1, source_target_pairs={{0,1},{1,0},{2,3},{3,2},{4,5},{5,4},{6,7},{7,6},{8,9},{9,8},{10,11... | collective-permute-start | bytes 3145736 | tf_op jit(solution)/shard_map/ppermute | solution.py:27
  123.5 12.6 %collective-permute-start.6 = (bf16[256,2048]{1,0:T(8,128)(2,1)S(1)}, bf16[256,2048]{1,0:T(8,128)(2,1)S(1)}, u32[]{:S(2)}, u32[]{:S(2)}) collective-permute-start(bf16[256,2048]{1,0:T(8,128)(2,1)S(1)} %collective-permute-done.1), channel_id=1, source_target_pairs={{0,1},{1,0},{2,3},{3,2},{4,5},{5,4},{6,7},{7,6},{8,9},{9,8},{10,11... | collective-permute-start | bytes 3145736 | tf_op jit(solution)/shard_map/ppermute | solution.py:27
  192.9 14.0 %collective-permute-start.18 = (bf16[128,2048]{1,0:T(8,128)(2,1)S(1)}, bf16[128,2048]{1,0:T(8,128)(2,1)S(1)}, u32[]{:S(2)}, u32[]{:S(2)}) collective-permute-start(bf16[128,2048]{1,0:T(8,128)(2,1)S(1)} %get-tuple-element.227), channel_id=1, source_target_pairs={{0,4},{4,0},{1,5},{5,1},{2,6},{6,2},{3,7},{7,3},{8,12},{12,8},{9,1... | collective-permute-start | bytes 1572872 | tf_op jit(solution)/shard_map/ppermute | solution.py:27
  194.5 17.3 %collective-permute-start.15 = (bf16[256,2048]{1,0:T(8,128)(2,1)}, bf16[256,2048]{1,0:T(8,128)(2,1)}, u32[]{:S(2)}, u32[]{:S(2)}) collective-permute-start(bf16[256,2048]{1,0:T(8,128)(2,1)} %get-tuple-element.197), channel_id=1, source_target_pairs={{0,1},{1,0},{2,3},{3,2},{4,5},{5,4},{6,7},{7,6},{8,9},{9,8},{10,11... | collective-permute-start | bytes 3145736 | tf_op jit(solution)/shard_map/ppermute | solution.py:27
  194.6 14.4 %collective-permute-start.21 = (bf16[128,2048]{1,0:T(8,128)(2,1)S(1)}, bf16[128,2048]{1,0:T(8,128)(2,1)S(1)}, u32[]{:S(2)}, u32[]{:S(2)}) collective-permute-start(bf16[128,2048]{1,0:T(8,128)(2,1)S(1)} %get-tuple-element.228), channel_id=1, source_target_pairs={{0,2},{2,0},{1,3},{3,1},{4,6},{6,4},{5,7},{7,5},{8,10},{10,8},{9,1... | collective-permute-start | bytes 1572872 | tf_op jit(solution)/shard_map/ppermute | solution.py:27
  207.1 24.6 %collective-permute-start.19 = (bf16[256,2048]{1,0:T(8,128)(2,1)S(1)}, bf16[256,2048]{1,0:T(8,128)(2,1)}, u32[]{:S(2)}, u32[]{:S(2)}) collective-permute-start(bf16[256,2048]{1,0:T(8,128)(2,1)S(1)} %pad_maximum_fusion.2), channel_id=1, source_target_pairs={{0,2},{2,0},{1,3},{3,1},{4,6},{6,4},{5,7},{7,5},{8,10},{10,8},{9,1... | collective-permute-start | bytes 3145736 | tf_op jit(solution)/shard_map/ppermute | solution.py:27
  209.2 25.1 %collective-permute-start.22 = (bf16[256,2048]{1,0:T(8,128)(2,1)S(1)}, bf16[256,2048]{1,0:T(8,128)(2,1)}, u32[]{:S(2)}, u32[]{:S(2)}) collective-permute-start(bf16[256,2048]{1,0:T(8,128)(2,1)S(1)} %pad_maximum_fusion.3), channel_id=1, source_target_pairs={{0,4},{4,0},{1,5},{5,1},{2,6},{6,2},{3,7},{7,3},{8,12},{12,8},{9,1... | collective-permute-start | bytes 3145736 | tf_op jit(solution)/shard_map/ppermute | solution.py:27
  211.6 151.9 %all-gather.11.cloned.1.call-start = ((), (), s32[]{:S(2)}) async-start(), calls=%async_computation.14 | async-start | bytes 2621440 | tf_op jit(solution)/shard_map/all_gather | solution.py:460
  238.8 24.2 %collective-permute-start.23 = (bf16[256,2048]{1,0:T(8,128)(2,1)}, bf16[256,2048]{1,0:T(8,128)(2,1)S(1)}, u32[]{:S(2)}, u32[]{:S(2)}) collective-permute-start(bf16[256,2048]{1,0:T(8,128)(2,1)} %get-tuple-element.180), channel_id=1, source_target_pairs={{0,2},{2,0},{1,3},{3,1},{4,6},{6,4},{5,7},{7,5},{8,10},{10,8},{9,1... | collective-permute-start | bytes 3145736 | tf_op jit(solution)/shard_map/ppermute | solution.py:27
  240.3 24.0 %collective-permute-start.24 = (bf16[256,2048]{1,0:T(8,128)(2,1)}, bf16[256,2048]{1,0:T(8,128)(2,1)S(1)}, u32[]{:S(2)}, u32[]{:S(2)}) collective-permute-start(bf16[256,2048]{1,0:T(8,128)(2,1)} %get-tuple-element.180), channel_id=1, source_target_pairs={{0,4},{4,0},{1,5},{5,1},{2,6},{6,2},{3,7},{7,3},{8,12},{12,8},{9,1... | collective-permute-start | bytes 3145736 | tf_op jit(solution)/shard_map/ppermute | solution.py:27
  240.8 40.4 %collective-permute-start.27 = (bf16[256,2048]{1,0:T(8,128)(2,1)}, bf16[256,2048]{1,0:T(8,128)(2,1)}, u32[]{:S(2)}, u32[]{:S(2)}) collective-permute-start(bf16[256,2048]{1,0:T(8,128)(2,1)} %get-tuple-element.180), channel_id=1, source_target_pairs={{0,1},{1,0},{2,3},{3,2},{4,5},{5,4},{6,7},{7,6},{8,9},{9,8},{10,11... | collective-permute-start | bytes 3145736 | tf_op jit(solution)/shard_map/ppermute | solution.py:27
  264.0 12.3 %collective-permute-start.25 = (bf16[128,2048]{1,0:T(8,128)(2,1)}, bf16[128,2048]{1,0:T(8,128)(2,1)}, u32[]{:S(2)}, u32[]{:S(2)}) collective-permute-start(bf16[128,2048]{1,0:T(8,128)(2,1)} %slice.413), channel_id=1, source_target_pairs={{0,4},{4,0},{1,5},{5,1},{2,6},{6,2},{3,7},{7,3},{8,12},{12,8},{9,1... | collective-permute-start | bytes 1572872 | tf_op jit(solution)/shard_map/ppermute | solution.py:27
  265.1 12.2 %collective-permute-start.26 = (bf16[128,2048]{1,0:T(8,128)(2,1)}, bf16[128,2048]{1,0:T(8,128)(2,1)}, u32[]{:S(2)}, u32[]{:S(2)}) collective-permute-start(bf16[128,2048]{1,0:T(8,128)(2,1)} %slice.414), channel_id=1, source_target_pairs={{0,2},{2,0},{1,3},{3,1},{4,6},{6,4},{5,7},{7,5},{8,10},{10,8},{9,1... | collective-permute-start | bytes 1572872 | tf_op jit(solution)/shard_map/ppermute | solution.py:27
  266.8 274.2 %reduce-scatter.5.cloned.1.call-start = ((), (), s32[]{:S(2)}) async-start(), calls=%async_computation.15 | async-start | bytes 5242880 | tf_op jit(solution)/shard_map/reduce_scatter | solution.py:509
  266.9 16.7 %collective-permute-start.28 = (bf16[256,2048]{1,0:T(8,128)(2,1)}, bf16[256,2048]{1,0:T(8,128)(2,1)S(1)}, u32[]{:S(2)}, u32[]{:S(2)}) collective-permute-start(bf16[256,2048]{1,0:T(8,128)(2,1)} %copy-done.22), channel_id=1, source_target_pairs={{0,1},{1,0},{2,3},{3,2},{4,5},{5,4},{6,7},{7,6},{8,9},{9,8},{10,11... | collective-permute-start | bytes 3145736 | tf_op jit(solution)/shard_map/ppermute | solution.py:27
  266.9 17.7 %collective-permute-start.29 = (bf16[256,2048]{1,0:T(8,128)(2,1)S(1)}, bf16[256,2048]{1,0:T(8,128)(2,1)S(1)}, u32[]{:S(2)}, u32[]{:S(2)}) collective-permute-start(bf16[256,2048]{1,0:T(8,128)(2,1)S(1)} %collective-permute-done.24), channel_id=1, source_target_pairs={{0,1},{1,0},{2,3},{3,2},{4,5},{5,4},{6,7},{7,6},{8,9},{9,8},{10,11... | collective-permute-start | bytes 3145736 | tf_op jit(solution)/shard_map/ppermute | solution.py:27
  337.0 13.3 %collective-permute-start.36 = (bf16[256,1024]{1,0:T(8,128)(2,1)S(1)}, bf16[256,1024]{1,0:T(8,128)(2,1)S(1)}, u32[]{:S(2)}, u32[]{:S(2)}) collective-permute-start(bf16[256,1024]{1,0:T(8,128)(2,1)S(1)} %pad_maximum_fusion.9), channel_id=1, source_target_pairs={{0,2},{2,0},{1,3},{3,1},{4,6},{6,4},{5,7},{7,5},{8,10},{10,8},{9,1... | collective-permute-start | bytes 1572872 | tf_op jit(solution)/shard_map/ppermute | solution.py:27
  339.0 13.7 %collective-permute-start.39 = (bf16[256,1024]{1,0:T(8,128)(2,1)S(1)}, bf16[256,1024]{1,0:T(8,128)(2,1)S(1)}, u32[]{:S(2)}, u32[]{:S(2)}) collective-permute-start(bf16[256,1024]{1,0:T(8,128)(2,1)S(1)} %pad_maximum_fusion.10), channel_id=1, source_target_pairs={{0,4},{4,0},{1,5},{5,1},{2,6},{6,2},{3,7},{7,3},{8,12},{12,8},{9,1... | collective-permute-start | bytes 1572872 | tf_op jit(solution)/shard_map/ppermute | solution.py:27
  379.1 15.0 %collective-permute-start.40 = (bf16[256,1024]{1,0:T(8,128)(2,1)}, bf16[256,1024]{1,0:T(8,128)(2,1)}, u32[]{:S(2)}, u32[]{:S(2)}) collective-permute-start(bf16[256,1024]{1,0:T(8,128)(2,1)} %get-tuple-element.204), channel_id=1, source_target_pairs={{0,1},{1,0},{2,3},{3,2},{4,5},{5,4},{6,7},{7,6},{8,9},{9,8},{10,11... | collective-permute-start | bytes 1572872 | tf_op jit(solution)/shard_map/ppermute | solution.py:27
  388.0 13.5 %collective-permute-start.44 = (bf16[256,1024]{1,0:T(8,128)(2,1)}, bf16[256,1024]{1,0:T(8,128)(2,1)}, u32[]{:S(2)}, u32[]{:S(2)}) collective-permute-start(bf16[256,1024]{1,0:T(8,128)(2,1)} %pad_maximum_fusion.11), channel_id=1, source_target_pairs={{0,2},{2,0},{1,3},{3,1},{4,6},{6,4},{5,7},{7,5},{8,10},{10,8},{9,1... | collective-permute-start | bytes 1572872 | tf_op jit(solution)/shard_map/ppermute | solution.py:27
  391.6 13.4 %collective-permute-start.47 = (bf16[256,1024]{1,0:T(8,128)(2,1)}, bf16[256,1024]{1,0:T(8,128)(2,1)}, u32[]{:S(2)}, u32[]{:S(2)}) collective-permute-start(bf16[256,1024]{1,0:T(8,128)(2,1)} %pad_maximum_fusion.12), channel_id=1, source_target_pairs={{0,4},{4,0},{1,5},{5,1},{2,6},{6,2},{3,7},{7,3},{8,12},{12,8},{9,1... | collective-permute-start | bytes 1572872 | tf_op jit(solution)/shard_map/ppermute | solution.py:27
  411.6 23.8 %collective-permute-start.48 = (bf16[256,2048]{1,0:T(8,128)(2,1)S(1)}, bf16[256,2048]{1,0:T(8,128)(2,1)S(1)}, u32[]{:S(2)}, u32[]{:S(2)}) collective-permute-start(bf16[256,2048]{1,0:T(8,128)(2,1)S(1)} %get-tuple-element.256), channel_id=1, source_target_pairs={{0,2},{2,0},{1,3},{3,1},{4,6},{6,4},{5,7},{7,5},{8,10},{10,8},{9,1... | collective-permute-start | bytes 3145736 | tf_op jit(solution)/shard_map/ppermute | solution.py:27
  413.3 24.5 %collective-permute-start.49 = (bf16[256,2048]{1,0:T(8,128)(2,1)S(1)}, bf16[256,2048]{1,0:T(8,128)(2,1)S(1)}, u32[]{:S(2)}, u32[]{:S(2)}) collective-permute-start(bf16[256,2048]{1,0:T(8,128)(2,1)S(1)} %get-tuple-element.256), channel_id=1, source_target_pairs={{0,4},{4,0},{1,5},{5,1},{2,6},{6,2},{3,7},{7,3},{8,12},{12,8},{9,1... | collective-permute-start | bytes 3145736 | tf_op jit(solution)/shard_map/ppermute | solution.py:27
  413.7 35.1 %collective-permute-start.52 = (bf16[256,2048]{1,0:T(8,128)(2,1)S(1)}, bf16[256,2048]{1,0:T(8,128)(2,1)S(1)}, u32[]{:S(2)}, u32[]{:S(2)}) collective-permute-start(bf16[256,2048]{1,0:T(8,128)(2,1)S(1)} %get-tuple-element.256), channel_id=1, source_target_pairs={{0,1},{1,0},{2,3},{3,2},{4,5},{5,4},{6,7},{7,6},{8,9},{9,8},{10,11... | collective-permute-start | bytes 3145736 | tf_op jit(solution)/shard_map/ppermute | solution.py:27
  435.5 12.6 %collective-permute-start.50 = (bf16[128,2048]{1,0:T(8,128)(2,1)S(1)}, bf16[128,2048]{1,0:T(8,128)(2,1)S(1)}, u32[]{:S(2)}, u32[]{:S(2)}) collective-permute-start(bf16[128,2048]{1,0:T(8,128)(2,1)S(1)} %slice.444), channel_id=1, source_target_pairs={{0,4},{4,0},{1,5},{5,1},{2,6},{6,2},{3,7},{7,3},{8,12},{12,8},{9,1... | collective-permute-start | bytes 1572872 | tf_op jit(solution)/shard_map/ppermute | solution.py:27
  438.0 10.9 %collective-permute-start.53 = (bf16[256,2048]{1,0:T(8,128)(2,1)S(1)}, bf16[256,2048]{1,0:T(8,128)(2,1)S(1)}, u32[]{:S(2)}, u32[]{:S(2)}) collective-permute-start(bf16[256,2048]{1,0:T(8,128)(2,1)S(1)} %collective-permute-done.48), channel_id=1, source_target_pairs={{0,1},{1,0},{2,3},{3,2},{4,5},{5,4},{6,7},{7,6},{8,9},{9,8},{10,11... | collective-permute-start | bytes 3145736 | tf_op jit(solution)/shard_map/ppermute | solution.py:27
  438.0 10.9 %collective-permute-start.54 = (bf16[256,2048]{1,0:T(8,128)(2,1)S(1)}, bf16[256,2048]{1,0:T(8,128)(2,1)S(1)}, u32[]{:S(2)}, u32[]{:S(2)}) collective-permute-start(bf16[256,2048]{1,0:T(8,128)(2,1)S(1)} %collective-permute-done.49), channel_id=1, source_target_pairs={{0,1},{1,0},{2,3},{3,2},{4,5},{5,4},{6,7},{7,6},{8,9},{9,8},{10,11... | collective-permute-start | bytes 3145736 | tf_op jit(solution)/shard_map/ppermute | solution.py:27
  465.2 221.8 %reduce-scatter.7.cloned.1.call-start = ((), (), s32[]{:S(2)}) async-start(), calls=%async_computation.16 | async-start | bytes 10485760 | tf_op jit(solution)/shard_map/reduce_scatter | solution.py:509
  518.5 22.6 %collective-permute-start.60 = (bf16[128,2048]{1,0:T(8,128)(2,1)}, bf16[128,2048]{1,0:T(8,128)(2,1)}, u32[]{:S(2)}, u32[]{:S(2)}) collective-permute-start(bf16[128,2048]{1,0:T(8,128)(2,1)} %get-tuple-element.224), channel_id=1, source_target_pairs={{0,2},{2,0},{1,3},{3,1},{4,6},{6,4},{5,7},{7,5},{8,10},{10,8},{9,1... | collective-permute-start | bytes 1572872 | tf_op jit(solution)/shard_map/ppermute | solution.py:27
  519.3 21.7 %collective-permute-start.61 = (bf16[128,2048]{1,0:T(8,128)(2,1)}, bf16[128,2048]{1,0:T(8,128)(2,1)}, u32[]{:S(2)}, u32[]{:S(2)}) collective-permute-start(bf16[128,2048]{1,0:T(8,128)(2,1)} %get-tuple-element.223), channel_id=1, source_target_pairs={{0,4},{4,0},{1,5},{5,1},{2,6},{6,2},{3,7},{7,3},{8,12},{12,8},{9,1... | collective-permute-start | bytes 1572872 | tf_op jit(solution)/shard_map/ppermute | solution.py:27
  541.1 209.8 %reduce-scatter.9.cloned.1.call-start = ((), (), s32[]{:S(2)}) async-start(), calls=%async_computation.17 | async-start | bytes 3932160 | tf_op jit(solution)/shard_map/reduce_scatter | solution.py:509
  545.7 25.5 %collective-permute-start.62 = (bf16[256,2048]{1,0:T(8,128)(2,1)S(1)}, bf16[256,2048]{1,0:T(8,128)(2,1)S(1)}, u32[]{:S(2)}, u32[]{:S(2)}) collective-permute-start(bf16[256,2048]{1,0:T(8,128)(2,1)S(1)} %pad_maximum_fusion.4), channel_id=1, source_target_pairs={{0,2},{2,0},{1,3},{3,1},{4,6},{6,4},{5,7},{7,5},{8,10},{10,8},{9,1... | collective-permute-start | bytes 3145736 | tf_op jit(solution)/shard_map/ppermute | solution.py:27
  547.3 25.3 %collective-permute-start.64 = (bf16[256,2048]{1,0:T(8,128)(2,1)S(1)}, bf16[256,2048]{1,0:T(8,128)(2,1)S(1)}, u32[]{:S(2)}, u32[]{:S(2)}) collective-permute-start(bf16[256,2048]{1,0:T(8,128)(2,1)S(1)} %pad_maximum_fusion.5), channel_id=1, source_target_pairs={{0,4},{4,0},{1,5},{5,1},{2,6},{6,2},{3,7},{7,3},{8,12},{12,8},{9,1... | collective-permute-start | bytes 3145736 | tf_op jit(solution)/shard_map/ppermute | solution.py:27
  577.4 24.6 %collective-permute-start.65 = (bf16[256,2048]{1,0:T(8,128)(2,1)S(1)}, bf16[256,2048]{1,0:T(8,128)(2,1)S(1)}, u32[]{:S(2)}, u32[]{:S(2)}) collective-permute-start(bf16[256,2048]{1,0:T(8,128)(2,1)S(1)} %get-tuple-element.177), channel_id=1, source_target_pairs={{0,2},{2,0},{1,3},{3,1},{4,6},{6,4},{5,7},{7,5},{8,10},{10,8},{9,1... | collective-permute-start | bytes 3145736 | tf_op jit(solution)/shard_map/ppermute | solution.py:27
  579.0 24.6 %collective-permute-start.66 = (bf16[256,2048]{1,0:T(8,128)(2,1)S(1)}, bf16[256,2048]{1,0:T(8,128)(2,1)S(1)}, u32[]{:S(2)}, u32[]{:S(2)}) collective-permute-start(bf16[256,2048]{1,0:T(8,128)(2,1)S(1)} %get-tuple-element.177), channel_id=1, source_target_pairs={{0,4},{4,0},{1,5},{5,1},{2,6},{6,2},{3,7},{7,3},{8,12},{12,8},{9,1... | collective-permute-start | bytes 3145736 | tf_op jit(solution)/shard_map/ppermute | solution.py:27
  580.0 35.9 %collective-permute-start.69 = (bf16[256,2048]{1,0:T(8,128)(2,1)S(1)}, bf16[256,2048]{1,0:T(8,128)(2,1)S(1)}, u32[]{:S(2)}, u32[]{:S(2)}) collective-permute-start(bf16[256,2048]{1,0:T(8,128)(2,1)S(1)} %get-tuple-element.177), channel_id=1, source_target_pairs={{0,1},{1,0},{2,3},{3,2},{4,5},{5,4},{6,7},{7,6},{8,9},{9,8},{10,11... | collective-permute-start | bytes 3145736 | tf_op jit(solution)/shard_map/ppermute | solution.py:27
  602.0 12.6 %collective-permute-start.67 = (bf16[128,2048]{1,0:T(8,128)(2,1)S(1)}, bf16[128,2048]{1,0:T(8,128)(2,1)S(1)}, u32[]{:S(2)}, u32[]{:S(2)}) collective-permute-start(bf16[128,2048]{1,0:T(8,128)(2,1)S(1)} %slice.452), channel_id=1, source_target_pairs={{0,4},{4,0},{1,5},{5,1},{2,6},{6,2},{3,7},{7,3},{8,12},{12,8},{9,1... | collective-permute-start | bytes 1572872 | tf_op jit(solution)/shard_map/ppermute | solution.py:27
  603.7 12.1 %collective-permute-start.68 = (bf16[128,2048]{1,0:T(8,128)(2,1)S(1)}, bf16[128,2048]{1,0:T(8,128)(2,1)S(1)}, u32[]{:S(2)}, u32[]{:S(2)}) collective-permute-start(bf16[128,2048]{1,0:T(8,128)(2,1)S(1)} %slice.453), channel_id=1, source_target_pairs={{0,2},{2,0},{1,3},{3,1},{4,6},{6,4},{5,7},{7,5},{8,10},{10,8},{9,1... | collective-permute-start | bytes 1572872 | tf_op jit(solution)/shard_map/ppermute | solution.py:27
  604.6 11.4 %collective-permute-start.70 = (bf16[256,2048]{1,0:T(8,128)(2,1)S(1)}, bf16[256,2048]{1,0:T(8,128)(2,1)S(1)}, u32[]{:S(2)}, u32[]{:S(2)}) collective-permute-start(bf16[256,2048]{1,0:T(8,128)(2,1)S(1)} %collective-permute-done.65), channel_id=1, source_target_pairs={{0,1},{1,0},{2,3},{3,2},{4,5},{5,4},{6,7},{7,6},{8,9},{9,8},{10,11... | collective-permute-start | bytes 3145736 | tf_op jit(solution)/shard_map/ppermute | solution.py:27
  604.6 11.6 %collective-permute-start.71 = (bf16[256,2048]{1,0:T(8,128)(2,1)S(1)}, bf16[256,2048]{1,0:T(8,128)(2,1)S(1)}, u32[]{:S(2)}, u32[]{:S(2)}) collective-permute-start(bf16[256,2048]{1,0:T(8,128)(2,1)S(1)} %collective-permute-done.66), channel_id=1, source_target_pairs={{0,1},{1,0},{2,3},{3,2},{4,5},{5,4},{6,7},{7,6},{8,9},{9,8},{10,11... | collective-permute-start | bytes 3145736 | tf_op jit(solution)/shard_map/ppermute | solution.py:27
  699.7 14.1 %collective-permute-start.80 = (bf16[128,2048]{1,0:T(8,128)(2,1)S(1)}, bf16[128,2048]{1,0:T(8,128)(2,1)S(1)}, u32[]{:S(2)}, u32[]{:S(2)}) collective-permute-start(bf16[128,2048]{1,0:T(8,128)(2,1)S(1)} %get-tuple-element.221), channel_id=1, source_target_pairs={{0,4},{4,0},{1,5},{5,1},{2,6},{6,2},{3,7},{7,3},{8,12},{12,8},{9,1... | collective-permute-start | bytes 1572872 | tf_op jit(solution)/shard_map/ppermute | solution.py:27
  701.3 51.6 %collective-permute-start.77 = (bf16[256,2048]{1,0:T(8,128)(2,1)}, bf16[256,2048]{1,0:T(8,128)(2,1)}, u32[]{:S(2)}, u32[]{:S(2)}) collective-permute-start(bf16[256,2048]{1,0:T(8,128)(2,1)} %get-tuple-element.183), channel_id=1, source_target_pairs={{0,1},{1,0},{2,3},{3,2},{4,5},{5,4},{6,7},{7,6},{8,9},{9,8},{10,11... | collective-permute-start | bytes 3145736 | tf_op jit(solution)/shard_map/ppermute | solution.py:27
  701.4 15.1 %collective-permute-start.83 = (bf16[128,2048]{1,0:T(8,128)(2,1)S(1)}, bf16[128,2048]{1,0:T(8,128)(2,1)S(1)}, u32[]{:S(2)}, u32[]{:S(2)}) collective-permute-start(bf16[128,2048]{1,0:T(8,128)(2,1)S(1)} %get-tuple-element.222), channel_id=1, source_target_pairs={{0,2},{2,0},{1,3},{3,1},{4,6},{6,4},{5,7},{7,5},{8,10},{10,8},{9,1... | collective-permute-start | bytes 1572872 | tf_op jit(solution)/shard_map/ppermute | solution.py:27
  715.0 38.0 %collective-permute-start.81 = (bf16[256,2048]{1,0:T(8,128)(2,1)}, bf16[256,2048]{1,0:T(8,128)(2,1)}, u32[]{:S(2)}, u32[]{:S(2)}) collective-permute-start(bf16[256,2048]{1,0:T(8,128)(2,1)} %pad_maximum_fusion.6), channel_id=1, source_target_pairs={{0,2},{2,0},{1,3},{3,1},{4,6},{6,4},{5,7},{7,5},{8,10},{10,8},{9,1... | collective-permute-start | bytes 3145736 | tf_op jit(solution)/shard_map/ppermute | solution.py:27
  717.8 36.1 %collective-permute-start.84 = (bf16[256,2048]{1,0:T(8,128)(2,1)}, bf16[256,2048]{1,0:T(8,128)(2,1)}, u32[]{:S(2)}, u32[]{:S(2)}) collective-permute-start(bf16[256,2048]{1,0:T(8,128)(2,1)} %pad_maximum_fusion.7), channel_id=1, source_target_pairs={{0,4},{4,0},{1,5},{5,1},{2,6},{6,2},{3,7},{7,3},{8,12},{12,8},{9,1... | collective-permute-start | bytes 3145736 | tf_op jit(solution)/shard_map/ppermute | solution.py:27
  720.3 39.3 %all-to-all-start.6 = ((f32[32,1,256]{2,1,0:T(1,128)}), f32[32,1,256]{2,1,0:T(1,128)S(1)}, u32[]{:S(2)}, u32[]{:S(2)}) async-start(f32[32,1,256]{2,1,0:T(1,128)} %reshape.310), calls=%async_computation.10 | async-start | bytes 65536 | tf_op jit(solution)/shard_map/all_to_all | solution.py:571
  724.0 75.1 %reduce-scatter.11.cloned.1.call-start = ((), (), s32[]{:S(2)}) async-start(), calls=%async_computation.18 | async-start | bytes 1310720 | tf_op jit(solution)/shard_map/reduce_scatter | solution.py:509
  759.6 42.1 %all-to-all-start.5 = ((bf16[2,128,2048]{2,0,1:T(2,128)(2,1)}), bf16[2,128,2048]{2,0,1:T(2,128)(2,1)}, u32[]{:S(2)}, u32[]{:S(2)}) async-start(bf16[2,128,2048]{2,0,1:T(2,128)(2,1)} %copy.132), calls=%async_computation.8 | async-start | bytes 2097152 | tf_op jit(solution)/shard_map/all_to_all | solution.py:546
  780.9 13.1 %collective-permute-start.89 = (bf16[1,64,768]{2,1,0:T(8,128)(2,1)S(1)}, bf16[1,64,768]{2,1,0:T(8,128)(2,1)S(1)}, u32[]{:S(2)}, u32[]{:S(2)}) collective-permute-start(bf16[1,64,768]{2,1,0:T(8,128)(2,1)S(1)} %get-tuple-element.234), channel_id=1, source_target_pairs={{0,5},{1,4},{2,7},{3,6},{4,1},{5,0},{6,3},{7,2},{8,13},{9,12},{10,... | collective-permute-start | bytes 294920 | tf_op jit(solution)/shard_map/ppermute | solution.py:370
  781.1 12.8 %collective-permute-start.90 = (bf16[1,64,768]{2,1,0:T(8,128)(2,1)S(1)}, bf16[1,64,768]{2,1,0:T(8,128)(2,1)S(1)}, u32[]{:S(2)}, u32[]{:S(2)}) collective-permute-start(bf16[1,64,768]{2,1,0:T(8,128)(2,1)S(1)} %get-tuple-element.233), channel_id=1, source_target_pairs={{0,6},{1,7},{2,4},{3,5},{4,2},{5,3},{6,0},{7,1},{8,14},{9,15},{10,... | collective-permute-start | bytes 294920 | tf_op jit(solution)/shard_map/ppermute | solution.py:370
  (84 other events, 976.0 us)
Sparse Core Ops, SparseCore 0:
  39.5 80.0 all-gather.4
  121.7 148.6 all-gather.6
  272.6 44.1 all-gather.8
  318.8 44.6 all-gather.10
  465.3 74.3 reduce-scatter.4
  542.0 144.9 reduce-scatter.6
  689.4 61.4 reduce-scatter.8
  753.3 37.2 reduce-scatter.10

commit v8 on v7

--- a/solution.py
+++ b/solution.py
@@ -534,11 +534,19 @@
     grad_att = lax.dot_general(grad_out_wide, w_out, contract_last, preferred_element_type=F32).astype(BF)
     scaled, grad_value, dots, gain_term = attend_back(qkv_raw, inverses, gain_heads, tables, own_heads, grad_att)
     scaled = after(scaled, output_term)
+    placed = jnp.zeros((2, spread, own_heads, fan, head_dim), F32)
+    own = gain_term.reshape(2, 1, own_heads, 1, head_dim)
+    placed = lax.dynamic_update_slice(placed, own, (0, lane, 0, lead, 0)).reshape(2, width)
+    gain_terms = jnp.concatenate([placed, jnp.stack([grad_gain_attn, grad_gain_mlp])])
+    gain_terms = gain_terms.reshape(4, total, shard).transpose(1, 0, 2)
+    gain_part = jnp.sum(
+        lax.all_to_all(gain_terms, ALL, split_axis=0, concat_axis=0, tiled=True), axis=0
+    )
     means = group_total(dots) * (1.0 / width)
     grad_qkv, grad_input = finish(qkv_raw, inverses, means, scaled, grad_value, seq_len, own_heads, w_qkv)
 
     qkv_term = weight_term(x_wide, grad_qkv)((output_term,))
-    moved, _ = group_scatter(after(grad_input, qkv_term))
+    moved, _ = group_scatter(after(grad_input, qkv_term, gain_part))
     grad_input = grad_hidden + moved
 
     qkv_rows = owners(after(qkv_term, unit_part))
@@ -562,14 +570,6 @@
     key_part = heads_in(qkv_back[:, :, own_width : 2 * own_width])
     value_part = heads_in(qkv_back[:, :, 2 * own_width :])
 
-    placed = jnp.zeros((2, spread, own_heads, fan, head_dim), F32)
-    own = gain_term.reshape(2, 1, own_heads, 1, head_dim)
-    placed = lax.dynamic_update_slice(placed, own, (0, lane, 0, lead, 0)).reshape(2, width)
-    gain_terms = jnp.concatenate([placed, jnp.stack([grad_gain_attn, grad_gain_mlp])])
-    gain_terms = gain_terms.reshape(4, total, shard).transpose(1, 0, 2)
-    gain_part = jnp.sum(
-        lax.all_to_all(gain_terms, ALL, split_axis=0, concat_axis=0, tiled=True), axis=0
-    )
     return (
         block_out,
         input_grad,

time: 824 us -> 823 us (level)
  blocking collectives: 9.78 us -> 22.2 us
  starting transfers between devices: 91.8 us -> 82.3 us
    all_to_all x0 -> x1, blocking collectives: none -> 12.4 us  [per_device(): lax.all_to_all(gain_terms, ALL, split_axis=0, concat_axis=0, tiled=True)]
  transfers between devices with their start and end apart: 105 -> 104, of which waited for: 62 -> 63; matrix products, arithmetic and copies ran while one was open for 22% -> 22% of each run, Pallas kernels for 15% -> 15%
where the time goes in v8:
time: 823 us; the launch traced here: 815 us
  waiting for transfers between devices  352 us (43%)
  Pallas kernels  125 us (15%)
  local copies, waits for them, and re-layouts  90.6 us (11%)
  starting transfers between devices  82.3 us (10%)
  matrix products  67.1 us (8%)
  other arithmetic  59.2 us (7%)
  blocking collectives  22.2 us (3%)
  between operations  16.2 us (2%)
    ppermute x82, waiting for transfers between devices, swap(): return lax.ppermute(value, axis, SWAP)  249 us
    ppermute x82, starting transfers between devices, swap(): return lax.ppermute(value, axis, SWAP)  54.2 us
    all_to_all x1, waiting for transfers between devices, per_device(): lax.all_to_all(outgoing, ALL, split_axis=0, concat_axis=1, tiled=True)  44 us
    unnamed x128, local copies, waits for them, and re-layouts  39.9 us
    pallas_call x1, Pallas kernels, gated_back(): pl.pallas_call(lambda *refs: gated_back_kernel(groups, *refs), grid=(wide...  37.4 us
    dot_general x2, matrix products, weight_term(): lax.dot_general(after(left, *(token if isinstance(token, tuple) else (tok...  32.1 us
    pallas_call x1, Pallas kernels, gated(): pl.pallas_call(lambda *refs: gated_kernel(groups, *refs), grid=(wide // b...  24.5 us
    reduce_scatter x4, waiting for transfers between devices, owners(): return lax.psum_scatter(term, REST, scatter_dimension=0, tiled=True)  21.4 us
  transfers between devices with their start and end apart: 104, of which 63 were waited for; matrix products, arithmetic and copies ran while one was open for 22% of the time, Pallas kernels for 15%

profile of v8, /device:TPU:0, one launch (start us, length us, event | category | flops | bytes accessed | tf_op | source)
XLA Modules:
  0.0 814.7 jit_solution(11518892055650705701)
XLA Ops:
  7.2 3.1 collective-permute-start.9
  10.3 2.6 collective-permute-start.10
  22.1 3.7 all-to-all-start.1
  26.2 4.0 collective-permute-done.10
  30.3 8.2 %all-to-all-done.1 = bf16[8,64,768]{2,1,0:T(8,128)(2,1)S(1)} async-done(((bf16[8,64,768]{2,1,0:T(8,128)(2,1)}), bf16[8,64,768]{2,1,0:T(8,128)(2,1)S(1)}, u32[]{:S(2)}, u32[]{:S(2)}) %all-to-all-start.1) | async-done | bytes 786464 | tf_op jit(solution)/shard_map/all_to_all | solution.py:433
  39.4 2.7 all-to-all-start
  45.9 2.7 pad_maximum_fusion
  48.7 44.0 %all-to-all-done = bf16[64,4,2048]{2,1,0:T(4,128)(2,1)S(1)} async-done(((bf16[64,4,2048]{2,1,0:T(4,128)(2,1)}), bf16[64,4,2048]{2,1,0:T(4,128)(2,1)S(1)}, u32[]{:S(2)}, u32[]{:S(2)}) %all-to-all-start) | async-done | bytes 1048608 | tf_op jit(solution)/shard_map/all_to_all | solution.py:428
  97.8 4.5 all-to-all-start.2
  102.6 15.0 %collective-permute-done = bf16[256,2048]{1,0:T(8,128)(2,1)} collective-permute-done((bf16[256,2048]{1,0:T(8,128)(2,1)S(1)}, bf16[256,2048]{1,0:T(8,128)(2,1)}, u32[]{:S(2)}, u32[]{:S(2)}) %collective-permute-start) | collective-permute-done | bytes 1048608 | tf_op jit(solution)/shard_map/ppermute | solution.py:27
  127.3 3.4 collective-permute-done.2
  138.8 13.0 %project.1 = (f32[2048,768]{1,0:T(8,128)}, f32[2,2048]{1,0:T(2,128)}) custom-call(bf16[2048,2048]{1,0:T(8,128)(2,1)} %constant_dynamic-update-slice_fusion.refs_0_, bf16[2048,768]{1,0:T(8,128)(2,1)} %bitcast.132), custom_call_target="tpu_custom_call" | custom-call | flops 6442450944 | bytes 17825792 | tf_op jit(solution)/shard_map/project/pallas_call | solution.py:78
  159.3 5.0 all_to_all.81
  165.2 15.3 %attend.1 = bf16[2048,256]{1,0:T(8,128)(2,1)} custom-call(f32[2048,768]{1,0:T(8,128)} %get-tuple-element.50.refs_0_, f32[2,2048]{1,0:T(2,128)} %rsqrt.26.refs_1_, f32[2,256]{1,0:T(2,128)} %bitcast.124, f32[128,128]{1,0:T(8,128)} %get-tuple-element.257.refs_3_, f32[128,128]{1,0:T(8,128)} %get-tuple-element.258.refs_4_), custom_call_target="tpu_custom_call" | custom-call | flops 268435456 | bytes 7340032 | tf_op jit(solution)/shard_map/attend/pallas_call | solution.py:191
  180.5 3.6 convolution_convert_fusion.1
  196.3 10.7 %collective-permute-done.18 = bf16[128,2048]{1,0:T(8,128)(2,1)S(1)} collective-permute-done((bf16[128,2048]{1,0:T(8,128)(2,1)S(1)}, bf16[128,2048]{1,0:T(8,128)(2,1)S(1)}, u32[]{:S(2)}, u32[]{:S(2)}) %collective-permute-start.18) | collective-permute-done | bytes 524320 | tf_op jit(solution)/shard_map/ppermute | solution.py:27
  211.9 20.0 %collective-permute-done.19 = bf16[256,2048]{1,0:T(8,128)(2,1)} collective-permute-done((bf16[256,2048]{1,0:T(8,128)(2,1)S(1)}, bf16[256,2048]{1,0:T(8,128)(2,1)}, u32[]{:S(2)}, u32[]{:S(2)}) %collective-permute-start.19) | collective-permute-done | bytes 1048608 | tf_op jit(solution)/shard_map/ppermute | solution.py:27
  231.9 2.5 collective-permute-done.22
  234.3 2.9 multiply_reduce_fusion.5
  240.9 22.3 %collective-permute-done.23 = bf16[256,2048]{1,0:T(8,128)(2,1)S(1)} collective-permute-done((bf16[256,2048]{1,0:T(8,128)(2,1)}, bf16[256,2048]{1,0:T(8,128)(2,1)S(1)}, u32[]{:S(2)}, u32[]{:S(2)}) %collective-permute-start.23) | collective-permute-done | bytes 1048608 | tf_op jit(solution)/shard_map/ppermute | solution.py:27
  270.9 5.4 collective-permute-done.25
  287.4 24.5 %gated.1 = (f32[2048,2048]{1,0:T(8,128)}, bf16[2048,1024]{1,0:T(8,128)(2,1)}) custom-call(bf16[2048,2048]{1,0:T(8,128)(2,1)} %constant_dynamic-update-slice_fusion.10.refs_0_, bf16[2048,2048]{1,0:T(8,128)(2,1)} %all-gather.7.cloned.1.call-done.refs_1_.refs_4_), custom_call_target="tpu_custom_call" | custom-call | flops 17179869184 | bytes 37748736 | tf_op jit(solution)/shard_map/gated/pallas_call | solution.py:300
  312.0 4.8 all-gather.9.cloned.1.call-done.refs_1_
  316.8 7.4 convolution_convert_fusion.4
  331.6 5.3 collective-permute-done.35
  340.2 10.1 %collective-permute-done.36 = bf16[256,1024]{1,0:T(8,128)(2,1)S(1)} collective-permute-done((bf16[256,1024]{1,0:T(8,128)(2,1)S(1)}, bf16[256,1024]{1,0:T(8,128)(2,1)S(1)}, u32[]{:S(2)}, u32[]{:S(2)}) %collective-permute-start.36) | collective-permute-done | bytes 524320 | tf_op jit(solution)/shard_map/ppermute | solution.py:27
  350.3 2.4 collective-permute-done.39
  354.0 9.7 %all-gather.11.cloned.1.call-done.refs_2_ = bf16[1024,1024]{1,0:T(8,128)(2,1)} async-done(((bf16[256,1024]{1,0:T(8,128)(2,1)}), bf16[1024,1024]{1,0:T(8,128)(2,1)}) %all-gather.11.cloned.1.call-update) | async-done | bytes 2097168 | tf_op jit(solution)/shard_map/all_gather | solution.py:460
  363.7 7.4 convolution_convert_fusion.3
  383.0 3.2 collective-permute-done.43
  394.2 7.5 collective-permute-done.44
  401.6 3.5 collective-permute-done.47
  413.8 21.7 %collective-permute-done.48 = bf16[256,2048]{1,0:T(8,128)(2,1)S(1)} collective-permute-done((bf16[256,2048]{1,0:T(8,128)(2,1)S(1)}, bf16[256,2048]{1,0:T(8,128)(2,1)S(1)}, u32[]{:S(2)}, u32[]{:S(2)}) %collective-permute-start.48) | collective-permute-done | bytes 1048608 | tf_op jit(solution)/shard_map/ppermute | solution.py:27
  438.9 9.3 %collective-permute-done.50 = bf16[128,2048]{1,0:T(8,128)(2,1)S(1)} collective-permute-done((bf16[128,2048]{1,0:T(8,128)(2,1)S(1)}, bf16[128,2048]{1,0:T(8,128)(2,1)S(1)}, u32[]{:S(2)}, u32[]{:S(2)}) %collective-permute-start.50) | collective-permute-done | bytes 524320 | tf_op jit(solution)/shard_map/ppermute | solution.py:27
  450.9 3.3 copy-done.27
  454.2 11.0 %convolution_convert_fusion.2 = bf16[1024,2048]{1,0:T(8,128)(2,1)} fusion(bf16[2048,1024]{1,0:T(8,128)(2,1)S(1)} %copy-done.39, bf16[2048,2048]{1,0:T(8,128)(2,1)S(1)} %constant_dynamic-update-slice_fusion.20.refs_0_), kind=kOutput, calls=%fused_computation.5 | convolution fusion | flops 8592031744 | bytes 16777216 | tf_op jit(solution)/shard_map/dot_general | solution.py:498
  465.3 37.4 %gated_back.1 = (bf16[2048,2048]{1,0:T(8,128)(2,1)}, bf16[2048,2048]{1,0:T(8,128)(2,1)}) custom-call(bf16[2048,2048]{1,0:T(8,128)(2,1)} %copy-done.27, bf16[1024,1024]{1,0:T(8,128)(2,1)} %all-gather.9.cloned.1.call-done.refs_1_, bf16[1024,1024]{1,0:T(8,128)(2,1)} %all-gather.11.cloned.1.call-done.refs_2_, f32[2048,2048]{1,0:T(8,128)} %get-tuple-element.58.refs_3_, ...), custom_call_target="tpu_custom_call" | custom-call | flops 25769803776 | bytes 54525952 | tf_op jit(solution)/shard_map/gated_back/pallas_call | solution.py:337
  502.7 4.0 fusion.19
  512.3 5.1 convert_add_fusion.3
  520.2 20.7 %convolution_convert_fusion = bf16[2048,2048]{1,0:T(8,128)(2,1)} fusion(bf16[2048,2048]{1,0:T(8,128)(2,1)S(1)} %copy-done.40, bf16[2048,2048]{1,0:T(8,128)(2,1)S(1)} %bitcast.123), kind=kOutput, calls=%fused_computation.3 | convolution fusion | flops 17184063488 | bytes 25165824 | tf_op jit(solution)/shard_map/dot_general | solution.py:504
  549.3 21.7 %collective-permute-done.62 = bf16[256,2048]{1,0:T(8,128)(2,1)S(1)} collective-permute-done((bf16[256,2048]{1,0:T(8,128)(2,1)S(1)}, bf16[256,2048]{1,0:T(8,128)(2,1)S(1)}, u32[]{:S(2)}, u32[]{:S(2)}) %collective-permute-start.62) | collective-permute-done | bytes 1048608 | tf_op jit(solution)/shard_map/ppermute | solution.py:27
  572.8 4.2 multiply_reduce_fusion.1
  580.0 22.0 %collective-permute-done.65 = bf16[256,2048]{1,0:T(8,128)(2,1)S(1)} collective-permute-done((bf16[256,2048]{1,0:T(8,128)(2,1)S(1)}, bf16[256,2048]{1,0:T(8,128)(2,1)S(1)}, u32[]{:S(2)}, u32[]{:S(2)}) %collective-permute-start.65) | collective-permute-done | bytes 1048608 | tf_op jit(solution)/shard_map/ppermute | solution.py:27
  605.3 9.1 %collective-permute-done.67 = bf16[128,2048]{1,0:T(8,128)(2,1)S(1)} collective-permute-done((bf16[128,2048]{1,0:T(8,128)(2,1)S(1)}, bf16[128,2048]{1,0:T(8,128)(2,1)S(1)}, u32[]{:S(2)}, u32[]{:S(2)}) %collective-permute-start.67) | collective-permute-done | bytes 524320 | tf_op jit(solution)/shard_map/ppermute | solution.py:27
  620.2 3.4 convolution_convert_fusion.6.refs_5_
  623.6 20.6 %attend_back.1 = (f32[2048,512]{1,0:T(8,128)}, bf16[2048,256]{1,0:T(8,128)(2,1)}, f32[2,2048]{1,0:T(2,128)}, f32[2,256]{1,0:T(2,128)}) custom-call(f32[2048,768]{1,0:T(8,128)} %get-tuple-element.50.refs_0_, f32[2,2048]{1,0:T(2,128)} %rsqrt.26.refs_1_, f32[2,256]{1,0:T(2,128)} %bitcast.125, f32[128,128]{1,0:T(8,128)} %get-tuple-element.257.refs_3_, ...), custom_call_target="tpu_custom_call" | custom-call | flops 671088640 | bytes 13631488 | tf_op jit(solution)/shard_map/attend_back/pallas_call | solution.py:209
  647.0 2.9 collective-permute-done.75
  652.2 4.8 all_to_all.82
  659.1 14.3 %finish.1 = (bf16[2048,768]{1,0:T(8,128)(2,1)}, bf16[2048,2048]{1,0:T(8,128)(2,1)}) custom-call(f32[2048,768]{1,0:T(8,128)} %get-tuple-element.50.refs_0_, f32[2,2048]{1,0:T(2,128)} %rsqrt.26.refs_1_, f32[2,2048]{1,0:T(2,128)} %mul.240.refs_2_, f32[2048,512]{1,0:T(8,128)} %get-tuple-element.67.refs_3_, bf16[2048,256]{1,0:T(8,128)(2,1)} %get-tuple-element.68.refs_4_, ...), custom_call_target="tpu_custom_call" | custom-call | flops 6442450944 | bytes 23068672 | tf_op jit(solution)/shard_map/finish/pallas_call | solution.py:232
  673.4 11.4 %convolution_convert_fusion.5 = bf16[2048,768]{1,0:T(8,128)(2,1)} fusion(bf16[2048,2048]{1,0:T(8,128)(2,1)} %constant_dynamic-update-slice_fusion.refs_0_, bf16[2048,768]{1,0:T(8,128)(2,1)} %get-tuple-element.71), kind=kOutput, calls=%fused_computation.8 | convolution fusion | flops 6444023808 | bytes 14680064 | tf_op jit(solution)/shard_map/dot_general | solution.py:504
  684.8 2.7 reduce-scatter.7.cloned.1.call-done
  688.0 12.4 %all_to_all.83 = f32[32,1,256]{2,1,0:T(1,128)S(1)} all-to-all(f32[32,1,256]{2,1,0:T(1,128)S(1)} %reshape.310), channel_id=1, replica_groups=mesh['z'=4,'m'=1,'y'=2,'x'=2,'c'=2] {'z','m','y','x','c'}, dimensions={0} | all-to-all | bytes 65536 | tf_op jit(solution)/shard_map/all_to_all | solution.py:543
  701.7 3.7 fusion.18
  711.1 3.1 convert_add_fusion.1
  715.8 12.6 %collective-permute-done.80 = bf16[128,2048]{1,0:T(8,128)(2,1)S(1)} collective-permute-done((bf16[128,2048]{1,0:T(8,128)(2,1)S(1)}, bf16[128,2048]{1,0:T(8,128)(2,1)S(1)}, u32[]{:S(2)}, u32[]{:S(2)}) %collective-permute-start.80) | collective-permute-done | bytes 524320 | tf_op jit(solution)/shard_map/ppermute | solution.py:27
  732.1 18.7 %reduce-scatter.9.cloned.1.call-done = bf16[512,768]{1,0:T(8,128)(2,1)} async-done(((bf16[2048,768]{1,0:T(8,128)(2,1)}), bf16[512,768]{1,0:T(8,128)(2,1)}) %reduce-scatter.9.cloned.1.call-update) | async-done | bytes 786448 | tf_op jit(solution)/shard_map/reduce_scatter | solution.py:509
  755.8 3.0 add_convert_fusion
  761.6 3.6 all-to-all-start.6
  765.8 2.8 convert_element_type.411
  768.5 3.4 convert_bitcast_fusion
  772.0 3.0 copy.140
  780.3 2.6 collective-permute-start.90
  786.9 7.0 collective-permute-done.89
  803.9 2.5 scatter_fusion
  (465 shorter events, 210.2 us)
Async XLA Ops:
  7.2 18.9 %collective-permute-start.9 = (bf16[64,2048]{1,0:T(8,128)(2,1)}, bf16[64,2048]{1,0:T(8,128)(2,1)S(1)}, u32[]{:S(2)}, u32[]{:S(2)}) collective-permute-start(bf16[64,2048]{1,0:T(8,128)(2,1)} %param.21), channel_id=1, source_target_pairs={{0,8},{8,16},{16,24},{24,0},{1,9},{9,17},{17,25},{25,1},{2,10},{10... | collective-permute-start | bytes 786440 | tf_op jit(solution)/shard_map/ppermute | solution.py:360
  10.3 19.9 %collective-permute-start.10 = (bf16[64,2048]{1,0:T(8,128)(2,1)}, bf16[64,2048]{1,0:T(8,128)(2,1)S(1)}, u32[]{:S(2)}, u32[]{:S(2)}) collective-permute-start(bf16[64,2048]{1,0:T(8,128)(2,1)} %param.21), channel_id=1, source_target_pairs={{0,16},{8,24},{16,0},{24,8},{1,17},{9,25},{17,1},{25,9},{2,18},{10... | collective-permute-start | bytes 786440 | tf_op jit(solution)/shard_map/ppermute | solution.py:360
  12.9 17.4 %collective-permute-start.11 = (bf16[64,2048]{1,0:T(8,128)(2,1)}, bf16[64,2048]{1,0:T(8,128)(2,1)S(1)}, u32[]{:S(2)}, u32[]{:S(2)}) collective-permute-start(bf16[64,2048]{1,0:T(8,128)(2,1)} %param.21), channel_id=1, source_target_pairs={{0,24},{8,0},{16,8},{24,16},{1,25},{9,1},{17,9},{25,17},{2,26},{10... | collective-permute-start | bytes 786440 | tf_op jit(solution)/shard_map/ppermute | solution.py:360
  22.1 16.3 %all-to-all-start.1 = ((bf16[8,64,768]{2,1,0:T(8,128)(2,1)}), bf16[8,64,768]{2,1,0:T(8,128)(2,1)S(1)}, u32[]{:S(2)}, u32[]{:S(2)}) async-start(bf16[8,64,768]{2,1,0:T(8,128)(2,1)} %pad_maximum_fusion.8), calls=%async_computation.1 | async-start | bytes 1572864 | tf_op jit(solution)/shard_map/all_to_all | solution.py:433
  25.9 113.0 %all-gather.5.cloned.1.call-start = ((), (), s32[]{:S(2)}) async-start(), calls=%async_computation.11 | async-start | bytes 3932160 | tf_op jit(solution)/shard_map/all_gather | solution.py:451
  39.4 53.3 %all-to-all-start = ((bf16[64,4,2048]{2,1,0:T(4,128)(2,1)}), bf16[64,4,2048]{2,1,0:T(4,128)(2,1)S(1)}, u32[]{:S(2)}, u32[]{:S(2)}) async-start(bf16[64,4,2048]{2,1,0:T(4,128)(2,1)} %broadcast_select_fusion), calls=%async_computation | async-start | bytes 2097152 | tf_op jit(solution)/shard_map/all_to_all | solution.py:428
  42.0 245.4 %all-gather.7.cloned.1.call-start = ((), (), s32[]{:S(2)}) async-start(), calls=%async_computation.12 | async-start | bytes 10485760 | tf_op jit(solution)/shard_map/all_gather | solution.py:457
  93.5 24.2 %collective-permute-start = (bf16[256,2048]{1,0:T(8,128)(2,1)S(1)}, bf16[256,2048]{1,0:T(8,128)(2,1)}, u32[]{:S(2)}, u32[]{:S(2)}) collective-permute-start(bf16[256,2048]{1,0:T(8,128)(2,1)S(1)} %reshape.237), channel_id=1, source_target_pairs={{0,2},{2,0},{1,3},{3,1},{4,6},{6,4},{5,7},{7,5},{8,10},{10,8},{9,1... | collective-permute-start | bytes 3145736 | tf_op jit(solution)/shard_map/ppermute | solution.py:27
  95.2 25.6 %collective-permute-start.1 = (bf16[256,2048]{1,0:T(8,128)(2,1)S(1)}, bf16[256,2048]{1,0:T(8,128)(2,1)S(1)}, u32[]{:S(2)}, u32[]{:S(2)}) collective-permute-start(bf16[256,2048]{1,0:T(8,128)(2,1)S(1)} %reshape.237), channel_id=1, source_target_pairs={{0,4},{4,0},{1,5},{5,1},{2,6},{6,2},{3,7},{7,3},{8,12},{12,8},{9,1... | collective-permute-start | bytes 3145736 | tf_op jit(solution)/shard_map/ppermute | solution.py:27
  97.8 58.6 %all-to-all-start.2 = ((bf16[32,2,128]{2,1,0:T(2,128)(2,1)}), bf16[32,2,128]{2,1,0:T(2,128)(2,1)S(1)}, u32[]{:S(2)}, u32[]{:S(2)}) async-start(bf16[32,2,128]{2,1,0:T(2,128)(2,1)} %reshape.308), calls=%async_computation.2 | async-start | bytes 32768 | tf_op jit(solution)/shard_map/all_to_all | solution.py:436
  102.3 214.5 %all-gather.9.cloned.1.call-start = ((), (), s32[]{:S(2)}) async-start(), calls=%async_computation.13 | async-start | bytes 2621440 | tf_op jit(solution)/shard_map/all_gather | solution.py:460
  102.3 31.7 %collective-permute-start.4 = (bf16[256,2048]{1,0:T(8,128)(2,1)S(1)}, bf16[256,2048]{1,0:T(8,128)(2,1)S(1)}, u32[]{:S(2)}, u32[]{:S(2)}) collective-permute-start(bf16[256,2048]{1,0:T(8,128)(2,1)S(1)} %reshape.237), channel_id=1, source_target_pairs={{0,1},{1,0},{2,3},{3,2},{4,5},{5,4},{6,7},{7,6},{8,9},{9,8},{10,11... | collective-permute-start | bytes 3145736 | tf_op jit(solution)/shard_map/ppermute | solution.py:27
  118.7 12.0 %collective-permute-start.2 = (bf16[128,2048]{1,0:T(8,128)(2,1)S(1)}, bf16[128,2048]{1,0:T(8,128)(2,1)S(1)}, u32[]{:S(2)}, u32[]{:S(2)}) collective-permute-start(bf16[128,2048]{1,0:T(8,128)(2,1)S(1)} %slice.395), channel_id=1, source_target_pairs={{0,4},{4,0},{1,5},{5,1},{2,6},{6,2},{3,7},{7,3},{8,12},{12,8},{9,1... | collective-permute-start | bytes 1572872 | tf_op jit(solution)/shard_map/ppermute | solution.py:27
  120.8 11.5 %collective-permute-start.3 = (bf16[128,2048]{1,0:T(8,128)(2,1)S(1)}, bf16[128,2048]{1,0:T(8,128)(2,1)S(1)}, u32[]{:S(2)}, u32[]{:S(2)}) collective-permute-start(bf16[128,2048]{1,0:T(8,128)(2,1)S(1)} %slice.396), channel_id=1, source_target_pairs={{0,2},{2,0},{1,3},{3,1},{4,6},{6,4},{5,7},{7,5},{8,10},{10,8},{9,1... | collective-permute-start | bytes 1572872 | tf_op jit(solution)/shard_map/ppermute | solution.py:27
  123.5 11.6 %collective-permute-start.5 = (bf16[256,2048]{1,0:T(8,128)(2,1)}, bf16[256,2048]{1,0:T(8,128)(2,1)S(1)}, u32[]{:S(2)}, u32[]{:S(2)}) collective-permute-start(bf16[256,2048]{1,0:T(8,128)(2,1)} %collective-permute-done), channel_id=1, source_target_pairs={{0,1},{1,0},{2,3},{3,2},{4,5},{5,4},{6,7},{7,6},{8,9},{9,8},{10,11... | collective-permute-start | bytes 3145736 | tf_op jit(solution)/shard_map/ppermute | solution.py:27
  123.5 12.6 %collective-permute-start.6 = (bf16[256,2048]{1,0:T(8,128)(2,1)S(1)}, bf16[256,2048]{1,0:T(8,128)(2,1)S(1)}, u32[]{:S(2)}, u32[]{:S(2)}) collective-permute-start(bf16[256,2048]{1,0:T(8,128)(2,1)S(1)} %collective-permute-done.1), channel_id=1, source_target_pairs={{0,1},{1,0},{2,3},{3,2},{4,5},{5,4},{6,7},{7,6},{8,9},{9,8},{10,11... | collective-permute-start | bytes 3145736 | tf_op jit(solution)/shard_map/ppermute | solution.py:27
  193.0 14.0 %collective-permute-start.18 = (bf16[128,2048]{1,0:T(8,128)(2,1)S(1)}, bf16[128,2048]{1,0:T(8,128)(2,1)S(1)}, u32[]{:S(2)}, u32[]{:S(2)}) collective-permute-start(bf16[128,2048]{1,0:T(8,128)(2,1)S(1)} %get-tuple-element.227), channel_id=1, source_target_pairs={{0,4},{4,0},{1,5},{5,1},{2,6},{6,2},{3,7},{7,3},{8,12},{12,8},{9,1... | collective-permute-start | bytes 1572872 | tf_op jit(solution)/shard_map/ppermute | solution.py:27
  194.6 17.3 %collective-permute-start.15 = (bf16[256,2048]{1,0:T(8,128)(2,1)}, bf16[256,2048]{1,0:T(8,128)(2,1)}, u32[]{:S(2)}, u32[]{:S(2)}) collective-permute-start(bf16[256,2048]{1,0:T(8,128)(2,1)} %get-tuple-element.197), channel_id=1, source_target_pairs={{0,1},{1,0},{2,3},{3,2},{4,5},{5,4},{6,7},{7,6},{8,9},{9,8},{10,11... | collective-permute-start | bytes 3145736 | tf_op jit(solution)/shard_map/ppermute | solution.py:27
  194.6 14.4 %collective-permute-start.21 = (bf16[128,2048]{1,0:T(8,128)(2,1)S(1)}, bf16[128,2048]{1,0:T(8,128)(2,1)S(1)}, u32[]{:S(2)}, u32[]{:S(2)}) collective-permute-start(bf16[128,2048]{1,0:T(8,128)(2,1)S(1)} %get-tuple-element.228), channel_id=1, source_target_pairs={{0,2},{2,0},{1,3},{3,1},{4,6},{6,4},{5,7},{7,5},{8,10},{10,8},{9,1... | collective-permute-start | bytes 1572872 | tf_op jit(solution)/shard_map/ppermute | solution.py:27
  207.2 24.6 %collective-permute-start.19 = (bf16[256,2048]{1,0:T(8,128)(2,1)S(1)}, bf16[256,2048]{1,0:T(8,128)(2,1)}, u32[]{:S(2)}, u32[]{:S(2)}) collective-permute-start(bf16[256,2048]{1,0:T(8,128)(2,1)S(1)} %pad_maximum_fusion.2), channel_id=1, source_target_pairs={{0,2},{2,0},{1,3},{3,1},{4,6},{6,4},{5,7},{7,5},{8,10},{10,8},{9,1... | collective-permute-start | bytes 3145736 | tf_op jit(solution)/shard_map/ppermute | solution.py:27
  209.3 25.1 %collective-permute-start.22 = (bf16[256,2048]{1,0:T(8,128)(2,1)S(1)}, bf16[256,2048]{1,0:T(8,128)(2,1)}, u32[]{:S(2)}, u32[]{:S(2)}) collective-permute-start(bf16[256,2048]{1,0:T(8,128)(2,1)S(1)} %pad_maximum_fusion.3), channel_id=1, source_target_pairs={{0,4},{4,0},{1,5},{5,1},{2,6},{6,2},{3,7},{7,3},{8,12},{12,8},{9,1... | collective-permute-start | bytes 3145736 | tf_op jit(solution)/shard_map/ppermute | solution.py:27
  211.7 152.0 %all-gather.11.cloned.1.call-start = ((), (), s32[]{:S(2)}) async-start(), calls=%async_computation.14 | async-start | bytes 2621440 | tf_op jit(solution)/shard_map/all_gather | solution.py:460
  238.9 24.2 %collective-permute-start.23 = (bf16[256,2048]{1,0:T(8,128)(2,1)}, bf16[256,2048]{1,0:T(8,128)(2,1)S(1)}, u32[]{:S(2)}, u32[]{:S(2)}) collective-permute-start(bf16[256,2048]{1,0:T(8,128)(2,1)} %get-tuple-element.180), channel_id=1, source_target_pairs={{0,2},{2,0},{1,3},{3,1},{4,6},{6,4},{5,7},{7,5},{8,10},{10,8},{9,1... | collective-permute-start | bytes 3145736 | tf_op jit(solution)/shard_map/ppermute | solution.py:27
  240.4 24.0 %collective-permute-start.24 = (bf16[256,2048]{1,0:T(8,128)(2,1)}, bf16[256,2048]{1,0:T(8,128)(2,1)S(1)}, u32[]{:S(2)}, u32[]{:S(2)}) collective-permute-start(bf16[256,2048]{1,0:T(8,128)(2,1)} %get-tuple-element.180), channel_id=1, source_target_pairs={{0,4},{4,0},{1,5},{5,1},{2,6},{6,2},{3,7},{7,3},{8,12},{12,8},{9,1... | collective-permute-start | bytes 3145736 | tf_op jit(solution)/shard_map/ppermute | solution.py:27
  240.9 40.4 %collective-permute-start.27 = (bf16[256,2048]{1,0:T(8,128)(2,1)}, bf16[256,2048]{1,0:T(8,128)(2,1)}, u32[]{:S(2)}, u32[]{:S(2)}) collective-permute-start(bf16[256,2048]{1,0:T(8,128)(2,1)} %get-tuple-element.180), channel_id=1, source_target_pairs={{0,1},{1,0},{2,3},{3,2},{4,5},{5,4},{6,7},{7,6},{8,9},{9,8},{10,11... | collective-permute-start | bytes 3145736 | tf_op jit(solution)/shard_map/ppermute | solution.py:27
  264.0 12.3 %collective-permute-start.25 = (bf16[128,2048]{1,0:T(8,128)(2,1)}, bf16[128,2048]{1,0:T(8,128)(2,1)}, u32[]{:S(2)}, u32[]{:S(2)}) collective-permute-start(bf16[128,2048]{1,0:T(8,128)(2,1)} %slice.413), channel_id=1, source_target_pairs={{0,4},{4,0},{1,5},{5,1},{2,6},{6,2},{3,7},{7,3},{8,12},{12,8},{9,1... | collective-permute-start | bytes 1572872 | tf_op jit(solution)/shard_map/ppermute | solution.py:27
  265.2 12.2 %collective-permute-start.26 = (bf16[128,2048]{1,0:T(8,128)(2,1)}, bf16[128,2048]{1,0:T(8,128)(2,1)}, u32[]{:S(2)}, u32[]{:S(2)}) collective-permute-start(bf16[128,2048]{1,0:T(8,128)(2,1)} %slice.414), channel_id=1, source_target_pairs={{0,2},{2,0},{1,3},{3,1},{4,6},{6,4},{5,7},{7,5},{8,10},{10,8},{9,1... | collective-permute-start | bytes 1572872 | tf_op jit(solution)/shard_map/ppermute | solution.py:27
  266.9 274.0 %reduce-scatter.5.cloned.1.call-start = ((), (), s32[]{:S(2)}) async-start(), calls=%async_computation.15 | async-start | bytes 5242880 | tf_op jit(solution)/shard_map/reduce_scatter | solution.py:509
  266.9 16.6 %collective-permute-start.28 = (bf16[256,2048]{1,0:T(8,128)(2,1)}, bf16[256,2048]{1,0:T(8,128)(2,1)S(1)}, u32[]{:S(2)}, u32[]{:S(2)}) collective-permute-start(bf16[256,2048]{1,0:T(8,128)(2,1)} %copy-done.22), channel_id=1, source_target_pairs={{0,1},{1,0},{2,3},{3,2},{4,5},{5,4},{6,7},{7,6},{8,9},{9,8},{10,11... | collective-permute-start | bytes 3145736 | tf_op jit(solution)/shard_map/ppermute | solution.py:27
  267.0 17.7 %collective-permute-start.29 = (bf16[256,2048]{1,0:T(8,128)(2,1)S(1)}, bf16[256,2048]{1,0:T(8,128)(2,1)S(1)}, u32[]{:S(2)}, u32[]{:S(2)}) collective-permute-start(bf16[256,2048]{1,0:T(8,128)(2,1)S(1)} %collective-permute-done.24), channel_id=1, source_target_pairs={{0,1},{1,0},{2,3},{3,2},{4,5},{5,4},{6,7},{7,6},{8,9},{9,8},{10,11... | collective-permute-start | bytes 3145736 | tf_op jit(solution)/shard_map/ppermute | solution.py:27
  337.0 13.3 %collective-permute-start.36 = (bf16[256,1024]{1,0:T(8,128)(2,1)S(1)}, bf16[256,1024]{1,0:T(8,128)(2,1)S(1)}, u32[]{:S(2)}, u32[]{:S(2)}) collective-permute-start(bf16[256,1024]{1,0:T(8,128)(2,1)S(1)} %pad_maximum_fusion.9), channel_id=1, source_target_pairs={{0,2},{2,0},{1,3},{3,1},{4,6},{6,4},{5,7},{7,5},{8,10},{10,8},{9,1... | collective-permute-start | bytes 1572872 | tf_op jit(solution)/shard_map/ppermute | solution.py:27
  339.0 13.7 %collective-permute-start.39 = (bf16[256,1024]{1,0:T(8,128)(2,1)S(1)}, bf16[256,1024]{1,0:T(8,128)(2,1)S(1)}, u32[]{:S(2)}, u32[]{:S(2)}) collective-permute-start(bf16[256,1024]{1,0:T(8,128)(2,1)S(1)} %pad_maximum_fusion.10), channel_id=1, source_target_pairs={{0,4},{4,0},{1,5},{5,1},{2,6},{6,2},{3,7},{7,3},{8,12},{12,8},{9,1... | collective-permute-start | bytes 1572872 | tf_op jit(solution)/shard_map/ppermute | solution.py:27
  379.3 14.9 %collective-permute-start.40 = (bf16[256,1024]{1,0:T(8,128)(2,1)}, bf16[256,1024]{1,0:T(8,128)(2,1)}, u32[]{:S(2)}, u32[]{:S(2)}) collective-permute-start(bf16[256,1024]{1,0:T(8,128)(2,1)} %get-tuple-element.204), channel_id=1, source_target_pairs={{0,1},{1,0},{2,3},{3,2},{4,5},{5,4},{6,7},{7,6},{8,9},{9,8},{10,11... | collective-permute-start | bytes 1572872 | tf_op jit(solution)/shard_map/ppermute | solution.py:27
  388.2 13.5 %collective-permute-start.44 = (bf16[256,1024]{1,0:T(8,128)(2,1)}, bf16[256,1024]{1,0:T(8,128)(2,1)}, u32[]{:S(2)}, u32[]{:S(2)}) collective-permute-start(bf16[256,1024]{1,0:T(8,128)(2,1)} %pad_maximum_fusion.11), channel_id=1, source_target_pairs={{0,2},{2,0},{1,3},{3,1},{4,6},{6,4},{5,7},{7,5},{8,10},{10,8},{9,1... | collective-permute-start | bytes 1572872 | tf_op jit(solution)/shard_map/ppermute | solution.py:27
  391.7 13.5 %collective-permute-start.47 = (bf16[256,1024]{1,0:T(8,128)(2,1)}, bf16[256,1024]{1,0:T(8,128)(2,1)}, u32[]{:S(2)}, u32[]{:S(2)}) collective-permute-start(bf16[256,1024]{1,0:T(8,128)(2,1)} %pad_maximum_fusion.12), channel_id=1, source_target_pairs={{0,4},{4,0},{1,5},{5,1},{2,6},{6,2},{3,7},{7,3},{8,12},{12,8},{9,1... | collective-permute-start | bytes 1572872 | tf_op jit(solution)/shard_map/ppermute | solution.py:27
  411.8 23.7 %collective-permute-start.48 = (bf16[256,2048]{1,0:T(8,128)(2,1)S(1)}, bf16[256,2048]{1,0:T(8,128)(2,1)S(1)}, u32[]{:S(2)}, u32[]{:S(2)}) collective-permute-start(bf16[256,2048]{1,0:T(8,128)(2,1)S(1)} %get-tuple-element.256), channel_id=1, source_target_pairs={{0,2},{2,0},{1,3},{3,1},{4,6},{6,4},{5,7},{7,5},{8,10},{10,8},{9,1... | collective-permute-start | bytes 3145736 | tf_op jit(solution)/shard_map/ppermute | solution.py:27
  413.3 24.7 %collective-permute-start.49 = (bf16[256,2048]{1,0:T(8,128)(2,1)S(1)}, bf16[256,2048]{1,0:T(8,128)(2,1)S(1)}, u32[]{:S(2)}, u32[]{:S(2)}) collective-permute-start(bf16[256,2048]{1,0:T(8,128)(2,1)S(1)} %get-tuple-element.256), channel_id=1, source_target_pairs={{0,4},{4,0},{1,5},{5,1},{2,6},{6,2},{3,7},{7,3},{8,12},{12,8},{9,1... | collective-permute-start | bytes 3145736 | tf_op jit(solution)/shard_map/ppermute | solution.py:27
  413.8 35.0 %collective-permute-start.52 = (bf16[256,2048]{1,0:T(8,128)(2,1)S(1)}, bf16[256,2048]{1,0:T(8,128)(2,1)S(1)}, u32[]{:S(2)}, u32[]{:S(2)}) collective-permute-start(bf16[256,2048]{1,0:T(8,128)(2,1)S(1)} %get-tuple-element.256), channel_id=1, source_target_pairs={{0,1},{1,0},{2,3},{3,2},{4,5},{5,4},{6,7},{7,6},{8,9},{9,8},{10,11... | collective-permute-start | bytes 3145736 | tf_op jit(solution)/shard_map/ppermute | solution.py:27
  435.5 12.6 %collective-permute-start.50 = (bf16[128,2048]{1,0:T(8,128)(2,1)S(1)}, bf16[128,2048]{1,0:T(8,128)(2,1)S(1)}, u32[]{:S(2)}, u32[]{:S(2)}) collective-permute-start(bf16[128,2048]{1,0:T(8,128)(2,1)S(1)} %slice.444), channel_id=1, source_target_pairs={{0,4},{4,0},{1,5},{5,1},{2,6},{6,2},{3,7},{7,3},{8,12},{12,8},{9,1... | collective-permute-start | bytes 1572872 | tf_op jit(solution)/shard_map/ppermute | solution.py:27
  438.1 10.4 %collective-permute-start.51 = (bf16[128,2048]{1,0:T(8,128)(2,1)S(1)}, bf16[128,2048]{1,0:T(8,128)(2,1)S(1)}, u32[]{:S(2)}, u32[]{:S(2)}) collective-permute-start(bf16[128,2048]{1,0:T(8,128)(2,1)S(1)} %slice.445), channel_id=1, source_target_pairs={{0,2},{2,0},{1,3},{3,1},{4,6},{6,4},{5,7},{7,5},{8,10},{10,8},{9,1... | collective-permute-start | bytes 1572872 | tf_op jit(solution)/shard_map/ppermute | solution.py:27
  438.1 10.7 %collective-permute-start.53 = (bf16[256,2048]{1,0:T(8,128)(2,1)S(1)}, bf16[256,2048]{1,0:T(8,128)(2,1)S(1)}, u32[]{:S(2)}, u32[]{:S(2)}) collective-permute-start(bf16[256,2048]{1,0:T(8,128)(2,1)S(1)} %collective-permute-done.48), channel_id=1, source_target_pairs={{0,1},{1,0},{2,3},{3,2},{4,5},{5,4},{6,7},{7,6},{8,9},{9,8},{10,11... | collective-permute-start | bytes 3145736 | tf_op jit(solution)/shard_map/ppermute | solution.py:27
  438.2 10.8 %collective-permute-start.54 = (bf16[256,2048]{1,0:T(8,128)(2,1)S(1)}, bf16[256,2048]{1,0:T(8,128)(2,1)S(1)}, u32[]{:S(2)}, u32[]{:S(2)}) collective-permute-start(bf16[256,2048]{1,0:T(8,128)(2,1)S(1)} %collective-permute-done.49), channel_id=1, source_target_pairs={{0,1},{1,0},{2,3},{3,2},{4,5},{5,4},{6,7},{7,6},{8,9},{9,8},{10,11... | collective-permute-start | bytes 3145736 | tf_op jit(solution)/shard_map/ppermute | solution.py:27
  465.2 222.2 %reduce-scatter.7.cloned.1.call-start = ((), (), s32[]{:S(2)}) async-start(), calls=%async_computation.16 | async-start | bytes 10485760 | tf_op jit(solution)/shard_map/reduce_scatter | solution.py:509
  518.5 22.4 %collective-permute-start.60 = (bf16[128,2048]{1,0:T(8,128)(2,1)}, bf16[128,2048]{1,0:T(8,128)(2,1)}, u32[]{:S(2)}, u32[]{:S(2)}) collective-permute-start(bf16[128,2048]{1,0:T(8,128)(2,1)} %get-tuple-element.224), channel_id=1, source_target_pairs={{0,2},{2,0},{1,3},{3,1},{4,6},{6,4},{5,7},{7,5},{8,10},{10,8},{9,1... | collective-permute-start | bytes 1572872 | tf_op jit(solution)/shard_map/ppermute | solution.py:27
  519.2 21.6 %collective-permute-start.61 = (bf16[128,2048]{1,0:T(8,128)(2,1)}, bf16[128,2048]{1,0:T(8,128)(2,1)}, u32[]{:S(2)}, u32[]{:S(2)}) collective-permute-start(bf16[128,2048]{1,0:T(8,128)(2,1)} %get-tuple-element.223), channel_id=1, source_target_pairs={{0,4},{4,0},{1,5},{5,1},{2,6},{6,2},{3,7},{7,3},{8,12},{12,8},{9,1... | collective-permute-start | bytes 1572872 | tf_op jit(solution)/shard_map/ppermute | solution.py:27
  540.9 209.9 %reduce-scatter.9.cloned.1.call-start = ((), (), s32[]{:S(2)}) async-start(), calls=%async_computation.17 | async-start | bytes 3932160 | tf_op jit(solution)/shard_map/reduce_scatter | solution.py:509
  545.5 25.5 %collective-permute-start.62 = (bf16[256,2048]{1,0:T(8,128)(2,1)S(1)}, bf16[256,2048]{1,0:T(8,128)(2,1)S(1)}, u32[]{:S(2)}, u32[]{:S(2)}) collective-permute-start(bf16[256,2048]{1,0:T(8,128)(2,1)S(1)} %pad_maximum_fusion.4), channel_id=1, source_target_pairs={{0,2},{2,0},{1,3},{3,1},{4,6},{6,4},{5,7},{7,5},{8,10},{10,8},{9,1... | collective-permute-start | bytes 3145736 | tf_op jit(solution)/shard_map/ppermute | solution.py:27
  547.6 25.2 %collective-permute-start.64 = (bf16[256,2048]{1,0:T(8,128)(2,1)S(1)}, bf16[256,2048]{1,0:T(8,128)(2,1)S(1)}, u32[]{:S(2)}, u32[]{:S(2)}) collective-permute-start(bf16[256,2048]{1,0:T(8,128)(2,1)S(1)} %pad_maximum_fusion.5), channel_id=1, source_target_pairs={{0,4},{4,0},{1,5},{5,1},{2,6},{6,2},{3,7},{7,3},{8,12},{12,8},{9,1... | collective-permute-start | bytes 3145736 | tf_op jit(solution)/shard_map/ppermute | solution.py:27
  577.5 24.5 %collective-permute-start.65 = (bf16[256,2048]{1,0:T(8,128)(2,1)S(1)}, bf16[256,2048]{1,0:T(8,128)(2,1)S(1)}, u32[]{:S(2)}, u32[]{:S(2)}) collective-permute-start(bf16[256,2048]{1,0:T(8,128)(2,1)S(1)} %get-tuple-element.177), channel_id=1, source_target_pairs={{0,2},{2,0},{1,3},{3,1},{4,6},{6,4},{5,7},{7,5},{8,10},{10,8},{9,1... | collective-permute-start | bytes 3145736 | tf_op jit(solution)/shard_map/ppermute | solution.py:27
  578.9 24.8 %collective-permute-start.66 = (bf16[256,2048]{1,0:T(8,128)(2,1)S(1)}, bf16[256,2048]{1,0:T(8,128)(2,1)S(1)}, u32[]{:S(2)}, u32[]{:S(2)}) collective-permute-start(bf16[256,2048]{1,0:T(8,128)(2,1)S(1)} %get-tuple-element.177), channel_id=1, source_target_pairs={{0,4},{4,0},{1,5},{5,1},{2,6},{6,2},{3,7},{7,3},{8,12},{12,8},{9,1... | collective-permute-start | bytes 3145736 | tf_op jit(solution)/shard_map/ppermute | solution.py:27
  580.0 36.0 %collective-permute-start.69 = (bf16[256,2048]{1,0:T(8,128)(2,1)S(1)}, bf16[256,2048]{1,0:T(8,128)(2,1)S(1)}, u32[]{:S(2)}, u32[]{:S(2)}) collective-permute-start(bf16[256,2048]{1,0:T(8,128)(2,1)S(1)} %get-tuple-element.177), channel_id=1, source_target_pairs={{0,1},{1,0},{2,3},{3,2},{4,5},{5,4},{6,7},{7,6},{8,9},{9,8},{10,11... | collective-permute-start | bytes 3145736 | tf_op jit(solution)/shard_map/ppermute | solution.py:27
  602.0 12.4 %collective-permute-start.67 = (bf16[128,2048]{1,0:T(8,128)(2,1)S(1)}, bf16[128,2048]{1,0:T(8,128)(2,1)S(1)}, u32[]{:S(2)}, u32[]{:S(2)}) collective-permute-start(bf16[128,2048]{1,0:T(8,128)(2,1)S(1)} %slice.452), channel_id=1, source_target_pairs={{0,4},{4,0},{1,5},{5,1},{2,6},{6,2},{3,7},{7,3},{8,12},{12,8},{9,1... | collective-permute-start | bytes 1572872 | tf_op jit(solution)/shard_map/ppermute | solution.py:27
  603.7 12.1 %collective-permute-start.68 = (bf16[128,2048]{1,0:T(8,128)(2,1)S(1)}, bf16[128,2048]{1,0:T(8,128)(2,1)S(1)}, u32[]{:S(2)}, u32[]{:S(2)}) collective-permute-start(bf16[128,2048]{1,0:T(8,128)(2,1)S(1)} %slice.453), channel_id=1, source_target_pairs={{0,2},{2,0},{1,3},{3,1},{4,6},{6,4},{5,7},{7,5},{8,10},{10,8},{9,1... | collective-permute-start | bytes 1572872 | tf_op jit(solution)/shard_map/ppermute | solution.py:27
  604.6 11.5 %collective-permute-start.70 = (bf16[256,2048]{1,0:T(8,128)(2,1)S(1)}, bf16[256,2048]{1,0:T(8,128)(2,1)S(1)}, u32[]{:S(2)}, u32[]{:S(2)}) collective-permute-start(bf16[256,2048]{1,0:T(8,128)(2,1)S(1)} %collective-permute-done.65), channel_id=1, source_target_pairs={{0,1},{1,0},{2,3},{3,2},{4,5},{5,4},{6,7},{7,6},{8,9},{9,8},{10,11... | collective-permute-start | bytes 3145736 | tf_op jit(solution)/shard_map/ppermute | solution.py:27
  604.6 11.6 %collective-permute-start.71 = (bf16[256,2048]{1,0:T(8,128)(2,1)S(1)}, bf16[256,2048]{1,0:T(8,128)(2,1)S(1)}, u32[]{:S(2)}, u32[]{:S(2)}) collective-permute-start(bf16[256,2048]{1,0:T(8,128)(2,1)S(1)} %collective-permute-done.66), channel_id=1, source_target_pairs={{0,1},{1,0},{2,3},{3,2},{4,5},{5,4},{6,7},{7,6},{8,9},{9,8},{10,11... | collective-permute-start | bytes 3145736 | tf_op jit(solution)/shard_map/ppermute | solution.py:27
  687.5 111.6 %reduce-scatter.11.cloned.1.call-start = ((), (), s32[]{:S(2)}) async-start(), calls=%async_computation.18 | async-start | bytes 1310720 | tf_op jit(solution)/shard_map/reduce_scatter | solution.py:509
  714.3 14.1 %collective-permute-start.80 = (bf16[128,2048]{1,0:T(8,128)(2,1)S(1)}, bf16[128,2048]{1,0:T(8,128)(2,1)S(1)}, u32[]{:S(2)}, u32[]{:S(2)}) collective-permute-start(bf16[128,2048]{1,0:T(8,128)(2,1)S(1)} %get-tuple-element.221), channel_id=1, source_target_pairs={{0,4},{4,0},{1,5},{5,1},{2,6},{6,2},{3,7},{7,3},{8,12},{12,8},{9,1... | collective-permute-start | bytes 1572872 | tf_op jit(solution)/shard_map/ppermute | solution.py:27
  714.9 38.0 %collective-permute-start.77 = (bf16[256,2048]{1,0:T(8,128)(2,1)}, bf16[256,2048]{1,0:T(8,128)(2,1)}, u32[]{:S(2)}, u32[]{:S(2)}) collective-permute-start(bf16[256,2048]{1,0:T(8,128)(2,1)} %get-tuple-element.183), channel_id=1, source_target_pairs={{0,1},{1,0},{2,3},{3,2},{4,5},{5,4},{6,7},{7,6},{8,9},{9,8},{10,11... | collective-permute-start | bytes 3145736 | tf_op jit(solution)/shard_map/ppermute | solution.py:27
  715.0 15.1 %collective-permute-start.83 = (bf16[128,2048]{1,0:T(8,128)(2,1)S(1)}, bf16[128,2048]{1,0:T(8,128)(2,1)S(1)}, u32[]{:S(2)}, u32[]{:S(2)}) collective-permute-start(bf16[128,2048]{1,0:T(8,128)(2,1)S(1)} %get-tuple-element.222), channel_id=1, source_target_pairs={{0,2},{2,0},{1,3},{3,1},{4,6},{6,4},{5,7},{7,5},{8,10},{10,8},{9,1... | collective-permute-start | bytes 1572872 | tf_op jit(solution)/shard_map/ppermute | solution.py:27
  729.6 24.9 %collective-permute-start.81 = (bf16[256,2048]{1,0:T(8,128)(2,1)}, bf16[256,2048]{1,0:T(8,128)(2,1)}, u32[]{:S(2)}, u32[]{:S(2)}) collective-permute-start(bf16[256,2048]{1,0:T(8,128)(2,1)} %pad_maximum_fusion.6), channel_id=1, source_target_pairs={{0,2},{2,0},{1,3},{3,1},{4,6},{6,4},{5,7},{7,5},{8,10},{10,8},{9,1... | collective-permute-start | bytes 3145736 | tf_op jit(solution)/shard_map/ppermute | solution.py:27
  731.3 24.6 %collective-permute-start.84 = (bf16[256,2048]{1,0:T(8,128)(2,1)}, bf16[256,2048]{1,0:T(8,128)(2,1)}, u32[]{:S(2)}, u32[]{:S(2)}) collective-permute-start(bf16[256,2048]{1,0:T(8,128)(2,1)} %pad_maximum_fusion.7), channel_id=1, source_target_pairs={{0,4},{4,0},{1,5},{5,1},{2,6},{6,2},{3,7},{7,3},{8,12},{12,8},{9,1... | collective-permute-start | bytes 3145736 | tf_op jit(solution)/shard_map/ppermute | solution.py:27
  761.6 40.0 %all-to-all-start.6 = ((bf16[2,128,2048]{2,0,1:T(2,128)(2,1)}), bf16[2,128,2048]{2,0,1:T(2,128)(2,1)}, u32[]{:S(2)}, u32[]{:S(2)}) async-start(bf16[2,128,2048]{2,0,1:T(2,128)(2,1)} %copy.134), calls=%async_computation.9 | async-start | bytes 2097152 | tf_op jit(solution)/shard_map/all_to_all | solution.py:554
  780.0 13.9 %collective-permute-start.89 = (bf16[1,64,768]{2,1,0:T(8,128)(2,1)S(1)}, bf16[1,64,768]{2,1,0:T(8,128)(2,1)S(1)}, u32[]{:S(2)}, u32[]{:S(2)}) collective-permute-start(bf16[1,64,768]{2,1,0:T(8,128)(2,1)S(1)} %get-tuple-element.234), channel_id=1, source_target_pairs={{0,5},{1,4},{2,7},{3,6},{4,1},{5,0},{6,3},{7,2},{8,13},{9,12},{10,... | collective-permute-start | bytes 294920 | tf_op jit(solution)/shard_map/ppermute | solution.py:370
  780.3 13.6 %collective-permute-start.90 = (bf16[1,64,768]{2,1,0:T(8,128)(2,1)S(1)}, bf16[1,64,768]{2,1,0:T(8,128)(2,1)S(1)}, u32[]{:S(2)}, u32[]{:S(2)}) collective-permute-start(bf16[1,64,768]{2,1,0:T(8,128)(2,1)S(1)} %get-tuple-element.233), channel_id=1, source_target_pairs={{0,6},{1,7},{2,4},{3,5},{4,2},{5,3},{6,0},{7,1},{8,14},{9,15},{10,... | collective-permute-start | bytes 294920 | tf_op jit(solution)/shard_map/ppermute | solution.py:370
  (83 other events, 952.3 us)
Sparse Core Ops, SparseCore 0:
  39.5 80.0 all-gather.4
  121.7 148.6 all-gather.6
  272.6 44.1 all-gather.8
  318.8 44.8 all-gather.10
  465.3 74.7 reduce-scatter.4
  542.4 144.9 reduce-scatter.6
  689.8 60.9 reduce-scatter.8
  753.2 36.5 reduce-scatter.10
